TPU v7x, 512 devices: a whole 4x8x8 slice. The times are simulated.
512 devices in a mesh: mp: 2 (over z_lo), blk: 32 (over x, y), tok: 8 (over z_hi, core).
Axes of the slice: x: 4, y: 8, z: 8 (z_hi: 4, z_lo: 2; z = z_hi * 2 + z_lo), core: 2. Of those that a mesh axis runs over, the one named last changes fastest.
Arguments:
- inputs: bfloat16 [2, 1024, 28672], P('mp', 'tok', 'blk'), may hold values from -1.1953125 to 1.1953125
- down_weight: bfloat16 [2, 512, 28672], P('mp', None, 'blk'), may hold values from -0.03125 to 0.03125
Outputs:
- denominator: float32 [1024, 28672], P('blk', 'tok')
- numerator: float32 [1024, 512], P('blk', 'tok')
All inputs are finite; a program needn't handle non-finite values.
Results may differ from a plain program's by a relative error of at most 0.0003.
Values may be sent and summed in bfloat16 or wider, within the bound.
No kernel may reach another device: no remote copies, remote signals or barrier semaphores. Data moves between devices by JAX's collectives and lax.ppermute only.
A program may use at most 64 MiB of HBM per device.

v0:
```python
import jax
import jax.numpy as jnp
from jax import lax
from jax.sharding import PartitionSpec as P

DIN = 28672
COLS = 512
ROW_DEV = 32


OFF_SCALE = 0.9


def local(inputs, down_weight):
    x_local = inputs[0]
    w_local = down_weight[0]
    span_width = x_local.shape[1]
    x_rows = x_local[:, :ROW_DEV]
    blk_index = lax.axis_index("blk")
    tok_index = lax.axis_index("tok")
    tok_count = lax.axis_size("tok")
    col_share = DIN // tok_count
    col_parts = COLS // tok_count
    partial_value = lax.dot_general(
        x_rows,
        lax.all_gather(x_local, "blk", axis=1, tiled=True),
        (((0,), (0,)), ((), ())),
        preferred_element_type=jnp.float32,
    )
    gram_panel = lax.psum(partial_value, "tok")
    col_ids = lax.broadcasted_iota(jnp.int32, gram_panel.shape, 1)
    row_ids = lax.broadcasted_iota(jnp.int32, gram_panel.shape, 0)
    on_diag = col_ids == blk_index * span_width + row_ids
    reduced = jnp.where(on_diag, gram_panel, OFF_SCALE * gram_panel)
    denominator = lax.dynamic_slice_in_dim(reduced, tok_index * col_share, col_share, 1)
    w_group = lax.dynamic_slice_in_dim(w_local, tok_index * col_parts, col_parts, 0)
    numerator = lax.dot_general(
        reduced,
        lax.all_gather(w_group, "blk", axis=1, tiled=True).astype(jnp.float32),
        (((1,), (1,)), ((), ())),
        precision=lax.Precision.HIGHEST,
        preferred_element_type=jnp.float32,
    )
    denominator, numerator = lax.psum((denominator, numerator), "mp")
    return (denominator, numerator)


def solution(mesh):
    placed = (P("mp", "tok", "blk"), P("mp", None, "blk"))
    return jax.shard_map(
        local,
        mesh=mesh,
        in_specs=placed,
        out_specs=(P("blk", "tok"), P("blk", "tok")),
        check_vma=False,
    )
```

profile of v0, /device:TPU:1, one launch (start us, length us, event | category | flops | bytes accessed | tf_op | source)
XLA Modules:
  0.0 373.1 jit_solution(2469359406197091980)
XLA Ops:
  7.2 0.0 copy-start
  7.2 0.0 all-gather.5.cloned.1.call-start
  7.2 0.7 all-gather.5.cloned.1.call-update
  7.9 0.0 all-reduce.3.cloned.1.call-start
  8.0 106.5 %all-gather.5.cloned.1.call-done = bf16[1,128,28672]{2,1,0:T(8,128)(2,1)} async-done(((bf16[1,128,896]{2,1,0:T(8,128)(2,1)}), bf16[1,128,28672]{2,1,0:T(8,128)(2,1)}) %all-gather.5.cloned.1.call-update) | async-done | bytes 7340048 | tf_op jit(solution)/shard_map/all_gather | solution.py:26
  114.4 6.1 %fusion = f32[32,28672]{1,0:T(8,128)} fusion(bf16[1,128,28672]{2,1,0:T(8,128)(2,1)} %all-gather.5.cloned.1.call-done, bf16[128,896]{1,0:T(8,128)(2,1)} %bitcast.8), kind=kOutput, calls=%fused_computation | convolution fusion | flops 234881024 | bytes 11042816 | tf_op jit(solution)/shard_map/dot_general | solution.py:24
  120.6 0.0 all-reduce.3.cloned.1.call-update
  120.6 0.0 all-gather.7.cloned.1.call-start
  120.7 0.0 copy-done
  120.7 0.7 constant_dynamic-slice_fusion
  121.3 0.0 all-gather.7.cloned.1.call-update
  121.4 0.0 all-reduce.5.cloned.1.call-start
  121.4 107.3 %all-reduce.3.cloned.1.call-done = f32[32,28672]{1,0:T(8,128)} async-done(((f32[32,28672]{1,0:T(8,128)}), f32[32,28672]{1,0:T(8,128)}) %all-reduce.3.cloned.1.call-update) | async-done | bytes 3670032 | tf_op jit(solution)/shard_map/psum | solution.py:30
  228.8 2.5 multiply_select_fusion
  231.3 0.0 copy-start.1
  231.3 1.8 copy-done.1
  233.1 0.8 constant_dynamic-slice_fusion.1
  233.9 0.0 all-reduce.5.cloned.1.call-update
  234.0 82.6 %all-gather.7.cloned.1.call-done = bf16[1,64,28672]{2,1,0:T(8,128)(2,1)} async-done(((bf16[1,64,896]{2,1,0:T(8,128)(2,1)}), bf16[1,64,28672]{2,1,0:T(8,128)(2,1)}) %all-gather.7.cloned.1.call-update) | async-done | bytes 3670032 | tf_op jit(solution)/shard_map/all_gather | solution.py:39
  316.6 6.1 %fusion.2 = f32[32,64]{1,0:T(8,128)S(1)} fusion(f32[32,28672]{1,0:T(8,128)} %copy-done.1, bf16[1,64,28672]{2,1,0:T(8,128)(2,1)} %all-gather.7.cloned.1.call-done), kind=kOutput, calls=%fused_computation.3 | convolution fusion | flops 704643072 | bytes 7348224 | tf_op jit(solution)/shard_map/dot_general | solution.py:37
  322.7 6.9 %psum.23 = f32[32,64]{1,0:T(8,128)} all-reduce(f32[32,64]{1,0:T(8,128)S(1)} %fusion.2), channel_id=1, replica_groups=mesh['mp'=2,'blk'=32,'tok'=8] {'mp'}, use_global_device_ids=true, to_apply=%region_2.3 | all-reduce | flops 2048 | bytes 16384 | tf_op jit(solution)/shard_map/psum | solution.py:44
  329.6 35.2 %all-reduce.5.cloned.1.call-done = f32[32,3584]{1,0:T(8,128)} async-done(((f32[32,3584]{1,0:T(8,128)}), f32[32,3584]{1,0:T(8,128)}) %all-reduce.5.cloned.1.call-update) | async-done | bytes 458768 | tf_op jit(solution)/shard_map/psum | solution.py:44
  364.8 1.8 copy.6
  (1 shorter events, 0.0 us)
Async XLA Ops:
  7.2 113.5 %copy-start = (bf16[1,512,896]{2,1,0:T(8,128)(2,1)S(1)}, bf16[1,512,896]{2,1,0:T(8,128)(2,1)}, u32[]{:S(2)}) copy-start(bf16[1,512,896]{2,1,0:T(8,128)(2,1)} %param.3) | copy-start | bytes 2752516
  7.2 107.3 %all-gather.5.cloned.1.call-start = ((), (), s32[]{:S(2)}) async-start(), calls=%async_computation.2 | async-start | bytes 7569408 | tf_op jit(solution)/shard_map/all_gather | solution.py:26
  7.9 220.9 %all-reduce.3.cloned.1.call-start = ((), (), s32[]{:S(2)}) async-start(), calls=%async_computation | async-start | bytes 7340032 | tf_op jit(solution)/shard_map/psum | solution.py:30
  120.6 196.0 %all-gather.7.cloned.1.call-start = ((), (), s32[]{:S(2)}) async-start(), calls=%async_computation.3 | async-start | bytes 3784704 | tf_op jit(solution)/shard_map/all_gather | solution.py:39
  121.4 243.4 %all-reduce.5.cloned.1.call-start = ((), (), s32[]{:S(2)}) async-start(), calls=%async_computation.1 | async-start | bytes 917504 | tf_op jit(solution)/shard_map/psum | solution.py:44
  231.3 1.8 copy-start.1
Sparse Core Ops, SparseCore 0:
  11.2 103.2 all-gather.4
  120.7 107.9 all-reduce.2
  232.0 84.5 all-gather.6
  319.9 44.7 all-reduce.4
where the time goes:
time: 373 us
  waiting for transfers between devices  332 us (89%)
  between operations  13.8 us (4%)
  matrix products  12.3 us (3%)
  blocking collectives  6.89 us (2%)
  local copies, waits for them, and re-layouts  5.12 us (1%)
    psum x1, waiting for transfers between devices, local(): gram_panel = lax.psum(partial_value, 'tok')  107 us
    all_gather x1, waiting for transfers between devices, local(): lax.all_gather(x_local, 'blk', axis=1, tiled=True)  106 us
    all_gather x1, waiting for transfers between devices, local(): lax.all_gather(w_group, 'blk', axis=1, tiled=True).astype(jnp.float32)  82.6 us
    psum x1, waiting for transfers between devices, local(): denominator, numerator = lax.psum((denominator, numerator), 'mp')  35.2 us
  transfers between devices with their start and end apart: 4, of which 4 were waited for; matrix products, arithmetic and copies ran while one was open for 3% of the time, Pallas kernels for 0%

commit v1 on v0

v1 whole, which is shorter than its diff:
```python
import jax
import jax.numpy as jnp
from jax import lax
from jax.sharding import PartitionSpec as P

ROW_DEV = 32


OFF_SCALE = 0.9


def local(inputs, down_weight):
    x_local = inputs[0]
    w_local = down_weight[0]
    span_width = x_local.shape[1]
    blk_index = lax.axis_index("blk")
    tok_index = lax.axis_index("tok")
    blk_count = lax.axis_size("blk")
    tok_count = lax.axis_size("tok")
    group = blk_count // tok_count
    group_rows = group * ROW_DEV

    x_win = x_local[:, :ROW_DEV]

    y_part = lax.dot_general(
        x_local, w_local, (((1,), (1,)), ((), ())), preferred_element_type=jnp.float32
    )
    y_full = lax.psum(y_part, "blk")
    win_f = x_win.astype(jnp.float32)
    cross = lax.dot_general(
        win_f, y_full, (((0,), (0,)), ((), ())),
        precision=lax.Precision.HIGHEST, preferred_element_type=jnp.float32,
    )
    diag_part = jnp.sum(win_f * win_f, axis=0)
    w_diag = w_local[:, :ROW_DEV].astype(jnp.float32).T
    num_part = OFF_SCALE * cross + (1.0 - OFF_SCALE) * diag_part[:, None] * w_diag
    numerator = lax.psum_scatter(num_part, "tok", scatter_dimension=1, tiled=True)
    numerator = lax.psum(numerator, "mp")

    x_full = lax.all_gather(x_local, "tok", axis=0, tiled=True)
    win_all = lax.all_gather(x_win, "blk", axis=1, tiled=True)
    win_mine = lax.all_to_all(win_all, "tok", 1, 0, tiled=True)
    gram = lax.dot_general(
        win_mine, x_full, (((0,), (0,)), ((), ())), preferred_element_type=jnp.float32
    )
    gram = lax.psum(gram, "mp")
    row_ids = lax.broadcasted_iota(jnp.int32, gram.shape, 0)
    col_ids = lax.broadcasted_iota(jnp.int32, gram.shape, 1)
    row_blk = tok_index * group + row_ids // ROW_DEV
    on_diag = (row_blk == blk_index) & (col_ids == row_ids % ROW_DEV)
    reduced = jnp.where(on_diag, gram, OFF_SCALE * gram)

    pieces = []
    for d in range(group):
        perm = []
        for b in range(blk_count):
            for t in range(tok_count):
                s = (b % group + d) % group
                dest = (t * group + s) * tok_count + b // group
                perm.append((b * tok_count + t, dest))
        s_me = (blk_index % group + d) % group
        piece = lax.dynamic_slice_in_dim(reduced, s_me * ROW_DEV, ROW_DEV, 0)
        pieces.append(lax.ppermute(piece, ("blk", "tok"), perm))
    stacked = jnp.stack(pieces)
    c = blk_index % group
    order = (c - jnp.arange(group)) % group
    denominator = jnp.take(stacked, order, axis=0)
    denominator = jnp.transpose(denominator, (1, 0, 2)).reshape(ROW_DEV, group * span_width)
    return (denominator, numerator)


def solution(mesh):
    placed = (P("mp", "tok", "blk"), P("mp", None, "blk"))
    return jax.shard_map(
        local,
        mesh=mesh,
        in_specs=placed,
        out_specs=(P("blk", "tok"), P("blk", "tok")),
        check_vma=False,
    )
```

time: 373 us -> 332 us (0.89)
  the two profiles are of different devices: /device:TPU:1 before, /device:TPU:21 now
where the time goes in v1:
time: 332 us; the launch traced here: 331 us
  waiting for transfers between devices  203 us (61%)
  starting transfers between devices  52.1 us (16%)
  blocking collectives  47.4 us (14%)
  between operations  15.8 us (5%)
  matrix products  6.34 us (2%)
  local copies, waits for them, and re-layouts  4.89 us (1%)
    psum x1, waiting for transfers between devices, local(): y_full = lax.psum(y_part, 'blk')  135 us
    psum x1, waiting for transfers between devices, local(): gram = lax.psum(gram, 'mp')  50 us
    all_gather x1, blocking collectives, local(): win_all = lax.all_gather(x_win, 'blk', axis=1, tiled=True)  41.6 us
    ppermute x4, starting transfers between devices, local(): pieces.append(lax.ppermute(piece, ('blk', 'tok'), perm))  30.6 us
    all_to_all x1, starting transfers between devices, local(): win_mine = lax.all_to_all(win_all, 'tok', 1, 0, tiled=True)  21.4 us
    all_to_all x1, waiting for transfers between devices, local(): win_mine = lax.all_to_all(win_all, 'tok', 1, 0, tiled=True)  9.42 us
    ppermute x4, waiting for transfers between devices, local(): pieces.append(lax.ppermute(piece, ('blk', 'tok'), perm))  7.48 us
  transfers between devices with their start and end apart: 9, of which 4 were waited for; matrix products, arithmetic and copies ran while one was open for 3% of the time, Pallas kernels for 0%

profile of v1, /device:TPU:21, one launch (start us, length us, event | category | flops | bytes accessed | tf_op | source)
XLA Modules:
  0.0 331.1 jit_solution(1614253673475882280)
XLA Ops:
  8.0 0.0 all-gather.3.cloned.1.call-start
  8.0 0.7 all-gather.3.cloned.1.call-update
  8.7 1.1 copy.11
  9.9 41.6 %all_gather.6 = bf16[128,1024]{0,1:T(8,128)(2,1)} all-gather(bf16[128,32]{0,1:T(8,128)(2,1)S(1)} %slice.10), channel_id=1, replica_groups=mesh['mp'=2,'blk'=32,'tok'=8] {'blk'}, dimensions={1}, use_global_device_ids=true | all-gather | bytes 270336 | tf_op jit(solution)/shard_map/all_gather | solution.py:41
  51.5 21.4 %all-to-all-start = ((bf16[128,8,128]{0,2,1:T(8,128)(2,1)}), bf16[128,8,128]{0,2,1:T(8,128)(2,1)S(1)}, u32[]{:S(2)}, u32[]{:S(2)}) async-start(bf16[128,8,128]{0,2,1:T(8,128)(2,1)} %bitcast.1), calls=%async_computation | async-start | bytes 524288 | tf_op jit(solution)/shard_map/all_to_all | solution.py:42
  72.8 0.0 all-reduce.5.cloned.1.call-start
  72.8 2.4 fusion.4
  75.3 0.0 all-reduce.5.cloned.1.call-update
  75.3 0.0 all-reduce.3.cloned.1.call-start
  75.4 0.0 copy-start
  75.5 0.1 multiply_reduce_fusion
  75.6 9.4 %all-to-all-done = bf16[128,8,128]{0,2,1:T(8,128)(2,1)S(1)} async-done(((bf16[128,8,128]{0,2,1:T(8,128)(2,1)}), bf16[128,8,128]{0,2,1:T(8,128)(2,1)S(1)}, u32[]{:S(2)}, u32[]{:S(2)}) %all-to-all-start) | async-done | bytes 262176 | tf_op jit(solution)/shard_map/all_to_all | solution.py:42
  85.0 0.2 copy.12
  85.2 0.0 all-gather.3.cloned.1.call-done
  85.2 2.7 fusion
  88.0 0.0 all-reduce.3.cloned.1.call-update
  88.0 0.0 reduce-scatter.4.cloned.1.call-start
  88.1 0.0 copy-done
  88.1 0.5 copy.14
  88.7 135.4 %all-reduce.5.cloned.1.call-done = f32[128,512]{1,0:T(8,128)} async-done(((f32[128,512]{1,0:T(8,128)}), f32[128,512]{1,0:T(8,128)}) %all-reduce.5.cloned.1.call-update) | async-done | bytes 262160 | tf_op jit(solution)/shard_map/psum | solution.py:28
  224.1 1.2 fusion.3
  225.2 0.8 copy.15
  226.1 0.0 reduce-scatter.4.cloned.1.call-update
  226.1 50.0 %all-reduce.3.cloned.1.call-done = f32[128,896]{1,0:T(8,128)} async-done(((f32[128,896]{1,0:T(8,128)}), f32[128,896]{1,0:T(8,128)}) %all-reduce.3.cloned.1.call-update) | async-done | bytes 458768 | tf_op jit(solution)/shard_map/psum | solution.py:46
  276.1 1.2 multiply_select_fusion
  277.4 10.6 %collective-permute-start.3 = (f32[32,896]{1,0:T(8,128)S(1)}, f32[32,896]{1,0:T(8,128)S(1)}, u32[]{:S(2)}, u32[]{:S(2)}) collective-permute-start(f32[32,896]{1,0:T(8,128)S(1)} %get-tuple-element.3), channel_id=1, source_target_pairs={{0,24},{1,56},{2,88},{3,120},{4,152},{5,184},{6,216},{7,248},{8,0}... | collective-permute-start | bytes 344072 | tf_op jit(solution)/shard_map/ppermute | solution.py:63
  287.9 4.3 %collective-permute-start.2 = (f32[32,896]{1,0:T(8,128)S(1)}, f32[32,896]{1,0:T(8,128)S(1)}, u32[]{:S(2)}, u32[]{:S(2)}) collective-permute-start(f32[32,896]{1,0:T(8,128)S(1)} %get-tuple-element.4), channel_id=1, source_target_pairs={{0,16},{1,48},{2,80},{3,112},{4,144},{5,176},{6,208},{7,240},{8,24... | collective-permute-start | bytes 344072 | tf_op jit(solution)/shard_map/ppermute | solution.py:63
  292.3 11.4 %collective-permute-start.1 = (f32[32,896]{1,0:T(8,128)S(1)}, f32[32,896]{1,0:T(8,128)S(1)}, u32[]{:S(2)}, u32[]{:S(2)}) collective-permute-start(f32[32,896]{1,0:T(8,128)S(1)} %get-tuple-element.5), channel_id=1, source_target_pairs={{0,8},{1,40},{2,72},{3,104},{4,136},{5,168},{6,200},{7,232},{8,16}... | collective-permute-start | bytes 344072 | tf_op jit(solution)/shard_map/ppermute | solution.py:63
  303.7 4.3 %collective-permute-start = (f32[32,896]{1,0:T(8,128)S(1)}, f32[32,896]{1,0:T(8,128)S(1)}, u32[]{:S(2)}, u32[]{:S(2)}) collective-permute-start(f32[32,896]{1,0:T(8,128)S(1)} %get-tuple-element.2), channel_id=1, source_target_pairs={{0,0},{1,32},{2,64},{3,96},{4,128},{5,160},{6,192},{7,224},{8,8},{... | collective-permute-start | bytes 344072 | tf_op jit(solution)/shard_map/ppermute | solution.py:63
  308.0 0.0 reduce-scatter.4.cloned.1.call-done
  308.1 0.8 copy.16
  308.9 5.8 %psum.23 = f32[32,64]{1,0:T(8,128)} all-reduce(f32[32,64]{1,0:T(8,128)S(1)} %copy.16), channel_id=1, replica_groups=mesh['mp'=2,'blk'=32,'tok'=8] {'mp'}, use_global_device_ids=true, to_apply=%region_4.0 | all-reduce | flops 2048 | bytes 16384 | tf_op jit(solution)/shard_map/psum | solution.py:38
  314.7 0.0 collective-permute-done.3
  314.7 0.0 collective-permute-done.2
  314.7 0.0 collective-permute-done.1
  314.7 7.5 %collective-permute-done = f32[32,896]{1,0:T(8,128)S(1)} collective-permute-done((f32[32,896]{1,0:T(8,128)S(1)}, f32[32,896]{1,0:T(8,128)S(1)}, u32[]{:S(2)}, u32[]{:S(2)}) %collective-permute-start) | collective-permute-done | bytes 114720 | tf_op jit(solution)/shard_map/ppermute | solution.py:63
  322.2 0.6 gather_fusion
  322.8 0.1 select_bitcast_fusion
  322.9 0.8 copy.17
  (10 shorter events, 0.1 us)
Async XLA Ops:
  8.0 77.2 %all-gather.3.cloned.1.call-start = ((), (), s32[]{:S(2)}) async-start(), calls=%async_computation.4 | async-start | bytes 2064384 | tf_op jit(solution)/shard_map/all_gather | solution.py:40
  51.5 33.6 %all-to-all-start = ((bf16[128,8,128]{0,2,1:T(8,128)(2,1)}), bf16[128,8,128]{0,2,1:T(8,128)(2,1)S(1)}, u32[]{:S(2)}, u32[]{:S(2)}) async-start(bf16[128,8,128]{0,2,1:T(8,128)(2,1)} %bitcast.1), calls=%async_computation | async-start | bytes 524288 | tf_op jit(solution)/shard_map/all_to_all | solution.py:42
  72.8 151.2 %all-reduce.5.cloned.1.call-start = ((), (), s32[]{:S(2)}) async-start(), calls=%async_computation.3 | async-start | bytes 524288 | tf_op jit(solution)/shard_map/psum | solution.py:28
  75.3 200.8 %all-reduce.3.cloned.1.call-start = ((), (), s32[]{:S(2)}) async-start(), calls=%async_computation.2 | async-start | bytes 917504 | tf_op jit(solution)/shard_map/psum | solution.py:46
  75.4 12.7 %copy-start = (bf16[1,512,896]{2,1,0:T(8,128)(2,1)S(1)}, bf16[1,512,896]{2,1,0:T(8,128)(2,1)}, u32[]{:S(2)}) copy-start(bf16[1,512,896]{2,1,0:T(8,128)(2,1)} %param.3) | copy-start | bytes 2752516
  88.0 220.1 %reduce-scatter.4.cloned.1.call-start = ((), (), s32[]{:S(2)}) async-start(), calls=%async_computation.5 | async-start | bytes 294912
  277.4 37.3 %collective-permute-start.3 = (f32[32,896]{1,0:T(8,128)S(1)}, f32[32,896]{1,0:T(8,128)S(1)}, u32[]{:S(2)}, u32[]{:S(2)}) collective-permute-start(f32[32,896]{1,0:T(8,128)S(1)} %get-tuple-element.3), channel_id=1, source_target_pairs={{0,24},{1,56},{2,88},{3,120},{4,152},{5,184},{6,216},{7,248},{8,0}... | collective-permute-start | bytes 344072 | tf_op jit(solution)/shard_map/ppermute | solution.py:63
  287.9 26.8 %collective-permute-start.2 = (f32[32,896]{1,0:T(8,128)S(1)}, f32[32,896]{1,0:T(8,128)S(1)}, u32[]{:S(2)}, u32[]{:S(2)}) collective-permute-start(f32[32,896]{1,0:T(8,128)S(1)} %get-tuple-element.4), channel_id=1, source_target_pairs={{0,16},{1,48},{2,80},{3,112},{4,144},{5,176},{6,208},{7,240},{8,24... | collective-permute-start | bytes 344072 | tf_op jit(solution)/shard_map/ppermute | solution.py:63
  292.3 22.4 %collective-permute-start.1 = (f32[32,896]{1,0:T(8,128)S(1)}, f32[32,896]{1,0:T(8,128)S(1)}, u32[]{:S(2)}, u32[]{:S(2)}) collective-permute-start(f32[32,896]{1,0:T(8,128)S(1)} %get-tuple-element.5), channel_id=1, source_target_pairs={{0,8},{1,40},{2,72},{3,104},{4,136},{5,168},{6,200},{7,232},{8,16}... | collective-permute-start | bytes 344072 | tf_op jit(solution)/shard_map/ppermute | solution.py:63
  303.7 18.5 %collective-permute-start = (f32[32,896]{1,0:T(8,128)S(1)}, f32[32,896]{1,0:T(8,128)S(1)}, u32[]{:S(2)}, u32[]{:S(2)}) collective-permute-start(f32[32,896]{1,0:T(8,128)S(1)} %get-tuple-element.2), channel_id=1, source_target_pairs={{0,0},{1,32},{2,64},{3,96},{4,128},{5,160},{6,192},{7,224},{8,8},{... | collective-permute-start | bytes 344072 | tf_op jit(solution)/shard_map/ppermute | solution.py:63
Sparse Core Ops, SparseCore 0:
  11.0 43.5 all-gather.2
  226.2 45.6 reduce-scatter.3
Sparse Core Ops, SparseCore 1:
  76.7 147.3 all-reduce.4
  227.4 48.6 all-reduce.2

commit v2 on v1

v2 whole, which is shorter than its diff:
```python
import jax
import jax.numpy as jnp
from jax import lax
from jax.sharding import PartitionSpec as P

ROW_DEV = 32


OFF_SCALE = 0.9


def local(inputs, down_weight):
    x_local = inputs[0]
    w_local = down_weight[0]
    tokens, span_width = x_local.shape
    cols = w_local.shape[0]
    blk_index = lax.axis_index("blk")
    tok_index = lax.axis_index("tok")
    blk_count = lax.axis_size("blk")
    tok_count = lax.axis_size("tok")
    group = blk_count // tok_count
    col_group = cols // blk_count

    y_part = lax.dot_general(
        x_local, w_local, (((1,), (1,)), ((), ())), preferred_element_type=jnp.float32
    )
    y_parts = lax.all_to_all(y_part, "blk", 1, 0, tiled=True)
    y_mine = jnp.sum(y_parts.reshape(blk_count, tokens, col_group), axis=0)
    y_tok = lax.all_gather(y_mine, "tok", axis=0, tiled=True)

    x_full = lax.all_gather(x_local, "tok", axis=0, tiled=True)
    win_own = x_full[:, :ROW_DEV]

    win_own_f = win_own.astype(jnp.float32)
    diag = jnp.sum(win_own_f * win_own_f, axis=0)
    w_cols = lax.dynamic_slice_in_dim(w_local, tok_index * (cols // tok_count), cols // tok_count, 0)
    diag_term = (1.0 - OFF_SCALE) * diag[:, None] * w_cols[:, :ROW_DEV].astype(jnp.float32).T
    diag_term = diag_term + lax.ppermute(diag_term, "mp", [(0, 1), (1, 0)])

    bundles = []
    for d in range(group):
        perm = []
        for b in range(blk_count):
            for t in range(tok_count):
                dest_b = group * t + ((b % group - d) % group)
                perm.append((b * tok_count + t, dest_b * tok_count + b // group))
        win = lax.ppermute(win_own, ("blk", "tok"), perm)
        gram = lax.dot_general(
            win, x_full, (((0,), (0,)), ((), ())), preferred_element_type=jnp.float32
        )
        cross = lax.dot_general(
            win.astype(jnp.float32), y_tok, (((0,), (0,)), ((), ())),
            precision=lax.Precision.HIGHEST, preferred_element_type=jnp.float32,
        )
        bundles.append(jnp.concatenate([gram, OFF_SCALE * cross], axis=1))
    stacked = jnp.stack(bundles)
    stacked = stacked + lax.ppermute(stacked, "mp", [(0, 1), (1, 0)])

    pieces = []
    row_ids = lax.broadcasted_iota(jnp.int32, (ROW_DEV, span_width), 0)
    col_ids = lax.broadcasted_iota(jnp.int32, (ROW_DEV, span_width), 1)
    for d in range(group):
        perm = []
        for b in range(blk_count):
            for t in range(tok_count):
                s = (b % group + d) % group
                perm.append((b * tok_count + t, (group * t + s) * tok_count + b // group))
        row_blk = group * tok_index + (blk_index % group + d) % group
        on_diag = (row_blk == blk_index) & (col_ids == row_ids)
        gram = stacked[d, :, :span_width]
        reduced = jnp.where(on_diag, gram, OFF_SCALE * gram)
        bundle = jnp.concatenate([reduced, stacked[d, :, span_width:]], axis=1)
        pieces.append(lax.ppermute(bundle, ("blk", "tok"), perm))
    got = jnp.stack(pieces)
    order = (blk_index % group - jnp.arange(group)) % group
    got = jnp.take(got, order, axis=0)
    denominator = jnp.transpose(got[:, :, :span_width], (1, 0, 2)).reshape(ROW_DEV, group * span_width)
    numerator = jnp.transpose(got[:, :, span_width:], (1, 0, 2)).reshape(ROW_DEV, group * col_group)
    numerator = numerator + diag_term
    return (denominator, numerator)


def solution(mesh):
    placed = (P("mp", "tok", "blk"), P("mp", None, "blk"))
    return jax.shard_map(
        local,
        mesh=mesh,
        in_specs=placed,
        out_specs=(P("blk", "tok"), P("blk", "tok")),
        check_vma=False,
    )
```

time: 332 us -> 210 us (0.63)
  the two profiles are of different devices: /device:TPU:21 before, /device:TPU:78 now
where the time goes in v2:
time: 210 us
  waiting for transfers between devices  101 us (48%)
  starting transfers between devices  57.6 us (27%)
  blocking collectives  25.4 us (12%)
  between operations  14.4 us (7%)
  local copies, waits for them, and re-layouts  6.03 us (3%)
  matrix products  4.55 us (2%)
    ppermute x4, waiting for transfers between devices, local(): win = lax.ppermute(win_own, ('blk', 'tok'), perm)  42.4 us
    all_gather x1, waiting for transfers between devices, local(): x_full = lax.all_gather(x_local, 'tok', axis=0, tiled=True)  30.7 us
    all_gather x1, blocking collectives, local(): y_tok = lax.all_gather(y_mine, 'tok', axis=0, tiled=True)  25.4 us
    ppermute x4, starting transfers between devices, local(): win = lax.ppermute(win_own, ('blk', 'tok'), perm)  22.8 us
    ppermute x4, starting transfers between devices, local(): pieces.append(lax.ppermute(bundle, ('blk', 'tok'), perm))  20.2 us
    ppermute x4, waiting for transfers between devices, local(): pieces.append(lax.ppermute(bundle, ('blk', 'tok'), perm))  18.1 us
    all_to_all x1, starting transfers between devices, local(): y_parts = lax.all_to_all(y_part, 'blk', 1, 0, tiled=True)  10.1 us
    ppermute x1, waiting for transfers between devices, local(): stacked = stacked + lax.ppermute(stacked, 'mp', [(0, 1), (1, 0)])  8.97 us
  transfers between devices with their start and end apart: 12, of which 8 were waited for; matrix products, arithmetic and copies ran while one was open for 3% of the time, Pallas kernels for 0%

profile of v2, /device:TPU:78, one launch (start us, length us, event | category | flops | bytes accessed | tf_op | source)
XLA Modules:
  0.0 209.6 jit_solution(6822859176248670282)
XLA Ops:
  7.2 0.0 copy-start
  7.2 0.0 all-gather.3.cloned.1.call-start
  7.2 0.7 all-gather.3.cloned.1.call-update
  7.9 0.4 copy-done
  8.3 2.0 fusion.4
  10.4 10.1 %all-to-all-start = ((f32[128,32,16]{0,2,1:T(8,128)}), f32[128,32,16]{0,2,1:T(8,128)S(1)}, u32[]{:S(2)}, u32[]{:S(2)}) async-start(f32[128,32,16]{0,2,1:T(8,128)} %fusion.4), calls=%async_computation | async-start | bytes 524288 | tf_op jit(solution)/shard_map/all_to_all | solution.py:27
  20.6 30.7 %all-gather.3.cloned.1.call-done = bf16[1,1024,896]{2,1,0:T(8,128)(2,1)} async-done(((bf16[1,128,896]{2,1,0:T(8,128)(2,1)}), bf16[1,1024,896]{2,1,0:T(8,128)(2,1)}) %all-gather.3.cloned.1.call-update) | async-done | bytes 1835024 | tf_op jit(solution)/shard_map/all_gather | solution.py:31
  51.3 0.0 copy-start.1
  51.3 1.8 slice.50
  53.1 4.6 %collective-permute-start.3 = (bf16[1024,32]{1,0:T(8,128)(2,1)}, bf16[1024,32]{1,0:T(8,128)(2,1)S(1)}, u32[]{:S(2)}, u32[]{:S(2)}) collective-permute-start(bf16[1024,32]{1,0:T(8,128)(2,1)} %slice.50), channel_id=1, source_target_pairs={{0,8},{1,40},{2,72},{3,104},{4,136},{5,168},{6,200},{7,232},{8,16}... | collective-permute-start | bytes 196616 | tf_op jit(solution)/shard_map/ppermute | solution.py:47
  57.8 0.0 all-to-all-done
  57.9 25.4 %all_gather.7 = f32[1024,16]{0,1:T(8,128)S(1)} all-gather(f32[128,16]{0,1:T(8,128)S(1)} %reduce_sum.18), channel_id=1, replica_groups=mesh['mp'=2,'blk'=32,'tok'=8] {'tok'}, dimensions={0}, use_global_device_ids=true | all-gather | bytes 73728 | tf_op jit(solution)/shard_map/all_gather | solution.py:29
  83.2 5.2 %collective-permute-start.2 = (bf16[1024,32]{1,0:T(8,128)(2,1)}, bf16[1024,32]{1,0:T(8,128)(2,1)S(1)}, u32[]{:S(2)}, u32[]{:S(2)}) collective-permute-start(bf16[1024,32]{1,0:T(8,128)(2,1)} %slice.50), channel_id=1, source_target_pairs={{0,16},{1,48},{2,80},{3,112},{4,144},{5,176},{6,208},{7,240},{8,24... | collective-permute-start | bytes 196616 | tf_op jit(solution)/shard_map/ppermute | solution.py:47
  88.5 6.5 %collective-permute-start.1 = (bf16[1024,32]{1,0:T(8,128)(2,1)}, bf16[1024,32]{1,0:T(8,128)(2,1)S(1)}, u32[]{:S(2)}, u32[]{:S(2)}) collective-permute-start(bf16[1024,32]{1,0:T(8,128)(2,1)} %slice.50), channel_id=1, source_target_pairs={{0,24},{1,56},{2,88},{3,120},{4,152},{5,184},{6,216},{7,248},{8,0}... | collective-permute-start | bytes 196616 | tf_op jit(solution)/shard_map/ppermute | solution.py:47
  95.0 6.5 %collective-permute-start = (bf16[1024,32]{1,0:T(8,128)(2,1)}, bf16[1024,32]{1,0:T(8,128)(2,1)S(1)}, u32[]{:S(2)}, u32[]{:S(2)}) collective-permute-start(bf16[1024,32]{1,0:T(8,128)(2,1)} %slice.50), channel_id=1, source_target_pairs={{0,0},{1,32},{2,64},{3,96},{4,128},{5,160},{6,192},{7,224},{8,8},{... | collective-permute-start | bytes 196616 | tf_op jit(solution)/shard_map/ppermute | solution.py:47
  101.5 0.0 collective-permute-done.3
  101.5 0.2 fusion
  101.7 0.1 collective-permute-done.2
  101.8 0.0 copy-start.4
  101.8 0.2 fusion.1
  102.0 25.9 %collective-permute-done.1 = bf16[1024,32]{1,0:T(8,128)(2,1)S(1)} collective-permute-done((bf16[1024,32]{1,0:T(8,128)(2,1)}, bf16[1024,32]{1,0:T(8,128)(2,1)S(1)}, u32[]{:S(2)}, u32[]{:S(2)}) %collective-permute-start.1) | collective-permute-done | bytes 65568 | tf_op jit(solution)/shard_map/ppermute | solution.py:47
  127.9 0.0 copy-done.4
  127.9 0.0 copy-start.2
  127.9 0.7 copy-done.2
  128.6 0.2 fusion.2
  128.9 0.1 copy.34
  128.9 0.1 copy.33
  129.0 0.1 copy.32
  129.1 16.5 %collective-permute-done = bf16[1024,32]{1,0:T(8,128)(2,1)S(1)} collective-permute-done((bf16[1024,32]{1,0:T(8,128)(2,1)}, bf16[1024,32]{1,0:T(8,128)(2,1)S(1)}, u32[]{:S(2)}, u32[]{:S(2)}) %collective-permute-start) | collective-permute-done | bytes 65568 | tf_op jit(solution)/shard_map/ppermute | solution.py:47
  145.6 0.2 fusion.3
  145.8 0.1 copy.31
  145.9 0.0 copy-done.1
  145.9 0.0 copy-start.5
  145.9 0.4 fusion.13
  146.3 0.0 copy-start.3
  146.3 0.5 copy-done.5
  146.8 0.4 fusion.15
  147.3 0.0 copy-done.3
  147.3 0.4 fusion.17
  147.7 0.4 fusion.19
  148.2 1.9 collective-permute-start.4
  150.1 0.2 multiply_reduce_fusion
  150.3 9.0 %collective-permute-done.4 = f32[4,32,912]{2,1,0:T(8,128)S(1)} collective-permute-done((f32[4,32,912]{2,1,0:T(8,128)S(1)}, f32[4,32,912]{2,1,0:T(8,128)S(1)}, u32[]{:S(2)}, u32[]{:S(2)}) %collective-permute-start.4) | collective-permute-done | bytes 466976 | tf_op jit(solution)/shard_map/ppermute | solution.py:57
  159.3 0.1 fusion.21
  159.4 0.1 multiply_select_fusion.3
  159.4 4.9 %collective-permute-start.6 = (f32[32,912]{1,0:T(8,128)S(1)}, f32[32,912]{1,0:T(8,128)S(1)}, u32[]{:S(2)}, u32[]{:S(2)}) collective-permute-start(f32[32,912]{1,0:T(8,128)S(1)} %pad_maximum_fusion.3), channel_id=1, source_target_pairs={{0,8},{1,40},{2,72},{3,104},{4,136},{5,168},{6,200},{7,232},{8,16}... | collective-permute-start | bytes 350216 | tf_op jit(solution)/shard_map/ppermute | solution.py:73
  164.4 7.0 %collective-permute-start.7 = (f32[32,912]{1,0:T(8,128)S(1)}, f32[32,912]{1,0:T(8,128)S(1)}, u32[]{:S(2)}, u32[]{:S(2)}) collective-permute-start(f32[32,912]{1,0:T(8,128)S(1)} %pad_maximum_fusion.4), channel_id=1, source_target_pairs={{0,16},{1,48},{2,80},{3,112},{4,144},{5,176},{6,208},{7,240},{8,24... | collective-permute-start | bytes 350216 | tf_op jit(solution)/shard_map/ppermute | solution.py:73
  171.5 1.9 collective-permute-start.8
  173.4 6.3 %collective-permute-start.5 = (f32[32,912]{1,0:T(8,128)S(1)}, f32[32,912]{1,0:T(8,128)S(1)}, u32[]{:S(2)}, u32[]{:S(2)}) collective-permute-start(f32[32,912]{1,0:T(8,128)S(1)} %pad_maximum_fusion.2), channel_id=1, source_target_pairs={{0,0},{1,32},{2,64},{3,96},{4,128},{5,160},{6,192},{7,224},{8,8},{... | collective-permute-start | bytes 350216 | tf_op jit(solution)/shard_map/ppermute | solution.py:73
  179.7 2.5 %collective-permute-start.9 = (f32[32,64]{0,1:T(8,128)S(1)}, f32[32,64]{0,1:T(8,128)S(1)}, u32[]{:S(2)}, u32[]{:S(2)}) collective-permute-start(f32[32,64]{0,1:T(8,128)S(1)} %multiply_bitcast_fusion), channel_id=1, source_target_pairs={{0,256},{256,0},{1,257},{257,1},{2,258},{258,2},{3,259},{259,3},{4... | collective-permute-start | bytes 24584 | tf_op jit(solution)/shard_map/ppermute | solution.py:38
  182.2 0.6 collective-permute-done.6
  182.9 0.0 collective-permute-done.7
  182.9 5.8 %collective-permute-done.8 = f32[32,912]{1,0:T(8,128)S(1)} collective-permute-done((f32[32,912]{1,0:T(8,128)S(1)}, f32[32,912]{1,0:T(8,128)S(1)}, u32[]{:S(2)}, u32[]{:S(2)}) %collective-permute-start.8) | collective-permute-done | bytes 116768 | tf_op jit(solution)/shard_map/ppermute | solution.py:73
  188.7 11.7 %collective-permute-done.5 = f32[32,912]{1,0:T(8,128)S(1)} collective-permute-done((f32[32,912]{1,0:T(8,128)S(1)}, f32[32,912]{1,0:T(8,128)S(1)}, u32[]{:S(2)}, u32[]{:S(2)}) %collective-permute-start.5) | collective-permute-done | bytes 116768 | tf_op jit(solution)/shard_map/ppermute | solution.py:73
  200.4 0.6 gather_fusion
  201.0 0.1 broadcast_select_fusion
  201.2 0.1 copy.36
  201.3 0.0 collective-permute-done.9
  201.3 0.7 copy.37
  202.0 0.8 copy.41
  (21 shorter events, 0.4 us)
Async XLA Ops:
  7.2 1.2 copy-start
  7.2 44.1 %all-gather.3.cloned.1.call-start = ((), (), s32[]{:S(2)}) async-start(), calls=%async_computation.1 | async-start | bytes 2064384 | tf_op jit(solution)/shard_map/all_gather | solution.py:31
  10.4 47.4 %all-to-all-start = ((f32[128,32,16]{0,2,1:T(8,128)}), f32[128,32,16]{0,2,1:T(8,128)S(1)}, u32[]{:S(2)}, u32[]{:S(2)}) async-start(f32[128,32,16]{0,2,1:T(8,128)} %fusion.4), calls=%async_computation | async-start | bytes 524288 | tf_op jit(solution)/shard_map/all_to_all | solution.py:27
  51.3 94.6 %copy-start.1 = (bf16[1,1024,896]{2,1,0:T(8,128)(2,1)S(1)}, bf16[1,1024,896]{2,1,0:T(8,128)(2,1)}, u32[]{:S(2)}) copy-start(bf16[1,1024,896]{2,1,0:T(8,128)(2,1)} %all-gather.3.cloned.1.call-done) | copy-start | bytes 5505028
  53.1 48.4 %collective-permute-start.3 = (bf16[1024,32]{1,0:T(8,128)(2,1)}, bf16[1024,32]{1,0:T(8,128)(2,1)S(1)}, u32[]{:S(2)}, u32[]{:S(2)}) collective-permute-start(bf16[1024,32]{1,0:T(8,128)(2,1)} %slice.50), channel_id=1, source_target_pairs={{0,8},{1,40},{2,72},{3,104},{4,136},{5,168},{6,200},{7,232},{8,16}... | collective-permute-start | bytes 196616 | tf_op jit(solution)/shard_map/ppermute | solution.py:47
  83.2 18.6 %collective-permute-start.2 = (bf16[1024,32]{1,0:T(8,128)(2,1)}, bf16[1024,32]{1,0:T(8,128)(2,1)S(1)}, u32[]{:S(2)}, u32[]{:S(2)}) collective-permute-start(bf16[1024,32]{1,0:T(8,128)(2,1)} %slice.50), channel_id=1, source_target_pairs={{0,16},{1,48},{2,80},{3,112},{4,144},{5,176},{6,208},{7,240},{8,24... | collective-permute-start | bytes 196616 | tf_op jit(solution)/shard_map/ppermute | solution.py:47
  88.5 39.4 %collective-permute-start.1 = (bf16[1024,32]{1,0:T(8,128)(2,1)}, bf16[1024,32]{1,0:T(8,128)(2,1)S(1)}, u32[]{:S(2)}, u32[]{:S(2)}) collective-permute-start(bf16[1024,32]{1,0:T(8,128)(2,1)} %slice.50), channel_id=1, source_target_pairs={{0,24},{1,56},{2,88},{3,120},{4,152},{5,184},{6,216},{7,248},{8,0}... | collective-permute-start | bytes 196616 | tf_op jit(solution)/shard_map/ppermute | solution.py:47
  95.0 50.6 %collective-permute-start = (bf16[1024,32]{1,0:T(8,128)(2,1)}, bf16[1024,32]{1,0:T(8,128)(2,1)S(1)}, u32[]{:S(2)}, u32[]{:S(2)}) collective-permute-start(bf16[1024,32]{1,0:T(8,128)(2,1)} %slice.50), channel_id=1, source_target_pairs={{0,0},{1,32},{2,64},{3,96},{4,128},{5,160},{6,192},{7,224},{8,8},{... | collective-permute-start | bytes 196616 | tf_op jit(solution)/shard_map/ppermute | solution.py:47
  101.8 26.1 %copy-start.4 = (bf16[1024,32]{1,0:T(8,128)(2,1)}, bf16[1024,32]{1,0:T(8,128)(2,1)S(1)}, u32[]{:S(2)}) copy-start(bf16[1024,32]{1,0:T(8,128)(2,1)S(1)} %collective-permute-done.2) | copy-start | bytes 196612
  127.9 0.7 copy-start.2
  145.9 1.0 copy-start.5
  146.3 1.0 copy-start.3
  148.2 11.1 %collective-permute-start.4 = (f32[4,32,912]{2,1,0:T(8,128)S(1)}, f32[4,32,912]{2,1,0:T(8,128)S(1)}, u32[]{:S(2)}, u32[]{:S(2)}) collective-permute-start(f32[4,32,912]{2,1,0:T(8,128)S(1)} %pad_maximum_fusion), channel_id=1, source_target_pairs={{0,256},{256,0},{1,257},{257,1},{2,258},{258,2},{3,259},{259,3},{4... | collective-permute-start | bytes 1400840 | tf_op jit(solution)/shard_map/ppermute | solution.py:57
  159.4 23.4 %collective-permute-start.6 = (f32[32,912]{1,0:T(8,128)S(1)}, f32[32,912]{1,0:T(8,128)S(1)}, u32[]{:S(2)}, u32[]{:S(2)}) collective-permute-start(f32[32,912]{1,0:T(8,128)S(1)} %pad_maximum_fusion.3), channel_id=1, source_target_pairs={{0,8},{1,40},{2,72},{3,104},{4,136},{5,168},{6,200},{7,232},{8,16}... | collective-permute-start | bytes 350216 | tf_op jit(solution)/shard_map/ppermute | solution.py:73
  164.4 18.5 %collective-permute-start.7 = (f32[32,912]{1,0:T(8,128)S(1)}, f32[32,912]{1,0:T(8,128)S(1)}, u32[]{:S(2)}, u32[]{:S(2)}) collective-permute-start(f32[32,912]{1,0:T(8,128)S(1)} %pad_maximum_fusion.4), channel_id=1, source_target_pairs={{0,16},{1,48},{2,80},{3,112},{4,144},{5,176},{6,208},{7,240},{8,24... | collective-permute-start | bytes 350216 | tf_op jit(solution)/shard_map/ppermute | solution.py:73
  171.5 17.2 %collective-permute-start.8 = (f32[32,912]{1,0:T(8,128)S(1)}, f32[32,912]{1,0:T(8,128)S(1)}, u32[]{:S(2)}, u32[]{:S(2)}) collective-permute-start(f32[32,912]{1,0:T(8,128)S(1)} %pad_maximum_fusion.5), channel_id=1, source_target_pairs={{0,24},{1,56},{2,88},{3,120},{4,152},{5,184},{6,216},{7,248},{8,0}... | collective-permute-start | bytes 350216 | tf_op jit(solution)/shard_map/ppermute | solution.py:73
  173.4 27.0 %collective-permute-start.5 = (f32[32,912]{1,0:T(8,128)S(1)}, f32[32,912]{1,0:T(8,128)S(1)}, u32[]{:S(2)}, u32[]{:S(2)}) collective-permute-start(f32[32,912]{1,0:T(8,128)S(1)} %pad_maximum_fusion.2), channel_id=1, source_target_pairs={{0,0},{1,32},{2,64},{3,96},{4,128},{5,160},{6,192},{7,224},{8,8},{... | collective-permute-start | bytes 350216 | tf_op jit(solution)/shard_map/ppermute | solution.py:73
  179.7 21.6 %collective-permute-start.9 = (f32[32,64]{0,1:T(8,128)S(1)}, f32[32,64]{0,1:T(8,128)S(1)}, u32[]{:S(2)}, u32[]{:S(2)}) collective-permute-start(f32[32,64]{0,1:T(8,128)S(1)} %multiply_bitcast_fusion), channel_id=1, source_target_pairs={{0,256},{256,0},{1,257},{257,1},{2,258},{258,2},{3,259},{259,3},{4... | collective-permute-start | bytes 24584 | tf_op jit(solution)/shard_map/ppermute | solution.py:38
Sparse Core Ops, SparseCore 0:
  10.1 41.0 all-gather.2

commit v3 on v0

v3 whole, which is shorter than its diff:
```python
import jax
import jax.numpy as jnp
import numpy as np
from jax import lax
from jax.sharding import Mesh, PartitionSpec as P

ROW_DEV = 32


OFF_SCALE = 0.9


def local(inputs, down_weight):
    x_local = inputs[0]
    w_local = down_weight[0]
    tokens, span_width = x_local.shape
    cols = w_local.shape[0]
    hi_index = lax.axis_index("hi")
    lo_index = lax.axis_index("lo")
    tok_index = lax.axis_index("tok")
    group = lax.axis_size("lo")
    hi_count = lax.axis_size("hi")
    tok_count = lax.axis_size("tok")
    mp_count = lax.axis_size("mp")
    blk_count = hi_count * group
    col_group = cols // blk_count
    tok_cols = cols // tok_count

    y_part = lax.dot_general(
        x_local, w_local, (((1,), (1,)), ((), ())), preferred_element_type=jnp.float32
    )
    y_parts = lax.all_to_all(y_part, ("hi", "lo"), 1, 0, tiled=True)
    y_mine = jnp.sum(y_parts.reshape(blk_count, tokens, col_group), axis=0)
    y_round = lax.reduce_precision(y_mine, exponent_bits=8, mantissa_bits=7)
    y_high = y_round.astype(jnp.bfloat16)
    y_low = (y_mine - y_round).astype(jnp.bfloat16)

    win_lo = lax.all_gather(x_local[:, :ROW_DEV], "lo", axis=1, tiled=True)
    payload = jnp.concatenate([x_local, win_lo, y_high, y_low], axis=1)
    full = lax.all_gather(payload, "tok", axis=0, tiled=True)
    x_full = full[:, :span_width]
    win_end = span_width + group * ROW_DEV
    wins = full[:, span_width:win_end]
    y_tok = full[:, win_end:win_end + col_group].astype(jnp.float32) + full[:, win_end + col_group:].astype(jnp.float32)

    swap = [(h * tok_count + t, t * tok_count + h) for h in range(hi_count) for t in range(tok_count)]
    wins = lax.ppermute(wins, ("hi", "tok"), swap)

    gram = lax.dot_general(
        wins, x_full, (((0,), (0,)), ((), ())), preferred_element_type=jnp.float32
    )
    cross = lax.dot_general(
        wins.astype(jnp.float32), y_tok, (((0,), (0,)), ((), ())),
        precision=lax.Precision.HIGHEST, preferred_element_type=jnp.float32,
    )
    pieces = jnp.concatenate([gram, OFF_SCALE * cross], axis=1)
    pieces = lax.ppermute(pieces, ("hi", "tok"), swap)
    pieces = pieces.reshape(group, ROW_DEV, span_width + col_group)

    win_own = x_full[:, :ROW_DEV].astype(jnp.float32)
    diag = jnp.sum(win_own * win_own, axis=0)
    w_cols = lax.dynamic_slice_in_dim(w_local, tok_index * tok_cols, tok_cols, 0)
    diag_term = (1.0 - OFF_SCALE) * diag[:, None] * w_cols[:, :ROW_DEV].astype(jnp.float32).T
    is_self = (jnp.arange(group) == lo_index)[:, None, None]
    diag_part = jnp.where(is_self, diag_term[None], 0.0)

    send = jnp.concatenate([pieces, diag_part], axis=2)
    send = jnp.concatenate([send] * mp_count, axis=0)
    got = lax.all_to_all(send, ("mp", "lo"), 0, 0, tiled=True)
    got = jnp.sum(got.reshape(mp_count, group, ROW_DEV, -1), axis=0)

    gram = got[:, :, :span_width]
    slot = lax.broadcasted_iota(jnp.int32, gram.shape, 0)
    row_ids = lax.broadcasted_iota(jnp.int32, gram.shape, 1)
    col_ids = lax.broadcasted_iota(jnp.int32, gram.shape, 2)
    on_diag = (tok_index == hi_index) & (slot == lo_index) & (col_ids == row_ids)
    reduced = jnp.where(on_diag, gram, OFF_SCALE * gram)
    denominator = jnp.transpose(reduced, (1, 0, 2)).reshape(ROW_DEV, group * span_width)
    numerator = jnp.transpose(got[:, :, span_width:span_width + col_group], (1, 0, 2)).reshape(ROW_DEV, tok_cols)
    numerator = numerator + jnp.sum(got[:, :, span_width + col_group:], axis=0)
    return (denominator, numerator)


def solution(mesh):
    mp_count, blk_count, tok_count = (mesh.shape[a] for a in ("mp", "blk", "tok"))
    group = blk_count // tok_count
    devices = np.asarray(mesh.devices).reshape(mp_count, tok_count, group, tok_count)
    split = Mesh(devices, ("mp", "hi", "lo", "tok"))
    placed = (P("mp", "tok", ("hi", "lo")), P("mp", None, ("hi", "lo")))
    return jax.shard_map(
        local,
        mesh=split,
        in_specs=placed,
        out_specs=(P(("hi", "lo"), "tok"), P(("hi", "lo"), "tok")),
        check_vma=False,
    )
```

time: 373 us -> 184 us (0.49)
  the two profiles are of different devices: /device:TPU:1 before, /device:TPU:6 now
where the time goes in v3:
time: 184 us
  waiting for transfers between devices  114 us (62%)
  starting transfers between devices  28 us (15%)
  blocking collectives  14.3 us (8%)
  between operations  14.2 us (8%)
  matrix products  5.32 us (3%)
  other arithmetic  3.89 us (2%)
  local copies, waits for them, and re-layouts  3.47 us (2%)
    all_gather x1, waiting for transfers between devices, local(): full = lax.all_gather(payload, 'tok', axis=0, tiled=True)  47.4 us
    ppermute x1, waiting for transfers between devices, local(): pieces = lax.ppermute(pieces, ('hi', 'tok'), swap)  30.7 us
    ppermute x1, waiting for transfers between devices, local(): wins = lax.ppermute(wins, ('hi', 'tok'), swap)  19.5 us
    all_to_all x1, waiting for transfers between devices, local(): got = lax.all_to_all(send, ('mp', 'lo'), 0, 0, tiled=True)  16.8 us
    all_gather x1, blocking collectives, local(): win_lo = lax.all_gather(x_local[:, :ROW_DEV], 'lo', axis=1, tiled=True)  14.3 us
    all_to_all x1, starting transfers between devices, local(): y_parts = lax.all_to_all(y_part, ('hi', 'lo'), 1, 0, tiled=True)  10.2 us
    all_to_all x1, starting transfers between devices, local(): got = lax.all_to_all(send, ('mp', 'lo'), 0, 0, tiled=True)  9.73 us
    ppermute x1, starting transfers between devices, local(): pieces = lax.ppermute(pieces, ('hi', 'tok'), swap)  4.7 us
  transfers between devices with their start and end apart: 5, of which 4 were waited for; matrix products, arithmetic and copies ran while one was open for 1% of the time, Pallas kernels for 0%

profile of v3, /device:TPU:6, one launch (start us, length us, event | category | flops | bytes accessed | tf_op | source)
XLA Modules:
  0.0 183.7 jit_solution(11057553404396737976)
XLA Ops:
  7.2 0.0 copy-start
  7.2 0.0 copy-start.1
  7.2 1.2 copy-done
  8.3 2.0 %fusion.4 = f32[128,32,16]{0,2,1:T(8,128)} fusion(bf16[32,16,896]{2,1,0:T(8,128)(2,1)S(1)} %bitcast.23, bf16[1,128,896]{2,1,0:T(8,128)(2,1)} %param.2), kind=kOutput, calls=%fused_computation.10 | convolution fusion | flops 117440512 | bytes 1409024 | tf_op jit(solution)/shard_map/dot_general | solution.py:29
  10.4 10.2 %all-to-all-start = ((f32[128,32,16]{0,2,1:T(8,128)}), f32[128,32,16]{0,2,1:T(8,128)S(1)}, u32[]{:S(2)}, u32[]{:S(2)}) async-start(f32[128,32,16]{0,2,1:T(8,128)} %fusion.4), calls=%async_computation | async-start | bytes 524288 | tf_op jit(solution)/shard_map/all_to_all | solution.py:32
  20.6 0.0 all-gather.2.cloned.1.call-start
  20.7 0.0 copy-done.1
  20.7 0.2 copy.40
  20.9 14.3 %all_gather.6 = bf16[128,128]{0,1:T(8,128)(2,1)S(1)} all-gather(bf16[128,32]{0,1:T(8,128)(2,1)S(1)} %slice.41), channel_id=1, replica_groups=mesh['mp'=2,'hi'=8,'lo'=4,'tok'=8] {'lo'}, dimensions={1}, use_global_device_ids=true | all-gather | bytes 40960 | tf_op jit(solution)/shard_map/all_gather | solution.py:38
  35.2 0.0 all-to-all-done
  35.3 0.7 pad_maximum_fusion.1
  36.0 0.0 all-gather.2.cloned.1.call-update
  36.0 47.4 %all-gather.2.cloned.1.call-done = bf16[1024,1056]{0,1:T(8,128)(2,1)} async-done(((bf16[128,1056]{0,1:T(8,128)(2,1)}), bf16[1024,1056]{0,1:T(8,128)(2,1)}) %all-gather.2.cloned.1.call-update) | async-done | bytes 2162704 | tf_op jit(solution)/shard_map/all_gather | solution.py:40
  83.5 1.0 slice.42
  84.4 3.3 %collective-permute-start = (bf16[1024,128]{0,1:T(8,128)(2,1)S(1)}, bf16[1024,128]{0,1:T(8,128)(2,1)S(1)}, u32[]{:S(2)}, u32[]{:S(2)}) collective-permute-start(bf16[1024,128]{0,1:T(8,128)(2,1)S(1)} %slice.42), channel_id=1, source_target_pairs={{0,0},{1,32},{2,64},{3,96},{4,128},{5,160},{6,192},{7,224},{32,1},... | collective-permute-start | bytes 786440 | tf_op jit(solution)/shard_map/ppermute | solution.py:47
  87.8 1.0 multiply_reduce_fusion
  88.7 19.5 %collective-permute-done = bf16[1024,128]{0,1:T(8,128)(2,1)S(1)} collective-permute-done((bf16[1024,128]{0,1:T(8,128)(2,1)S(1)}, bf16[1024,128]{0,1:T(8,128)(2,1)S(1)}, u32[]{:S(2)}, u32[]{:S(2)}) %collective-permute-start) | collective-permute-done | bytes 262176 | tf_op jit(solution)/shard_map/ppermute | solution.py:47
  108.3 1.1 convolution_multiply_fusion
  109.3 0.1 copy.45
  109.5 2.2 %fusion = f32[128,896]{1,0:T(8,128)S(1)} fusion(bf16[1024,128]{0,1:T(8,128)(2,1)S(1)} %collective-permute-done, bf16[1024,1056]{0,1:T(8,128)(2,1)} %all-gather.2.cloned.1.call-done), kind=kOutput, calls=%fused_computation | convolution fusion | flops 234881024 | bytes 2555904 | tf_op jit(solution)/shard_map/dot_general | solution.py:49
  111.7 4.7 %collective-permute-start.1 = (f32[128,912]{1,0:T(8,128)S(1)}, f32[128,912]{1,0:T(8,128)S(1)}, u32[]{:S(2)}, u32[]{:S(2)}) collective-permute-start(f32[128,912]{1,0:T(8,128)S(1)} %pad_maximum_fusion), channel_id=1, source_target_pairs={{0,0},{1,32},{2,64},{3,96},{4,128},{5,160},{6,192},{7,224},{32,1},... | collective-permute-start | bytes 1400840 | tf_op jit(solution)/shard_map/ppermute | solution.py:57
  116.5 0.1 copy.46
  116.5 0.1 broadcast_select_fusion
  116.6 30.7 %collective-permute-done.1 = f32[128,912]{1,0:T(8,128)S(1)} collective-permute-done((f32[128,912]{1,0:T(8,128)S(1)}, f32[128,912]{1,0:T(8,128)S(1)}, u32[]{:S(2)}, u32[]{:S(2)}) %collective-permute-start.1) | collective-permute-done | bytes 466976 | tf_op jit(solution)/shard_map/ppermute | solution.py:57
  147.3 1.1 maximum_maximum_fusion
  148.4 9.7 %all-to-all-start.1 = ((f32[8,32,976]{2,1,0:T(8,128)}), f32[8,32,976]{2,1,0:T(8,128)S(1)}, u32[]{:S(2)}, u32[]{:S(2)}) async-start(f32[8,32,976]{2,1,0:T(8,128)} %maximum_maximum_fusion), calls=%async_computation.1 | async-start | bytes 2097152 | tf_op jit(solution)/shard_map/all_to_all | solution.py:69
  158.1 16.8 %all-to-all-done.1 = f32[8,32,976]{2,1,0:T(8,128)S(1)} async-done(((f32[8,32,976]{2,1,0:T(8,128)}), f32[8,32,976]{2,1,0:T(8,128)S(1)}, u32[]{:S(2)}, u32[]{:S(2)}) %all-to-all-start.1) | async-done | bytes 999456 | tf_op jit(solution)/shard_map/all_to_all | solution.py:69
  174.9 0.1 reduce_sum.38
  175.1 0.1 slice_reduce_fusion
  175.2 0.1 fusion.2
  175.2 0.1 copy.48
  175.3 0.1 copy.49
  175.4 0.8 copy.55
  176.2 0.6 add.11
  (10 shorter events, 0.1 us)
Async XLA Ops:
  7.2 1.2 copy-start
  7.2 13.5 %copy-start.1 = (bf16[1,128,896]{2,1,0:T(8,128)(2,1)S(1)}, bf16[1,128,896]{2,1,0:T(8,128)(2,1)}, u32[]{:S(2)}) copy-start(bf16[1,128,896]{2,1,0:T(8,128)(2,1)} %param.2) | copy-start | bytes 688132
  10.4 24.8 %all-to-all-start = ((f32[128,32,16]{0,2,1:T(8,128)}), f32[128,32,16]{0,2,1:T(8,128)S(1)}, u32[]{:S(2)}, u32[]{:S(2)}) async-start(f32[128,32,16]{0,2,1:T(8,128)} %fusion.4), calls=%async_computation | async-start | bytes 524288 | tf_op jit(solution)/shard_map/all_to_all | solution.py:32
  20.6 62.8 %all-gather.2.cloned.1.call-start = ((), (), s32[]{:S(2)}) async-start(), calls=%async_computation.2 | async-start | bytes 2433024 | tf_op jit(solution)/shard_map/all_gather | solution.py:40
  84.4 23.8 %collective-permute-start = (bf16[1024,128]{0,1:T(8,128)(2,1)S(1)}, bf16[1024,128]{0,1:T(8,128)(2,1)S(1)}, u32[]{:S(2)}, u32[]{:S(2)}) collective-permute-start(bf16[1024,128]{0,1:T(8,128)(2,1)S(1)} %slice.42), channel_id=1, source_target_pairs={{0,0},{1,32},{2,64},{3,96},{4,128},{5,160},{6,192},{7,224},{32,1},... | collective-permute-start | bytes 786440 | tf_op jit(solution)/shard_map/ppermute | solution.py:47
  111.7 35.5 %collective-permute-start.1 = (f32[128,912]{1,0:T(8,128)S(1)}, f32[128,912]{1,0:T(8,128)S(1)}, u32[]{:S(2)}, u32[]{:S(2)}) collective-permute-start(f32[128,912]{1,0:T(8,128)S(1)} %pad_maximum_fusion), channel_id=1, source_target_pairs={{0,0},{1,32},{2,64},{3,96},{4,128},{5,160},{6,192},{7,224},{32,1},... | collective-permute-start | bytes 1400840 | tf_op jit(solution)/shard_map/ppermute | solution.py:57
  148.4 26.5 %all-to-all-start.1 = ((f32[8,32,976]{2,1,0:T(8,128)}), f32[8,32,976]{2,1,0:T(8,128)S(1)}, u32[]{:S(2)}, u32[]{:S(2)}) async-start(f32[8,32,976]{2,1,0:T(8,128)} %maximum_maximum_fusion), calls=%async_computation.1 | async-start | bytes 2097152 | tf_op jit(solution)/shard_map/all_to_all | solution.py:69
Sparse Core Ops, SparseCore 0:
  36.2 47.2 all-gather.1

commit v4 on v3

--- a/solution.py
+++ b/solution.py
@@ -26,25 +26,27 @@
     col_group = cols // blk_count
     tok_cols = cols // tok_count
 
+    win_parts = lax.all_gather(x_local[:, :ROW_DEV], ("lo", "tok"), axis=0, tiled=False)
+    wins = jnp.transpose(win_parts.reshape(group, tok_count, tokens, ROW_DEV), (1, 2, 0, 3))
+    wins = wins.reshape(tok_count * tokens, group * ROW_DEV)
+
+    swap = [(h * tok_count + t, t * tok_count + h) for h in range(hi_count) for t in range(tok_count)]
+    x_swapped = lax.ppermute(x_local, ("hi", "tok"), swap)
+
     y_part = lax.dot_general(
         x_local, w_local, (((1,), (1,)), ((), ())), preferred_element_type=jnp.float32
     )
     y_parts = lax.all_to_all(y_part, ("hi", "lo"), 1, 0, tiled=True)
     y_mine = jnp.sum(y_parts.reshape(blk_count, tokens, col_group), axis=0)
+    y_mine = lax.ppermute(y_mine, ("hi", "tok"), swap)
     y_round = lax.reduce_precision(y_mine, exponent_bits=8, mantissa_bits=7)
     y_high = y_round.astype(jnp.bfloat16)
     y_low = (y_mine - y_round).astype(jnp.bfloat16)
 
-    win_lo = lax.all_gather(x_local[:, :ROW_DEV], "lo", axis=1, tiled=True)
-    payload = jnp.concatenate([x_local, win_lo, y_high, y_low], axis=1)
-    full = lax.all_gather(payload, "tok", axis=0, tiled=True)
+    payload = jnp.concatenate([x_swapped, y_high, y_low], axis=1)
+    full = lax.all_gather(payload, "hi", axis=0, tiled=True)
     x_full = full[:, :span_width]
-    win_end = span_width + group * ROW_DEV
-    wins = full[:, span_width:win_end]
-    y_tok = full[:, win_end:win_end + col_group].astype(jnp.float32) + full[:, win_end + col_group:].astype(jnp.float32)
-
-    swap = [(h * tok_count + t, t * tok_count + h) for h in range(hi_count) for t in range(tok_count)]
-    wins = lax.ppermute(wins, ("hi", "tok"), swap)
+    y_tok = full[:, span_width:span_width + col_group].astype(jnp.float32) + full[:, span_width + col_group:].astype(jnp.float32)
 
     gram = lax.dot_general(
         wins, x_full, (((0,), (0,)), ((), ())), preferred_element_type=jnp.float32
@@ -54,10 +56,9 @@
         precision=lax.Precision.HIGHEST, preferred_element_type=jnp.float32,
     )
     pieces = jnp.concatenate([gram, OFF_SCALE * cross], axis=1)
-    pieces = lax.ppermute(pieces, ("hi", "tok"), swap)
     pieces = pieces.reshape(group, ROW_DEV, span_width + col_group)
 
-    win_own = x_full[:, :ROW_DEV].astype(jnp.float32)
+    win_own = lax.dynamic_slice_in_dim(wins, lo_index * ROW_DEV, ROW_DEV, 1).astype(jnp.float32)
     diag = jnp.sum(win_own * win_own, axis=0)
     w_cols = lax.dynamic_slice_in_dim(w_local, tok_index * tok_cols, tok_cols, 0)
     diag_term = (1.0 - OFF_SCALE) * diag[:, None] * w_cols[:, :ROW_DEV].astype(jnp.float32).T

time: 184 us -> 185 us (level)
  the two profiles are of different devices: /device:TPU:6 before, /device:TPU:1 now
where the time goes in v4:
time: 185 us; the launch traced here: 184 us
  blocking collectives  85.3 us (46%)
  waiting for transfers between devices  59.2 us (32%)
  between operations  14.2 us (8%)
  starting transfers between devices  14.1 us (8%)
  matrix products  5.2 us (3%)
  other arithmetic  3.15 us (2%)
  local copies, waits for them, and re-layouts  3.02 us (2%)
    all_gather x1, blocking collectives, local(): lax.all_gather(x_local[:, :ROW_DEV], ('lo', 'tok'), axis=0, tiled=False)  65.3 us
    all_to_all x1, waiting for transfers between devices, local(): got = lax.all_to_all(send, ('mp', 'lo'), 0, 0, tiled=True)  24.2 us
    all_gather x1, waiting for transfers between devices, local(): full = lax.all_gather(payload, 'hi', axis=0, tiled=True)  23.9 us
    all_to_all x1, blocking collectives, local(): y_parts = lax.all_to_all(y_part, ('hi', 'lo'), 1, 0, tiled=True)  20 us
    ppermute x1, waiting for transfers between devices, local(): x_swapped = lax.ppermute(x_local, ('hi', 'tok'), swap)  11.1 us
    ppermute x1, starting transfers between devices, local(): y_mine = lax.ppermute(y_mine, ('hi', 'tok'), swap)  7.12 us
    all_to_all x1, starting transfers between devices, local(): got = lax.all_to_all(send, ('mp', 'lo'), 0, 0, tiled=True)  4.63 us
  transfers between devices with their start and end apart: 4, of which 3 were waited for; matrix products, arithmetic and copies ran while one was open for 1% of the time, Pallas kernels for 0%

profile of v4, /device:TPU:1, one launch (start us, length us, event | category | flops | bytes accessed | tf_op | source)
XLA Modules:
  0.0 184.2 jit_solution(12507758105608670214)
XLA Ops:
  7.2 0.0 copy-start
  7.2 0.0 copy-start.1
  7.2 0.0 all-gather.3.cloned.1.call-start
  7.2 1.1 copy-done
  8.3 1.3 fusion.13
  9.7 20.0 %all_to_all.15 = f32[128,32,16]{0,2,1:T(8,128)S(1)} all-to-all(f32[128,32,16]{0,2,1:T(8,128)S(1)} %fusion.13), channel_id=1, replica_groups=mesh['mp'=2,'hi'=8,'lo'=4,'tok'=8] {'hi','lo'}, dimensions={1} | all-to-all | bytes 524288 | tf_op jit(solution)/shard_map/all_to_all | solution.py:39
  29.7 7.1 %collective-permute-start.1 = (f32[128,16]{0,1:T(8,128)S(1)}, f32[128,16]{0,1:T(8,128)S(1)}, u32[]{:S(2)}, u32[]{:S(2)}) collective-permute-start(f32[128,16]{0,1:T(8,128)S(1)} %reduce_sum.36), channel_id=1, source_target_pairs={{0,0},{1,32},{2,64},{3,96},{4,128},{5,160},{6,192},{7,224},{32,1},... | collective-permute-start | bytes 24584 | tf_op jit(solution)/shard_map/ppermute | solution.py:41
  36.8 0.0 copy-done.1
  36.9 2.3 %collective-permute-start = (bf16[128,896]{1,0:T(8,128)(2,1)S(1)}, bf16[128,896]{1,0:T(8,128)(2,1)S(1)}, u32[]{:S(2)}, u32[]{:S(2)}) collective-permute-start(bf16[128,896]{1,0:T(8,128)(2,1)S(1)} %bitcast.43), channel_id=1, source_target_pairs={{0,0},{1,32},{2,64},{3,96},{4,128},{5,160},{6,192},{7,224},{32,1},... | collective-permute-start | bytes 688136 | tf_op jit(solution)/shard_map/ppermute | solution.py:34
  39.2 0.0 collective-permute-done.1
  39.2 0.1 copy.40
  39.4 0.1 copy.41
  39.5 11.1 %collective-permute-done = bf16[128,896]{1,0:T(8,128)(2,1)S(1)} collective-permute-done((bf16[128,896]{1,0:T(8,128)(2,1)S(1)}, bf16[128,896]{1,0:T(8,128)(2,1)S(1)}, u32[]{:S(2)}, u32[]{:S(2)}) %collective-permute-start) | collective-permute-done | bytes 229408 | tf_op jit(solution)/shard_map/ppermute | solution.py:34
  50.6 0.8 pad_maximum_fusion.1
  51.4 0.0 all-gather.3.cloned.1.call-update
  51.4 65.3 %all-gather = bf16[4096,32]{1,0:T(8,128)(2,1)S(1)} all-gather(bf16[128,32]{1,0:T(8,128)(2,1)S(1)} %slice.33), channel_id=2, replica_groups=mesh['mp'=2,'hi'=8,'lo'=4,'tok'=8] {'lo','tok'}, dimensions={0}, use_global_device_ids=true | all-gather | bytes 270336 | tf_op jit(solution)/shard_map/all_gather | solution.py:29
  116.7 0.4 copy.42
  117.1 0.1 multiply_reduce_fusion
  117.3 0.1 copy.44
  117.4 0.1 broadcast_select_fusion
  117.5 23.9 %all-gather.3.cloned.1.call-done = bf16[1024,928]{1,0:T(8,128)(2,1)} async-done(((bf16[128,928]{1,0:T(8,128)(2,1)}), bf16[1024,928]{1,0:T(8,128)(2,1)}) %all-gather.3.cloned.1.call-update) | async-done | bytes 1900560 | tf_op jit(solution)/shard_map/all_gather | solution.py:47
  141.4 2.2 %fusion.2 = f32[128,896]{0,1:T(8,128)S(1)} fusion(bf16[1024,928]{1,0:T(8,128)(2,1)} %all-gather.3.cloned.1.call-done, bf16[16,8,8,128]{3,2,1,0:T(8,128)(2,1)S(1)} %bitcast.39), kind=kOutput, calls=%fused_computation.2 | convolution fusion | flops 234881024 | bytes 2555904 | tf_op jit(solution)/shard_map/dot_general | solution.py:51
  143.5 1.7 fusion.5
  145.3 0.2 copy.43
  145.5 1.1 maximum_maximum_fusion
  146.6 4.6 %all-to-all-start.1 = ((f32[8,32,976]{2,1,0:T(8,128)}), f32[8,32,976]{2,1,0:T(8,128)S(1)}, u32[]{:S(2)}, u32[]{:S(2)}) async-start(f32[8,32,976]{2,1,0:T(8,128)} %maximum_maximum_fusion), calls=%async_computation.1 | async-start | bytes 2097152 | tf_op jit(solution)/shard_map/all_to_all | solution.py:70
  151.3 24.2 %all-to-all-done.1 = f32[8,32,976]{2,1,0:T(8,128)S(1)} async-done(((f32[8,32,976]{2,1,0:T(8,128)}), f32[8,32,976]{2,1,0:T(8,128)S(1)}, u32[]{:S(2)}, u32[]{:S(2)}) %all-to-all-start.1) | async-done | bytes 999456 | tf_op jit(solution)/shard_map/all_to_all | solution.py:70
  175.5 0.1 reduce_sum.38
  175.6 0.1 slice_reduce_fusion
  175.7 0.1 copy.46
  175.8 0.1 copy.47
  175.8 0.1 fusion.9
  175.9 0.8 copy.51
  176.7 0.6 add.15
  (11 shorter events, 0.2 us)
Async XLA Ops:
  7.2 1.2 copy-start
  7.2 29.7 %copy-start.1 = (bf16[1,128,896]{2,1,0:T(8,128)(2,1)S(1)}, bf16[1,128,896]{2,1,0:T(8,128)(2,1)}, u32[]{:S(2)}) copy-start(bf16[1,128,896]{2,1,0:T(8,128)(2,1)} %param.2) | copy-start | bytes 688132
  7.2 134.2 %all-gather.3.cloned.1.call-start = ((), (), s32[]{:S(2)}) async-start(), calls=%async_computation.2 | async-start | bytes 2359296 | tf_op jit(solution)/shard_map/all_gather | solution.py:47
  29.7 9.5 %collective-permute-start.1 = (f32[128,16]{0,1:T(8,128)S(1)}, f32[128,16]{0,1:T(8,128)S(1)}, u32[]{:S(2)}, u32[]{:S(2)}) collective-permute-start(f32[128,16]{0,1:T(8,128)S(1)} %reduce_sum.36), channel_id=1, source_target_pairs={{0,0},{1,32},{2,64},{3,96},{4,128},{5,160},{6,192},{7,224},{32,1},... | collective-permute-start | bytes 24584 | tf_op jit(solution)/shard_map/ppermute | solution.py:41
  36.9 13.7 %collective-permute-start = (bf16[128,896]{1,0:T(8,128)(2,1)S(1)}, bf16[128,896]{1,0:T(8,128)(2,1)S(1)}, u32[]{:S(2)}, u32[]{:S(2)}) collective-permute-start(bf16[128,896]{1,0:T(8,128)(2,1)S(1)} %bitcast.43), channel_id=1, source_target_pairs={{0,0},{1,32},{2,64},{3,96},{4,128},{5,160},{6,192},{7,224},{32,1},... | collective-permute-start | bytes 688136 | tf_op jit(solution)/shard_map/ppermute | solution.py:34
  146.6 28.8 %all-to-all-start.1 = ((f32[8,32,976]{2,1,0:T(8,128)}), f32[8,32,976]{2,1,0:T(8,128)S(1)}, u32[]{:S(2)}, u32[]{:S(2)}) async-start(f32[8,32,976]{2,1,0:T(8,128)} %maximum_maximum_fusion), calls=%async_computation.1 | async-start | bytes 2097152 | tf_op jit(solution)/shard_map/all_to_all | solution.py:70
Sparse Core Ops, SparseCore 0:
  51.5 89.7 all-gather.2

commit v5 on v4

--- a/solution.py
+++ b/solution.py
@@ -26,9 +26,8 @@
     col_group = cols // blk_count
     tok_cols = cols // tok_count
 
-    win_parts = lax.all_gather(x_local[:, :ROW_DEV], ("lo", "tok"), axis=0, tiled=False)
-    wins = jnp.transpose(win_parts.reshape(group, tok_count, tokens, ROW_DEV), (1, 2, 0, 3))
-    wins = wins.reshape(tok_count * tokens, group * ROW_DEV)
+    win_lo = lax.all_gather(x_local[:, :ROW_DEV], "lo", axis=1, tiled=True)
+    wins = lax.all_gather(win_lo, "tok", axis=0, tiled=True)
 
     swap = [(h * tok_count + t, t * tok_count + h) for h in range(hi_count) for t in range(tok_count)]
     x_swapped = lax.ppermute(x_local, ("hi", "tok"), swap)

time: 185 us -> 183 us (0.989)
  blocking collectives: 85.3 us -> 60.9 us
  waiting for transfers between devices: 59.2 us -> 81.9 us
    all_gather x1 -> x2, blocking collectives: 65.3 us -> 40.9 us  [the longest x1 30.7 us: local(): wins = lax.all_gather(win_lo, 'tok', axis=0, tiled=True)]
    all_gather x1, waiting for transfers between devices: 23.9 us -> 45.7 us  [local(): full = lax.all_gather(payload, 'hi', axis=0, tiled=True)]
  transfers between devices with their start and end apart: 4 -> 4, of which waited for: 3 -> 3; matrix products, arithmetic and copies ran while one was open for 1% -> 0% of each run, Pallas kernels for 0% -> 0%
where the time goes in v5:
time: 183 us; the launch traced here: 182 us
  waiting for transfers between devices  81.9 us (45%)
  blocking collectives  60.9 us (33%)
  starting transfers between devices  14.8 us (8%)
  between operations  14.2 us (8%)
  matrix products  4.57 us (2%)
  other arithmetic  3.03 us (2%)
  local copies, waits for them, and re-layouts  2.54 us (1%)
    all_gather x1, waiting for transfers between devices, local(): full = lax.all_gather(payload, 'hi', axis=0, tiled=True)  45.7 us
    all_gather x1, blocking collectives, local(): wins = lax.all_gather(win_lo, 'tok', axis=0, tiled=True)  30.7 us
    all_to_all x1, waiting for transfers between devices, local(): got = lax.all_to_all(send, ('mp', 'lo'), 0, 0, tiled=True)  24.8 us
    all_to_all x1, blocking collectives, local(): y_parts = lax.all_to_all(y_part, ('hi', 'lo'), 1, 0, tiled=True)  20 us
    ppermute x1, waiting for transfers between devices, local(): x_swapped = lax.ppermute(x_local, ('hi', 'tok'), swap)  11.4 us
    all_gather x1, blocking collectives, local(): win_lo = lax.all_gather(x_local[:, :ROW_DEV], 'lo', axis=1, tiled=True)  10.2 us
    ppermute x1, starting transfers between devices, local(): y_mine = lax.ppermute(y_mine, ('hi', 'tok'), swap)  7.12 us
    all_to_all x1, starting transfers between devices, local(): got = lax.all_to_all(send, ('mp', 'lo'), 0, 0, tiled=True)  5.3 us
  transfers between devices with their start and end apart: 4, of which 3 were waited for; matrix products, arithmetic and copies ran while one was open for 0% of the time, Pallas kernels for 0%

profile of v5, /device:TPU:1, one launch (start us, length us, event | category | flops | bytes accessed | tf_op | source)
XLA Modules:
  0.0 181.9 jit_solution(1390320148594302713)
XLA Ops:
  7.2 0.0 copy-start
  7.2 0.0 copy-start.1
  7.2 0.0 all-gather.2.cloned.1.call-start
  7.2 1.1 copy-done
  8.3 1.3 fusion.8
  9.7 20.0 %all_to_all.15 = f32[128,32,16]{0,2,1:T(8,128)S(1)} all-to-all(f32[128,32,16]{0,2,1:T(8,128)S(1)} %fusion.8), channel_id=1, replica_groups=mesh['mp'=2,'hi'=8,'lo'=4,'tok'=8] {'hi','lo'}, dimensions={1} | all-to-all | bytes 524288 | tf_op jit(solution)/shard_map/all_to_all | solution.py:38
  29.7 7.1 %collective-permute-start.1 = (f32[128,16]{0,1:T(8,128)S(1)}, f32[128,16]{0,1:T(8,128)S(1)}, u32[]{:S(2)}, u32[]{:S(2)}) collective-permute-start(f32[128,16]{0,1:T(8,128)S(1)} %reduce_sum.36), channel_id=1, source_target_pairs={{0,0},{1,32},{2,64},{3,96},{4,128},{5,160},{6,192},{7,224},{32,1},... | collective-permute-start | bytes 24584 | tf_op jit(solution)/shard_map/ppermute | solution.py:40
  36.8 0.0 copy-done.1
  36.9 0.2 copy.33
  37.0 2.3 %collective-permute-start = (bf16[128,896]{0,1:T(8,128)(2,1)S(1)}, bf16[128,896]{0,1:T(8,128)(2,1)S(1)}, u32[]{:S(2)}, u32[]{:S(2)}) collective-permute-start(bf16[128,896]{0,1:T(8,128)(2,1)S(1)} %bitcast.31), channel_id=1, source_target_pairs={{0,0},{1,32},{2,64},{3,96},{4,128},{5,160},{6,192},{7,224},{32,1},... | collective-permute-start | bytes 688136 | tf_op jit(solution)/shard_map/ppermute | solution.py:33
  39.4 0.0 collective-permute-done.1
  39.4 11.4 %collective-permute-done = bf16[128,896]{0,1:T(8,128)(2,1)S(1)} collective-permute-done((bf16[128,896]{0,1:T(8,128)(2,1)S(1)}, bf16[128,896]{0,1:T(8,128)(2,1)S(1)}, u32[]{:S(2)}, u32[]{:S(2)}) %collective-permute-start) | collective-permute-done | bytes 229408 | tf_op jit(solution)/shard_map/ppermute | solution.py:33
  50.8 0.7 pad_maximum_fusion.1
  51.5 0.0 all-gather.2.cloned.1.call-update
  51.5 10.2 %all_gather.10 = bf16[128,128]{0,1:T(8,128)(2,1)S(1)} all-gather(bf16[128,32]{0,1:T(8,128)(2,1)S(1)} %slice.33), channel_id=1, replica_groups=mesh['mp'=2,'hi'=8,'lo'=4,'tok'=8] {'lo'}, dimensions={1}, use_global_device_ids=true | all-gather | bytes 40960 | tf_op jit(solution)/shard_map/all_gather | solution.py:29
  61.8 30.7 %all_gather.11 = bf16[1024,128]{0,1:T(8,128)(2,1)S(1)} all-gather(bf16[128,128]{0,1:T(8,128)(2,1)S(1)} %all_gather.10), channel_id=1, replica_groups=mesh['mp'=2,'hi'=8,'lo'=4,'tok'=8] {'tok'}, dimensions={0}, use_global_device_ids=true | all-gather | bytes 294912 | tf_op jit(solution)/shard_map/all_gather | solution.py:30
  92.4 0.1 multiply_reduce_fusion
  92.6 0.1 copy.39
  92.7 0.1 broadcast_select_fusion
  92.7 45.7 %all-gather.2.cloned.1.call-done = bf16[1024,928]{0,1:T(8,128)(2,1)} async-done(((bf16[128,928]{0,1:T(8,128)(2,1)}), bf16[1024,928]{0,1:T(8,128)(2,1)}) %all-gather.2.cloned.1.call-update) | async-done | bytes 1900560 | tf_op jit(solution)/shard_map/all_gather | solution.py:46
  138.4 1.1 fusion.5
  139.5 2.2 %fusion.2 = f32[128,896]{0,1:T(8,128)S(1)} fusion(bf16[1024,128]{0,1:T(8,128)(2,1)S(1)} %all_gather.11, bf16[1024,928]{0,1:T(8,128)(2,1)} %all-gather.2.cloned.1.call-done), kind=kOutput, calls=%fused_computation.2 | convolution fusion | flops 234881024 | bytes 2555904 | tf_op jit(solution)/shard_map/dot_general | solution.py:50
  141.7 0.2 copy.38
  141.9 1.1 maximum_maximum_fusion
  143.1 5.3 %all-to-all-start.1 = ((f32[8,32,976]{2,1,0:T(8,128)}), f32[8,32,976]{2,1,0:T(8,128)S(1)}, u32[]{:S(2)}, u32[]{:S(2)}) async-start(f32[8,32,976]{2,1,0:T(8,128)} %maximum_maximum_fusion), calls=%async_computation.1 | async-start | bytes 2097152 | tf_op jit(solution)/shard_map/all_to_all | solution.py:69
  148.4 24.8 %all-to-all-done.1 = f32[8,32,976]{2,1,0:T(8,128)S(1)} async-done(((f32[8,32,976]{2,1,0:T(8,128)}), f32[8,32,976]{2,1,0:T(8,128)S(1)}, u32[]{:S(2)}, u32[]{:S(2)}) %all-to-all-start.1) | async-done | bytes 999456 | tf_op jit(solution)/shard_map/all_to_all | solution.py:69
  173.2 0.1 reduce_sum.38
  173.3 0.1 slice_reduce_fusion
  173.4 0.1 fusion.6
  173.5 0.1 copy.41
  173.6 0.1 copy.42
  173.6 0.8 copy.48
  174.5 0.6 add.15
  (10 shorter events, 0.1 us)
Async XLA Ops:
  7.2 1.2 copy-start
  7.2 29.7 %copy-start.1 = (bf16[1,128,896]{2,1,0:T(8,128)(2,1)S(1)}, bf16[1,128,896]{2,1,0:T(8,128)(2,1)}, u32[]{:S(2)}) copy-start(bf16[1,128,896]{2,1,0:T(8,128)(2,1)} %param.2) | copy-start | bytes 688132
  7.2 131.3 %all-gather.2.cloned.1.call-start = ((), (), s32[]{:S(2)}) async-start(), calls=%async_computation.2 | async-start | bytes 2138112 | tf_op jit(solution)/shard_map/all_gather | solution.py:46
  29.7 9.7 %collective-permute-start.1 = (f32[128,16]{0,1:T(8,128)S(1)}, f32[128,16]{0,1:T(8,128)S(1)}, u32[]{:S(2)}, u32[]{:S(2)}) collective-permute-start(f32[128,16]{0,1:T(8,128)S(1)} %reduce_sum.36), channel_id=1, source_target_pairs={{0,0},{1,32},{2,64},{3,96},{4,128},{5,160},{6,192},{7,224},{32,1},... | collective-permute-start | bytes 24584 | tf_op jit(solution)/shard_map/ppermute | solution.py:40
  37.0 13.7 %collective-permute-start = (bf16[128,896]{0,1:T(8,128)(2,1)S(1)}, bf16[128,896]{0,1:T(8,128)(2,1)S(1)}, u32[]{:S(2)}, u32[]{:S(2)}) collective-permute-start(bf16[128,896]{0,1:T(8,128)(2,1)S(1)} %bitcast.31), channel_id=1, source_target_pairs={{0,0},{1,32},{2,64},{3,96},{4,128},{5,160},{6,192},{7,224},{32,1},... | collective-permute-start | bytes 688136 | tf_op jit(solution)/shard_map/ppermute | solution.py:33
  143.1 30.1 %all-to-all-start.1 = ((f32[8,32,976]{2,1,0:T(8,128)}), f32[8,32,976]{2,1,0:T(8,128)S(1)}, u32[]{:S(2)}, u32[]{:S(2)}) async-start(f32[8,32,976]{2,1,0:T(8,128)} %maximum_maximum_fusion), calls=%async_computation.1 | async-start | bytes 2097152 | tf_op jit(solution)/shard_map/all_to_all | solution.py:69
Sparse Core Ops, SparseCore 0:
  51.6 86.7 all-gather.1

commit v6 on v5

--- a/solution.py
+++ b/solution.py
@@ -43,7 +43,8 @@
     y_low = (y_mine - y_round).astype(jnp.bfloat16)
 
     payload = jnp.concatenate([x_swapped, y_high, y_low], axis=1)
-    full = lax.all_gather(payload, "hi", axis=0, tiled=True)
+    spread = jnp.broadcast_to(payload[None], (hi_count,) + payload.shape)
+    full = lax.all_to_all(spread, "hi", 0, 0, tiled=True).reshape(hi_count * tokens, -1)
     x_full = full[:, :span_width]
     y_tok = full[:, span_width:span_width + col_group].astype(jnp.float32) + full[:, span_width + col_group:].astype(jnp.float32)
 

time: 183 us -> 168 us (0.918)
  waiting for transfers between devices: 81.9 us -> 37.6 us
  blocking collectives: 60.9 us -> 86.4 us
  starting transfers between devices: 14.8 us -> 34.1 us
  between operations: 14.2 us -> 0.8 us
  matrix products: 4.57 us -> 2.31 us
  local copies, waits for them, and re-layouts: 2.54 us -> 4.38 us
    all_gather x1 -> x0, waiting for transfers between devices: 45.7 us -> none  [local(): full = lax.all_gather(payload, 'hi', axis=0, tiled=True)]
    all_gather x1, blocking collectives: 10.2 us -> 49.5 us  [local(): win_lo = lax.all_gather(x_local[:, :ROW_DEV], 'lo', axis=1, tiled=True)]
    all_to_all x0 -> x1, starting transfers between devices: none -> 20.1 us  [local(): lax.all_to_all(spread, 'hi', 0, 0, tiled=True)]
    all_gather x1, blocking collectives: 30.7 us -> 16.9 us  [local(): wins = lax.all_gather(win_lo, 'tok', axis=0, tiled=True)]
  transfers between devices with their start and end apart: 4 -> 4, of which waited for: 3 -> 2; matrix products, arithmetic and copies ran while one was open for 0% -> 0% of each run, Pallas kernels for 0% -> 0%
where the time goes in v6:
time: 168 us
  blocking collectives  86.4 us (51%)
  waiting for transfers between devices  37.6 us (22%)
  starting transfers between devices  34.1 us (20%)
  local copies, waits for them, and re-layouts  4.38 us (3%)
  other arithmetic  2.34 us (1%)
  matrix products  2.31 us (1%)
    all_gather x1, blocking collectives, local(): win_lo = lax.all_gather(x_local[:, :ROW_DEV], 'lo', axis=1, tiled=True)  49.5 us
    all_to_all x1, waiting for transfers between devices, local(): got = lax.all_to_all(send, ('mp', 'lo'), 0, 0, tiled=True)  26.3 us
    all_to_all x1, starting transfers between devices, local(): lax.all_to_all(spread, 'hi', 0, 0, tiled=True)  20.1 us
    all_to_all x1, blocking collectives, local(): y_parts = lax.all_to_all(y_part, ('hi', 'lo'), 1, 0, tiled=True)  20 us
    all_gather x1, blocking collectives, local(): wins = lax.all_gather(win_lo, 'tok', axis=0, tiled=True)  16.9 us
    ppermute x1, waiting for transfers between devices, local(): x_swapped = lax.ppermute(x_local, ('hi', 'tok'), swap)  11.3 us
    ppermute x1, starting transfers between devices, local(): y_mine = lax.ppermute(y_mine, ('hi', 'tok'), swap)  7.12 us
    all_to_all x1, starting transfers between devices, local(): got = lax.all_to_all(send, ('mp', 'lo'), 0, 0, tiled=True)  4.57 us
  transfers between devices with their start and end apart: 4, of which 2 were waited for; matrix products, arithmetic and copies ran while one was open for 0% of the time, Pallas kernels for 0%

profile of v6, /device:TPU:1, one launch (start us, length us, event | category | flops | bytes accessed | tf_op | source)
XLA Modules:
  0.0 168.0 jit_solution(6764497929651095927)
XLA Ops:
  0.6 0.0 copy-start
  0.6 0.0 copy-start.1
  0.7 1.2 copy-done
  1.8 1.3 fusion.8
  3.2 20.0 %all_to_all.20 = f32[128,32,16]{0,2,1:T(8,128)S(1)} all-to-all(f32[128,32,16]{0,2,1:T(8,128)S(1)} %fusion.8), channel_id=1, replica_groups=mesh['mp'=2,'hi'=8,'lo'=4,'tok'=8] {'hi','lo'}, dimensions={1} | all-to-all | bytes 524288 | tf_op jit(solution)/shard_map/all_to_all | solution.py:38
  23.2 7.1 %collective-permute-start.1 = (f32[128,16]{0,1:T(8,128)S(1)}, f32[128,16]{0,1:T(8,128)S(1)}, u32[]{:S(2)}, u32[]{:S(2)}) collective-permute-start(f32[128,16]{0,1:T(8,128)S(1)} %reduce_sum.36), channel_id=1, source_target_pairs={{0,0},{1,32},{2,64},{3,96},{4,128},{5,160},{6,192},{7,224},{32,1},... | collective-permute-start | bytes 24584 | tf_op jit(solution)/shard_map/ppermute | solution.py:40
  30.3 0.0 copy-done.1
  30.3 0.2 copy.34
  30.5 2.4 %collective-permute-start = (bf16[128,896]{0,1:T(8,128)(2,1)S(1)}, bf16[128,896]{0,1:T(8,128)(2,1)S(1)}, u32[]{:S(2)}, u32[]{:S(2)}) collective-permute-start(bf16[128,896]{0,1:T(8,128)(2,1)S(1)} %bitcast.36), channel_id=1, source_target_pairs={{0,0},{1,32},{2,64},{3,96},{4,128},{5,160},{6,192},{7,224},{32,1},... | collective-permute-start | bytes 688136 | tf_op jit(solution)/shard_map/ppermute | solution.py:33
  32.9 0.0 collective-permute-done.1
  32.9 11.3 %collective-permute-done = bf16[128,896]{0,1:T(8,128)(2,1)S(1)} collective-permute-done((bf16[128,896]{0,1:T(8,128)(2,1)S(1)}, bf16[128,896]{0,1:T(8,128)(2,1)S(1)}, u32[]{:S(2)}, u32[]{:S(2)}) %collective-permute-start) | collective-permute-done | bytes 229408 | tf_op jit(solution)/shard_map/ppermute | solution.py:33
  44.2 1.5 broadcast_in_dim.29
  45.8 20.1 %all-to-all-start.1 = ((bf16[8,128,928]{1,2,0:T(8,128)(2,1)}), bf16[8,128,928]{1,2,0:T(8,128)(2,1)S(1)}, u32[]{:S(2)}, u32[]{:S(2)}) async-start(bf16[8,128,928]{1,2,0:T(8,128)(2,1)} %broadcast_in_dim.29), calls=%async_computation.1 | async-start | bytes 3801088 | tf_op jit(solution)/shard_map/all_to_all | solution.py:47
  65.9 49.5 %all_gather.6 = bf16[128,128]{0,1:T(8,128)(2,1)S(1)} all-gather(bf16[128,32]{0,1:T(8,128)(2,1)S(1)} %slice.33), channel_id=1, replica_groups=mesh['mp'=2,'hi'=8,'lo'=4,'tok'=8] {'lo'}, dimensions={1}, use_global_device_ids=true | all-gather | bytes 40960 | tf_op jit(solution)/shard_map/all_gather | solution.py:29
  115.3 16.9 %all_gather.7 = bf16[1024,128]{0,1:T(8,128)(2,1)S(1)} all-gather(bf16[128,128]{0,1:T(8,128)(2,1)S(1)} %all_gather.6), channel_id=1, replica_groups=mesh['mp'=2,'hi'=8,'lo'=4,'tok'=8] {'tok'}, dimensions={0}, use_global_device_ids=true | all-gather | bytes 294912 | tf_op jit(solution)/shard_map/all_gather | solution.py:30
  132.3 0.1 multiply_reduce_fusion
  132.4 0.1 copy.41
  132.5 0.1 broadcast_select_fusion
  132.6 0.0 all-to-all-done.1
  132.6 0.3 copy_bitcast_fusion
  132.9 0.3 fusion.5
  133.2 0.7 fusion.2
  133.9 0.2 copy.40
  134.1 1.1 maximum_maximum_fusion
  135.2 4.6 %all-to-all-start.2 = ((f32[8,32,976]{2,1,0:T(8,128)}), f32[8,32,976]{2,1,0:T(8,128)S(1)}, u32[]{:S(2)}, u32[]{:S(2)}) async-start(f32[8,32,976]{2,1,0:T(8,128)} %maximum_maximum_fusion), calls=%async_computation.2 | async-start | bytes 2097152 | tf_op jit(solution)/shard_map/all_to_all | solution.py:70
  139.8 26.3 %all-to-all-done.2 = f32[8,32,976]{2,1,0:T(8,128)S(1)} async-done(((f32[8,32,976]{2,1,0:T(8,128)}), f32[8,32,976]{2,1,0:T(8,128)S(1)}, u32[]{:S(2)}, u32[]{:S(2)}) %all-to-all-start.2) | async-done | bytes 999456 | tf_op jit(solution)/shard_map/all_to_all | solution.py:70
  166.1 0.1 reduce_sum.38
  166.2 0.1 slice_reduce_fusion
  166.3 0.1 fusion.6
  166.4 0.1 copy.43
  166.5 0.1 copy.44
  166.6 0.8 copy.51
  167.4 0.6 add.15
  (11 shorter events, 0.1 us)
Async XLA Ops:
  0.6 1.2 copy-start
  0.6 29.7 %copy-start.1 = (bf16[1,128,896]{2,1,0:T(8,128)(2,1)S(1)}, bf16[1,128,896]{2,1,0:T(8,128)(2,1)}, u32[]{:S(2)}) copy-start(bf16[1,128,896]{2,1,0:T(8,128)(2,1)} %param.2) | copy-start | bytes 688132
  23.2 9.7 %collective-permute-start.1 = (f32[128,16]{0,1:T(8,128)S(1)}, f32[128,16]{0,1:T(8,128)S(1)}, u32[]{:S(2)}, u32[]{:S(2)}) collective-permute-start(f32[128,16]{0,1:T(8,128)S(1)} %reduce_sum.36), channel_id=1, source_target_pairs={{0,0},{1,32},{2,64},{3,96},{4,128},{5,160},{6,192},{7,224},{32,1},... | collective-permute-start | bytes 24584 | tf_op jit(solution)/shard_map/ppermute | solution.py:40
  30.5 13.7 %collective-permute-start = (bf16[128,896]{0,1:T(8,128)(2,1)S(1)}, bf16[128,896]{0,1:T(8,128)(2,1)S(1)}, u32[]{:S(2)}, u32[]{:S(2)}) collective-permute-start(bf16[128,896]{0,1:T(8,128)(2,1)S(1)} %bitcast.36), channel_id=1, source_target_pairs={{0,0},{1,32},{2,64},{3,96},{4,128},{5,160},{6,192},{7,224},{32,1},... | collective-permute-start | bytes 688136 | tf_op jit(solution)/shard_map/ppermute | solution.py:33
  45.8 86.8 %all-to-all-start.1 = ((bf16[8,128,928]{1,2,0:T(8,128)(2,1)}), bf16[8,128,928]{1,2,0:T(8,128)(2,1)S(1)}, u32[]{:S(2)}, u32[]{:S(2)}) async-start(bf16[8,128,928]{1,2,0:T(8,128)(2,1)} %broadcast_in_dim.29), calls=%async_computation.1 | async-start | bytes 3801088 | tf_op jit(solution)/shard_map/all_to_all | solution.py:47
  135.2 30.9 %all-to-all-start.2 = ((f32[8,32,976]{2,1,0:T(8,128)}), f32[8,32,976]{2,1,0:T(8,128)S(1)}, u32[]{:S(2)}, u32[]{:S(2)}) async-start(f32[8,32,976]{2,1,0:T(8,128)} %maximum_maximum_fusion), calls=%async_computation.2 | async-start | bytes 2097152 | tf_op jit(solution)/shard_map/all_to_all | solution.py:70

commit v7 on v6

--- a/solution.py
+++ b/solution.py
@@ -28,6 +28,7 @@
 
     win_lo = lax.all_gather(x_local[:, :ROW_DEV], "lo", axis=1, tiled=True)
     wins = lax.all_gather(win_lo, "tok", axis=0, tiled=True)
+    x_local, w_local, wins = lax.optimization_barrier((x_local, w_local, wins))
 
     swap = [(h * tok_count + t, t * tok_count + h) for h in range(hi_count) for t in range(tok_count)]
     x_swapped = lax.ppermute(x_local, ("hi", "tok"), swap)

time: 168 us -> 177 us (1.054)
  blocking collectives: 86.4 us -> 54.4 us
  waiting for transfers between devices: 37.6 us -> 60.5 us
  starting transfers between devices: 34.1 us -> 50.9 us
    all_gather x1, blocking collectives: 49.5 us -> 11.3 us  [local(): win_lo = lax.all_gather(x_local[:, :ROW_DEV], 'lo', axis=1, tiled=True)]
    all_to_all x1, waiting for transfers between devices: 0.01 us -> 27 us  [local(): lax.all_to_all(spread, 'hi', 0, 0, tiled=True)]
    all_to_all x1, starting transfers between devices: 4.57 us -> 25.4 us  [local(): got = lax.all_to_all(send, ('mp', 'lo'), 0, 0, tiled=True)]
    all_gather x1, blocking collectives: 16.9 us -> 23.7 us  [local(): wins = lax.all_gather(win_lo, 'tok', axis=0, tiled=True)]
    all_to_all x1, starting transfers between devices: 20.1 us -> 16 us  [local(): lax.all_to_all(spread, 'hi', 0, 0, tiled=True)]
    ppermute x1, waiting for transfers between devices: 11.3 us -> 8.53 us  [local(): x_swapped = lax.ppermute(x_local, ('hi', 'tok'), swap)]
  transfers between devices with their start and end apart: 4 -> 4, of which waited for: 2 -> 3; matrix products, arithmetic and copies ran while one was open for 0% -> 1% of each run, Pallas kernels for 0% -> 0%
where the time goes in v7:
time: 177 us; the launch traced here: 176 us
  waiting for transfers between devices  60.5 us (34%)
  blocking collectives  54.4 us (31%)
  starting transfers between devices  50.9 us (29%)
  local copies, waits for them, and re-layouts  4.01 us (2%)
  other arithmetic  3.09 us (2%)
  matrix products  2.61 us (1%)
    all_to_all x1, waiting for transfers between devices, local(): lax.all_to_all(spread, 'hi', 0, 0, tiled=True)  27 us
    all_to_all x1, starting transfers between devices, local(): got = lax.all_to_all(send, ('mp', 'lo'), 0, 0, tiled=True)  25.4 us
    all_to_all x1, waiting for transfers between devices, local(): got = lax.all_to_all(send, ('mp', 'lo'), 0, 0, tiled=True)  25 us
    all_gather x1, blocking collectives, local(): wins = lax.all_gather(win_lo, 'tok', axis=0, tiled=True)  23.7 us
    all_to_all x1, blocking collectives, local(): y_parts = lax.all_to_all(y_part, ('hi', 'lo'), 1, 0, tiled=True)  19.3 us
    all_to_all x1, starting transfers between devices, local(): lax.all_to_all(spread, 'hi', 0, 0, tiled=True)  16 us
    all_gather x1, blocking collectives, local(): win_lo = lax.all_gather(x_local[:, :ROW_DEV], 'lo', axis=1, tiled=True)  11.3 us
    ppermute x1, waiting for transfers between devices, local(): x_swapped = lax.ppermute(x_local, ('hi', 'tok'), swap)  8.53 us
  transfers between devices with their start and end apart: 4, of which 3 were waited for; matrix products, arithmetic and copies ran while one was open for 1% of the time, Pallas kernels for 0%

profile of v7, /device:TPU:1, one launch (start us, length us, event | category | flops | bytes accessed | tf_op | source)
XLA Modules:
  0.0 176.3 jit_solution(4596481121518355712)
XLA Ops:
  0.6 1.1 copy.33
  1.7 11.3 %all_gather.6 = bf16[128,128]{0,1:T(8,128)(2,1)S(1)} all-gather(bf16[128,32]{0,1:T(8,128)(2,1)S(1)} %slice.32), channel_id=1, replica_groups=mesh['mp'=2,'hi'=8,'lo'=4,'tok'=8] {'lo'}, dimensions={1}, use_global_device_ids=true | all-gather | bytes 40960 | tf_op jit(solution)/shard_map/all_gather | solution.py:29
  13.0 23.7 %all_gather.7 = bf16[1024,128]{0,1:T(8,128)(2,1)S(1)} all-gather(bf16[128,128]{0,1:T(8,128)(2,1)S(1)} %all_gather.6), channel_id=1, replica_groups=mesh['mp'=2,'hi'=8,'lo'=4,'tok'=8] {'tok'}, dimensions={0}, use_global_device_ids=true | all-gather | bytes 294912 | tf_op jit(solution)/shard_map/all_gather | solution.py:30
  36.8 1.6 fusion.10
  38.4 19.3 %all_to_all.23 = f32[128,32,16]{0,2,1:T(8,128)S(1)} all-to-all(f32[128,32,16]{0,2,1:T(8,128)S(1)} %bitcast.25), channel_id=1, replica_groups=mesh['mp'=2,'hi'=8,'lo'=4,'tok'=8] {'hi','lo'}, dimensions={1} | all-to-all | bytes 524288 | tf_op jit(solution)/shard_map/all_to_all | solution.py:39
  57.8 6.6 %collective-permute-start.1 = (f32[128,16]{0,1:T(8,128)S(1)}, f32[128,16]{0,1:T(8,128)S(1)}, u32[]{:S(2)}, u32[]{:S(2)}) collective-permute-start(f32[128,16]{0,1:T(8,128)S(1)} %reduce_sum.36), channel_id=1, source_target_pairs={{0,0},{1,32},{2,64},{3,96},{4,128},{5,160},{6,192},{7,224},{32,1},... | collective-permute-start | bytes 24584 | tf_op jit(solution)/shard_map/ppermute | solution.py:41
  64.4 2.8 %collective-permute-start = (bf16[128,896]{0,1:T(8,128)(2,1)S(1)}, bf16[128,896]{0,1:T(8,128)(2,1)S(1)}, u32[]{:S(2)}, u32[]{:S(2)}) collective-permute-start(bf16[128,896]{0,1:T(8,128)(2,1)S(1)} %bitcast.30), channel_id=1, source_target_pairs={{0,0},{1,32},{2,64},{3,96},{4,128},{5,160},{6,192},{7,224},{32,1},... | collective-permute-start | bytes 688136 | tf_op jit(solution)/shard_map/ppermute | solution.py:34
  67.3 0.0 collective-permute-done.1
  67.3 8.5 %collective-permute-done = bf16[128,896]{0,1:T(8,128)(2,1)S(1)} collective-permute-done((bf16[128,896]{0,1:T(8,128)(2,1)S(1)}, bf16[128,896]{0,1:T(8,128)(2,1)S(1)}, u32[]{:S(2)}, u32[]{:S(2)}) %collective-permute-start) | collective-permute-done | bytes 229408 | tf_op jit(solution)/shard_map/ppermute | solution.py:34
  75.8 1.5 broadcast_in_dim.29
  77.4 16.0 %all-to-all-start.1 = ((bf16[8,128,928]{1,2,0:T(8,128)(2,1)}), bf16[8,128,928]{1,2,0:T(8,128)(2,1)S(1)}, u32[]{:S(2)}, u32[]{:S(2)}) async-start(bf16[8,128,928]{1,2,0:T(8,128)(2,1)} %broadcast_in_dim.29), calls=%async_computation.1 | async-start | bytes 3801088 | tf_op jit(solution)/shard_map/all_to_all | solution.py:48
  93.4 0.1 multiply_reduce_fusion
  93.5 0.7 multiply_bitcast_fusion
  94.2 0.1 copy.37
  94.3 0.1 broadcast_select_fusion
  94.4 27.0 %all-to-all-done.1 = bf16[8,128,928]{1,2,0:T(8,128)(2,1)S(1)} async-done(((bf16[8,128,928]{1,2,0:T(8,128)(2,1)}), bf16[8,128,928]{1,2,0:T(8,128)(2,1)S(1)}, u32[]{:S(2)}, u32[]{:S(2)}) %all-to-all-start.1) | async-done | bytes 1900576 | tf_op jit(solution)/shard_map/all_to_all | solution.py:48
  121.3 0.2 copy_bitcast_fusion
  121.6 0.7 fusion
  122.3 0.3 convolution_multiply_fusion
  122.6 0.1 copy.36
  122.8 0.1 pad_maximum_fusion
  122.8 1.1 maximum_maximum_fusion
  124.0 25.4 %all-to-all-start.2 = ((f32[8,32,976]{2,1,0:T(8,128)}), f32[8,32,976]{2,1,0:T(8,128)S(1)}, u32[]{:S(2)}, u32[]{:S(2)}) async-start(f32[8,32,976]{2,1,0:T(8,128)} %maximum_maximum_fusion), calls=%async_computation.2 | async-start | bytes 2097152 | tf_op jit(solution)/shard_map/all_to_all | solution.py:71
  149.4 25.0 %all-to-all-done.2 = f32[8,32,976]{2,1,0:T(8,128)S(1)} async-done(((f32[8,32,976]{2,1,0:T(8,128)}), f32[8,32,976]{2,1,0:T(8,128)S(1)}, u32[]{:S(2)}, u32[]{:S(2)}) %all-to-all-start.2) | async-done | bytes 999456 | tf_op jit(solution)/shard_map/all_to_all | solution.py:71
  174.4 0.1 reduce_sum.38
  174.6 0.1 slice_reduce_fusion
  174.6 0.1 copy.39
  174.7 0.1 copy.40
  174.8 0.1 fusion.2
  174.9 0.8 copy.43
  175.7 0.6 add.15
  (8 shorter events, 0.1 us)
Async XLA Ops:
  57.8 9.5 %collective-permute-start.1 = (f32[128,16]{0,1:T(8,128)S(1)}, f32[128,16]{0,1:T(8,128)S(1)}, u32[]{:S(2)}, u32[]{:S(2)}) collective-permute-start(f32[128,16]{0,1:T(8,128)S(1)} %reduce_sum.36), channel_id=1, source_target_pairs={{0,0},{1,32},{2,64},{3,96},{4,128},{5,160},{6,192},{7,224},{32,1},... | collective-permute-start | bytes 24584 | tf_op jit(solution)/shard_map/ppermute | solution.py:41
  64.4 11.4 %collective-permute-start = (bf16[128,896]{0,1:T(8,128)(2,1)S(1)}, bf16[128,896]{0,1:T(8,128)(2,1)S(1)}, u32[]{:S(2)}, u32[]{:S(2)}) collective-permute-start(bf16[128,896]{0,1:T(8,128)(2,1)S(1)} %bitcast.30), channel_id=1, source_target_pairs={{0,0},{1,32},{2,64},{3,96},{4,128},{5,160},{6,192},{7,224},{32,1},... | collective-permute-start | bytes 688136 | tf_op jit(solution)/shard_map/ppermute | solution.py:34
  77.4 44.0 %all-to-all-start.1 = ((bf16[8,128,928]{1,2,0:T(8,128)(2,1)}), bf16[8,128,928]{1,2,0:T(8,128)(2,1)S(1)}, u32[]{:S(2)}, u32[]{:S(2)}) async-start(bf16[8,128,928]{1,2,0:T(8,128)(2,1)} %broadcast_in_dim.29), calls=%async_computation.1 | async-start | bytes 3801088 | tf_op jit(solution)/shard_map/all_to_all | solution.py:48
  124.0 50.4 %all-to-all-start.2 = ((f32[8,32,976]{2,1,0:T(8,128)}), f32[8,32,976]{2,1,0:T(8,128)S(1)}, u32[]{:S(2)}, u32[]{:S(2)}) async-start(f32[8,32,976]{2,1,0:T(8,128)} %maximum_maximum_fusion), calls=%async_computation.2 | async-start | bytes 2097152 | tf_op jit(solution)/shard_map/all_to_all | solution.py:71

commit v8 on v6

--- a/solution.py
+++ b/solution.py
@@ -2,12 +2,39 @@
 import jax.numpy as jnp
 import numpy as np
 from jax import lax
+from jax.experimental import pallas as pl
+from jax.experimental.pallas import tpu as pltpu
 from jax.sharding import Mesh, PartitionSpec as P
 
 ROW_DEV = 32
 
 
 OFF_SCALE = 0.9
+
+
+def _pieces_kernel(span_width, col_group, win_ref, full_ref, out_ref):
+    wins = win_ref[...]
+    x_full = full_ref[:, :span_width]
+    y_tok = (full_ref[:, span_width:span_width + col_group].astype(jnp.float32)
+             + full_ref[:, span_width + col_group:].astype(jnp.float32))
+    out_ref[:, :span_width] = lax.dot_general(
+        wins, x_full, (((0,), (0,)), ((), ())), preferred_element_type=jnp.float32
+    )
+    cross = lax.dot_general(
+        wins.astype(jnp.float32), y_tok, (((0,), (0,)), ((), ())),
+        precision=lax.Precision.HIGHEST, preferred_element_type=jnp.float32,
+    )
+    out_ref[:, span_width:] = OFF_SCALE * cross
+
+
+def window_pieces(wins, full, span_width, col_group):
+    rows = wins.shape[1]
+    return pl.pallas_call(
+        lambda *refs: _pieces_kernel(span_width, col_group, *refs),
+        out_shape=jax.ShapeDtypeStruct((rows, span_width + col_group), jnp.float32),
+        in_specs=[pl.BlockSpec(memory_space=pltpu.VMEM)] * 2,
+        out_specs=pl.BlockSpec(memory_space=pltpu.VMEM),
+    )(wins, full)
 
 
 def local(inputs, down_weight):
@@ -45,17 +72,7 @@
     payload = jnp.concatenate([x_swapped, y_high, y_low], axis=1)
     spread = jnp.broadcast_to(payload[None], (hi_count,) + payload.shape)
     full = lax.all_to_all(spread, "hi", 0, 0, tiled=True).reshape(hi_count * tokens, -1)
-    x_full = full[:, :span_width]
-    y_tok = full[:, span_width:span_width + col_group].astype(jnp.float32) + full[:, span_width + col_group:].astype(jnp.float32)
-
-    gram = lax.dot_general(
-        wins, x_full, (((0,), (0,)), ((), ())), preferred_element_type=jnp.float32
-    )
-    cross = lax.dot_general(
-        wins.astype(jnp.float32), y_tok, (((0,), (0,)), ((), ())),
-        precision=lax.Precision.HIGHEST, preferred_element_type=jnp.float32,
-    )
-    pieces = jnp.concatenate([gram, OFF_SCALE * cross], axis=1)
+    pieces = window_pieces(wins, full, span_width, col_group)
     pieces = pieces.reshape(group, ROW_DEV, span_width + col_group)
 
     win_own = lax.dynamic_slice_in_dim(wins, lo_index * ROW_DEV, ROW_DEV, 1).astype(jnp.float32)

time: 168 us -> 175 us (1.042)
  Pallas kernels: 0 us -> 3.45 us
  local copies, waits for them, and re-layouts: 4.38 us -> 6.89 us
    pallas_call x0 -> x1, Pallas kernels: none -> 3.45 us  [window_pieces(): pl.pallas_call(lambda *refs: _pieces_kernel(span_width, col_group, *refs)...]
    all_to_all x0 -> x1, local copies, waits for them, and re-layouts: none -> 2.86 us  [local(): lax.all_to_all(spread, 'hi', 0, 0, tiled=True)]
where the time goes in v8:
time: 175 us; the launch traced here: 174 us
  blocking collectives  87.3 us (50%)
  waiting for transfers between devices  37.6 us (21%)
  starting transfers between devices  33.1 us (19%)
  local copies, waits for them, and re-layouts  6.89 us (4%)
  other arithmetic  3.6 us (2%)
  Pallas kernels  3.45 us (2%)
    all_gather x1, blocking collectives, local(): win_lo = lax.all_gather(x_local[:, :ROW_DEV], 'lo', axis=1, tiled=True)  49.5 us
    all_to_all x1, waiting for transfers between devices, local(): got = lax.all_to_all(send, ('mp', 'lo'), 0, 0, tiled=True)  26.3 us
    all_to_all x1, starting transfers between devices, local(): lax.all_to_all(spread, 'hi', 0, 0, tiled=True)  20.1 us
    all_to_all x1, blocking collectives, local(): y_parts = lax.all_to_all(y_part, ('hi', 'lo'), 1, 0, tiled=True)  20 us
    all_gather x1, blocking collectives, local(): wins = lax.all_gather(win_lo, 'tok', axis=0, tiled=True)  17.8 us
    ppermute x1, waiting for transfers between devices, local(): x_swapped = lax.ppermute(x_local, ('hi', 'tok'), swap)  11.4 us
    ppermute x1, starting transfers between devices, local(): y_mine = lax.ppermute(y_mine, ('hi', 'tok'), swap)  7.12 us
    all_to_all x1, starting transfers between devices, local(): got = lax.all_to_all(send, ('mp', 'lo'), 0, 0, tiled=True)  3.61 us
  transfers between devices with their start and end apart: 4, of which 2 were waited for; matrix products, arithmetic and copies ran while one was open for 0% of the time, Pallas kernels for 0%

profile of v8, /device:TPU:1, one launch (start us, length us, event | category | flops | bytes accessed | tf_op | source)
XLA Modules:
  0.0 174.1 jit_solution(3000124928014536376)
XLA Ops:
  0.6 0.0 copy-start
  0.6 0.0 copy-start.2
  0.7 1.2 copy-done
  1.8 1.3 fusion.2
  3.2 20.0 %all_to_all.20 = f32[128,32,16]{0,2,1:T(8,128)S(1)} all-to-all(f32[128,32,16]{0,2,1:T(8,128)S(1)} %fusion.2), channel_id=1, replica_groups=mesh['mp'=2,'hi'=8,'lo'=4,'tok'=8] {'hi','lo'}, dimensions={1} | all-to-all | bytes 524288 | tf_op jit(solution)/shard_map/all_to_all | solution.py:65
  23.2 7.1 %collective-permute-start.1 = (f32[128,16]{0,1:T(8,128)S(1)}, f32[128,16]{0,1:T(8,128)S(1)}, u32[]{:S(2)}, u32[]{:S(2)}) collective-permute-start(f32[128,16]{0,1:T(8,128)S(1)} %reduce_sum.36), channel_id=1, source_target_pairs={{0,0},{1,32},{2,64},{3,96},{4,128},{5,160},{6,192},{7,224},{32,1},... | collective-permute-start | bytes 24584 | tf_op jit(solution)/shard_map/ppermute | solution.py:67
  30.3 0.0 copy-done.2
  30.3 0.2 copy.30
  30.5 2.3 %collective-permute-start = (bf16[128,896]{0,1:T(8,128)(2,1)S(1)}, bf16[128,896]{0,1:T(8,128)(2,1)S(1)}, u32[]{:S(2)}, u32[]{:S(2)}) collective-permute-start(bf16[128,896]{0,1:T(8,128)(2,1)S(1)} %bitcast.27), channel_id=1, source_target_pairs={{0,0},{1,32},{2,64},{3,96},{4,128},{5,160},{6,192},{7,224},{32,1},... | collective-permute-start | bytes 688136 | tf_op jit(solution)/shard_map/ppermute | solution.py:60
  32.9 0.0 collective-permute-done.1
  32.9 11.4 %collective-permute-done = bf16[128,896]{0,1:T(8,128)(2,1)S(1)} collective-permute-done((bf16[128,896]{0,1:T(8,128)(2,1)S(1)}, bf16[128,896]{0,1:T(8,128)(2,1)S(1)}, u32[]{:S(2)}, u32[]{:S(2)}) %collective-permute-start) | collective-permute-done | bytes 229408 | tf_op jit(solution)/shard_map/ppermute | solution.py:60
  44.2 1.5 broadcast_in_dim.29
  45.8 20.1 %all-to-all-start.1 = ((bf16[8,128,928]{1,2,0:T(8,128)(2,1)}), bf16[8,128,928]{1,2,0:T(8,128)(2,1)S(1)}, u32[]{:S(2)}, u32[]{:S(2)}) async-start(bf16[8,128,928]{1,2,0:T(8,128)(2,1)} %broadcast_in_dim.29), calls=%async_computation.1 | async-start | bytes 3801088 | tf_op jit(solution)/shard_map/all_to_all | solution.py:74
  65.9 49.5 %all_gather.6 = bf16[128,128]{0,1:T(8,128)(2,1)S(1)} all-gather(bf16[128,32]{0,1:T(8,128)(2,1)S(1)} %slice.20), channel_id=1, replica_groups=mesh['mp'=2,'hi'=8,'lo'=4,'tok'=8] {'lo'}, dimensions={1}, use_global_device_ids=true | all-gather | bytes 40960 | tf_op jit(solution)/shard_map/all_gather | solution.py:56
  115.3 0.1 copy.31
  115.5 17.8 %all_gather.7.refs_0_ = bf16[1024,128]{1,0:T(8,128)(2,1)S(1)} all-gather(bf16[128,128]{1,0:T(8,128)(2,1)S(1)} %copy.31), channel_id=1, replica_groups=mesh['mp'=2,'hi'=8,'lo'=4,'tok'=8] {'tok'}, dimensions={0}, use_global_device_ids=true | all-gather | bytes 294912 | tf_op jit(solution)/shard_map/all_gather | solution.py:57
  133.2 0.0 copy-start.1
  133.2 0.2 multiply_reduce_fusion
  133.5 0.1 copy.37
  133.6 0.1 broadcast_select_fusion
  133.7 0.0 all-to-all-done.1
  133.7 2.9 %copy.36 = bf16[8,128,928]{2,1,0:T(8,128)(2,1)} copy(bf16[8,128,928]{1,2,0:T(8,128)(2,1)S(1)} %all-to-all-done.1) | data formatting | bytes 3801088 | tf_op jit(solution)/shard_map/all_to_all | solution.py:74
  136.5 0.0 copy-done.1
  136.5 3.5 %shard_map.41 = f32[128,912]{1,0:T(8,128)} custom-call(bf16[1024,128]{1,0:T(8,128)(2,1)} %copy-done.1, bf16[1024,928]{1,0:T(8,128)(2,1)} %bitcast.23), custom_call_target="tpu_custom_call" | custom-call | tf_op jit(solution)/shard_map/pallas_call | solution.py:32
  140.0 2.3 %maximum_maximum_fusion = f32[8,32,976]{2,1,0:T(8,128)} fusion(f32[4,32,64]{2,1,0:T(8,128)S(1)} %broadcast_select_fusion, f32[4,32,912]{2,1,0:T(8,128)} %bitcast.25), kind=kLoop, calls=%fused_computation | loop fusion | flops 749568 | bytes 1499136 | tf_op jit(solution)/shard_map/concatenate | solution.py:86
  142.3 3.6 %all-to-all-start.2 = ((f32[8,32,976]{2,1,0:T(8,128)}), f32[8,32,976]{2,1,0:T(8,128)S(1)}, u32[]{:S(2)}, u32[]{:S(2)}) async-start(f32[8,32,976]{2,1,0:T(8,128)} %maximum_maximum_fusion), calls=%async_computation.2 | async-start | bytes 2097152 | tf_op jit(solution)/shard_map/all_to_all | solution.py:87
  145.9 26.3 %all-to-all-done.2 = f32[8,32,976]{2,1,0:T(8,128)S(1)} async-done(((f32[8,32,976]{2,1,0:T(8,128)}), f32[8,32,976]{2,1,0:T(8,128)S(1)}, u32[]{:S(2)}, u32[]{:S(2)}) %all-to-all-start.2) | async-done | bytes 999456 | tf_op jit(solution)/shard_map/all_to_all | solution.py:87
  172.2 0.1 reduce_sum.38
  172.3 0.1 slice_reduce_fusion
  172.4 0.1 fusion
  172.5 0.1 copy.39
  172.6 0.1 copy.40
  172.7 0.8 copy.46
  173.5 0.6 add.11
  (10 shorter events, 0.1 us)
Async XLA Ops:
  0.6 1.2 copy-start
  0.6 29.7 %copy-start.2 = (bf16[1,128,896]{2,1,0:T(8,128)(2,1)S(1)}, bf16[1,128,896]{2,1,0:T(8,128)(2,1)}, u32[]{:S(2)}) copy-start(bf16[1,128,896]{2,1,0:T(8,128)(2,1)} %param.2) | copy-start | bytes 688132
  23.2 9.7 %collective-permute-start.1 = (f32[128,16]{0,1:T(8,128)S(1)}, f32[128,16]{0,1:T(8,128)S(1)}, u32[]{:S(2)}, u32[]{:S(2)}) collective-permute-start(f32[128,16]{0,1:T(8,128)S(1)} %reduce_sum.36), channel_id=1, source_target_pairs={{0,0},{1,32},{2,64},{3,96},{4,128},{5,160},{6,192},{7,224},{32,1},... | collective-permute-start | bytes 24584 | tf_op jit(solution)/shard_map/ppermute | solution.py:67
  30.5 13.7 %collective-permute-start = (bf16[128,896]{0,1:T(8,128)(2,1)S(1)}, bf16[128,896]{0,1:T(8,128)(2,1)S(1)}, u32[]{:S(2)}, u32[]{:S(2)}) collective-permute-start(bf16[128,896]{0,1:T(8,128)(2,1)S(1)} %bitcast.27), channel_id=1, source_target_pairs={{0,0},{1,32},{2,64},{3,96},{4,128},{5,160},{6,192},{7,224},{32,1},... | collective-permute-start | bytes 688136 | tf_op jit(solution)/shard_map/ppermute | solution.py:60
  45.8 87.9 %all-to-all-start.1 = ((bf16[8,128,928]{1,2,0:T(8,128)(2,1)}), bf16[8,128,928]{1,2,0:T(8,128)(2,1)S(1)}, u32[]{:S(2)}, u32[]{:S(2)}) async-start(bf16[8,128,928]{1,2,0:T(8,128)(2,1)} %broadcast_in_dim.29), calls=%async_computation.1 | async-start | bytes 3801088 | tf_op jit(solution)/shard_map/all_to_all | solution.py:74
  133.2 3.3 %copy-start.1 = (bf16[1024,128]{1,0:T(8,128)(2,1)}, bf16[1024,128]{1,0:T(8,128)(2,1)S(1)}, u32[]{:S(2)}) copy-start(bf16[1024,128]{1,0:T(8,128)(2,1)S(1)} %all_gather.7.refs_0_) | copy-start | bytes 786436
  142.3 29.9 %all-to-all-start.2 = ((f32[8,32,976]{2,1,0:T(8,128)}), f32[8,32,976]{2,1,0:T(8,128)S(1)}, u32[]{:S(2)}, u32[]{:S(2)}) async-start(f32[8,32,976]{2,1,0:T(8,128)} %maximum_maximum_fusion), calls=%async_computation.2 | async-start | bytes 2097152 | tf_op jit(solution)/shard_map/all_to_all | solution.py:87

commit v9 on v5

--- a/solution.py
+++ b/solution.py
@@ -43,7 +43,12 @@
     y_low = (y_mine - y_round).astype(jnp.bfloat16)
 
     payload = jnp.concatenate([x_swapped, y_high, y_low], axis=1)
-    full = lax.all_gather(payload, "hi", axis=0, tiled=True)
+    half = span_width // 2
+    first = lax.all_gather(payload[:, :half], "hi", axis=0, tiled=True)
+    rest = payload[:, half:]
+    spread = jnp.broadcast_to(rest[None], (hi_count,) + rest.shape)
+    second = lax.all_to_all(spread, "hi", 0, 0, tiled=True).reshape(hi_count * tokens, -1)
+    full = jnp.concatenate([first, second], axis=1)
     x_full = full[:, :span_width]
     y_tok = full[:, span_width:span_width + col_group].astype(jnp.float32) + full[:, span_width + col_group:].astype(jnp.float32)
 

time: 183 us -> 196 us (1.071)
  the two profiles are of different devices: /device:TPU:1 before, /device:TPU:4 now
where the time goes in v9:
time: 196 us
  blocking collectives  119 us (61%)
  waiting for transfers between devices  35.6 us (18%)
  starting transfers between devices  32.4 us (17%)
  local copies, waits for them, and re-layouts  3.8 us (2%)
  matrix products  2.38 us (1%)
  other arithmetic  2.34 us (1%)
    all_gather x1, blocking collectives, local(): first = lax.all_gather(payload[:, :half], 'hi', axis=0, tiled=True)  50.9 us
    all_gather x1, blocking collectives, local(): win_lo = lax.all_gather(x_local[:, :ROW_DEV], 'lo', axis=1, tiled=True)  32.8 us
    all_to_all x1, waiting for transfers between devices, local(): got = lax.all_to_all(send, ('mp', 'lo'), 0, 0, tiled=True)  22.8 us
    all_to_all x1, blocking collectives, local(): y_parts = lax.all_to_all(y_part, ('hi', 'lo'), 1, 0, tiled=True)  20.6 us
    all_gather x1, blocking collectives, local(): wins = lax.all_gather(win_lo, 'tok', axis=0, tiled=True)  14.2 us
    ppermute x1, waiting for transfers between devices, local(): x_swapped = lax.ppermute(x_local, ('hi', 'tok'), swap)  12.7 us
    all_to_all x1, starting transfers between devices, local(): lax.all_to_all(spread, 'hi', 0, 0, tiled=True)  12.7 us
    ppermute x1, starting transfers between devices, local(): y_mine = lax.ppermute(y_mine, ('hi', 'tok'), swap)  12.4 us
  transfers between devices with their start and end apart: 4, of which 2 were waited for; matrix products, arithmetic and copies ran while one was open for 0% of the time, Pallas kernels for 0%

profile of v9, /device:TPU:4, one launch (start us, length us, event | category | flops | bytes accessed | tf_op | source)
XLA Modules:
  0.0 195.8 jit_solution(6101303253316539399)
XLA Ops:
  0.6 0.0 copy-start
  0.6 1.2 copy-done
  1.8 0.0 copy-start.1
  1.8 1.4 fusion.6
  3.2 20.6 %all_to_all.20 = f32[128,32,16]{0,2,1:T(8,128)S(1)} all-to-all(f32[128,32,16]{0,2,1:T(8,128)S(1)} %fusion.6), channel_id=1, replica_groups=mesh['mp'=2,'hi'=8,'lo'=4,'tok'=8] {'hi','lo'}, dimensions={1} | all-to-all | bytes 524288 | tf_op jit(solution)/shard_map/all_to_all | solution.py:38
  23.9 12.4 %collective-permute-start.1 = (f32[128,16]{0,1:T(8,128)S(1)}, f32[128,16]{0,1:T(8,128)S(1)}, u32[]{:S(2)}, u32[]{:S(2)}) collective-permute-start(f32[128,16]{0,1:T(8,128)S(1)} %reduce_sum.36), channel_id=1, source_target_pairs={{0,0},{1,32},{2,64},{3,96},{4,128},{5,160},{6,192},{7,224},{32,1},... | collective-permute-start | bytes 24584 | tf_op jit(solution)/shard_map/ppermute | solution.py:40
  36.3 0.0 copy-done.1
  36.3 0.2 copy.35
  36.5 1.9 collective-permute-start
  38.5 0.0 collective-permute-done.1
  38.5 12.7 %collective-permute-done = bf16[128,896]{0,1:T(8,128)(2,1)S(1)} collective-permute-done((bf16[128,896]{0,1:T(8,128)(2,1)S(1)}, bf16[128,896]{0,1:T(8,128)(2,1)S(1)}, u32[]{:S(2)}, u32[]{:S(2)}) %collective-permute-start) | collective-permute-done | bytes 229408 | tf_op jit(solution)/shard_map/ppermute | solution.py:33
  51.2 1.1 broadcast_in_dim.29
  52.3 12.7 %all-to-all-start.1 = ((bf16[8,128,480]{1,2,0:T(8,128)(2,1)}), bf16[8,128,480]{1,2,0:T(8,128)(2,1)S(1)}, u32[]{:S(2)}, u32[]{:S(2)}) async-start(bf16[8,128,480]{1,2,0:T(8,128)(2,1)} %broadcast_in_dim.29), calls=%async_computation.1 | async-start | bytes 1966080 | tf_op jit(solution)/shard_map/all_to_all | solution.py:50
  65.0 32.8 %all_gather.10 = bf16[128,128]{0,1:T(8,128)(2,1)S(1)} all-gather(bf16[128,32]{0,1:T(8,128)(2,1)S(1)} %slice.41), channel_id=1, replica_groups=mesh['mp'=2,'hi'=8,'lo'=4,'tok'=8] {'lo'}, dimensions={1}, use_global_device_ids=true | all-gather | bytes 40960 | tf_op jit(solution)/shard_map/all_gather | solution.py:29
  97.8 14.2 %all_gather.11 = bf16[1024,128]{0,1:T(8,128)(2,1)S(1)} all-gather(bf16[128,128]{0,1:T(8,128)(2,1)S(1)} %all_gather.10), channel_id=1, replica_groups=mesh['mp'=2,'hi'=8,'lo'=4,'tok'=8] {'tok'}, dimensions={0}, use_global_device_ids=true | all-gather | bytes 294912 | tf_op jit(solution)/shard_map/all_gather | solution.py:30
  112.0 0.1 multiply_reduce_fusion
  112.2 0.1 copy.42
  112.3 0.1 broadcast_select_fusion
  112.4 50.9 %all_gather.9 = bf16[1024,448]{0,1:T(8,128)(2,1)S(1)} all-gather(bf16[128,448]{0,1:T(8,128)(2,1)S(1)} %slice.40), channel_id=1, replica_groups=mesh['mp'=2,'hi'=8,'lo'=4,'tok'=8] {'hi'}, dimensions={0}, use_global_device_ids=true | all-gather | bytes 1032192 | tf_op jit(solution)/shard_map/all_gather | solution.py:47
  163.3 0.0 all-to-all-done.1
  163.3 0.1 copy_bitcast_fusion
  163.4 0.3 fusion.3
  163.8 0.7 fusion.2
  164.5 0.2 copy.41
  164.7 1.1 maximum_maximum_fusion
  165.8 5.3 %all-to-all-start.2 = ((f32[8,32,976]{2,1,0:T(8,128)}), f32[8,32,976]{2,1,0:T(8,128)S(1)}, u32[]{:S(2)}, u32[]{:S(2)}) async-start(f32[8,32,976]{2,1,0:T(8,128)} %maximum_maximum_fusion), calls=%async_computation.2 | async-start | bytes 2097152 | tf_op jit(solution)/shard_map/all_to_all | solution.py:74
  171.1 22.8 %all-to-all-done.2 = f32[8,32,976]{2,1,0:T(8,128)S(1)} async-done(((f32[8,32,976]{2,1,0:T(8,128)}), f32[8,32,976]{2,1,0:T(8,128)S(1)}, u32[]{:S(2)}, u32[]{:S(2)}) %all-to-all-start.2) | async-done | bytes 999456 | tf_op jit(solution)/shard_map/all_to_all | solution.py:74
  194.0 0.1 reduce_sum.38
  194.1 0.1 slice_reduce_fusion
  194.2 0.1 copy.44
  194.3 0.1 copy.45
  194.3 0.1 fusion.4
  194.4 0.8 copy.52
  195.2 0.6 add.15
  (12 shorter events, 0.1 us)
Async XLA Ops:
  0.6 1.2 copy-start
  1.8 34.5 %copy-start.1 = (bf16[1,128,896]{2,1,0:T(8,128)(2,1)S(1)}, bf16[1,128,896]{2,1,0:T(8,128)(2,1)}, u32[]{:S(2)}) copy-start(bf16[1,128,896]{2,1,0:T(8,128)(2,1)} %param.2) | copy-start | bytes 688132
  23.9 14.6 %collective-permute-start.1 = (f32[128,16]{0,1:T(8,128)S(1)}, f32[128,16]{0,1:T(8,128)S(1)}, u32[]{:S(2)}, u32[]{:S(2)}) collective-permute-start(f32[128,16]{0,1:T(8,128)S(1)} %reduce_sum.36), channel_id=1, source_target_pairs={{0,0},{1,32},{2,64},{3,96},{4,128},{5,160},{6,192},{7,224},{32,1},... | collective-permute-start | bytes 24584 | tf_op jit(solution)/shard_map/ppermute | solution.py:40
  36.5 14.7 %collective-permute-start = (bf16[128,896]{0,1:T(8,128)(2,1)S(1)}, bf16[128,896]{0,1:T(8,128)(2,1)S(1)}, u32[]{:S(2)}, u32[]{:S(2)}) collective-permute-start(bf16[128,896]{0,1:T(8,128)(2,1)S(1)} %bitcast.36), channel_id=1, source_target_pairs={{0,0},{1,32},{2,64},{3,96},{4,128},{5,160},{6,192},{7,224},{32,1},... | collective-permute-start | bytes 688136 | tf_op jit(solution)/shard_map/ppermute | solution.py:33
  52.3 111.0 %all-to-all-start.1 = ((bf16[8,128,480]{1,2,0:T(8,128)(2,1)}), bf16[8,128,480]{1,2,0:T(8,128)(2,1)S(1)}, u32[]{:S(2)}, u32[]{:S(2)}) async-start(bf16[8,128,480]{1,2,0:T(8,128)(2,1)} %broadcast_in_dim.29), calls=%async_computation.1 | async-start | bytes 1966080 | tf_op jit(solution)/shard_map/all_to_all | solution.py:50
  165.8 28.1 %all-to-all-start.2 = ((f32[8,32,976]{2,1,0:T(8,128)}), f32[8,32,976]{2,1,0:T(8,128)S(1)}, u32[]{:S(2)}, u32[]{:S(2)}) async-start(f32[8,32,976]{2,1,0:T(8,128)} %maximum_maximum_fusion), calls=%async_computation.2 | async-start | bytes 2097152 | tf_op jit(solution)/shard_map/all_to_all | solution.py:74

commit v10 on v6

--- a/solution.py
+++ b/solution.py
@@ -32,8 +32,9 @@
     swap = [(h * tok_count + t, t * tok_count + h) for h in range(hi_count) for t in range(tok_count)]
     x_swapped = lax.ppermute(x_local, ("hi", "tok"), swap)
 
+    x_for_y, w_for_y, wins, x_swapped = lax.optimization_barrier((x_local, w_local, wins, x_swapped))
     y_part = lax.dot_general(
-        x_local, w_local, (((1,), (1,)), ((), ())), preferred_element_type=jnp.float32
+        x_for_y, w_for_y, (((1,), (1,)), ((), ())), preferred_element_type=jnp.float32
     )
     y_parts = lax.all_to_all(y_part, ("hi", "lo"), 1, 0, tiled=True)
     y_mine = jnp.sum(y_parts.reshape(blk_count, tokens, col_group), axis=0)

time: 168 us -> 171 us (1.018)
  blocking collectives: 86.4 us -> 53.9 us
  starting transfers between devices: 34.1 us -> 56.2 us
  waiting for transfers between devices: 37.6 us -> 51.8 us
    all_gather x1, blocking collectives: 49.5 us -> 11.8 us  [local(): win_lo = lax.all_gather(x_local[:, :ROW_DEV], 'lo', axis=1, tiled=True)]
    all_to_all x1, starting transfers between devices: 4.57 us -> 30.4 us  [local(): got = lax.all_to_all(send, ('mp', 'lo'), 0, 0, tiled=True)]
    all_to_all x1, waiting for transfers between devices: 0.01 us -> 24.3 us  [local(): lax.all_to_all(spread, 'hi', 0, 0, tiled=True)]
    ppermute x1, waiting for transfers between devices: 11.3 us -> 0.01 us  [local(): x_swapped = lax.ppermute(x_local, ('hi', 'tok'), swap)]
    all_to_all x1, starting transfers between devices: 20.1 us -> 10.2 us  [local(): lax.all_to_all(spread, 'hi', 0, 0, tiled=True)]
    ppermute x1, starting transfers between devices: 2.35 us -> 8.84 us  [local(): x_swapped = lax.ppermute(x_local, ('hi', 'tok'), swap)]
    all_to_all x1, blocking collectives: 20 us -> 22.6 us  [local(): y_parts = lax.all_to_all(y_part, ('hi', 'lo'), 1, 0, tiled=True)]
    all_gather x1, blocking collectives: 16.9 us -> 19.5 us  [local(): wins = lax.all_gather(win_lo, 'tok', axis=0, tiled=True)]
  transfers between devices with their start and end apart: 4 -> 4, of which waited for: 2 -> 3; matrix products, arithmetic and copies ran while one was open for 0% -> 0% of each run, Pallas kernels for 0% -> 0%
where the time goes in v10:
time: 171 us
  starting transfers between devices  56.2 us (33%)
  blocking collectives  53.9 us (32%)
  waiting for transfers between devices  51.8 us (30%)
  local copies, waits for them, and re-layouts  4.12 us (2%)
  other arithmetic  2.38 us (1%)
    all_to_all x1, starting transfers between devices, local(): got = lax.all_to_all(send, ('mp', 'lo'), 0, 0, tiled=True)  30.4 us
    all_to_all x1, waiting for transfers between devices, local(): got = lax.all_to_all(send, ('mp', 'lo'), 0, 0, tiled=True)  25.3 us
    all_to_all x1, waiting for transfers between devices, local(): lax.all_to_all(spread, 'hi', 0, 0, tiled=True)  24.3 us
    all_to_all x1, blocking collectives, local(): y_parts = lax.all_to_all(y_part, ('hi', 'lo'), 1, 0, tiled=True)  22.6 us
    all_gather x1, blocking collectives, local(): wins = lax.all_gather(win_lo, 'tok', axis=0, tiled=True)  19.5 us
    all_gather x1, blocking collectives, local(): win_lo = lax.all_gather(x_local[:, :ROW_DEV], 'lo', axis=1, tiled=True)  11.8 us
    all_to_all x1, starting transfers between devices, local(): lax.all_to_all(spread, 'hi', 0, 0, tiled=True)  10.2 us
    ppermute x1, starting transfers between devices, local(): x_swapped = lax.ppermute(x_local, ('hi', 'tok'), swap)  8.84 us
  transfers between devices with their start and end apart: 4, of which 3 were waited for; matrix products, arithmetic and copies ran while one was open for 0% of the time, Pallas kernels for 0%

profile of v10, /device:TPU:1, one launch (start us, length us, event | category | flops | bytes accessed | tf_op | source)
XLA Modules:
  0.0 170.6 jit_solution(891080645483371175)
XLA Ops:
  0.6 0.0 copy-start
  0.6 1.2 copy.32
  1.8 8.8 %collective-permute-start = (bf16[128,896]{0,1:T(8,128)(2,1)S(1)}, bf16[128,896]{0,1:T(8,128)(2,1)S(1)}, u32[]{:S(2)}, u32[]{:S(2)}) collective-permute-start(bf16[128,896]{0,1:T(8,128)(2,1)S(1)} %bitcast.29), channel_id=1, source_target_pairs={{0,0},{1,32},{2,64},{3,96},{4,128},{5,160},{6,192},{7,224},{32,1},... | collective-permute-start | bytes 688136 | tf_op jit(solution)/shard_map/ppermute | solution.py:33
  10.7 11.8 %all_gather.6 = bf16[128,128]{0,1:T(8,128)(2,1)S(1)} all-gather(bf16[128,32]{0,1:T(8,128)(2,1)S(1)} %slice.32), channel_id=1, replica_groups=mesh['mp'=2,'hi'=8,'lo'=4,'tok'=8] {'lo'}, dimensions={1}, use_global_device_ids=true | all-gather | bytes 40960 | tf_op jit(solution)/shard_map/all_gather | solution.py:29
  22.5 19.5 %all_gather.7 = bf16[1024,128]{0,1:T(8,128)(2,1)S(1)} all-gather(bf16[128,128]{0,1:T(8,128)(2,1)S(1)} %all_gather.6), channel_id=1, replica_groups=mesh['mp'=2,'hi'=8,'lo'=4,'tok'=8] {'tok'}, dimensions={0}, use_global_device_ids=true | all-gather | bytes 294912 | tf_op jit(solution)/shard_map/all_gather | solution.py:30
  42.0 0.0 collective-permute-done
  42.0 0.0 copy-done
  42.0 0.4 fusion.10
  42.4 22.6 %all_to_all.23 = f32[128,32,16]{0,2,1:T(8,128)S(1)} all-to-all(f32[128,32,16]{0,2,1:T(8,128)S(1)} %bitcast.28), channel_id=1, replica_groups=mesh['mp'=2,'hi'=8,'lo'=4,'tok'=8] {'hi','lo'}, dimensions={1} | all-to-all | bytes 524288 | tf_op jit(solution)/shard_map/all_to_all | solution.py:39
  65.1 6.6 %collective-permute-start.1 = (f32[128,16]{0,1:T(8,128)S(1)}, f32[128,16]{0,1:T(8,128)S(1)}, u32[]{:S(2)}, u32[]{:S(2)}) collective-permute-start(f32[128,16]{0,1:T(8,128)S(1)} %reduce_sum.36), channel_id=1, source_target_pairs={{0,0},{1,32},{2,64},{3,96},{4,128},{5,160},{6,192},{7,224},{32,1},... | collective-permute-start | bytes 24584 | tf_op jit(solution)/shard_map/ppermute | solution.py:41
  71.7 2.2 %collective-permute-done.1 = f32[128,16]{0,1:T(8,128)S(1)} collective-permute-done((f32[128,16]{0,1:T(8,128)S(1)}, f32[128,16]{0,1:T(8,128)S(1)}, u32[]{:S(2)}, u32[]{:S(2)}) %collective-permute-start.1) | collective-permute-done | bytes 8224 | tf_op jit(solution)/shard_map/ppermute | solution.py:41
  74.0 1.5 broadcast_in_dim.29
  75.5 10.2 %all-to-all-start.1 = ((bf16[8,128,928]{1,2,0:T(8,128)(2,1)}), bf16[8,128,928]{1,2,0:T(8,128)(2,1)S(1)}, u32[]{:S(2)}, u32[]{:S(2)}) async-start(bf16[8,128,928]{1,2,0:T(8,128)(2,1)} %broadcast_in_dim.29), calls=%async_computation.1 | async-start | bytes 3801088 | tf_op jit(solution)/shard_map/all_to_all | solution.py:48
  85.8 0.1 multiply_reduce_fusion
  85.9 0.1 copy.36
  86.0 0.1 broadcast_select_fusion
  86.1 24.3 %all-to-all-done.1 = bf16[8,128,928]{1,2,0:T(8,128)(2,1)S(1)} async-done(((bf16[8,128,928]{1,2,0:T(8,128)(2,1)}), bf16[8,128,928]{1,2,0:T(8,128)(2,1)S(1)}, u32[]{:S(2)}, u32[]{:S(2)}) %all-to-all-start.1) | async-done | bytes 1900576 | tf_op jit(solution)/shard_map/all_to_all | solution.py:48
  110.3 0.2 copy_bitcast_fusion
  110.6 0.7 fusion
  111.3 0.3 convolution_multiply_fusion
  111.6 0.1 copy.35
  111.7 0.1 pad_maximum_fusion
  111.8 1.1 maximum_maximum_fusion
  112.9 30.4 %all-to-all-start.2 = ((f32[8,32,976]{2,1,0:T(8,128)}), f32[8,32,976]{2,1,0:T(8,128)S(1)}, u32[]{:S(2)}, u32[]{:S(2)}) async-start(f32[8,32,976]{2,1,0:T(8,128)} %maximum_maximum_fusion), calls=%async_computation.2 | async-start | bytes 2097152 | tf_op jit(solution)/shard_map/all_to_all | solution.py:71
  143.4 25.3 %all-to-all-done.2 = f32[8,32,976]{2,1,0:T(8,128)S(1)} async-done(((f32[8,32,976]{2,1,0:T(8,128)}), f32[8,32,976]{2,1,0:T(8,128)S(1)}, u32[]{:S(2)}, u32[]{:S(2)}) %all-to-all-start.2) | async-done | bytes 999456 | tf_op jit(solution)/shard_map/all_to_all | solution.py:71
  168.7 0.1 reduce_sum.38
  168.9 0.1 slice_reduce_fusion
  169.0 0.1 copy.38
  169.0 0.1 copy.39
  169.1 0.1 fusion.2
  169.2 0.8 copy.42
  170.0 0.6 add.15
  (10 shorter events, 0.1 us)
Async XLA Ops:
  0.6 41.3 %copy-start = (bf16[1,512,896]{2,1,0:T(8,128)(2,1)S(1)}, bf16[1,512,896]{2,1,0:T(8,128)(2,1)}, u32[]{:S(2)}) copy-start(bf16[1,512,896]{2,1,0:T(8,128)(2,1)} %param.3) | copy-start | bytes 2752516
  1.8 40.1 %collective-permute-start = (bf16[128,896]{0,1:T(8,128)(2,1)S(1)}, bf16[128,896]{0,1:T(8,128)(2,1)S(1)}, u32[]{:S(2)}, u32[]{:S(2)}) collective-permute-start(bf16[128,896]{0,1:T(8,128)(2,1)S(1)} %bitcast.29), channel_id=1, source_target_pairs={{0,0},{1,32},{2,64},{3,96},{4,128},{5,160},{6,192},{7,224},{32,1},... | collective-permute-start | bytes 688136 | tf_op jit(solution)/shard_map/ppermute | solution.py:33
  65.1 8.9 %collective-permute-start.1 = (f32[128,16]{0,1:T(8,128)S(1)}, f32[128,16]{0,1:T(8,128)S(1)}, u32[]{:S(2)}, u32[]{:S(2)}) collective-permute-start(f32[128,16]{0,1:T(8,128)S(1)} %reduce_sum.36), channel_id=1, source_target_pairs={{0,0},{1,32},{2,64},{3,96},{4,128},{5,160},{6,192},{7,224},{32,1},... | collective-permute-start | bytes 24584 | tf_op jit(solution)/shard_map/ppermute | solution.py:41
  75.5 34.8 %all-to-all-start.1 = ((bf16[8,128,928]{1,2,0:T(8,128)(2,1)}), bf16[8,128,928]{1,2,0:T(8,128)(2,1)S(1)}, u32[]{:S(2)}, u32[]{:S(2)}) async-start(bf16[8,128,928]{1,2,0:T(8,128)(2,1)} %broadcast_in_dim.29), calls=%async_computation.1 | async-start | bytes 3801088 | tf_op jit(solution)/shard_map/all_to_all | solution.py:48
  112.9 55.8 %all-to-all-start.2 = ((f32[8,32,976]{2,1,0:T(8,128)}), f32[8,32,976]{2,1,0:T(8,128)S(1)}, u32[]{:S(2)}, u32[]{:S(2)}) async-start(f32[8,32,976]{2,1,0:T(8,128)} %maximum_maximum_fusion), calls=%async_computation.2 | async-start | bytes 2097152 | tf_op jit(solution)/shard_map/all_to_all | solution.py:71

commit v11 on v10

--- a/solution.py
+++ b/solution.py
@@ -33,6 +33,8 @@
     x_swapped = lax.ppermute(x_local, ("hi", "tok"), swap)
 
     x_for_y, w_for_y, wins, x_swapped = lax.optimization_barrier((x_local, w_local, wins, x_swapped))
+    spread = jnp.broadcast_to(x_swapped[None], (hi_count,) + x_swapped.shape)
+    x_full = lax.all_to_all(spread, "hi", 0, 0, tiled=True).reshape(hi_count * tokens, span_width)
     y_part = lax.dot_general(
         x_for_y, w_for_y, (((1,), (1,)), ((), ())), preferred_element_type=jnp.float32
     )
@@ -43,11 +45,10 @@
     y_high = y_round.astype(jnp.bfloat16)
     y_low = (y_mine - y_round).astype(jnp.bfloat16)
 
-    payload = jnp.concatenate([x_swapped, y_high, y_low], axis=1)
-    spread = jnp.broadcast_to(payload[None], (hi_count,) + payload.shape)
-    full = lax.all_to_all(spread, "hi", 0, 0, tiled=True).reshape(hi_count * tokens, -1)
-    x_full = full[:, :span_width]
-    y_tok = full[:, span_width:span_width + col_group].astype(jnp.float32) + full[:, span_width + col_group:].astype(jnp.float32)
+    y_pair = jnp.concatenate([y_high, y_low], axis=1)
+    y_spread = jnp.broadcast_to(y_pair[None], (hi_count,) + y_pair.shape)
+    y_pair = lax.all_to_all(y_spread, "hi", 0, 0, tiled=True).reshape(hi_count * tokens, -1)
+    y_tok = y_pair[:, :col_group].astype(jnp.float32) + y_pair[:, col_group:].astype(jnp.float32)
 
     gram = lax.dot_general(
         wins, x_full, (((0,), (0,)), ((), ())), preferred_element_type=jnp.float32

time: 171 us -> 182 us (1.064)
  waiting for transfers between devices: 51.8 us -> 58.7 us
  starting transfers between devices: 56.2 us -> 60.4 us
    all_to_all x0 -> x1, starting transfers between devices: none -> 10.2 us  [local(): lax.all_to_all(y_spread, 'hi', 0, 0, tiled=True)]
    all_to_all x0 -> x1, waiting for transfers between devices: none -> 8.94 us  [local(): lax.all_to_all(y_spread, 'hi', 0, 0, tiled=True)]
    all_to_all x1, starting transfers between devices: 10.2 us -> 3.59 us  [local(): lax.all_to_all(spread, 'hi', 0, 0, tiled=True)]
    all_to_all x1, waiting for transfers between devices: 24.3 us -> 22.1 us  [local(): lax.all_to_all(spread, 'hi', 0, 0, tiled=True)]
  transfers between devices with their start and end apart: 4 -> 5, of which waited for: 3 -> 4; matrix products, arithmetic and copies ran while one was open for 0% -> 1% of each run, Pallas kernels for 0% -> 0%
where the time goes in v11:
time: 182 us
  starting transfers between devices  60.4 us (33%)
  waiting for transfers between devices  58.7 us (32%)
  blocking collectives  53.9 us (30%)
  local copies, waits for them, and re-layouts  4.66 us (3%)
  other arithmetic  2.37 us (1%)
    all_to_all x1, starting transfers between devices, local(): got = lax.all_to_all(send, ('mp', 'lo'), 0, 0, tiled=True)  31.1 us
    all_to_all x1, waiting for transfers between devices, local(): got = lax.all_to_all(send, ('mp', 'lo'), 0, 0, tiled=True)  25.4 us
    all_to_all x1, blocking collectives, local(): y_parts = lax.all_to_all(y_part, ('hi', 'lo'), 1, 0, tiled=True)  22.6 us
    all_to_all x1, waiting for transfers between devices, local(): lax.all_to_all(spread, 'hi', 0, 0, tiled=True)  22.1 us
    all_gather x1, blocking collectives, local(): wins = lax.all_gather(win_lo, 'tok', axis=0, tiled=True)  19.5 us
    all_gather x1, blocking collectives, local(): win_lo = lax.all_gather(x_local[:, :ROW_DEV], 'lo', axis=1, tiled=True)  11.8 us
    all_to_all x1, starting transfers between devices, local(): lax.all_to_all(y_spread, 'hi', 0, 0, tiled=True)  10.2 us
    all_to_all x1, waiting for transfers between devices, local(): lax.all_to_all(y_spread, 'hi', 0, 0, tiled=True)  8.94 us
  transfers between devices with their start and end apart: 5, of which 4 were waited for; matrix products, arithmetic and copies ran while one was open for 1% of the time, Pallas kernels for 0%

profile of v11, /device:TPU:1, one launch (start us, length us, event | category | flops | bytes accessed | tf_op | source)
XLA Modules:
  0.0 181.9 jit_solution(3488901938208034412)
XLA Ops:
  0.6 0.0 copy-start
  0.6 1.2 copy.35
  1.8 8.8 %collective-permute-start = (bf16[128,896]{0,1:T(8,128)(2,1)S(1)}, bf16[128,896]{0,1:T(8,128)(2,1)S(1)}, u32[]{:S(2)}, u32[]{:S(2)}) collective-permute-start(bf16[128,896]{0,1:T(8,128)(2,1)S(1)} %bitcast.32), channel_id=1, source_target_pairs={{0,0},{1,32},{2,64},{3,96},{4,128},{5,160},{6,192},{7,224},{32,1},... | collective-permute-start | bytes 688136 | tf_op jit(solution)/shard_map/ppermute | solution.py:33
  10.7 11.8 %all_gather.6 = bf16[128,128]{0,1:T(8,128)(2,1)S(1)} all-gather(bf16[128,32]{0,1:T(8,128)(2,1)S(1)} %slice.28), channel_id=1, replica_groups=mesh['mp'=2,'hi'=8,'lo'=4,'tok'=8] {'lo'}, dimensions={1}, use_global_device_ids=true | all-gather | bytes 40960 | tf_op jit(solution)/shard_map/all_gather | solution.py:29
  22.5 19.5 %all_gather.7 = bf16[1024,128]{0,1:T(8,128)(2,1)S(1)} all-gather(bf16[128,128]{0,1:T(8,128)(2,1)S(1)} %all_gather.6), channel_id=1, replica_groups=mesh['mp'=2,'hi'=8,'lo'=4,'tok'=8] {'tok'}, dimensions={0}, use_global_device_ids=true | all-gather | bytes 294912 | tf_op jit(solution)/shard_map/all_gather | solution.py:30
  42.0 0.0 collective-permute-done
  42.0 0.0 copy-done
  42.0 0.4 fusion.9
  42.4 22.6 %all_to_all.28 = f32[128,32,16]{0,2,1:T(8,128)S(1)} all-to-all(f32[128,32,16]{0,2,1:T(8,128)S(1)} %bitcast.31), channel_id=1, replica_groups=mesh['mp'=2,'hi'=8,'lo'=4,'tok'=8] {'hi','lo'}, dimensions={1} | all-to-all | bytes 524288 | tf_op jit(solution)/shard_map/all_to_all | solution.py:41
  65.1 6.6 %collective-permute-start.1 = (f32[128,16]{0,1:T(8,128)S(1)}, f32[128,16]{0,1:T(8,128)S(1)}, u32[]{:S(2)}, u32[]{:S(2)}) collective-permute-start(f32[128,16]{0,1:T(8,128)S(1)} %reduce_sum.36), channel_id=1, source_target_pairs={{0,0},{1,32},{2,64},{3,96},{4,128},{5,160},{6,192},{7,224},{32,1},... | collective-permute-start | bytes 24584 | tf_op jit(solution)/shard_map/ppermute | solution.py:43
  71.7 2.2 %collective-permute-done.1 = f32[128,16]{0,1:T(8,128)S(1)} collective-permute-done((f32[128,16]{0,1:T(8,128)S(1)}, f32[128,16]{0,1:T(8,128)S(1)}, u32[]{:S(2)}, u32[]{:S(2)}) %collective-permute-start.1) | collective-permute-done | bytes 8224 | tf_op jit(solution)/shard_map/ppermute | solution.py:43
  73.9 0.6 broadcast_in_dim.36
  74.6 10.2 %all-to-all-start.2 = ((bf16[8,128,32]{1,2,0:T(8,128)(2,1)}), bf16[8,128,32]{1,2,0:T(8,128)(2,1)S(1)}, u32[]{:S(2)}, u32[]{:S(2)}) async-start(bf16[8,128,32]{1,2,0:T(8,128)(2,1)} %broadcast_in_dim.36), calls=%async_computation.2 | async-start | bytes 131072 | tf_op jit(solution)/shard_map/all_to_all | solution.py:50
  84.8 0.2 copy.36
  85.0 8.9 %all-to-all-done.2 = bf16[8,128,32]{1,2,0:T(8,128)(2,1)S(1)} async-done(((bf16[8,128,32]{1,2,0:T(8,128)(2,1)}), bf16[8,128,32]{1,2,0:T(8,128)(2,1)S(1)}, u32[]{:S(2)}, u32[]{:S(2)}) %all-to-all-start.2) | async-done | bytes 65568 | tf_op jit(solution)/shard_map/all_to_all | solution.py:50
  93.9 1.5 broadcast_in_dim.17
  95.4 3.6 %all-to-all-start = ((bf16[8,128,896]{2,1,0:T(8,128)(2,1)}), bf16[8,128,896]{2,1,0:T(8,128)(2,1)S(1)}, u32[]{:S(2)}, u32[]{:S(2)}) async-start(bf16[8,128,896]{2,1,0:T(8,128)(2,1)} %broadcast_in_dim.17), calls=%async_computation | async-start | bytes 3670016 | tf_op jit(solution)/shard_map/all_to_all | solution.py:37
  99.1 0.1 multiply_reduce_fusion
  99.2 0.1 copy.40
  99.3 0.1 broadcast_select_fusion
  99.4 0.3 convolution_multiply_fusion
  99.7 0.1 copy.39
  99.8 22.1 %all-to-all-done = bf16[8,128,896]{2,1,0:T(8,128)(2,1)S(1)} async-done(((bf16[8,128,896]{2,1,0:T(8,128)(2,1)}), bf16[8,128,896]{2,1,0:T(8,128)(2,1)S(1)}, u32[]{:S(2)}, u32[]{:S(2)}) %all-to-all-start) | async-done | bytes 1835040 | tf_op jit(solution)/shard_map/all_to_all | solution.py:37
  121.9 0.4 fusion.8
  122.4 1.1 maximum_maximum_fusion
  123.5 31.1 %all-to-all-start.3 = ((f32[8,32,976]{2,1,0:T(8,128)}), f32[8,32,976]{2,1,0:T(8,128)S(1)}, u32[]{:S(2)}, u32[]{:S(2)}) async-start(f32[8,32,976]{2,1,0:T(8,128)} %maximum_maximum_fusion), calls=%async_computation.3 | async-start | bytes 2097152 | tf_op jit(solution)/shard_map/all_to_all | solution.py:72
  154.6 25.4 %all-to-all-done.3 = f32[8,32,976]{2,1,0:T(8,128)S(1)} async-done(((f32[8,32,976]{2,1,0:T(8,128)}), f32[8,32,976]{2,1,0:T(8,128)S(1)}, u32[]{:S(2)}, u32[]{:S(2)}) %all-to-all-start.3) | async-done | bytes 999456 | tf_op jit(solution)/shard_map/all_to_all | solution.py:72
  180.1 0.1 reduce_sum.38
  180.2 0.1 slice_reduce_fusion
  180.3 0.1 copy.42
  180.4 0.1 copy.43
  180.4 0.1 fusion
  180.5 0.8 copy.46
  181.3 0.6 add.15
  (12 shorter events, 0.2 us)
Async XLA Ops:
  0.6 41.3 %copy-start = (bf16[1,512,896]{2,1,0:T(8,128)(2,1)S(1)}, bf16[1,512,896]{2,1,0:T(8,128)(2,1)}, u32[]{:S(2)}) copy-start(bf16[1,512,896]{2,1,0:T(8,128)(2,1)} %param.3) | copy-start | bytes 2752516
  1.8 40.1 %collective-permute-start = (bf16[128,896]{0,1:T(8,128)(2,1)S(1)}, bf16[128,896]{0,1:T(8,128)(2,1)S(1)}, u32[]{:S(2)}, u32[]{:S(2)}) collective-permute-start(bf16[128,896]{0,1:T(8,128)(2,1)S(1)} %bitcast.32), channel_id=1, source_target_pairs={{0,0},{1,32},{2,64},{3,96},{4,128},{5,160},{6,192},{7,224},{32,1},... | collective-permute-start | bytes 688136 | tf_op jit(solution)/shard_map/ppermute | solution.py:33
  65.1 8.9 %collective-permute-start.1 = (f32[128,16]{0,1:T(8,128)S(1)}, f32[128,16]{0,1:T(8,128)S(1)}, u32[]{:S(2)}, u32[]{:S(2)}) collective-permute-start(f32[128,16]{0,1:T(8,128)S(1)} %reduce_sum.36), channel_id=1, source_target_pairs={{0,0},{1,32},{2,64},{3,96},{4,128},{5,160},{6,192},{7,224},{32,1},... | collective-permute-start | bytes 24584 | tf_op jit(solution)/shard_map/ppermute | solution.py:43
  74.6 19.3 %all-to-all-start.2 = ((bf16[8,128,32]{1,2,0:T(8,128)(2,1)}), bf16[8,128,32]{1,2,0:T(8,128)(2,1)S(1)}, u32[]{:S(2)}, u32[]{:S(2)}) async-start(bf16[8,128,32]{1,2,0:T(8,128)(2,1)} %broadcast_in_dim.36), calls=%async_computation.2 | async-start | bytes 131072 | tf_op jit(solution)/shard_map/all_to_all | solution.py:50
  95.4 26.5 %all-to-all-start = ((bf16[8,128,896]{2,1,0:T(8,128)(2,1)}), bf16[8,128,896]{2,1,0:T(8,128)(2,1)S(1)}, u32[]{:S(2)}, u32[]{:S(2)}) async-start(bf16[8,128,896]{2,1,0:T(8,128)(2,1)} %broadcast_in_dim.17), calls=%async_computation | async-start | bytes 3670016 | tf_op jit(solution)/shard_map/all_to_all | solution.py:37
  123.5 56.5 %all-to-all-start.3 = ((f32[8,32,976]{2,1,0:T(8,128)}), f32[8,32,976]{2,1,0:T(8,128)S(1)}, u32[]{:S(2)}, u32[]{:S(2)}) async-start(f32[8,32,976]{2,1,0:T(8,128)} %maximum_maximum_fusion), calls=%async_computation.3 | async-start | bytes 2097152 | tf_op jit(solution)/shard_map/all_to_all | solution.py:72

commit v12 on v6

--- a/solution.py
+++ b/solution.py
@@ -30,19 +30,17 @@
     wins = lax.all_gather(win_lo, "tok", axis=0, tiled=True)
 
     swap = [(h * tok_count + t, t * tok_count + h) for h in range(hi_count) for t in range(tok_count)]
-    x_swapped = lax.ppermute(x_local, ("hi", "tok"), swap)
 
     y_part = lax.dot_general(
         x_local, w_local, (((1,), (1,)), ((), ())), preferred_element_type=jnp.float32
     )
     y_parts = lax.all_to_all(y_part, ("hi", "lo"), 1, 0, tiled=True)
     y_mine = jnp.sum(y_parts.reshape(blk_count, tokens, col_group), axis=0)
-    y_mine = lax.ppermute(y_mine, ("hi", "tok"), swap)
     y_round = lax.reduce_precision(y_mine, exponent_bits=8, mantissa_bits=7)
     y_high = y_round.astype(jnp.bfloat16)
     y_low = (y_mine - y_round).astype(jnp.bfloat16)
-
-    payload = jnp.concatenate([x_swapped, y_high, y_low], axis=1)
+    payload = jnp.concatenate([x_local, y_high, y_low], axis=1)
+    payload = lax.ppermute(payload, ("hi", "tok"), swap)
     spread = jnp.broadcast_to(payload[None], (hi_count,) + payload.shape)
     full = lax.all_to_all(spread, "hi", 0, 0, tiled=True).reshape(hi_count * tokens, -1)
     x_full = full[:, :span_width]

time: 168 us -> 162 us (0.964)
  blocking collectives: 86.4 us -> 68.3 us
  starting transfers between devices: 34.1 us -> 42.8 us
  waiting for transfers between devices: 37.6 us -> 40.3 us
    all_to_all x1 -> x0, blocking collectives: 20 us -> none  [local(): y_parts = lax.all_to_all(y_part, ('hi', 'lo'), 1, 0, tiled=True)]
    all_to_all x0 -> x1, starting transfers between devices: none -> 10.5 us  [local(): y_parts = lax.all_to_all(y_part, ('hi', 'lo'), 1, 0, tiled=True)]
    all_to_all x0 -> x1, waiting for transfers between devices: none -> 9.5 us  [local(): y_parts = lax.all_to_all(y_part, ('hi', 'lo'), 1, 0, tiled=True)]
    ppermute x2 -> x1, waiting for transfers between devices: 11.4 us -> 4.31 us  [local(): payload = lax.ppermute(payload, ('hi', 'tok'), swap)]
    all_gather x1, blocking collectives: 16.9 us -> 21.5 us  [local(): wins = lax.all_gather(win_lo, 'tok', axis=0, tiled=True)]
    all_gather x1, blocking collectives: 49.5 us -> 46.8 us  [local(): win_lo = lax.all_gather(x_local[:, :ROW_DEV], 'lo', axis=1, tiled=True)]
    ppermute x2 -> x1, starting transfers between devices: 9.47 us -> 7.12 us  [local(): payload = lax.ppermute(payload, ('hi', 'tok'), swap)]
  transfers between devices with their start and end apart: 4 -> 4, of which waited for: 2 -> 3; matrix products, arithmetic and copies ran while one was open for 0% -> 0% of each run, Pallas kernels for 0% -> 0%
where the time goes in v12:
time: 162 us
  blocking collectives  68.3 us (42%)
  starting transfers between devices  42.8 us (26%)
  waiting for transfers between devices  40.3 us (25%)
  local copies, waits for them, and re-layouts  4.38 us (3%)
  matrix products  3.02 us (2%)
  other arithmetic  2.34 us (1%)
    all_gather x1, blocking collectives, local(): win_lo = lax.all_gather(x_local[:, :ROW_DEV], 'lo', axis=1, tiled=True)  46.8 us
    all_to_all x1, waiting for transfers between devices, local(): got = lax.all_to_all(send, ('mp', 'lo'), 0, 0, tiled=True)  26.5 us
    all_to_all x1, starting transfers between devices, local(): lax.all_to_all(spread, 'hi', 0, 0, tiled=True)  21.6 us
    all_gather x1, blocking collectives, local(): wins = lax.all_gather(win_lo, 'tok', axis=0, tiled=True)  21.5 us
    all_to_all x1, starting transfers between devices, local(): y_parts = lax.all_to_all(y_part, ('hi', 'lo'), 1, 0, tiled=True)  10.5 us
    all_to_all x1, waiting for transfers between devices, local(): y_parts = lax.all_to_all(y_part, ('hi', 'lo'), 1, 0, tiled=True)  9.5 us
    ppermute x1, starting transfers between devices, local(): payload = lax.ppermute(payload, ('hi', 'tok'), swap)  7.12 us
    ppermute x1, waiting for transfers between devices, local(): payload = lax.ppermute(payload, ('hi', 'tok'), swap)  4.31 us
  transfers between devices with their start and end apart: 4, of which 3 were waited for; matrix products, arithmetic and copies ran while one was open for 0% of the time, Pallas kernels for 0%

profile of v12, /device:TPU:1, one launch (start us, length us, event | category | flops | bytes accessed | tf_op | source)
XLA Modules:
  0.0 162.0 jit_solution(14994116656639238797)
XLA Ops:
  0.6 0.0 copy-start
  0.6 0.0 copy-start.1
  0.7 1.2 copy-done
  1.8 2.0 %fusion.8 = f32[128,32,16]{0,2,1:T(8,128)} fusion(bf16[32,16,896]{2,1,0:T(8,128)(2,1)S(1)} %bitcast.32, bf16[1,128,896]{2,1,0:T(8,128)(2,1)} %param.2), kind=kOutput, calls=%fused_computation.13 | convolution fusion | flops 117440512 | bytes 1409024 | tf_op jit(solution)/shard_map/dot_general | solution.py:34
  3.9 10.5 %all-to-all-start = ((f32[128,32,16]{0,2,1:T(8,128)}), f32[128,32,16]{0,2,1:T(8,128)S(1)}, u32[]{:S(2)}, u32[]{:S(2)}) async-start(f32[128,32,16]{0,2,1:T(8,128)} %fusion.8), calls=%async_computation | async-start | bytes 524288 | tf_op jit(solution)/shard_map/all_to_all | solution.py:37
  14.4 0.0 copy-done.1
  14.4 0.2 copy.34
  14.5 9.5 %all-to-all-done = f32[128,32,16]{0,2,1:T(8,128)S(1)} async-done(((f32[128,32,16]{0,2,1:T(8,128)}), f32[128,32,16]{0,2,1:T(8,128)S(1)}, u32[]{:S(2)}, u32[]{:S(2)}) %all-to-all-start) | async-done | bytes 262176 | tf_op jit(solution)/shard_map/all_to_all | solution.py:37
  24.1 7.1 %collective-permute-start = (bf16[128,928]{0,1:T(8,128)(2,1)S(1)}, bf16[128,928]{0,1:T(8,128)(2,1)S(1)}, u32[]{:S(2)}, u32[]{:S(2)}) collective-permute-start(bf16[128,928]{0,1:T(8,128)(2,1)S(1)} %pad_maximum_fusion.1), channel_id=1, source_target_pairs={{0,0},{1,32},{2,64},{3,96},{4,128},{5,160},{6,192},{7,224},{32,1},... | collective-permute-start | bytes 712712 | tf_op jit(solution)/shard_map/ppermute | solution.py:43
  31.2 4.3 %collective-permute-done = bf16[128,928]{0,1:T(8,128)(2,1)S(1)} collective-permute-done((bf16[128,928]{0,1:T(8,128)(2,1)S(1)}, bf16[128,928]{0,1:T(8,128)(2,1)S(1)}, u32[]{:S(2)}, u32[]{:S(2)}) %collective-permute-start) | collective-permute-done | bytes 237600 | tf_op jit(solution)/shard_map/ppermute | solution.py:43
  35.6 1.5 broadcast_in_dim.29
  37.1 21.6 %all-to-all-start.1 = ((bf16[8,128,928]{1,2,0:T(8,128)(2,1)}), bf16[8,128,928]{1,2,0:T(8,128)(2,1)S(1)}, u32[]{:S(2)}, u32[]{:S(2)}) async-start(bf16[8,128,928]{1,2,0:T(8,128)(2,1)} %broadcast_in_dim.29), calls=%async_computation.1 | async-start | bytes 3801088 | tf_op jit(solution)/shard_map/all_to_all | solution.py:45
  58.7 46.8 %all_gather.6 = bf16[128,128]{0,1:T(8,128)(2,1)S(1)} all-gather(bf16[128,32]{0,1:T(8,128)(2,1)S(1)} %slice.33), channel_id=1, replica_groups=mesh['mp'=2,'hi'=8,'lo'=4,'tok'=8] {'lo'}, dimensions={1}, use_global_device_ids=true | all-gather | bytes 40960 | tf_op jit(solution)/shard_map/all_gather | solution.py:29
  105.5 21.5 %all_gather.7 = bf16[1024,128]{0,1:T(8,128)(2,1)S(1)} all-gather(bf16[128,128]{0,1:T(8,128)(2,1)S(1)} %all_gather.6), channel_id=1, replica_groups=mesh['mp'=2,'hi'=8,'lo'=4,'tok'=8] {'tok'}, dimensions={0}, use_global_device_ids=true | all-gather | bytes 294912 | tf_op jit(solution)/shard_map/all_gather | solution.py:30
  127.1 0.1 multiply_reduce_fusion
  127.2 0.1 copy.41
  127.3 0.1 broadcast_select_fusion
  127.4 0.0 all-to-all-done.1
  127.4 0.3 copy_bitcast_fusion
  127.7 0.3 fusion.5
  128.0 0.7 fusion.2
  128.7 0.2 copy.40
  128.9 1.1 maximum_maximum_fusion
  130.0 3.6 %all-to-all-start.2 = ((f32[8,32,976]{2,1,0:T(8,128)}), f32[8,32,976]{2,1,0:T(8,128)S(1)}, u32[]{:S(2)}, u32[]{:S(2)}) async-start(f32[8,32,976]{2,1,0:T(8,128)} %maximum_maximum_fusion), calls=%async_computation.2 | async-start | bytes 2097152 | tf_op jit(solution)/shard_map/all_to_all | solution.py:68
  133.6 26.5 %all-to-all-done.2 = f32[8,32,976]{2,1,0:T(8,128)S(1)} async-done(((f32[8,32,976]{2,1,0:T(8,128)}), f32[8,32,976]{2,1,0:T(8,128)S(1)}, u32[]{:S(2)}, u32[]{:S(2)}) %all-to-all-start.2) | async-done | bytes 999456 | tf_op jit(solution)/shard_map/all_to_all | solution.py:68
  160.1 0.1 reduce_sum.38
  160.3 0.1 slice_reduce_fusion
  160.4 0.1 fusion.6
  160.4 0.1 copy.43
  160.5 0.1 copy.44
  160.6 0.8 copy.51
  161.4 0.6 add.15
  (11 shorter events, 0.1 us)
Async XLA Ops:
  0.6 1.2 copy-start
  0.6 13.7 %copy-start.1 = (bf16[1,128,896]{2,1,0:T(8,128)(2,1)S(1)}, bf16[1,128,896]{2,1,0:T(8,128)(2,1)}, u32[]{:S(2)}) copy-start(bf16[1,128,896]{2,1,0:T(8,128)(2,1)} %param.2) | copy-start | bytes 688132
  3.9 20.2 %all-to-all-start = ((f32[128,32,16]{0,2,1:T(8,128)}), f32[128,32,16]{0,2,1:T(8,128)S(1)}, u32[]{:S(2)}, u32[]{:S(2)}) async-start(f32[128,32,16]{0,2,1:T(8,128)} %fusion.8), calls=%async_computation | async-start | bytes 524288 | tf_op jit(solution)/shard_map/all_to_all | solution.py:37
  24.1 11.4 %collective-permute-start = (bf16[128,928]{0,1:T(8,128)(2,1)S(1)}, bf16[128,928]{0,1:T(8,128)(2,1)S(1)}, u32[]{:S(2)}, u32[]{:S(2)}) collective-permute-start(bf16[128,928]{0,1:T(8,128)(2,1)S(1)} %pad_maximum_fusion.1), channel_id=1, source_target_pairs={{0,0},{1,32},{2,64},{3,96},{4,128},{5,160},{6,192},{7,224},{32,1},... | collective-permute-start | bytes 712712 | tf_op jit(solution)/shard_map/ppermute | solution.py:43
  37.1 90.3 %all-to-all-start.1 = ((bf16[8,128,928]{1,2,0:T(8,128)(2,1)}), bf16[8,128,928]{1,2,0:T(8,128)(2,1)S(1)}, u32[]{:S(2)}, u32[]{:S(2)}) async-start(bf16[8,128,928]{1,2,0:T(8,128)(2,1)} %broadcast_in_dim.29), calls=%async_computation.1 | async-start | bytes 3801088 | tf_op jit(solution)/shard_map/all_to_all | solution.py:45
  130.0 30.1 %all-to-all-start.2 = ((f32[8,32,976]{2,1,0:T(8,128)}), f32[8,32,976]{2,1,0:T(8,128)S(1)}, u32[]{:S(2)}, u32[]{:S(2)}) async-start(f32[8,32,976]{2,1,0:T(8,128)} %maximum_maximum_fusion), calls=%async_computation.2 | async-start | bytes 2097152 | tf_op jit(solution)/shard_map/all_to_all | solution.py:68

commit v13 on v12

--- a/solution.py
+++ b/solution.py
@@ -26,16 +26,23 @@
     col_group = cols // blk_count
     tok_cols = cols // tok_count
 
-    win_lo = lax.all_gather(x_local[:, :ROW_DEV], "lo", axis=1, tiled=True)
-    wins = lax.all_gather(win_lo, "tok", axis=0, tiled=True)
-
     swap = [(h * tok_count + t, t * tok_count + h) for h in range(hi_count) for t in range(tok_count)]
 
     y_part = lax.dot_general(
         x_local, w_local, (((1,), (1,)), ((), ())), preferred_element_type=jnp.float32
     )
-    y_parts = lax.all_to_all(y_part, ("hi", "lo"), 1, 0, tiled=True)
-    y_mine = jnp.sum(y_parts.reshape(blk_count, tokens, col_group), axis=0)
+    y_part_round = lax.reduce_precision(y_part, exponent_bits=8, mantissa_bits=7)
+    y_part_high = y_part_round.astype(jnp.bfloat16).reshape(tokens, blk_count, col_group)
+    y_part_low = (y_part - y_part_round).astype(jnp.bfloat16).reshape(tokens, blk_count, col_group)
+    win_spread = jnp.broadcast_to(x_local[:, None, :ROW_DEV], (tokens, blk_count, ROW_DEV))
+    send_y = jnp.concatenate([y_part_high, y_part_low, win_spread], axis=2)
+    got_y = lax.all_to_all(send_y, ("hi", "lo"), 1, 1, tiled=True)
+    y_mine = jnp.sum(
+        got_y[:, :, :col_group].astype(jnp.float32) + got_y[:, :, col_group:2 * col_group].astype(jnp.float32),
+        axis=1,
+    )
+    win_lo = lax.dynamic_slice_in_dim(got_y[:, :, 2 * col_group:], hi_index * group, group, 1)
+    wins = lax.all_gather(win_lo.reshape(tokens, group * ROW_DEV), "tok", axis=0, tiled=True)
     y_round = lax.reduce_precision(y_mine, exponent_bits=8, mantissa_bits=7)
     y_high = y_round.astype(jnp.bfloat16)
     y_low = (y_mine - y_round).astype(jnp.bfloat16)

time: 162 us -> 148 us (0.914)
  blocking collectives: 68.3 us -> 41.9 us
  waiting for transfers between devices: 40.3 us -> 57.1 us
  starting transfers between devices: 42.8 us -> 38.1 us
    all_gather x2 -> x1, blocking collectives: 68.3 us -> 17.3 us  [local(): lax.all_gather(win_lo.reshape(tokens, group * ROW_DEV), 'tok', axis=0, ti...]
    all_to_all x1, waiting for transfers between devices: 0.01 us -> 28.1 us  [local(): lax.all_to_all(spread, 'hi', 0, 0, tiled=True)]
    all_to_all x0 -> x1, blocking collectives: none -> 24.6 us  [local(): got_y = lax.all_to_all(send_y, ('hi', 'lo'), 1, 1, tiled=True)]
    all_to_all x1 -> x0, starting transfers between devices: 10.5 us -> none  [local(): y_parts = lax.all_to_all(y_part, ('hi', 'lo'), 1, 0, tiled=True)]
    all_to_all x1 -> x0, waiting for transfers between devices: 9.5 us -> none  [local(): y_parts = lax.all_to_all(y_part, ('hi', 'lo'), 1, 0, tiled=True)]
    all_to_all x1, starting transfers between devices: 3.56 us -> 6.69 us  [local(): got = lax.all_to_all(send, ('mp', 'lo'), 0, 0, tiled=True)]
    all_to_all x1, starting transfers between devices: 21.6 us -> 23.8 us  [local(): lax.all_to_all(spread, 'hi', 0, 0, tiled=True)]
  transfers between devices with their start and end apart: 4 -> 3, of which waited for: 3 -> 3; matrix products, arithmetic and copies ran while one was open for 0% -> 0% of each run, Pallas kernels for 0% -> 0%
where the time goes in v13:
time: 148 us
  waiting for transfers between devices  57.1 us (39%)
  blocking collectives  41.9 us (28%)
  starting transfers between devices  38.1 us (26%)
  local copies, waits for them, and re-layouts  4.93 us (3%)
  other arithmetic  2.52 us (2%)
  matrix products  2.39 us (2%)
    all_to_all x1, waiting for transfers between devices, local(): lax.all_to_all(spread, 'hi', 0, 0, tiled=True)  28.1 us
    all_to_all x1, waiting for transfers between devices, local(): got = lax.all_to_all(send, ('mp', 'lo'), 0, 0, tiled=True)  24.9 us
    all_to_all x1, blocking collectives, local(): got_y = lax.all_to_all(send_y, ('hi', 'lo'), 1, 1, tiled=True)  24.6 us
    all_to_all x1, starting transfers between devices, local(): lax.all_to_all(spread, 'hi', 0, 0, tiled=True)  23.8 us
    all_gather x1, blocking collectives, local(): lax.all_gather(win_lo.reshape(tokens, group * ROW_DEV), 'tok', axis=0, ti...  17.3 us
    ppermute x1, starting transfers between devices, local(): payload = lax.ppermute(payload, ('hi', 'tok'), swap)  7.6 us
    all_to_all x1, starting transfers between devices, local(): got = lax.all_to_all(send, ('mp', 'lo'), 0, 0, tiled=True)  6.69 us
    ppermute x1, waiting for transfers between devices, local(): payload = lax.ppermute(payload, ('hi', 'tok'), swap)  4.14 us
  transfers between devices with their start and end apart: 3, of which 3 were waited for; matrix products, arithmetic and copies ran while one was open for 0% of the time, Pallas kernels for 0%

profile of v13, /device:TPU:1, one launch (start us, length us, event | category | flops | bytes accessed | tf_op | source)
XLA Modules:
  0.0 147.7 jit_solution(1522312090904033009)
XLA Ops:
  0.6 0.0 copy-start
  0.6 0.0 copy-start.1
  0.7 1.2 copy-done
  1.8 1.4 reduce-precision_convert_fusion
  3.2 0.1 copy.46
  3.3 0.1 copy.47
  3.4 0.0 copy-done.1
  3.5 0.1 copy.48
  3.5 0.1 broadcast_in_dim.17
  3.6 0.1 pad_maximum_fusion
  3.7 24.6 %all_to_all.15 = bf16[128,32,64]{0,2,1:T(8,128)(2,1)S(1)} all-to-all(bf16[128,32,64]{0,2,1:T(8,128)(2,1)S(1)} %pad_maximum_fusion), channel_id=1, replica_groups=mesh['mp'=2,'hi'=8,'lo'=4,'tok'=8] {'hi','lo'}, dimensions={1} | all-to-all | bytes 1048576 | tf_op jit(solution)/shard_map/all_to_all | solution.py:39
  28.3 0.1 copy.49
  28.5 0.1 copy.50
  28.6 0.1 pad_maximum_fusion.2
  28.7 7.6 %collective-permute-start = (bf16[128,928]{1,0:T(8,128)(2,1)S(1)}, bf16[128,928]{1,0:T(8,128)(2,1)S(1)}, u32[]{:S(2)}, u32[]{:S(2)}) collective-permute-start(bf16[128,928]{1,0:T(8,128)(2,1)S(1)} %pad_maximum_fusion.2), channel_id=1, source_target_pairs={{0,0},{1,32},{2,64},{3,96},{4,128},{5,160},{6,192},{7,224},{32,1},... | collective-permute-start | bytes 712712 | tf_op jit(solution)/shard_map/ppermute | solution.py:50
  36.3 4.1 %collective-permute-done = bf16[128,928]{1,0:T(8,128)(2,1)S(1)} collective-permute-done((bf16[128,928]{1,0:T(8,128)(2,1)S(1)}, bf16[128,928]{1,0:T(8,128)(2,1)S(1)}, u32[]{:S(2)}, u32[]{:S(2)}) %collective-permute-start) | collective-permute-done | bytes 237600 | tf_op jit(solution)/shard_map/ppermute | solution.py:50
  40.4 0.2 copy.51
  40.6 1.5 %broadcast_in_dim.36 = bf16[8,128,928]{1,2,0:T(8,128)(2,1)} broadcast(bf16[128,928]{0,1:T(8,128)(2,1)S(1)} %copy.51), dimensions={1,2} | broadcast | bytes 2138112 | tf_op jit(solution)/shard_map/broadcast_in_dim | solution.py:51
  42.1 23.8 %all-to-all-start.1 = ((bf16[8,128,928]{1,2,0:T(8,128)(2,1)}), bf16[8,128,928]{1,2,0:T(8,128)(2,1)S(1)}, u32[]{:S(2)}, u32[]{:S(2)}) async-start(bf16[8,128,928]{1,2,0:T(8,128)(2,1)} %broadcast_in_dim.36), calls=%async_computation.1 | async-start | bytes 3801088 | tf_op jit(solution)/shard_map/all_to_all | solution.py:52
  66.0 17.3 %all_gather.3 = bf16[1024,128]{0,1:T(8,128)(2,1)S(1)} all-gather(bf16[128,128]{0,1:T(8,128)(2,1)S(1)} %bitcast.40), channel_id=1, replica_groups=mesh['mp'=2,'hi'=8,'lo'=4,'tok'=8] {'tok'}, dimensions={0}, use_global_device_ids=true | all-gather | bytes 294912 | tf_op jit(solution)/shard_map/all_gather | solution.py:45
  83.3 0.1 multiply_reduce_fusion
  83.4 0.1 copy.54
  83.5 0.1 broadcast_select_fusion
  83.5 28.1 %all-to-all-done.1 = bf16[8,128,928]{1,2,0:T(8,128)(2,1)S(1)} async-done(((bf16[8,128,928]{1,2,0:T(8,128)(2,1)}), bf16[8,128,928]{1,2,0:T(8,128)(2,1)S(1)}, u32[]{:S(2)}, u32[]{:S(2)}) %all-to-all-start.1) | async-done | bytes 1900576 | tf_op jit(solution)/shard_map/all_to_all | solution.py:52
  111.6 0.2 copy_bitcast_fusion
  111.9 0.7 fusion
  112.6 0.3 convolution_multiply_fusion
  112.9 0.1 copy.53
  113.0 0.1 pad_maximum_fusion.1
  113.1 1.1 maximum_maximum_fusion
  114.2 6.7 %all-to-all-start.2 = ((f32[8,32,976]{2,1,0:T(8,128)}), f32[8,32,976]{2,1,0:T(8,128)S(1)}, u32[]{:S(2)}, u32[]{:S(2)}) async-start(f32[8,32,976]{2,1,0:T(8,128)} %maximum_maximum_fusion), calls=%async_computation.2 | async-start | bytes 2097152 | tf_op jit(solution)/shard_map/all_to_all | solution.py:75
  120.9 24.9 %all-to-all-done.2 = f32[8,32,976]{2,1,0:T(8,128)S(1)} async-done(((f32[8,32,976]{2,1,0:T(8,128)}), f32[8,32,976]{2,1,0:T(8,128)S(1)}, u32[]{:S(2)}, u32[]{:S(2)}) %all-to-all-start.2) | async-done | bytes 999456 | tf_op jit(solution)/shard_map/all_to_all | solution.py:75
  145.8 0.1 reduce_sum.38
  146.0 0.1 slice_reduce_fusion
  146.1 0.1 copy.56
  146.1 0.1 copy.57
  146.2 0.1 fusion.4
  146.3 0.8 copy.59
  147.1 0.6 add.23
  (11 shorter events, 0.2 us)
Async XLA Ops:
  0.6 1.2 copy-start
  0.6 2.8 %copy-start.1 = (bf16[1,128,896]{2,1,0:T(8,128)(2,1)S(1)}, bf16[1,128,896]{2,1,0:T(8,128)(2,1)}, u32[]{:S(2)}) copy-start(bf16[1,128,896]{2,1,0:T(8,128)(2,1)} %param.2) | copy-start | bytes 688132
  28.7 11.7 %collective-permute-start = (bf16[128,928]{1,0:T(8,128)(2,1)S(1)}, bf16[128,928]{1,0:T(8,128)(2,1)S(1)}, u32[]{:S(2)}, u32[]{:S(2)}) collective-permute-start(bf16[128,928]{1,0:T(8,128)(2,1)S(1)} %pad_maximum_fusion.2), channel_id=1, source_target_pairs={{0,0},{1,32},{2,64},{3,96},{4,128},{5,160},{6,192},{7,224},{32,1},... | collective-permute-start | bytes 712712 | tf_op jit(solution)/shard_map/ppermute | solution.py:50
  42.1 69.5 %all-to-all-start.1 = ((bf16[8,128,928]{1,2,0:T(8,128)(2,1)}), bf16[8,128,928]{1,2,0:T(8,128)(2,1)S(1)}, u32[]{:S(2)}, u32[]{:S(2)}) async-start(bf16[8,128,928]{1,2,0:T(8,128)(2,1)} %broadcast_in_dim.36), calls=%async_computation.1 | async-start | bytes 3801088 | tf_op jit(solution)/shard_map/all_to_all | solution.py:52
  114.2 31.6 %all-to-all-start.2 = ((f32[8,32,976]{2,1,0:T(8,128)}), f32[8,32,976]{2,1,0:T(8,128)S(1)}, u32[]{:S(2)}, u32[]{:S(2)}) async-start(f32[8,32,976]{2,1,0:T(8,128)} %maximum_maximum_fusion), calls=%async_computation.2 | async-start | bytes 2097152 | tf_op jit(solution)/shard_map/all_to_all | solution.py:75

commit v14 on v13

--- a/solution.py
+++ b/solution.py
@@ -2,12 +2,38 @@
 import jax.numpy as jnp
 import numpy as np
 from jax import lax
+from jax.experimental import pallas as pl
+from jax.experimental.pallas import tpu as pltpu
 from jax.sharding import Mesh, PartitionSpec as P
 
 ROW_DEV = 32
 
 
 OFF_SCALE = 0.9
+
+
+def _send_kernel(copies, group, span_width, wt_ref, full_ref, y_ref, tail_ref, out_ref):
+    wt = wt_ref[...]
+    gram = jnp.dot(wt, full_ref[:, :span_width], preferred_element_type=jnp.float32)
+    cross = jnp.dot(
+        wt.astype(jnp.float32), y_ref[...],
+        precision=lax.Precision.HIGHEST, preferred_element_type=jnp.float32,
+    )
+    tail = OFF_SCALE * cross + tail_ref[...]
+    for m in range(copies):
+        for s in range(group):
+            out_ref[m * group + s, :, :span_width] = gram[s * ROW_DEV:(s + 1) * ROW_DEV]
+            out_ref[m * group + s, :, span_width:] = tail[s * ROW_DEV:(s + 1) * ROW_DEV]
+
+
+def send_buffer(wins_t, full, y_wide, tail, copies, group, span_width):
+    width = span_width + tail.shape[1]
+    return pl.pallas_call(
+        lambda *refs: _send_kernel(copies, group, span_width, *refs),
+        out_shape=jax.ShapeDtypeStruct((copies * group, ROW_DEV, width), jnp.float32),
+        in_specs=[pl.BlockSpec(memory_space=pltpu.VMEM)] * 4,
+        out_specs=pl.BlockSpec(memory_space=pltpu.VMEM),
+    )(wins_t, full, y_wide, tail)
 
 
 def local(inputs, down_weight):
@@ -50,28 +76,18 @@
     payload = lax.ppermute(payload, ("hi", "tok"), swap)
     spread = jnp.broadcast_to(payload[None], (hi_count,) + payload.shape)
     full = lax.all_to_all(spread, "hi", 0, 0, tiled=True).reshape(hi_count * tokens, -1)
-    x_full = full[:, :span_width]
     y_tok = full[:, span_width:span_width + col_group].astype(jnp.float32) + full[:, span_width + col_group:].astype(jnp.float32)
-
-    gram = lax.dot_general(
-        wins, x_full, (((0,), (0,)), ((), ())), preferred_element_type=jnp.float32
-    )
-    cross = lax.dot_general(
-        wins.astype(jnp.float32), y_tok, (((0,), (0,)), ((), ())),
-        precision=lax.Precision.HIGHEST, preferred_element_type=jnp.float32,
-    )
-    pieces = jnp.concatenate([gram, OFF_SCALE * cross], axis=1)
-    pieces = pieces.reshape(group, ROW_DEV, span_width + col_group)
 
     win_own = lax.dynamic_slice_in_dim(wins, lo_index * ROW_DEV, ROW_DEV, 1).astype(jnp.float32)
     diag = jnp.sum(win_own * win_own, axis=0)
     w_cols = lax.dynamic_slice_in_dim(w_local, tok_index * tok_cols, tok_cols, 0)
     diag_term = (1.0 - OFF_SCALE) * diag[:, None] * w_cols[:, :ROW_DEV].astype(jnp.float32).T
     is_self = (jnp.arange(group) == lo_index)[:, None, None]
-    diag_part = jnp.where(is_self, diag_term[None], 0.0)
+    diag_part = jnp.where(is_self, diag_term[None], 0.0).reshape(group * ROW_DEV, tok_cols)
 
-    send = jnp.concatenate([pieces, diag_part], axis=2)
-    send = jnp.concatenate([send] * mp_count, axis=0)
+    y_wide = jnp.pad(y_tok, ((0, 0), (0, tok_cols)))
+    tail = jnp.pad(diag_part, ((0, 0), (col_group, 0)))
+    send = send_buffer(wins.T, full, y_wide, tail, mp_count, group, span_width)
     got = lax.all_to_all(send, ("mp", "lo"), 0, 0, tiled=True)
     got = jnp.sum(got.reshape(mp_count, group, ROW_DEV, -1), axis=0)
 

time: 148 us -> 154 us (1.041)
  local copies, waits for them, and re-layouts: 4.93 us -> 9.49 us
  Pallas kernels: 0 us -> 3.63 us
    pallas_call x0 -> x1, Pallas kernels: none -> 3.63 us  [send_buffer(): pl.pallas_call(lambda *refs: _send_kernel(copies, group, span_width, *ref...]
    all_to_all x0 -> x1, local copies, waits for them, and re-layouts: none -> 2.81 us  [local(): lax.all_to_all(spread, 'hi', 0, 0, tiled=True)]
    pad x0 -> x2, local copies, waits for them, and re-layouts: none -> 1.71 us  [the longest x1 0.99 us: local(): y_wide = jnp.pad(y_tok, ((0, 0), (0, tok_cols)))]
  transfers between devices with their start and end apart: 3 -> 3, of which waited for: 3 -> 3; matrix products, arithmetic and copies ran while one was open for 0% -> 1% of each run, Pallas kernels for 0% -> 0%
where the time goes in v14:
time: 154 us; the launch traced here: 153 us
  waiting for transfers between devices  55.9 us (36%)
  blocking collectives  42.2 us (27%)
  starting transfers between devices  38.1 us (25%)
  local copies, waits for them, and re-layouts  9.49 us (6%)
  Pallas kernels  3.63 us (2%)
    all_to_all x1, waiting for transfers between devices, local(): lax.all_to_all(spread, 'hi', 0, 0, tiled=True)  26.9 us
    all_to_all x1, waiting for transfers between devices, local(): got = lax.all_to_all(send, ('mp', 'lo'), 0, 0, tiled=True)  24.9 us
    all_to_all x1, blocking collectives, local(): got_y = lax.all_to_all(send_y, ('hi', 'lo'), 1, 1, tiled=True)  24.6 us
    all_to_all x1, starting transfers between devices, local(): lax.all_to_all(spread, 'hi', 0, 0, tiled=True)  23.8 us
    all_gather x1, blocking collectives, local(): lax.all_gather(win_lo.reshape(tokens, group * ROW_DEV), 'tok', axis=0, ti...  17.6 us
    ppermute x1, starting transfers between devices, local(): payload = lax.ppermute(payload, ('hi', 'tok'), swap)  7.6 us
    all_to_all x1, starting transfers between devices, local(): got = lax.all_to_all(send, ('mp', 'lo'), 0, 0, tiled=True)  6.68 us
    ppermute x1, waiting for transfers between devices, local(): payload = lax.ppermute(payload, ('hi', 'tok'), swap)  4.14 us
  transfers between devices with their start and end apart: 3, of which 3 were waited for; matrix products, arithmetic and copies ran while one was open for 1% of the time, Pallas kernels for 0%

profile of v14, /device:TPU:1, one launch (start us, length us, event | category | flops | bytes accessed | tf_op | source)
XLA Modules:
  0.0 153.1 jit_solution(11444283272218883717)
XLA Ops:
  0.6 0.0 copy-start
  0.6 0.8 slice.40
  1.5 0.1 copy.36
  1.6 0.3 copy-done
  1.8 0.0 copy-start.3
  1.8 1.4 reduce-precision_convert_fusion
  3.3 0.1 copy.35
  3.4 0.1 copy.34
  3.6 0.1 pad_maximum_fusion
  3.6 24.6 %all_to_all.15 = bf16[128,32,64]{0,2,1:T(8,128)(2,1)S(1)} all-to-all(bf16[128,32,64]{0,2,1:T(8,128)(2,1)S(1)} %pad_maximum_fusion), channel_id=1, replica_groups=mesh['mp'=2,'hi'=8,'lo'=4,'tok'=8] {'hi','lo'}, dimensions={1} | all-to-all | bytes 1048576 | tf_op jit(solution)/shard_map/all_to_all | solution.py:65
  28.3 0.1 copy.38
  28.4 0.1 copy.37
  28.6 0.0 copy-done.3
  28.6 0.1 pad_maximum_fusion.1
  28.7 7.6 %collective-permute-start = (bf16[128,928]{1,0:T(8,128)(2,1)S(1)}, bf16[128,928]{1,0:T(8,128)(2,1)S(1)}, u32[]{:S(2)}, u32[]{:S(2)}) collective-permute-start(bf16[128,928]{1,0:T(8,128)(2,1)S(1)} %pad_maximum_fusion.1), channel_id=1, source_target_pairs={{0,0},{1,32},{2,64},{3,96},{4,128},{5,160},{6,192},{7,224},{32,1},... | collective-permute-start | bytes 712712 | tf_op jit(solution)/shard_map/ppermute | solution.py:76
  36.3 4.1 %collective-permute-done = bf16[128,928]{1,0:T(8,128)(2,1)S(1)} collective-permute-done((bf16[128,928]{1,0:T(8,128)(2,1)S(1)}, bf16[128,928]{1,0:T(8,128)(2,1)S(1)}, u32[]{:S(2)}, u32[]{:S(2)}) %collective-permute-start) | collective-permute-done | bytes 237600 | tf_op jit(solution)/shard_map/ppermute | solution.py:76
  40.4 0.2 copy.39
  40.6 1.5 broadcast_in_dim.42
  42.1 23.8 %all-to-all-start.1 = ((bf16[8,128,928]{1,2,0:T(8,128)(2,1)}), bf16[8,128,928]{1,2,0:T(8,128)(2,1)}, u32[]{:S(2)}, u32[]{:S(2)}) async-start(bf16[8,128,928]{1,2,0:T(8,128)(2,1)} %broadcast_in_dim.42), calls=%async_computation.1 | async-start | bytes 3801088 | tf_op jit(solution)/shard_map/all_to_all | solution.py:78
  65.9 0.1 broadcast_in_dim.43
  65.9 0.1 broadcast_in_dim.44
  66.1 17.6 %all_gather.3 = bf16[1024,128]{0,1:T(8,128)(2,1)S(1)} all-gather(bf16[128,128]{0,1:T(8,128)(2,1)S(1)} %bitcast.38), channel_id=1, replica_groups=mesh['mp'=2,'hi'=8,'lo'=4,'tok'=8] {'tok'}, dimensions={0}, use_global_device_ids=true | all-gather | bytes 294912 | tf_op jit(solution)/shard_map/all_gather | solution.py:71
  83.7 0.0 copy-start.2
  83.7 0.1 multiply_reduce_fusion
  83.9 0.1 copy.41
  83.9 0.1 bitcast_select_fusion
  84.0 0.7 pad.9.refs_3_
  84.8 26.9 %all-to-all-done.1 = bf16[8,128,928]{1,2,0:T(8,128)(2,1)} async-done(((bf16[8,128,928]{1,2,0:T(8,128)(2,1)}), bf16[8,128,928]{1,2,0:T(8,128)(2,1)}, u32[]{:S(2)}, u32[]{:S(2)}) %all-to-all-start.1) | async-done | bytes 1900576 | tf_op jit(solution)/shard_map/all_to_all | solution.py:78
  111.6 2.8 %copy.40 = bf16[8,128,928]{2,1,0:T(8,128)(2,1)S(1)} copy(bf16[8,128,928]{1,2,0:T(8,128)(2,1)} %all-to-all-done.1) | data formatting | bytes 3801088 | tf_op jit(solution)/shard_map/all_to_all | solution.py:78
  114.5 0.0 copy-done.2
  114.5 0.0 copy-start.1
  114.5 0.1 convert_add_fusion
  114.6 1.0 pad.8.refs_2_
  115.6 0.4 copy-done.1
  116.0 3.6 %shard_map.41 = f32[8,32,976]{2,1,0:T(8,128)} custom-call(bf16[128,1024]{1,0:T(8,128)(2,1)} %bitcast.32, bf16[1024,928]{1,0:T(8,128)(2,1)} %bitcast.30, f32[1024,80]{1,0:T(8,128)} %pad.8.refs_2_, f32[128,80]{1,0:T(8,128)} %pad.9.refs_3_), custom_call_target="tpu_custom_call" | custom-call | tf_op jit(solution)/shard_map/pallas_call | solution.py:31
  119.6 6.7 %all-to-all-start.2 = ((f32[8,32,976]{2,1,0:T(8,128)}), f32[8,32,976]{2,1,0:T(8,128)S(1)}, u32[]{:S(2)}, u32[]{:S(2)}) async-start(f32[8,32,976]{2,1,0:T(8,128)} %shard_map.41), calls=%async_computation.2 | async-start | bytes 2097152 | tf_op jit(solution)/shard_map/all_to_all | solution.py:91
  126.3 24.9 %all-to-all-done.2 = f32[8,32,976]{2,1,0:T(8,128)S(1)} async-done(((f32[8,32,976]{2,1,0:T(8,128)}), f32[8,32,976]{2,1,0:T(8,128)S(1)}, u32[]{:S(2)}, u32[]{:S(2)}) %all-to-all-start.2) | async-done | bytes 999456 | tf_op jit(solution)/shard_map/all_to_all | solution.py:91
  151.2 0.1 reduce_sum.38
  151.4 0.1 slice_reduce_fusion
  151.5 0.1 fusion.2
  151.5 0.8 copy.45
  152.3 0.1 copy.43
  152.4 0.1 copy.44
  152.5 0.6 add.27
  (11 shorter events, 0.2 us)
Async XLA Ops:
  0.6 1.2 copy-start
  1.8 26.7 %copy-start.3 = (bf16[1,128,896]{2,1,0:T(8,128)(2,1)S(1)}, bf16[1,128,896]{2,1,0:T(8,128)(2,1)}, u32[]{:S(2)}) copy-start(bf16[1,128,896]{2,1,0:T(8,128)(2,1)} %param.2) | copy-start | bytes 688132
  28.7 11.7 %collective-permute-start = (bf16[128,928]{1,0:T(8,128)(2,1)S(1)}, bf16[128,928]{1,0:T(8,128)(2,1)S(1)}, u32[]{:S(2)}, u32[]{:S(2)}) collective-permute-start(bf16[128,928]{1,0:T(8,128)(2,1)S(1)} %pad_maximum_fusion.1), channel_id=1, source_target_pairs={{0,0},{1,32},{2,64},{3,96},{4,128},{5,160},{6,192},{7,224},{32,1},... | collective-permute-start | bytes 712712 | tf_op jit(solution)/shard_map/ppermute | solution.py:76
  42.1 69.6 %all-to-all-start.1 = ((bf16[8,128,928]{1,2,0:T(8,128)(2,1)}), bf16[8,128,928]{1,2,0:T(8,128)(2,1)}, u32[]{:S(2)}, u32[]{:S(2)}) async-start(bf16[8,128,928]{1,2,0:T(8,128)(2,1)} %broadcast_in_dim.42), calls=%async_computation.1 | async-start | bytes 3801088 | tf_op jit(solution)/shard_map/all_to_all | solution.py:78
  83.7 30.7 %copy-start.2 = (bf16[1024,128]{0,1:T(8,128)(2,1)}, bf16[1024,128]{0,1:T(8,128)(2,1)S(1)}, u32[]{:S(2)}) copy-start(bf16[1024,128]{0,1:T(8,128)(2,1)S(1)} %all_gather.3) | copy-start | bytes 786436
  114.5 1.5 copy-start.1
  119.6 31.6 %all-to-all-start.2 = ((f32[8,32,976]{2,1,0:T(8,128)}), f32[8,32,976]{2,1,0:T(8,128)S(1)}, u32[]{:S(2)}, u32[]{:S(2)}) async-start(f32[8,32,976]{2,1,0:T(8,128)} %shard_map.41), calls=%async_computation.2 | async-start | bytes 2097152 | tf_op jit(solution)/shard_map/all_to_all | solution.py:91

commit v15 on v13

--- a/solution.py
+++ b/solution.py
@@ -42,7 +42,9 @@
         axis=1,
     )
     win_lo = lax.dynamic_slice_in_dim(got_y[:, :, 2 * col_group:], hi_index * group, group, 1)
-    wins = lax.all_gather(win_lo.reshape(tokens, group * ROW_DEV), "tok", axis=0, tiled=True)
+    win_lo = win_lo.reshape(tokens, group * ROW_DEV)
+    win_spread = jnp.broadcast_to(win_lo[None], (tok_count,) + win_lo.shape)
+    wins = lax.all_to_all(win_spread, "tok", 0, 0, tiled=True).reshape(tok_count * tokens, group * ROW_DEV)
     y_round = lax.reduce_precision(y_mine, exponent_bits=8, mantissa_bits=7)
     y_high = y_round.astype(jnp.bfloat16)
     y_low = (y_mine - y_round).astype(jnp.bfloat16)

time: 148 us -> 163 us (1.10)
  blocking collectives: 41.9 us -> 0 us
  starting transfers between devices: 38.1 us -> 72.9 us
  waiting for transfers between devices: 57.1 us -> 76.6 us
    all_to_all x1 -> x0, blocking collectives: 24.6 us -> none  [local(): got_y = lax.all_to_all(send_y, ('hi', 'lo'), 1, 1, tiled=True)]
    all_to_all x0 -> x2, starting transfers between devices: none -> 24.3 us  [the longest x1 13.8 us: local(): lax.all_to_all(win_spread, 'tok', 0, 0, tiled=True)]
    all_to_all x1, starting transfers between devices: 6.69 us -> 26.4 us  [local(): got = lax.all_to_all(send, ('mp', 'lo'), 0, 0, tiled=True)]
    all_gather x1 -> x0, blocking collectives: 17.3 us -> none  [local(): lax.all_gather(win_lo.reshape(tokens, group * ROW_DEV), 'tok', axis=0, ti...]
    all_to_all x0 -> x2, waiting for transfers between devices: none -> 14.3 us  [the longest x1 14.3 us: local(): got_y = lax.all_to_all(send_y, ('hi', 'lo'), 1, 1, tiled=True)]
    all_to_all x1, starting transfers between devices: 23.8 us -> 18.1 us  [local(): lax.all_to_all(spread, 'hi', 0, 0, tiled=True)]
    ppermute x1, waiting for transfers between devices: 4.14 us -> 7.86 us  [local(): payload = lax.ppermute(payload, ('hi', 'tok'), swap)]
    ppermute x1, starting transfers between devices: 7.6 us -> 4.09 us  [local(): payload = lax.ppermute(payload, ('hi', 'tok'), swap)]
  transfers between devices with their start and end apart: 3 -> 5, of which waited for: 3 -> 4; matrix products, arithmetic and copies ran while one was open for 0% -> 1% of each run, Pallas kernels for 0% -> 0%
where the time goes in v15:
time: 163 us; the launch traced here: 162 us
  waiting for transfers between devices  76.6 us (47%)
  starting transfers between devices  72.9 us (45%)
  local copies, waits for them, and re-layouts  6.07 us (4%)
  other arithmetic  3.3 us (2%)
  matrix products  2.32 us (1%)
    all_to_all x1, waiting for transfers between devices, local(): lax.all_to_all(spread, 'hi', 0, 0, tiled=True)  28.5 us
    all_to_all x1, starting transfers between devices, local(): got = lax.all_to_all(send, ('mp', 'lo'), 0, 0, tiled=True)  26.4 us
    all_to_all x1, waiting for transfers between devices, local(): got = lax.all_to_all(send, ('mp', 'lo'), 0, 0, tiled=True)  26 us
    all_to_all x1, starting transfers between devices, local(): lax.all_to_all(spread, 'hi', 0, 0, tiled=True)  18.1 us
    all_to_all x1, waiting for transfers between devices, local(): got_y = lax.all_to_all(send_y, ('hi', 'lo'), 1, 1, tiled=True)  14.3 us
    all_to_all x1, starting transfers between devices, local(): lax.all_to_all(win_spread, 'tok', 0, 0, tiled=True)  13.8 us
    all_to_all x1, starting transfers between devices, local(): got_y = lax.all_to_all(send_y, ('hi', 'lo'), 1, 1, tiled=True)  10.5 us
    ppermute x1, waiting for transfers between devices, local(): payload = lax.ppermute(payload, ('hi', 'tok'), swap)  7.86 us
  transfers between devices with their start and end apart: 5, of which 4 were waited for; matrix products, arithmetic and copies ran while one was open for 1% of the time, Pallas kernels for 0%

profile of v15, /device:TPU:1, one launch (start us, length us, event | category | flops | bytes accessed | tf_op | source)
XLA Modules:
  0.0 162.1 jit_solution(5758161808106635782)
XLA Ops:
  0.6 0.0 copy-start
  0.6 0.0 copy-start.1
  0.7 1.2 copy-done
  1.8 1.4 reduce-precision_convert_fusion
  3.2 0.1 copy.88
  3.3 0.1 copy.89
  3.4 0.0 copy-done.1
  3.5 0.1 copy.90
  3.5 0.1 broadcast_in_dim.42
  3.6 0.8 pad_maximum_fusion
  4.4 10.5 %all-to-all-start = ((bf16[128,32,64]{0,2,1:T(8,128)(2,1)}), bf16[128,32,64]{0,2,1:T(8,128)(2,1)S(1)}, u32[]{:S(2)}, u32[]{:S(2)}) async-start(bf16[128,32,64]{0,2,1:T(8,128)(2,1)} %pad_maximum_fusion), calls=%async_computation | async-start | bytes 1048576 | tf_op jit(solution)/shard_map/all_to_all | solution.py:39
  15.0 14.3 %all-to-all-done = bf16[128,32,64]{0,2,1:T(8,128)(2,1)S(1)} async-done(((bf16[128,32,64]{0,2,1:T(8,128)(2,1)}), bf16[128,32,64]{0,2,1:T(8,128)(2,1)S(1)}, u32[]{:S(2)}, u32[]{:S(2)}) %all-to-all-start) | async-done | bytes 524320 | tf_op jit(solution)/shard_map/all_to_all | solution.py:39
  29.3 0.7 broadcast_in_dim.44
  30.1 13.8 %all-to-all-start.1 = ((bf16[8,128,128]{1,2,0:T(8,128)(2,1)}), bf16[8,128,128]{1,2,0:T(8,128)(2,1)S(1)}, u32[]{:S(2)}, u32[]{:S(2)}) async-start(bf16[8,128,128]{1,2,0:T(8,128)(2,1)} %broadcast_in_dim.44), calls=%async_computation.1 | async-start | bytes 524288 | tf_op jit(solution)/shard_map/all_to_all | solution.py:47
  43.9 0.1 copy.92
  44.0 0.1 copy.93
  44.2 0.1 pad_maximum_fusion.2
  44.3 4.1 %collective-permute-start = (bf16[128,928]{1,0:T(8,128)(2,1)S(1)}, bf16[128,928]{1,0:T(8,128)(2,1)S(1)}, u32[]{:S(2)}, u32[]{:S(2)}) collective-permute-start(bf16[128,928]{1,0:T(8,128)(2,1)S(1)} %pad_maximum_fusion.2), channel_id=1, source_target_pairs={{0,0},{1,32},{2,64},{3,96},{4,128},{5,160},{6,192},{7,224},{32,1},... | collective-permute-start | bytes 712712 | tf_op jit(solution)/shard_map/ppermute | solution.py:52
  48.4 7.9 %collective-permute-done = bf16[128,928]{1,0:T(8,128)(2,1)S(1)} collective-permute-done((bf16[128,928]{1,0:T(8,128)(2,1)S(1)}, bf16[128,928]{1,0:T(8,128)(2,1)S(1)}, u32[]{:S(2)}, u32[]{:S(2)}) %collective-permute-start) | collective-permute-done | bytes 237600 | tf_op jit(solution)/shard_map/ppermute | solution.py:52
  56.2 0.2 copy.94
  56.4 0.0 all-to-all-done.1
  56.4 1.5 broadcast_in_dim.45
  57.9 18.1 %all-to-all-start.2 = ((bf16[8,128,928]{1,2,0:T(8,128)(2,1)}), bf16[8,128,928]{1,2,0:T(8,128)(2,1)S(1)}, u32[]{:S(2)}, u32[]{:S(2)}) async-start(bf16[8,128,928]{1,2,0:T(8,128)(2,1)} %broadcast_in_dim.45), calls=%async_computation.2 | async-start | bytes 3801088 | tf_op jit(solution)/shard_map/all_to_all | solution.py:54
  76.1 0.2 copy.91
  76.2 0.1 constant_dynamic-slice_fusion
  76.4 0.1 copy.102
  76.5 0.1 multiply_reduce_fusion
  76.7 0.1 copy.98
  76.7 0.1 broadcast_select_fusion
  76.8 28.5 %all-to-all-done.2 = bf16[8,128,928]{1,2,0:T(8,128)(2,1)S(1)} async-done(((bf16[8,128,928]{1,2,0:T(8,128)(2,1)}), bf16[8,128,928]{1,2,0:T(8,128)(2,1)S(1)}, u32[]{:S(2)}, u32[]{:S(2)}) %all-to-all-start.2) | async-done | bytes 1900576 | tf_op jit(solution)/shard_map/all_to_all | solution.py:54
  105.3 0.2 copy_bitcast_fusion
  105.5 0.7 fusion
  106.3 0.2 convolution_multiply_fusion
  106.5 0.1 copy.96
  106.6 0.1 pad_maximum_fusion.1
  106.7 1.1 maximum_maximum_fusion
  107.8 26.4 %all-to-all-start.3 = ((f32[8,32,976]{2,1,0:T(8,128)}), f32[8,32,976]{2,1,0:T(8,128)S(1)}, u32[]{:S(2)}, u32[]{:S(2)}) async-start(f32[8,32,976]{2,1,0:T(8,128)} %maximum_maximum_fusion), calls=%async_computation.3 | async-start | bytes 2097152 | tf_op jit(solution)/shard_map/all_to_all | solution.py:77
  134.2 26.0 %all-to-all-done.3 = f32[8,32,976]{2,1,0:T(8,128)S(1)} async-done(((f32[8,32,976]{2,1,0:T(8,128)}), f32[8,32,976]{2,1,0:T(8,128)S(1)}, u32[]{:S(2)}, u32[]{:S(2)}) %all-to-all-start.3) | async-done | bytes 999456 | tf_op jit(solution)/shard_map/all_to_all | solution.py:77
  160.2 0.1 reduce_sum.38
  160.3 0.1 slice_reduce_fusion
  160.4 0.1 copy.100
  160.5 0.1 copy.101
  160.6 0.1 fusion.4
  160.6 0.8 copy.104
  161.4 0.6 add.23
  (11 shorter events, 0.1 us)
Async XLA Ops:
  0.6 1.2 copy-start
  0.6 2.8 %copy-start.1 = (bf16[1,128,896]{2,1,0:T(8,128)(2,1)S(1)}, bf16[1,128,896]{2,1,0:T(8,128)(2,1)}, u32[]{:S(2)}) copy-start(bf16[1,128,896]{2,1,0:T(8,128)(2,1)} %param.2) | copy-start | bytes 688132
  4.4 24.8 %all-to-all-start = ((bf16[128,32,64]{0,2,1:T(8,128)(2,1)}), bf16[128,32,64]{0,2,1:T(8,128)(2,1)S(1)}, u32[]{:S(2)}, u32[]{:S(2)}) async-start(bf16[128,32,64]{0,2,1:T(8,128)(2,1)} %pad_maximum_fusion), calls=%async_computation | async-start | bytes 1048576 | tf_op jit(solution)/shard_map/all_to_all | solution.py:39
  30.1 26.3 %all-to-all-start.1 = ((bf16[8,128,128]{1,2,0:T(8,128)(2,1)}), bf16[8,128,128]{1,2,0:T(8,128)(2,1)S(1)}, u32[]{:S(2)}, u32[]{:S(2)}) async-start(bf16[8,128,128]{1,2,0:T(8,128)(2,1)} %broadcast_in_dim.44), calls=%async_computation.1 | async-start | bytes 524288 | tf_op jit(solution)/shard_map/all_to_all | solution.py:47
  44.3 12.0 %collective-permute-start = (bf16[128,928]{1,0:T(8,128)(2,1)S(1)}, bf16[128,928]{1,0:T(8,128)(2,1)S(1)}, u32[]{:S(2)}, u32[]{:S(2)}) collective-permute-start(bf16[128,928]{1,0:T(8,128)(2,1)S(1)} %pad_maximum_fusion.2), channel_id=1, source_target_pairs={{0,0},{1,32},{2,64},{3,96},{4,128},{5,160},{6,192},{7,224},{32,1},... | collective-permute-start | bytes 712712 | tf_op jit(solution)/shard_map/ppermute | solution.py:52
  57.9 47.4 %all-to-all-start.2 = ((bf16[8,128,928]{1,2,0:T(8,128)(2,1)}), bf16[8,128,928]{1,2,0:T(8,128)(2,1)S(1)}, u32[]{:S(2)}, u32[]{:S(2)}) async-start(bf16[8,128,928]{1,2,0:T(8,128)(2,1)} %broadcast_in_dim.45), calls=%async_computation.2 | async-start | bytes 3801088 | tf_op jit(solution)/shard_map/all_to_all | solution.py:54
  107.8 52.4 %all-to-all-start.3 = ((f32[8,32,976]{2,1,0:T(8,128)}), f32[8,32,976]{2,1,0:T(8,128)S(1)}, u32[]{:S(2)}, u32[]{:S(2)}) async-start(f32[8,32,976]{2,1,0:T(8,128)} %maximum_maximum_fusion), calls=%async_computation.3 | async-start | bytes 2097152 | tf_op jit(solution)/shard_map/all_to_all | solution.py:77

commit v16 on v13

--- a/solution.py
+++ b/solution.py
@@ -71,9 +71,8 @@
     diag_part = jnp.where(is_self, diag_term[None], 0.0)
 
     send = jnp.concatenate([pieces, diag_part], axis=2)
-    send = jnp.concatenate([send] * mp_count, axis=0)
-    got = lax.all_to_all(send, ("mp", "lo"), 0, 0, tiled=True)
-    got = jnp.sum(got.reshape(mp_count, group, ROW_DEV, -1), axis=0)
+    send = send + lax.ppermute(send, "mp", [(m, (m + 1) % mp_count) for m in range(mp_count)])
+    got = lax.all_to_all(send, "lo", 0, 0, tiled=True)
 
     gram = got[:, :, :span_width]
     slot = lax.broadcasted_iota(jnp.int32, gram.shape, 0)

time: 148 us -> 150 us (1.014)
  starting transfers between devices: 38.1 us -> 40 us
    ppermute x0 -> x1, waiting for transfers between devices: none -> 11.7 us  [local(): lax.ppermute(send, 'mp', [(m, (m + 1) % mp_count) for m in range(mp_count)])]
    all_to_all x1, waiting for transfers between devices: 24.9 us -> 14 us  [local(): got = lax.all_to_all(send, 'lo', 0, 0, tiled=True)]
    ppermute x0 -> x1, starting transfers between devices: none -> 1.92 us  [local(): lax.ppermute(send, 'mp', [(m, (m + 1) % mp_count) for m in range(mp_count)])]
  transfers between devices with their start and end apart: 3 -> 4, of which waited for: 3 -> 4; matrix products, arithmetic and copies ran while one was open for 0% -> 0% of each run, Pallas kernels for 0% -> 0%
where the time goes in v16:
time: 150 us
  waiting for transfers between devices  57.9 us (39%)
  blocking collectives  41.9 us (28%)
  starting transfers between devices  40 us (27%)
  local copies, waits for them, and re-layouts  4.91 us (3%)
  matrix products  2.4 us (2%)
  other arithmetic  2.22 us (1%)
    all_to_all x1, waiting for transfers between devices, local(): lax.all_to_all(spread, 'hi', 0, 0, tiled=True)  28.1 us
    all_to_all x1, blocking collectives, local(): got_y = lax.all_to_all(send_y, ('hi', 'lo'), 1, 1, tiled=True)  24.6 us
    all_to_all x1, starting transfers between devices, local(): lax.all_to_all(spread, 'hi', 0, 0, tiled=True)  23.8 us
    all_gather x1, blocking collectives, local(): lax.all_gather(win_lo.reshape(tokens, group * ROW_DEV), 'tok', axis=0, ti...  17.3 us
    all_to_all x1, waiting for transfers between devices, local(): got = lax.all_to_all(send, 'lo', 0, 0, tiled=True)  14 us
    ppermute x1, waiting for transfers between devices, local(): lax.ppermute(send, 'mp', [(m, (m + 1) % mp_count) for m in range(mp_count)])  11.7 us
    ppermute x1, starting transfers between devices, local(): payload = lax.ppermute(payload, ('hi', 'tok'), swap)  7.6 us
    all_to_all x1, starting transfers between devices, local(): got = lax.all_to_all(send, 'lo', 0, 0, tiled=True)  6.7 us
  transfers between devices with their start and end apart: 4, of which 4 were waited for; matrix products, arithmetic and copies ran while one was open for 0% of the time, Pallas kernels for 0%

profile of v16, /device:TPU:1, one launch (start us, length us, event | category | flops | bytes accessed | tf_op | source)
XLA Modules:
  0.0 150.1 jit_solution(15108329541179077608)
XLA Ops:
  0.6 0.0 copy-start
  0.6 0.0 copy-start.1
  0.7 1.2 copy-done
  1.8 1.4 reduce-precision_convert_fusion
  3.2 0.1 copy.48
  3.3 0.1 copy.49
  3.4 0.0 copy-done.1
  3.5 0.1 copy.50
  3.5 0.1 broadcast_in_dim.17
  3.6 0.1 pad_maximum_fusion
  3.7 24.6 %all_to_all.15 = bf16[128,32,64]{0,2,1:T(8,128)(2,1)S(1)} all-to-all(bf16[128,32,64]{0,2,1:T(8,128)(2,1)S(1)} %pad_maximum_fusion), channel_id=1, replica_groups=mesh['mp'=2,'hi'=8,'lo'=4,'tok'=8] {'hi','lo'}, dimensions={1} | all-to-all | bytes 1048576 | tf_op jit(solution)/shard_map/all_to_all | solution.py:39
  28.3 0.1 copy.51
  28.5 0.1 copy.52
  28.6 0.1 pad_maximum_fusion.3
  28.7 7.6 %collective-permute-start = (bf16[128,928]{1,0:T(8,128)(2,1)S(1)}, bf16[128,928]{1,0:T(8,128)(2,1)S(1)}, u32[]{:S(2)}, u32[]{:S(2)}) collective-permute-start(bf16[128,928]{1,0:T(8,128)(2,1)S(1)} %pad_maximum_fusion.3), channel_id=1, source_target_pairs={{0,0},{1,32},{2,64},{3,96},{4,128},{5,160},{6,192},{7,224},{32,1},... | collective-permute-start | bytes 712712 | tf_op jit(solution)/shard_map/ppermute | solution.py:50
  36.3 4.1 %collective-permute-done = bf16[128,928]{1,0:T(8,128)(2,1)S(1)} collective-permute-done((bf16[128,928]{1,0:T(8,128)(2,1)S(1)}, bf16[128,928]{1,0:T(8,128)(2,1)S(1)}, u32[]{:S(2)}, u32[]{:S(2)}) %collective-permute-start) | collective-permute-done | bytes 237600 | tf_op jit(solution)/shard_map/ppermute | solution.py:50
  40.4 0.2 copy.53
  40.6 1.5 %broadcast_in_dim.36 = bf16[8,128,928]{1,2,0:T(8,128)(2,1)} broadcast(bf16[128,928]{0,1:T(8,128)(2,1)S(1)} %copy.53), dimensions={1,2} | broadcast | bytes 2138112 | tf_op jit(solution)/shard_map/broadcast_in_dim | solution.py:51
  42.1 23.8 %all-to-all-start.1 = ((bf16[8,128,928]{1,2,0:T(8,128)(2,1)}), bf16[8,128,928]{1,2,0:T(8,128)(2,1)S(1)}, u32[]{:S(2)}, u32[]{:S(2)}) async-start(bf16[8,128,928]{1,2,0:T(8,128)(2,1)} %broadcast_in_dim.36), calls=%async_computation.1 | async-start | bytes 3801088 | tf_op jit(solution)/shard_map/all_to_all | solution.py:52
  66.0 17.3 %all_gather.3 = bf16[1024,128]{0,1:T(8,128)(2,1)S(1)} all-gather(bf16[128,128]{0,1:T(8,128)(2,1)S(1)} %bitcast.39), channel_id=1, replica_groups=mesh['mp'=2,'hi'=8,'lo'=4,'tok'=8] {'tok'}, dimensions={0}, use_global_device_ids=true | all-gather | bytes 294912 | tf_op jit(solution)/shard_map/all_gather | solution.py:45
  83.2 0.1 multiply_reduce_fusion
  83.4 0.1 copy.56
  83.4 0.1 broadcast_select_fusion
  83.5 28.1 %all-to-all-done.1 = bf16[8,128,928]{1,2,0:T(8,128)(2,1)S(1)} async-done(((bf16[8,128,928]{1,2,0:T(8,128)(2,1)}), bf16[8,128,928]{1,2,0:T(8,128)(2,1)S(1)}, u32[]{:S(2)}, u32[]{:S(2)}) %all-to-all-start.1) | async-done | bytes 1900576 | tf_op jit(solution)/shard_map/all_to_all | solution.py:52
  111.6 0.2 copy_bitcast_fusion
  111.8 0.7 fusion
  112.6 0.3 convolution_multiply_fusion
  112.9 0.1 copy.55
  113.0 0.1 pad_maximum_fusion.1
  113.1 0.1 pad_maximum_fusion.2
  113.1 1.9 %collective-permute-start.1 = (f32[4,32,976]{2,1,0:T(8,128)S(1)}, f32[4,32,976]{2,1,0:T(8,128)S(1)}, u32[]{:S(2)}, u32[]{:S(2)}) collective-permute-start(f32[4,32,976]{2,1,0:T(8,128)S(1)} %pad_maximum_fusion.2), channel_id=1, source_target_pairs={{0,256},{256,0},{1,257},{257,1},{2,258},{258,2},{3,259},{259,3},{4... | collective-permute-start | bytes 1499144 | tf_op jit(solution)/shard_map/ppermute | solution.py:74
  115.1 11.7 %collective-permute-done.1 = f32[4,32,976]{2,1,0:T(8,128)S(1)} collective-permute-done((f32[4,32,976]{2,1,0:T(8,128)S(1)}, f32[4,32,976]{2,1,0:T(8,128)S(1)}, u32[]{:S(2)}, u32[]{:S(2)}) %collective-permute-start.1) | collective-permute-done | bytes 499744 | tf_op jit(solution)/shard_map/ppermute | solution.py:74
  126.8 0.9 fusion.16
  127.7 6.7 %all-to-all-start.2 = ((f32[4,32,976]{2,1,0:T(8,128)}), f32[4,32,976]{2,1,0:T(8,128)S(1)}, u32[]{:S(2)}, u32[]{:S(2)}) async-start(f32[4,32,976]{2,1,0:T(8,128)} %fusion.16), calls=%async_computation.2 | async-start | bytes 1048576 | tf_op jit(solution)/shard_map/all_to_all | solution.py:75
  134.4 14.0 %all-to-all-done.2 = f32[4,32,976]{2,1,0:T(8,128)S(1)} async-done(((f32[4,32,976]{2,1,0:T(8,128)}), f32[4,32,976]{2,1,0:T(8,128)S(1)}, u32[]{:S(2)}, u32[]{:S(2)}) %all-to-all-start.2) | async-done | bytes 499744 | tf_op jit(solution)/shard_map/all_to_all | solution.py:75
  148.4 0.1 copy.58
  148.5 0.1 copy.59
  148.5 0.1 fusion.4
  148.6 0.8 copy.61
  149.4 0.1 slice_reduce_fusion
  149.5 0.6 add.27
  (11 shorter events, 0.1 us)
Async XLA Ops:
  0.6 1.2 copy-start
  0.6 2.8 %copy-start.1 = (bf16[1,128,896]{2,1,0:T(8,128)(2,1)S(1)}, bf16[1,128,896]{2,1,0:T(8,128)(2,1)}, u32[]{:S(2)}) copy-start(bf16[1,128,896]{2,1,0:T(8,128)(2,1)} %param.2) | copy-start | bytes 688132
  28.7 11.7 %collective-permute-start = (bf16[128,928]{1,0:T(8,128)(2,1)S(1)}, bf16[128,928]{1,0:T(8,128)(2,1)S(1)}, u32[]{:S(2)}, u32[]{:S(2)}) collective-permute-start(bf16[128,928]{1,0:T(8,128)(2,1)S(1)} %pad_maximum_fusion.3), channel_id=1, source_target_pairs={{0,0},{1,32},{2,64},{3,96},{4,128},{5,160},{6,192},{7,224},{32,1},... | collective-permute-start | bytes 712712 | tf_op jit(solution)/shard_map/ppermute | solution.py:50
  42.1 69.5 %all-to-all-start.1 = ((bf16[8,128,928]{1,2,0:T(8,128)(2,1)}), bf16[8,128,928]{1,2,0:T(8,128)(2,1)S(1)}, u32[]{:S(2)}, u32[]{:S(2)}) async-start(bf16[8,128,928]{1,2,0:T(8,128)(2,1)} %broadcast_in_dim.36), calls=%async_computation.1 | async-start | bytes 3801088 | tf_op jit(solution)/shard_map/all_to_all | solution.py:52
  113.1 13.7 %collective-permute-start.1 = (f32[4,32,976]{2,1,0:T(8,128)S(1)}, f32[4,32,976]{2,1,0:T(8,128)S(1)}, u32[]{:S(2)}, u32[]{:S(2)}) collective-permute-start(f32[4,32,976]{2,1,0:T(8,128)S(1)} %pad_maximum_fusion.2), channel_id=1, source_target_pairs={{0,256},{256,0},{1,257},{257,1},{2,258},{258,2},{3,259},{259,3},{4... | collective-permute-start | bytes 1499144 | tf_op jit(solution)/shard_map/ppermute | solution.py:74
  127.7 20.7 %all-to-all-start.2 = ((f32[4,32,976]{2,1,0:T(8,128)}), f32[4,32,976]{2,1,0:T(8,128)S(1)}, u32[]{:S(2)}, u32[]{:S(2)}) async-start(f32[4,32,976]{2,1,0:T(8,128)} %fusion.16), calls=%async_computation.2 | async-start | bytes 1048576 | tf_op jit(solution)/shard_map/all_to_all | solution.py:75

commit v17 on v13

--- a/solution.py
+++ b/solution.py
@@ -5,6 +5,7 @@
 from jax.sharding import Mesh, PartitionSpec as P
 
 ROW_DEV = 32
+HI = ("hx", "hy")
 
 
 OFF_SCALE = 0.9
@@ -15,11 +16,13 @@
     w_local = down_weight[0]
     tokens, span_width = x_local.shape
     cols = w_local.shape[0]
-    hi_index = lax.axis_index("hi")
+    hi_index = lax.axis_index(HI)
     lo_index = lax.axis_index("lo")
     tok_index = lax.axis_index("tok")
     group = lax.axis_size("lo")
-    hi_count = lax.axis_size("hi")
+    hi_count = lax.axis_size(HI)
+    half_count = lax.axis_size("hx")
+    hy_index = lax.axis_index("hy")
     tok_count = lax.axis_size("tok")
     mp_count = lax.axis_size("mp")
     blk_count = hi_count * group
@@ -36,7 +39,7 @@
     y_part_low = (y_part - y_part_round).astype(jnp.bfloat16).reshape(tokens, blk_count, col_group)
     win_spread = jnp.broadcast_to(x_local[:, None, :ROW_DEV], (tokens, blk_count, ROW_DEV))
     send_y = jnp.concatenate([y_part_high, y_part_low, win_spread], axis=2)
-    got_y = lax.all_to_all(send_y, ("hi", "lo"), 1, 1, tiled=True)
+    got_y = lax.all_to_all(send_y, HI + ("lo",), 1, 1, tiled=True)
     y_mine = jnp.sum(
         got_y[:, :, :col_group].astype(jnp.float32) + got_y[:, :, col_group:2 * col_group].astype(jnp.float32),
         axis=1,
@@ -47,9 +50,13 @@
     y_high = y_round.astype(jnp.bfloat16)
     y_low = (y_mine - y_round).astype(jnp.bfloat16)
     payload = jnp.concatenate([x_local, y_high, y_low], axis=1)
-    payload = lax.ppermute(payload, ("hi", "tok"), swap)
-    spread = jnp.broadcast_to(payload[None], (hi_count,) + payload.shape)
-    full = lax.all_to_all(spread, "hi", 0, 0, tiled=True).reshape(hi_count * tokens, -1)
+    mirror = [(h * tok_count + t, (t ^ 1) * tok_count + h) for h in range(hi_count) for t in range(tok_count)]
+    own = lax.ppermute(payload, HI + ("tok",), swap)
+    other = lax.ppermute(payload, HI + ("tok",), mirror)
+    even_first = hy_index == 0
+    pair = jnp.stack([jnp.where(even_first, own, other), jnp.where(even_first, other, own)])
+    spread = jnp.broadcast_to(pair[None], (half_count,) + pair.shape)
+    full = lax.all_to_all(spread, "hx", 0, 0, tiled=True).reshape(hi_count * tokens, -1)
     x_full = full[:, :span_width]
     y_tok = full[:, span_width:span_width + col_group].astype(jnp.float32) + full[:, span_width + col_group:].astype(jnp.float32)
 
@@ -90,13 +97,13 @@
 def solution(mesh):
     mp_count, blk_count, tok_count = (mesh.shape[a] for a in ("mp", "blk", "tok"))
     group = blk_count // tok_count
-    devices = np.asarray(mesh.devices).reshape(mp_count, tok_count, group, tok_count)
-    split = Mesh(devices, ("mp", "hi", "lo", "tok"))
-    placed = (P("mp", "tok", ("hi", "lo")), P("mp", None, ("hi", "lo")))
+    devices = np.asarray(mesh.devices).reshape(mp_count, tok_count // 2, 2, group, tok_count)
+    split = Mesh(devices, ("mp",) + HI + ("lo", "tok"))
+    placed = (P("mp", "tok", HI + ("lo",)), P("mp", None, HI + ("lo",)))
     return jax.shard_map(
         local,
         mesh=split,
         in_specs=placed,
-        out_specs=(P(("hi", "lo"), "tok"), P(("hi", "lo"), "tok")),
+        out_specs=(P(HI + ("lo",), "tok"), P(HI + ("lo",), "tok")),
         check_vma=False,
     )

time: 148 us -> 146 us (0.986); the launches traced: 148 us -> 144 us
  waiting for transfers between devices: 57.1 us -> 37.8 us
  local copies, waits for them, and re-layouts: 4.93 us -> 11.9 us
  starting transfers between devices: 38.1 us -> 44.5 us
  other arithmetic: 2.52 us -> 4.14 us
    all_to_all x1, waiting for transfers between devices: 28.1 us -> 3.88 us  [local(): lax.all_to_all(spread, 'hx', 0, 0, tiled=True)]
    all_to_all x1, starting transfers between devices: 23.8 us -> 30.8 us  [local(): lax.all_to_all(spread, 'hx', 0, 0, tiled=True)]
    ppermute x1 -> x2, waiting for transfers between devices: 4.14 us -> 10.5 us  [the longest x1 8.9 us: local(): own = lax.ppermute(payload, HI + ('tok',), swap)]
    reshape x1, local copies, waits for them, and re-layouts: 0.25 us -> 4.5 us  [local(): lax.all_to_all(spread, 'hx', 0, 0, tiled=True)]
    all_to_all x0 -> x1, local copies, waits for them, and re-layouts: none -> 2.75 us  [local(): lax.all_to_all(spread, 'hx', 0, 0, tiled=True)]
    all_to_all x1, starting transfers between devices: 6.69 us -> 4.12 us  [local(): got = lax.all_to_all(send, ('mp', 'lo'), 0, 0, tiled=True)]
    ppermute x1 -> x2, starting transfers between devices: 7.6 us -> 9.53 us  [the longest x1 5.43 us: local(): other = lax.ppermute(payload, HI + ('tok',), mirror)]
    all_to_all x1, waiting for transfers between devices: 24.9 us -> 23.4 us  [local(): got = lax.all_to_all(send, ('mp', 'lo'), 0, 0, tiled=True)]
  transfers between devices with their start and end apart: 3 -> 4, of which waited for: 3 -> 4; matrix products, arithmetic and copies ran while one was open for 0% -> 1% of each run, Pallas kernels for 0% -> 0%
where the time goes in v17:
time: 146 us; the launch traced here: 144 us
  starting transfers between devices  44.5 us (30%)
  blocking collectives  42.2 us (29%)
  waiting for transfers between devices  37.8 us (26%)
  local copies, waits for them, and re-layouts  11.9 us (8%)
  other arithmetic  4.14 us (3%)
  matrix products  2.4 us (2%)
    all_to_all x1, starting transfers between devices, local(): lax.all_to_all(spread, 'hx', 0, 0, tiled=True)  30.8 us
    all_to_all x1, blocking collectives, local(): got_y = lax.all_to_all(send_y, HI + ('lo',), 1, 1, tiled=True)  24.6 us
    all_to_all x1, waiting for transfers between devices, local(): got = lax.all_to_all(send, ('mp', 'lo'), 0, 0, tiled=True)  23.4 us
    all_gather x1, blocking collectives, local(): lax.all_gather(win_lo.reshape(tokens, group * ROW_DEV), 'tok', axis=0, ti...  17.6 us
    ppermute x1, waiting for transfers between devices, local(): own = lax.ppermute(payload, HI + ('tok',), swap)  8.9 us
    ppermute x1, starting transfers between devices, local(): other = lax.ppermute(payload, HI + ('tok',), mirror)  5.43 us
    reshape x1, local copies, waits for them, and re-layouts, local(): lax.all_to_all(spread, 'hx', 0, 0, tiled=True)  4.5 us
    all_to_all x1, starting transfers between devices, local(): got = lax.all_to_all(send, ('mp', 'lo'), 0, 0, tiled=True)  4.12 us
  transfers between devices with their start and end apart: 4, of which 4 were waited for; matrix products, arithmetic and copies ran while one was open for 1% of the time, Pallas kernels for 0%

profile of v17, /device:TPU:1, one launch (start us, length us, event | category | flops | bytes accessed | tf_op | source)
XLA Modules:
  0.0 143.8 jit_solution(9262212502553041920)
XLA Ops:
  0.6 0.0 copy-start
  0.6 0.8 slice.44
  1.5 0.1 copy.48
  1.6 0.3 copy-done
  1.8 1.4 reduce-precision_convert_fusion
  3.2 0.0 copy-start.1
  3.2 0.1 copy.46
  3.3 0.1 copy.47
  3.5 0.1 pad_maximum_fusion
  3.6 24.6 %all_to_all.15 = bf16[128,32,64]{0,2,1:T(8,128)(2,1)S(1)} all-to-all(bf16[128,32,64]{0,2,1:T(8,128)(2,1)S(1)} %pad_maximum_fusion), channel_id=1, replica_groups=mesh['mp'=2,'hx'=4,'hy'=2,'lo'=4,'tok'=8] {'hx','hy','lo'}, dimensions={1} | all-to-all | bytes 1048576 | tf_op jit(solution)/shard_map/all_to_all | solution.py:42
  28.2 0.1 copy.49
  28.4 0.1 copy.50
  28.5 0.0 copy-done.1
  28.5 0.1 pad_maximum_fusion.3
  28.6 5.4 %collective-permute-start.1 = (bf16[128,928]{1,0:T(8,128)(2,1)S(1)}, bf16[128,928]{1,0:T(8,128)(2,1)S(1)}, u32[]{:S(2)}, u32[]{:S(2)}) collective-permute-start(bf16[128,928]{1,0:T(8,128)(2,1)S(1)} %pad_maximum_fusion.3), channel_id=1, source_target_pairs={{0,32},{1,0},{2,96},{3,64},{4,160},{5,128},{6,224},{7,192},{32,33}... | collective-permute-start | bytes 712712 | tf_op jit(solution)/shard_map/ppermute | solution.py:55
  34.0 4.1 %collective-permute-start = (bf16[128,928]{1,0:T(8,128)(2,1)S(1)}, bf16[128,928]{1,0:T(8,128)(2,1)S(1)}, u32[]{:S(2)}, u32[]{:S(2)}) collective-permute-start(bf16[128,928]{1,0:T(8,128)(2,1)S(1)} %pad_maximum_fusion.3), channel_id=1, source_target_pairs={{0,0},{1,32},{2,64},{3,96},{4,128},{5,160},{6,192},{7,224},{32,1},... | collective-permute-start | bytes 712712 | tf_op jit(solution)/shard_map/ppermute | solution.py:54
  38.1 1.6 %collective-permute-done.1 = bf16[128,928]{1,0:T(8,128)(2,1)S(1)} collective-permute-done((bf16[128,928]{1,0:T(8,128)(2,1)S(1)}, bf16[128,928]{1,0:T(8,128)(2,1)S(1)}, u32[]{:S(2)}, u32[]{:S(2)}) %collective-permute-start.1) | collective-permute-done | bytes 237600 | tf_op jit(solution)/shard_map/ppermute | solution.py:55
  39.7 8.9 %collective-permute-done = bf16[128,928]{1,0:T(8,128)(2,1)S(1)} collective-permute-done((bf16[128,928]{1,0:T(8,128)(2,1)S(1)}, bf16[128,928]{1,0:T(8,128)(2,1)S(1)}, u32[]{:S(2)}, u32[]{:S(2)}) %collective-permute-start) | collective-permute-done | bytes 237600 | tf_op jit(solution)/shard_map/ppermute | solution.py:54
  48.7 0.1 pad_maximum_fusion.1
  48.7 0.3 copy.51
  49.0 1.5 %broadcast_in_dim.36 = bf16[4,2,128,928]{2,3,1,0:T(8,128)(2,1)} broadcast(bf16[2,128,928]{1,2,0:T(8,128)(2,1)S(1)} %copy.51), dimensions={1,2,3} | broadcast | bytes 2375680 | tf_op jit(solution)/shard_map/broadcast_in_dim | solution.py:58
  50.5 30.8 %all-to-all-start.1 = ((bf16[4,2,128,928]{2,3,1,0:T(8,128)(2,1)}), bf16[4,2,128,928]{2,3,1,0:T(8,128)(2,1)S(1)}, u32[]{:S(2)}, u32[]{:S(2)}) async-start(bf16[4,2,128,928]{2,3,1,0:T(8,128)(2,1)} %broadcast_in_dim.36), calls=%async_computation.1 | async-start | bytes 3801088 | tf_op jit(solution)/shard_map/all_to_all | solution.py:59
  81.4 17.6 %all_gather.3 = bf16[1024,128]{0,1:T(8,128)(2,1)S(1)} all-gather(bf16[128,128]{0,1:T(8,128)(2,1)S(1)} %bitcast.41), channel_id=1, replica_groups=mesh['mp'=2,'hx'=4,'hy'=2,'lo'=4,'tok'=8] {'tok'}, dimensions={0}, use_global_device_ids=true | all-gather | bytes 294912 | tf_op jit(solution)/shard_map/all_gather | solution.py:48
  99.0 0.1 multiply_reduce_fusion
  99.2 0.1 copy.54
  99.2 0.7 broadcast_select_fusion
  100.0 3.9 %all-to-all-done.1 = bf16[4,2,128,928]{2,3,1,0:T(8,128)(2,1)S(1)} async-done(((bf16[4,2,128,928]{2,3,1,0:T(8,128)(2,1)}), bf16[4,2,128,928]{2,3,1,0:T(8,128)(2,1)S(1)}, u32[]{:S(2)}, u32[]{:S(2)}) %all-to-all-start.1) | async-done | bytes 1900576 | tf_op jit(solution)/shard_map/all_to_all | solution.py:59
  103.8 2.7 %copy.52 = bf16[4,2,128,928]{2,1,0,3:T(2,128)(2,1)} copy(bf16[4,2,128,928]{2,3,1,0:T(8,128)(2,1)S(1)} %all-to-all-done.1) | data formatting | bytes 3801088 | tf_op jit(solution)/shard_map/all_to_all | solution.py:59
  106.6 4.5 %reshape.43 = bf16[1024,928]{0,1:T(8,128)(2,1)S(1)} reshape(bf16[4,2,128,928]{2,1,0,3:T(2,128)(2,1)} %copy.52) | data formatting | bytes 3801088 | tf_op jit(solution)/shard_map/reshape | solution.py:59
  111.1 0.3 convolution_multiply_fusion
  111.4 0.7 fusion
  112.1 0.1 copy.53
  112.3 2.1 %maximum_maximum_fusion = f32[8,32,976]{2,1,0:T(8,128)} fusion(f32[4,32,64]{2,1,0:T(8,128)} %broadcast_select_fusion, f32[4,32,912]{2,1,0:T(8,128)S(1)} %bitcast.35), kind=kLoop, calls=%fused_computation.3 | loop fusion | flops 749568 | bytes 1499136 | tf_op jit(solution)/shard_map/concatenate | solution.py:81
  114.3 4.1 %all-to-all-start.2 = ((f32[8,32,976]{2,1,0:T(8,128)}), f32[8,32,976]{2,1,0:T(8,128)S(1)}, u32[]{:S(2)}, u32[]{:S(2)}) async-start(f32[8,32,976]{2,1,0:T(8,128)} %maximum_maximum_fusion), calls=%async_computation.2 | async-start | bytes 2097152 | tf_op jit(solution)/shard_map/all_to_all | solution.py:82
  118.5 23.4 %all-to-all-done.2 = f32[8,32,976]{2,1,0:T(8,128)S(1)} async-done(((f32[8,32,976]{2,1,0:T(8,128)}), f32[8,32,976]{2,1,0:T(8,128)S(1)}, u32[]{:S(2)}, u32[]{:S(2)}) %all-to-all-start.2) | async-done | bytes 999456 | tf_op jit(solution)/shard_map/all_to_all | solution.py:82
  141.9 0.1 reduce_sum.38
  142.0 0.1 slice_reduce_fusion
  142.1 0.1 fusion.4
  142.2 0.1 copy.56
  142.3 0.1 copy.57
  142.3 0.8 copy.58
  143.1 0.6 add.27
  (13 shorter events, 0.3 us)
Async XLA Ops:
  0.6 1.2 copy-start
  3.2 25.3 %copy-start.1 = (bf16[1,128,896]{2,1,0:T(8,128)(2,1)S(1)}, bf16[1,128,896]{2,1,0:T(8,128)(2,1)}, u32[]{:S(2)}) copy-start(bf16[1,128,896]{2,1,0:T(8,128)(2,1)} %param.2) | copy-start | bytes 688132
  28.6 11.1 %collective-permute-start.1 = (bf16[128,928]{1,0:T(8,128)(2,1)S(1)}, bf16[128,928]{1,0:T(8,128)(2,1)S(1)}, u32[]{:S(2)}, u32[]{:S(2)}) collective-permute-start(bf16[128,928]{1,0:T(8,128)(2,1)S(1)} %pad_maximum_fusion.3), channel_id=1, source_target_pairs={{0,32},{1,0},{2,96},{3,64},{4,160},{5,128},{6,224},{7,192},{32,33}... | collective-permute-start | bytes 712712 | tf_op jit(solution)/shard_map/ppermute | solution.py:55
  34.0 14.6 %collective-permute-start = (bf16[128,928]{1,0:T(8,128)(2,1)S(1)}, bf16[128,928]{1,0:T(8,128)(2,1)S(1)}, u32[]{:S(2)}, u32[]{:S(2)}) collective-permute-start(bf16[128,928]{1,0:T(8,128)(2,1)S(1)} %pad_maximum_fusion.3), channel_id=1, source_target_pairs={{0,0},{1,32},{2,64},{3,96},{4,128},{5,160},{6,192},{7,224},{32,1},... | collective-permute-start | bytes 712712 | tf_op jit(solution)/shard_map/ppermute | solution.py:54
  50.5 53.3 %all-to-all-start.1 = ((bf16[4,2,128,928]{2,3,1,0:T(8,128)(2,1)}), bf16[4,2,128,928]{2,3,1,0:T(8,128)(2,1)S(1)}, u32[]{:S(2)}, u32[]{:S(2)}) async-start(bf16[4,2,128,928]{2,3,1,0:T(8,128)(2,1)} %broadcast_in_dim.36), calls=%async_computation.1 | async-start | bytes 3801088 | tf_op jit(solution)/shard_map/all_to_all | solution.py:59
  114.3 27.5 %all-to-all-start.2 = ((f32[8,32,976]{2,1,0:T(8,128)}), f32[8,32,976]{2,1,0:T(8,128)S(1)}, u32[]{:S(2)}, u32[]{:S(2)}) async-start(f32[8,32,976]{2,1,0:T(8,128)} %maximum_maximum_fusion), calls=%async_computation.2 | async-start | bytes 2097152 | tf_op jit(solution)/shard_map/all_to_all | solution.py:82

commit v18 on v17

--- a/solution.py
+++ b/solution.py
@@ -56,15 +56,15 @@
     even_first = hy_index == 0
     pair = jnp.stack([jnp.where(even_first, own, other), jnp.where(even_first, other, own)])
     spread = jnp.broadcast_to(pair[None], (half_count,) + pair.shape)
-    full = lax.all_to_all(spread, "hx", 0, 0, tiled=True).reshape(hi_count * tokens, -1)
-    x_full = full[:, :span_width]
-    y_tok = full[:, span_width:span_width + col_group].astype(jnp.float32) + full[:, span_width + col_group:].astype(jnp.float32)
+    full = lax.all_to_all(spread, "hx", 0, 0, tiled=True)
+    x_full = full[..., :span_width]
+    y_tok = full[..., span_width:span_width + col_group].astype(jnp.float32) + full[..., span_width + col_group:].astype(jnp.float32)
 
-    gram = lax.dot_general(
-        wins, x_full, (((0,), (0,)), ((), ())), preferred_element_type=jnp.float32
-    )
+    wins_split = wins.reshape(full.shape[:3] + (wins.shape[1],))
+    over_tokens = (((0, 1, 2), (0, 1, 2)), ((), ()))
+    gram = lax.dot_general(wins_split, x_full, over_tokens, preferred_element_type=jnp.float32)
     cross = lax.dot_general(
-        wins.astype(jnp.float32), y_tok, (((0,), (0,)), ((), ())),
+        wins_split.astype(jnp.float32), y_tok, over_tokens,
         precision=lax.Precision.HIGHEST, preferred_element_type=jnp.float32,
     )
     pieces = jnp.concatenate([gram, OFF_SCALE * cross], axis=1)

time: 146 us -> 138 us (0.945)
  local copies, waits for them, and re-layouts: 11.9 us -> 4.86 us
  other arithmetic: 4.14 us -> 2.6 us
    reshape x1 -> x0, local copies, waits for them, and re-layouts: 4.5 us -> none  [local(): lax.all_to_all(spread, 'hx', 0, 0, tiled=True)]
    all_to_all x1 -> x0, local copies, waits for them, and re-layouts: 2.75 us -> none  [local(): lax.all_to_all(spread, 'hx', 0, 0, tiled=True)]
  transfers between devices with their start and end apart: 4 -> 4, of which waited for: 4 -> 4; matrix products, arithmetic and copies ran while one was open for 1% -> 0% of each run, Pallas kernels for 0% -> 0%
where the time goes in v18:
time: 138 us; the launch traced here: 136 us
  starting transfers between devices  44.5 us (32%)
  blocking collectives  42.2 us (31%)
  waiting for transfers between devices  38.2 us (28%)
  local copies, waits for them, and re-layouts  4.86 us (4%)
  other arithmetic  2.6 us (2%)
  matrix products  2.3 us (2%)
    all_to_all x1, starting transfers between devices, local(): full = lax.all_to_all(spread, 'hx', 0, 0, tiled=True)  30.8 us
    all_to_all x1, blocking collectives, local(): got_y = lax.all_to_all(send_y, HI + ('lo',), 1, 1, tiled=True)  24.6 us
    all_to_all x1, waiting for transfers between devices, local(): got = lax.all_to_all(send, ('mp', 'lo'), 0, 0, tiled=True)  23.4 us
    all_gather x1, blocking collectives, local(): lax.all_gather(win_lo.reshape(tokens, group * ROW_DEV), 'tok', axis=0, ti...  17.6 us
    ppermute x1, waiting for transfers between devices, local(): own = lax.ppermute(payload, HI + ('tok',), swap)  8.9 us
    ppermute x1, starting transfers between devices, local(): other = lax.ppermute(payload, HI + ('tok',), mirror)  5.43 us
    all_to_all x1, waiting for transfers between devices, local(): full = lax.all_to_all(spread, 'hx', 0, 0, tiled=True)  4.34 us
    all_to_all x1, starting transfers between devices, local(): got = lax.all_to_all(send, ('mp', 'lo'), 0, 0, tiled=True)  4.13 us
  transfers between devices with their start and end apart: 4, of which 4 were waited for; matrix products, arithmetic and copies ran while one was open for 0% of the time, Pallas kernels for 0%

profile of v18, /device:TPU:1, one launch (start us, length us, event | category | flops | bytes accessed | tf_op | source)
XLA Modules:
  0.0 135.5 jit_solution(12007412067697859836)
XLA Ops:
  0.6 0.0 copy-start
  0.6 0.8 slice.44
  1.5 0.1 copy.60
  1.6 0.3 copy-done
  1.8 1.4 %reduce-precision_convert_fusion = (bf16[128,512]{1,0:T(8,128)(2,1)S(1)}, bf16[128,512]{1,0:T(8,128)(2,1)S(1)}) fusion(bf16[1,512,896]{2,1,0:T(8,128)(2,1)S(1)} %copy-done, bf16[1,128,896]{2,1,0:T(8,128)(2,1)} %param.2), kind=kOutput, calls=%fused_computation.16 | convolution fusion | flops 117702656 | bytes 1409024 | tf_op jit(solution)/shard_map/dot_general | solution.py:34
  3.2 0.0 copy-start.1
  3.2 0.1 copy.58
  3.3 0.1 copy.59
  3.5 0.1 pad_maximum_fusion
  3.6 24.6 %all_to_all.15 = bf16[128,32,64]{0,2,1:T(8,128)(2,1)S(1)} all-to-all(bf16[128,32,64]{0,2,1:T(8,128)(2,1)S(1)} %pad_maximum_fusion), channel_id=1, replica_groups=mesh['mp'=2,'hx'=4,'hy'=2,'lo'=4,'tok'=8] {'hx','hy','lo'}, dimensions={1} | all-to-all | bytes 1048576 | tf_op jit(solution)/shard_map/all_to_all | solution.py:42
  28.2 0.1 copy.62
  28.4 0.1 copy.63
  28.5 0.0 copy-done.1
  28.5 0.1 pad_maximum_fusion.3
  28.6 5.4 %collective-permute-start.1 = (bf16[128,928]{1,0:T(8,128)(2,1)S(1)}, bf16[128,928]{1,0:T(8,128)(2,1)S(1)}, u32[]{:S(2)}, u32[]{:S(2)}) collective-permute-start(bf16[128,928]{1,0:T(8,128)(2,1)S(1)} %pad_maximum_fusion.3), channel_id=1, source_target_pairs={{0,32},{1,0},{2,96},{3,64},{4,160},{5,128},{6,224},{7,192},{32,33}... | collective-permute-start | bytes 712712 | tf_op jit(solution)/shard_map/ppermute | solution.py:55
  34.0 4.1 %collective-permute-start = (bf16[128,928]{1,0:T(8,128)(2,1)S(1)}, bf16[128,928]{1,0:T(8,128)(2,1)S(1)}, u32[]{:S(2)}, u32[]{:S(2)}) collective-permute-start(bf16[128,928]{1,0:T(8,128)(2,1)S(1)} %pad_maximum_fusion.3), channel_id=1, source_target_pairs={{0,0},{1,32},{2,64},{3,96},{4,128},{5,160},{6,192},{7,224},{32,1},... | collective-permute-start | bytes 712712 | tf_op jit(solution)/shard_map/ppermute | solution.py:54
  38.1 1.6 %collective-permute-done.1 = bf16[128,928]{1,0:T(8,128)(2,1)S(1)} collective-permute-done((bf16[128,928]{1,0:T(8,128)(2,1)S(1)}, bf16[128,928]{1,0:T(8,128)(2,1)S(1)}, u32[]{:S(2)}, u32[]{:S(2)}) %collective-permute-start.1) | collective-permute-done | bytes 237600 | tf_op jit(solution)/shard_map/ppermute | solution.py:55
  39.7 8.9 %collective-permute-done = bf16[128,928]{1,0:T(8,128)(2,1)S(1)} collective-permute-done((bf16[128,928]{1,0:T(8,128)(2,1)S(1)}, bf16[128,928]{1,0:T(8,128)(2,1)S(1)}, u32[]{:S(2)}, u32[]{:S(2)}) %collective-permute-start) | collective-permute-done | bytes 237600 | tf_op jit(solution)/shard_map/ppermute | solution.py:54
  48.7 0.1 pad_maximum_fusion.1
  48.7 0.3 copy.64
  49.0 1.5 %broadcast_in_dim.36 = bf16[4,2,128,928]{2,3,1,0:T(8,128)(2,1)} broadcast(bf16[2,128,928]{1,2,0:T(8,128)(2,1)S(1)} %copy.64), dimensions={1,2,3} | broadcast | bytes 2375680 | tf_op jit(solution)/shard_map/broadcast_in_dim | solution.py:58
  50.5 30.8 %all-to-all-start.1 = ((bf16[4,2,128,928]{2,3,1,0:T(8,128)(2,1)}), bf16[4,2,128,928]{2,3,1,0:T(8,128)(2,1)S(1)}, u32[]{:S(2)}, u32[]{:S(2)}) async-start(bf16[4,2,128,928]{2,3,1,0:T(8,128)(2,1)} %broadcast_in_dim.36), calls=%async_computation.1 | async-start | bytes 3801088 | tf_op jit(solution)/shard_map/all_to_all | solution.py:59
  81.4 17.6 %all_gather.3 = bf16[1024,128]{0,1:T(8,128)(2,1)S(1)} all-gather(bf16[128,128]{0,1:T(8,128)(2,1)S(1)} %bitcast.52), channel_id=1, replica_groups=mesh['mp'=2,'hx'=4,'hy'=2,'lo'=4,'tok'=8] {'tok'}, dimensions={0}, use_global_device_ids=true | all-gather | bytes 294912 | tf_op jit(solution)/shard_map/all_gather | solution.py:48
  99.0 0.2 copy.61
  99.2 0.1 multiply_reduce_fusion
  99.4 0.1 copy.68
  99.4 0.1 broadcast_select_fusion
  99.5 4.3 %all-to-all-done.1 = bf16[4,2,128,928]{2,3,1,0:T(8,128)(2,1)S(1)} async-done(((bf16[4,2,128,928]{2,3,1,0:T(8,128)(2,1)}), bf16[4,2,128,928]{2,3,1,0:T(8,128)(2,1)S(1)}, u32[]{:S(2)}, u32[]{:S(2)}) %all-to-all-start.1) | async-done | bytes 1900576 | tf_op jit(solution)/shard_map/all_to_all | solution.py:59
  103.8 0.2 fusion.5
  104.1 0.1 copy.67
  104.2 0.7 fusion.2
  104.9 1.1 maximum_maximum_fusion
  106.1 4.1 %all-to-all-start.2 = ((f32[8,32,976]{2,1,0:T(8,128)}), f32[8,32,976]{2,1,0:T(8,128)S(1)}, u32[]{:S(2)}, u32[]{:S(2)}) async-start(f32[8,32,976]{2,1,0:T(8,128)} %maximum_maximum_fusion), calls=%async_computation.2 | async-start | bytes 2097152 | tf_op jit(solution)/shard_map/all_to_all | solution.py:82
  110.2 23.4 %all-to-all-done.2 = f32[8,32,976]{2,1,0:T(8,128)S(1)} async-done(((f32[8,32,976]{2,1,0:T(8,128)}), f32[8,32,976]{2,1,0:T(8,128)S(1)}, u32[]{:S(2)}, u32[]{:S(2)}) %all-to-all-start.2) | async-done | bytes 999456 | tf_op jit(solution)/shard_map/all_to_all | solution.py:82
  133.6 0.1 reduce_sum.38
  133.7 0.1 slice_reduce_fusion
  133.9 0.1 fusion.8
  133.9 0.1 copy.70
  134.0 0.1 copy.71
  134.1 0.8 copy.76
  134.9 0.6 add.27
  (13 shorter events, 0.3 us)
Async XLA Ops:
  0.6 1.2 copy-start
  3.2 25.3 %copy-start.1 = (bf16[1,128,896]{2,1,0:T(8,128)(2,1)S(1)}, bf16[1,128,896]{2,1,0:T(8,128)(2,1)}, u32[]{:S(2)}) copy-start(bf16[1,128,896]{2,1,0:T(8,128)(2,1)} %param.2) | copy-start | bytes 688132
  28.6 11.1 %collective-permute-start.1 = (bf16[128,928]{1,0:T(8,128)(2,1)S(1)}, bf16[128,928]{1,0:T(8,128)(2,1)S(1)}, u32[]{:S(2)}, u32[]{:S(2)}) collective-permute-start(bf16[128,928]{1,0:T(8,128)(2,1)S(1)} %pad_maximum_fusion.3), channel_id=1, source_target_pairs={{0,32},{1,0},{2,96},{3,64},{4,160},{5,128},{6,224},{7,192},{32,33}... | collective-permute-start | bytes 712712 | tf_op jit(solution)/shard_map/ppermute | solution.py:55
  34.0 14.6 %collective-permute-start = (bf16[128,928]{1,0:T(8,128)(2,1)S(1)}, bf16[128,928]{1,0:T(8,128)(2,1)S(1)}, u32[]{:S(2)}, u32[]{:S(2)}) collective-permute-start(bf16[128,928]{1,0:T(8,128)(2,1)S(1)} %pad_maximum_fusion.3), channel_id=1, source_target_pairs={{0,0},{1,32},{2,64},{3,96},{4,128},{5,160},{6,192},{7,224},{32,1},... | collective-permute-start | bytes 712712 | tf_op jit(solution)/shard_map/ppermute | solution.py:54
  50.5 53.3 %all-to-all-start.1 = ((bf16[4,2,128,928]{2,3,1,0:T(8,128)(2,1)}), bf16[4,2,128,928]{2,3,1,0:T(8,128)(2,1)S(1)}, u32[]{:S(2)}, u32[]{:S(2)}) async-start(bf16[4,2,128,928]{2,3,1,0:T(8,128)(2,1)} %broadcast_in_dim.36), calls=%async_computation.1 | async-start | bytes 3801088 | tf_op jit(solution)/shard_map/all_to_all | solution.py:59
  106.1 27.5 %all-to-all-start.2 = ((f32[8,32,976]{2,1,0:T(8,128)}), f32[8,32,976]{2,1,0:T(8,128)S(1)}, u32[]{:S(2)}, u32[]{:S(2)}) async-start(f32[8,32,976]{2,1,0:T(8,128)} %maximum_maximum_fusion), calls=%async_computation.2 | async-start | bytes 2097152 | tf_op jit(solution)/shard_map/all_to_all | solution.py:82

commit v19 on v18

--- a/solution.py
+++ b/solution.py
@@ -53,6 +53,7 @@
     mirror = [(h * tok_count + t, (t ^ 1) * tok_count + h) for h in range(hi_count) for t in range(tok_count)]
     own = lax.ppermute(payload, HI + ("tok",), swap)
     other = lax.ppermute(payload, HI + ("tok",), mirror)
+    own, other, wins = lax.optimization_barrier((own, other, wins))
     even_first = hy_index == 0
     pair = jnp.stack([jnp.where(even_first, own, other), jnp.where(even_first, other, own)])
     spread = jnp.broadcast_to(pair[None], (half_count,) + pair.shape)

time: 138 us -> 153 us (1.11); the launches traced: 136 us -> 152 us
  blocking collectives: 42.2 us -> 70.3 us
  starting transfers between devices: 44.5 us -> 23.3 us
  waiting for transfers between devices: 38.2 us -> 48.2 us
    all_gather x1, blocking collectives: 17.6 us -> 45.6 us  [local(): lax.all_gather(win_lo.reshape(tokens, group * ROW_DEV), 'tok', axis=0, ti...]
    all_to_all x1, starting transfers between devices: 30.8 us -> 7.71 us  [local(): full = lax.all_to_all(spread, 'hx', 0, 0, tiled=True)]
    all_to_all x1, waiting for transfers between devices: 4.34 us -> 23.4 us  [local(): full = lax.all_to_all(spread, 'hx', 0, 0, tiled=True)]
    ppermute x1, waiting for transfers between devices: 8.9 us -> 0.01 us  [local(): own = lax.ppermute(payload, HI + ('tok',), swap)]
    ppermute x1, starting transfers between devices: 5.43 us -> 1.92 us  [local(): other = lax.ppermute(payload, HI + ('tok',), mirror)]
    ppermute x1, starting transfers between devices: 4.1 us -> 7.6 us  [local(): own = lax.ppermute(payload, HI + ('tok',), swap)]
    all_to_all x1, starting transfers between devices: 4.13 us -> 6.08 us  [local(): got = lax.all_to_all(send, ('mp', 'lo'), 0, 0, tiled=True)]
    ppermute x1, waiting for transfers between devices: 1.57 us -> 0.01 us  [local(): other = lax.ppermute(payload, HI + ('tok',), mirror)]
  transfers between devices with their start and end apart: 4 -> 4, of which waited for: 4 -> 2; matrix products, arithmetic and copies ran while one was open for 0% -> 0% of each run, Pallas kernels for 0% -> 0%
where the time goes in v19:
time: 153 us; the launch traced here: 152 us
  blocking collectives  70.3 us (46%)
  waiting for transfers between devices  48.2 us (32%)
  starting transfers between devices  23.3 us (15%)
  local copies, waits for them, and re-layouts  4.92 us (3%)
  other arithmetic  2.61 us (2%)
  matrix products  2.3 us (2%)
    all_gather x1, blocking collectives, local(): lax.all_gather(win_lo.reshape(tokens, group * ROW_DEV), 'tok', axis=0, ti...  45.6 us
    all_to_all x1, waiting for transfers between devices, local(): got = lax.all_to_all(send, ('mp', 'lo'), 0, 0, tiled=True)  24.8 us
    all_to_all x1, blocking collectives, local(): got_y = lax.all_to_all(send_y, HI + ('lo',), 1, 1, tiled=True)  24.6 us
    all_to_all x1, waiting for transfers between devices, local(): full = lax.all_to_all(spread, 'hx', 0, 0, tiled=True)  23.4 us
    all_to_all x1, starting transfers between devices, local(): full = lax.all_to_all(spread, 'hx', 0, 0, tiled=True)  7.71 us
    ppermute x1, starting transfers between devices, local(): own = lax.ppermute(payload, HI + ('tok',), swap)  7.6 us
    all_to_all x1, starting transfers between devices, local(): got = lax.all_to_all(send, ('mp', 'lo'), 0, 0, tiled=True)  6.08 us
  transfers between devices with their start and end apart: 4, of which 2 were waited for; matrix products, arithmetic and copies ran while one was open for 0% of the time, Pallas kernels for 0%

profile of v19, /device:TPU:1, one launch (start us, length us, event | category | flops | bytes accessed | tf_op | source)
XLA Modules:
  0.0 152.4 jit_solution(9904789863063123360)
XLA Ops:
  0.6 0.0 copy-start
  0.6 0.0 copy-start.1
  0.7 1.2 copy-done
  1.8 1.4 reduce-precision_convert_fusion
  3.2 0.1 copy.58
  3.3 0.1 copy.59
  3.4 0.0 copy-done.1
  3.5 0.1 copy.60
  3.5 0.1 broadcast_in_dim.17
  3.6 0.1 pad_maximum_fusion
  3.7 24.6 %all_to_all.15 = bf16[128,32,64]{0,2,1:T(8,128)(2,1)S(1)} all-to-all(bf16[128,32,64]{0,2,1:T(8,128)(2,1)S(1)} %pad_maximum_fusion), channel_id=1, replica_groups=mesh['mp'=2,'hx'=4,'hy'=2,'lo'=4,'tok'=8] {'hx','hy','lo'}, dimensions={1} | all-to-all | bytes 1048576 | tf_op jit(solution)/shard_map/all_to_all | solution.py:42
  28.3 0.1 copy.61
  28.5 0.1 copy.62
  28.6 0.1 pad_maximum_fusion.3
  28.7 7.6 %collective-permute-start = (bf16[128,928]{1,0:T(8,128)(2,1)S(1)}, bf16[128,928]{1,0:T(8,128)(2,1)S(1)}, u32[]{:S(2)}, u32[]{:S(2)}) collective-permute-start(bf16[128,928]{1,0:T(8,128)(2,1)S(1)} %pad_maximum_fusion.3), channel_id=1, source_target_pairs={{0,0},{1,32},{2,64},{3,96},{4,128},{5,160},{6,192},{7,224},{32,1},... | collective-permute-start | bytes 712712 | tf_op jit(solution)/shard_map/ppermute | solution.py:54
  36.3 1.9 %collective-permute-start.1 = (bf16[128,928]{1,0:T(8,128)(2,1)S(1)}, bf16[128,928]{1,0:T(8,128)(2,1)S(1)}, u32[]{:S(2)}, u32[]{:S(2)}) collective-permute-start(bf16[128,928]{1,0:T(8,128)(2,1)S(1)} %pad_maximum_fusion.3), channel_id=1, source_target_pairs={{0,32},{1,0},{2,96},{3,64},{4,160},{5,128},{6,224},{7,192},{32,33}... | collective-permute-start | bytes 712712 | tf_op jit(solution)/shard_map/ppermute | solution.py:55
  38.3 45.6 %all_gather.3 = bf16[1024,128]{0,1:T(8,128)(2,1)S(1)} all-gather(bf16[128,128]{0,1:T(8,128)(2,1)S(1)} %bitcast.52), channel_id=1, replica_groups=mesh['mp'=2,'hx'=4,'hy'=2,'lo'=4,'tok'=8] {'tok'}, dimensions={0}, use_global_device_ids=true | all-gather | bytes 294912 | tf_op jit(solution)/shard_map/all_gather | solution.py:48
  83.9 0.0 collective-permute-done
  83.9 0.0 collective-permute-done.1
  84.0 0.1 pad_maximum_fusion.1
  84.0 0.3 copy.63
  84.3 1.5 %broadcast_in_dim.36 = bf16[4,2,128,928]{2,3,1,0:T(8,128)(2,1)} broadcast(bf16[2,128,928]{1,2,0:T(8,128)(2,1)S(1)} %copy.63), dimensions={1,2,3} | broadcast | bytes 2375680 | tf_op jit(solution)/shard_map/broadcast_in_dim | solution.py:59
  85.8 7.7 %all-to-all-start.1 = ((bf16[4,2,128,928]{2,3,1,0:T(8,128)(2,1)}), bf16[4,2,128,928]{2,3,1,0:T(8,128)(2,1)S(1)}, u32[]{:S(2)}, u32[]{:S(2)}) async-start(bf16[4,2,128,928]{2,3,1,0:T(8,128)(2,1)} %broadcast_in_dim.36), calls=%async_computation.1 | async-start | bytes 3801088 | tf_op jit(solution)/shard_map/all_to_all | solution.py:60
  93.6 0.2 copy.75
  93.7 0.1 multiply_reduce_fusion
  93.9 0.1 copy.68
  94.0 0.1 broadcast_select_fusion
  94.0 23.4 %all-to-all-done.1 = bf16[4,2,128,928]{2,3,1,0:T(8,128)(2,1)S(1)} async-done(((bf16[4,2,128,928]{2,3,1,0:T(8,128)(2,1)}), bf16[4,2,128,928]{2,3,1,0:T(8,128)(2,1)S(1)}, u32[]{:S(2)}, u32[]{:S(2)}) %all-to-all-start.1) | async-done | bytes 1900576 | tf_op jit(solution)/shard_map/all_to_all | solution.py:60
  117.4 0.2 fusion.5
  117.7 0.1 copy.67
  117.8 0.7 fusion.2
  118.5 1.1 maximum_maximum_fusion
  119.7 6.1 %all-to-all-start.2 = ((f32[8,32,976]{2,1,0:T(8,128)}), f32[8,32,976]{2,1,0:T(8,128)S(1)}, u32[]{:S(2)}, u32[]{:S(2)}) async-start(f32[8,32,976]{2,1,0:T(8,128)} %maximum_maximum_fusion), calls=%async_computation.2 | async-start | bytes 2097152 | tf_op jit(solution)/shard_map/all_to_all | solution.py:83
  125.8 24.8 %all-to-all-done.2 = f32[8,32,976]{2,1,0:T(8,128)S(1)} async-done(((f32[8,32,976]{2,1,0:T(8,128)}), f32[8,32,976]{2,1,0:T(8,128)S(1)}, u32[]{:S(2)}, u32[]{:S(2)}) %all-to-all-start.2) | async-done | bytes 999456 | tf_op jit(solution)/shard_map/all_to_all | solution.py:83
  150.6 0.1 reduce_sum.38
  150.7 0.1 slice_reduce_fusion
  150.8 0.1 copy.70
  150.9 0.1 copy.71
  150.9 0.1 fusion.8
  151.0 0.8 copy.76
  151.8 0.6 add.27
  (13 shorter events, 0.2 us)
Async XLA Ops:
  0.6 1.2 copy-start
  0.6 2.8 %copy-start.1 = (bf16[1,128,896]{2,1,0:T(8,128)(2,1)S(1)}, bf16[1,128,896]{2,1,0:T(8,128)(2,1)}, u32[]{:S(2)}) copy-start(bf16[1,128,896]{2,1,0:T(8,128)(2,1)} %param.2) | copy-start | bytes 688132
  28.7 55.2 %collective-permute-start = (bf16[128,928]{1,0:T(8,128)(2,1)S(1)}, bf16[128,928]{1,0:T(8,128)(2,1)S(1)}, u32[]{:S(2)}, u32[]{:S(2)}) collective-permute-start(bf16[128,928]{1,0:T(8,128)(2,1)S(1)} %pad_maximum_fusion.3), channel_id=1, source_target_pairs={{0,0},{1,32},{2,64},{3,96},{4,128},{5,160},{6,192},{7,224},{32,1},... | collective-permute-start | bytes 712712 | tf_op jit(solution)/shard_map/ppermute | solution.py:54
  36.3 47.6 %collective-permute-start.1 = (bf16[128,928]{1,0:T(8,128)(2,1)S(1)}, bf16[128,928]{1,0:T(8,128)(2,1)S(1)}, u32[]{:S(2)}, u32[]{:S(2)}) collective-permute-start(bf16[128,928]{1,0:T(8,128)(2,1)S(1)} %pad_maximum_fusion.3), channel_id=1, source_target_pairs={{0,32},{1,0},{2,96},{3,64},{4,160},{5,128},{6,224},{7,192},{32,33}... | collective-permute-start | bytes 712712 | tf_op jit(solution)/shard_map/ppermute | solution.py:55
  85.8 31.6 %all-to-all-start.1 = ((bf16[4,2,128,928]{2,3,1,0:T(8,128)(2,1)}), bf16[4,2,128,928]{2,3,1,0:T(8,128)(2,1)S(1)}, u32[]{:S(2)}, u32[]{:S(2)}) async-start(bf16[4,2,128,928]{2,3,1,0:T(8,128)(2,1)} %broadcast_in_dim.36), calls=%async_computation.1 | async-start | bytes 3801088 | tf_op jit(solution)/shard_map/all_to_all | solution.py:60
  119.7 30.9 %all-to-all-start.2 = ((f32[8,32,976]{2,1,0:T(8,128)}), f32[8,32,976]{2,1,0:T(8,128)S(1)}, u32[]{:S(2)}, u32[]{:S(2)}) async-start(f32[8,32,976]{2,1,0:T(8,128)} %maximum_maximum_fusion), calls=%async_computation.2 | async-start | bytes 2097152 | tf_op jit(solution)/shard_map/all_to_all | solution.py:83

commit v20 on v18

--- a/solution.py
+++ b/solution.py
@@ -49,10 +49,12 @@
     y_round = lax.reduce_precision(y_mine, exponent_bits=8, mantissa_bits=7)
     y_high = y_round.astype(jnp.bfloat16)
     y_low = (y_mine - y_round).astype(jnp.bfloat16)
-    payload = jnp.concatenate([x_local, y_high, y_low], axis=1)
     mirror = [(h * tok_count + t, (t ^ 1) * tok_count + h) for h in range(hi_count) for t in range(tok_count)]
-    own = lax.ppermute(payload, HI + ("tok",), swap)
-    other = lax.ppermute(payload, HI + ("tok",), mirror)
+    x_own = lax.ppermute(x_local, HI + ("tok",), swap)
+    x_other = lax.ppermute(x_local, HI + ("tok",), mirror)
+    y_pay = jnp.concatenate([y_high, y_low], axis=1)
+    own = jnp.concatenate([x_own, lax.ppermute(y_pay, HI + ("tok",), swap)], axis=1)
+    other = jnp.concatenate([x_other, lax.ppermute(y_pay, HI + ("tok",), mirror)], axis=1)
     even_first = hy_index == 0
     pair = jnp.stack([jnp.where(even_first, own, other), jnp.where(even_first, other, own)])
     spread = jnp.broadcast_to(pair[None], (half_count,) + pair.shape)

time: 138 us -> 127 us (0.920); the launches traced: 136 us -> 127 us
  blocking collectives: 42.2 us -> 13.3 us
  starting transfers between devices: 44.5 us -> 59.6 us
  waiting for transfers between devices: 38.2 us -> 42.3 us
    all_to_all x1 -> x0, blocking collectives: 24.6 us -> none  [local(): got_y = lax.all_to_all(send_y, HI + ('lo',), 1, 1, tiled=True)]
    ppermute x2 -> x4, starting transfers between devices: 9.53 us -> 21 us  [the longest x1 8.97 us: local(): lax.ppermute(y_pay, HI + ('tok',), swap)]
    all_to_all x0 -> x1, starting transfers between devices: none -> 10.5 us  [local(): got_y = lax.all_to_all(send_y, HI + ('lo',), 1, 1, tiled=True)]
    all_to_all x1, starting transfers between devices: 30.8 us -> 21.5 us  [local(): full = lax.all_to_all(spread, 'hx', 0, 0, tiled=True)]
    all_gather x1, blocking collectives: 17.6 us -> 13.3 us  [local(): lax.all_gather(win_lo.reshape(tokens, group * ROW_DEV), 'tok', axis=0, ti...]
    ppermute x2 -> x4, waiting for transfers between devices: 10.5 us -> 6.25 us  [the longest x1 4.21 us: local(): lax.ppermute(y_pay, HI + ('tok',), mirror)]
    all_to_all x0 -> x1, waiting for transfers between devices: none -> 4.2 us  [local(): got_y = lax.all_to_all(send_y, HI + ('lo',), 1, 1, tiled=True)]
    all_to_all x1, waiting for transfers between devices: 23.4 us -> 26.9 us  [local(): got = lax.all_to_all(send, ('mp', 'lo'), 0, 0, tiled=True)]
  transfers between devices with their start and end apart: 4 -> 7, of which waited for: 4 -> 5; matrix products, arithmetic and copies ran while one was open for 0% -> 1% of each run, Pallas kernels for 0% -> 0%
where the time goes in v20:
time: 127 us
  starting transfers between devices  59.6 us (47%)
  waiting for transfers between devices  42.3 us (33%)
  blocking collectives  13.3 us (10%)
  local copies, waits for them, and re-layouts  4.83 us (4%)
  other arithmetic  3.36 us (3%)
  matrix products  2.37 us (2%)
    all_to_all x1, waiting for transfers between devices, local(): got = lax.all_to_all(send, ('mp', 'lo'), 0, 0, tiled=True)  26.9 us
    all_to_all x1, starting transfers between devices, local(): full = lax.all_to_all(spread, 'hx', 0, 0, tiled=True)  21.5 us
    all_gather x1, blocking collectives, local(): lax.all_gather(win_lo.reshape(tokens, group * ROW_DEV), 'tok', axis=0, ti...  13.3 us
    all_to_all x1, starting transfers between devices, local(): got_y = lax.all_to_all(send_y, HI + ('lo',), 1, 1, tiled=True)  10.5 us
    ppermute x1, starting transfers between devices, local(): lax.ppermute(y_pay, HI + ('tok',), swap)  8.97 us
    ppermute x1, starting transfers between devices, local(): x_own = lax.ppermute(x_local, HI + ('tok',), swap)  8.17 us
    all_to_all x1, starting transfers between devices, local(): got = lax.all_to_all(send, ('mp', 'lo'), 0, 0, tiled=True)  6.57 us
    all_to_all x1, waiting for transfers between devices, local(): full = lax.all_to_all(spread, 'hx', 0, 0, tiled=True)  4.91 us
  transfers between devices with their start and end apart: 7, of which 5 were waited for; matrix products, arithmetic and copies ran while one was open for 1% of the time, Pallas kernels for 0%

profile of v20, /device:TPU:1, one launch (start us, length us, event | category | flops | bytes accessed | tf_op | source)
XLA Modules:
  0.0 126.5 jit_solution(685968807087958541)
XLA Ops:
  0.6 0.0 copy-start
  0.6 0.8 slice.44
  1.5 0.1 copy.60
  1.6 0.3 copy-done
  1.8 0.0 copy-start.1
  1.8 1.4 %reduce-precision_convert_fusion = (bf16[128,512]{1,0:T(8,128)(2,1)S(1)}, bf16[128,512]{1,0:T(8,128)(2,1)S(1)}) fusion(bf16[1,512,896]{2,1,0:T(8,128)(2,1)S(1)} %copy-done, bf16[1,128,896]{2,1,0:T(8,128)(2,1)} %param.2), kind=kOutput, calls=%fused_computation.16 | convolution fusion | flops 117702656 | bytes 1409024 | tf_op jit(solution)/shard_map/dot_general | solution.py:34
  3.3 0.1 copy.58
  3.4 0.1 copy.59
  3.6 0.9 pad_maximum_fusion
  4.4 10.5 %all-to-all-start = ((bf16[128,32,64]{0,2,1:T(8,128)(2,1)}), bf16[128,32,64]{0,2,1:T(8,128)(2,1)S(1)}, u32[]{:S(2)}, u32[]{:S(2)}) async-start(bf16[128,32,64]{0,2,1:T(8,128)(2,1)} %pad_maximum_fusion), calls=%async_computation | async-start | bytes 1048576 | tf_op jit(solution)/shard_map/all_to_all | solution.py:42
  14.9 0.0 copy-done.1
  15.0 8.2 %collective-permute-start = (bf16[128,896]{1,0:T(8,128)(2,1)S(1)}, bf16[128,896]{1,0:T(8,128)(2,1)S(1)}, u32[]{:S(2)}, u32[]{:S(2)}) collective-permute-start(bf16[128,896]{1,0:T(8,128)(2,1)S(1)} %bitcast.51), channel_id=1, source_target_pairs={{0,0},{1,32},{2,64},{3,96},{4,128},{5,160},{6,192},{7,224},{32,1},... | collective-permute-start | bytes 688136 | tf_op jit(solution)/shard_map/ppermute | solution.py:53
  23.1 1.9 %collective-permute-start.2 = (bf16[128,896]{1,0:T(8,128)(2,1)S(1)}, bf16[128,896]{1,0:T(8,128)(2,1)S(1)}, u32[]{:S(2)}, u32[]{:S(2)}) collective-permute-start(bf16[128,896]{1,0:T(8,128)(2,1)S(1)} %bitcast.52), channel_id=1, source_target_pairs={{0,32},{1,0},{2,96},{3,64},{4,160},{5,128},{6,224},{7,192},{32,33}... | collective-permute-start | bytes 688136 | tf_op jit(solution)/shard_map/ppermute | solution.py:54
  25.1 4.2 %all-to-all-done = bf16[128,32,64]{0,2,1:T(8,128)(2,1)S(1)} async-done(((bf16[128,32,64]{0,2,1:T(8,128)(2,1)}), bf16[128,32,64]{0,2,1:T(8,128)(2,1)S(1)}, u32[]{:S(2)}, u32[]{:S(2)}) %all-to-all-start) | async-done | bytes 524320 | tf_op jit(solution)/shard_map/all_to_all | solution.py:42
  29.3 9.0 %collective-permute-start.1 = (bf16[128,32]{0,1:T(8,128)(2,1)S(1)}, bf16[128,32]{0,1:T(8,128)(2,1)S(1)}, u32[]{:S(2)}, u32[]{:S(2)}) collective-permute-start(bf16[128,32]{0,1:T(8,128)(2,1)S(1)} %pad_maximum_fusion.5), channel_id=1, source_target_pairs={{0,0},{1,32},{2,64},{3,96},{4,128},{5,160},{6,192},{7,224},{32,1},... | collective-permute-start | bytes 24584 | tf_op jit(solution)/shard_map/ppermute | solution.py:56
  38.3 1.9 %collective-permute-start.3 = (bf16[128,32]{0,1:T(8,128)(2,1)S(1)}, bf16[128,32]{0,1:T(8,128)(2,1)S(1)}, u32[]{:S(2)}, u32[]{:S(2)}) collective-permute-start(bf16[128,32]{0,1:T(8,128)(2,1)S(1)} %pad_maximum_fusion.5), channel_id=1, source_target_pairs={{0,32},{1,0},{2,96},{3,64},{4,160},{5,128},{6,224},{7,192},{32,33}... | collective-permute-start | bytes 24584 | tf_op jit(solution)/shard_map/ppermute | solution.py:57
  40.2 2.0 %collective-permute-done.1 = bf16[128,32]{0,1:T(8,128)(2,1)S(1)} collective-permute-done((bf16[128,32]{0,1:T(8,128)(2,1)S(1)}, bf16[128,32]{0,1:T(8,128)(2,1)S(1)}, u32[]{:S(2)}, u32[]{:S(2)}) %collective-permute-start.1) | collective-permute-done | bytes 8224 | tf_op jit(solution)/shard_map/ppermute | solution.py:56
  42.3 0.1 copy.62
  42.4 4.2 %collective-permute-done.3 = bf16[128,32]{0,1:T(8,128)(2,1)S(1)} collective-permute-done((bf16[128,32]{0,1:T(8,128)(2,1)S(1)}, bf16[128,32]{0,1:T(8,128)(2,1)S(1)}, u32[]{:S(2)}, u32[]{:S(2)}) %collective-permute-start.3) | collective-permute-done | bytes 8224 | tf_op jit(solution)/shard_map/ppermute | solution.py:57
  46.6 0.1 copy.63
  46.7 0.0 collective-permute-done
  46.7 0.0 collective-permute-done.2
  46.7 0.1 broadcast_select_fusion.1
  46.9 0.1 pad_maximum_fusion.1
  46.9 0.3 copy.64
  47.2 1.5 %broadcast_in_dim.36 = bf16[4,2,128,928]{2,3,1,0:T(8,128)(2,1)} broadcast(bf16[2,128,928]{1,2,0:T(8,128)(2,1)S(1)} %copy.64), dimensions={1,2,3} | broadcast | bytes 2375680 | tf_op jit(solution)/shard_map/broadcast_in_dim | solution.py:60
  48.7 21.5 %all-to-all-start.1 = ((bf16[4,2,128,928]{2,3,1,0:T(8,128)(2,1)}), bf16[4,2,128,928]{2,3,1,0:T(8,128)(2,1)S(1)}, u32[]{:S(2)}, u32[]{:S(2)}) async-start(bf16[4,2,128,928]{2,3,1,0:T(8,128)(2,1)} %broadcast_in_dim.36), calls=%async_computation.1 | async-start | bytes 3801088 | tf_op jit(solution)/shard_map/all_to_all | solution.py:61
  70.3 13.3 %all_gather.3 = bf16[1024,128]{0,1:T(8,128)(2,1)S(1)} all-gather(bf16[128,128]{0,1:T(8,128)(2,1)S(1)} %bitcast.55), channel_id=1, replica_groups=mesh['mp'=2,'hx'=4,'hy'=2,'lo'=4,'tok'=8] {'tok'}, dimensions={0}, use_global_device_ids=true | all-gather | bytes 294912 | tf_op jit(solution)/shard_map/all_gather | solution.py:48
  83.6 0.2 copy.61
  83.7 0.1 multiply_reduce_fusion
  83.9 0.1 copy.68
  83.9 0.1 broadcast_select_fusion.2
  84.0 4.9 %all-to-all-done.1 = bf16[4,2,128,928]{2,3,1,0:T(8,128)(2,1)S(1)} async-done(((bf16[4,2,128,928]{2,3,1,0:T(8,128)(2,1)}), bf16[4,2,128,928]{2,3,1,0:T(8,128)(2,1)S(1)}, u32[]{:S(2)}, u32[]{:S(2)}) %all-to-all-start.1) | async-done | bytes 1900576 | tf_op jit(solution)/shard_map/all_to_all | solution.py:61
  88.9 0.2 fusion.5
  89.2 0.1 copy.67
  89.3 0.7 fusion.2
  90.0 1.1 maximum_maximum_fusion
  91.2 6.6 %all-to-all-start.2 = ((f32[8,32,976]{2,1,0:T(8,128)}), f32[8,32,976]{2,1,0:T(8,128)S(1)}, u32[]{:S(2)}, u32[]{:S(2)}) async-start(f32[8,32,976]{2,1,0:T(8,128)} %maximum_maximum_fusion), calls=%async_computation.2 | async-start | bytes 2097152 | tf_op jit(solution)/shard_map/all_to_all | solution.py:84
  97.7 26.9 %all-to-all-done.2 = f32[8,32,976]{2,1,0:T(8,128)S(1)} async-done(((f32[8,32,976]{2,1,0:T(8,128)}), f32[8,32,976]{2,1,0:T(8,128)S(1)}, u32[]{:S(2)}, u32[]{:S(2)}) %all-to-all-start.2) | async-done | bytes 999456 | tf_op jit(solution)/shard_map/all_to_all | solution.py:84
  124.7 0.1 reduce_sum.38
  124.8 0.1 slice_reduce_fusion
  124.9 0.1 fusion.8
  125.0 0.1 copy.70
  125.0 0.1 copy.71
  125.1 0.8 copy.76
  125.9 0.6 add.27
  (13 shorter events, 0.2 us)
Async XLA Ops:
  0.6 1.2 copy-start
  1.8 13.1 %copy-start.1 = (bf16[1,128,896]{2,1,0:T(8,128)(2,1)S(1)}, bf16[1,128,896]{2,1,0:T(8,128)(2,1)}, u32[]{:S(2)}) copy-start(bf16[1,128,896]{2,1,0:T(8,128)(2,1)} %param.2) | copy-start | bytes 688132
  4.4 24.8 %all-to-all-start = ((bf16[128,32,64]{0,2,1:T(8,128)(2,1)}), bf16[128,32,64]{0,2,1:T(8,128)(2,1)S(1)}, u32[]{:S(2)}, u32[]{:S(2)}) async-start(bf16[128,32,64]{0,2,1:T(8,128)(2,1)} %pad_maximum_fusion), calls=%async_computation | async-start | bytes 1048576 | tf_op jit(solution)/shard_map/all_to_all | solution.py:42
  15.0 31.8 %collective-permute-start = (bf16[128,896]{1,0:T(8,128)(2,1)S(1)}, bf16[128,896]{1,0:T(8,128)(2,1)S(1)}, u32[]{:S(2)}, u32[]{:S(2)}) collective-permute-start(bf16[128,896]{1,0:T(8,128)(2,1)S(1)} %bitcast.51), channel_id=1, source_target_pairs={{0,0},{1,32},{2,64},{3,96},{4,128},{5,160},{6,192},{7,224},{32,1},... | collective-permute-start | bytes 688136 | tf_op jit(solution)/shard_map/ppermute | solution.py:53
  23.1 23.6 %collective-permute-start.2 = (bf16[128,896]{1,0:T(8,128)(2,1)S(1)}, bf16[128,896]{1,0:T(8,128)(2,1)S(1)}, u32[]{:S(2)}, u32[]{:S(2)}) collective-permute-start(bf16[128,896]{1,0:T(8,128)(2,1)S(1)} %bitcast.52), channel_id=1, source_target_pairs={{0,32},{1,0},{2,96},{3,64},{4,160},{5,128},{6,224},{7,192},{32,33}... | collective-permute-start | bytes 688136 | tf_op jit(solution)/shard_map/ppermute | solution.py:54
  29.3 13.0 %collective-permute-start.1 = (bf16[128,32]{0,1:T(8,128)(2,1)S(1)}, bf16[128,32]{0,1:T(8,128)(2,1)S(1)}, u32[]{:S(2)}, u32[]{:S(2)}) collective-permute-start(bf16[128,32]{0,1:T(8,128)(2,1)S(1)} %pad_maximum_fusion.5), channel_id=1, source_target_pairs={{0,0},{1,32},{2,64},{3,96},{4,128},{5,160},{6,192},{7,224},{32,1},... | collective-permute-start | bytes 24584 | tf_op jit(solution)/shard_map/ppermute | solution.py:56
  38.3 8.3 %collective-permute-start.3 = (bf16[128,32]{0,1:T(8,128)(2,1)S(1)}, bf16[128,32]{0,1:T(8,128)(2,1)S(1)}, u32[]{:S(2)}, u32[]{:S(2)}) collective-permute-start(bf16[128,32]{0,1:T(8,128)(2,1)S(1)} %pad_maximum_fusion.5), channel_id=1, source_target_pairs={{0,32},{1,0},{2,96},{3,64},{4,160},{5,128},{6,224},{7,192},{32,33}... | collective-permute-start | bytes 24584 | tf_op jit(solution)/shard_map/ppermute | solution.py:57
  48.7 40.2 %all-to-all-start.1 = ((bf16[4,2,128,928]{2,3,1,0:T(8,128)(2,1)}), bf16[4,2,128,928]{2,3,1,0:T(8,128)(2,1)S(1)}, u32[]{:S(2)}, u32[]{:S(2)}) async-start(bf16[4,2,128,928]{2,3,1,0:T(8,128)(2,1)} %broadcast_in_dim.36), calls=%async_computation.1 | async-start | bytes 3801088 | tf_op jit(solution)/shard_map/all_to_all | solution.py:61
  91.2 33.5 %all-to-all-start.2 = ((f32[8,32,976]{2,1,0:T(8,128)}), f32[8,32,976]{2,1,0:T(8,128)S(1)}, u32[]{:S(2)}, u32[]{:S(2)}) async-start(f32[8,32,976]{2,1,0:T(8,128)} %maximum_maximum_fusion), calls=%async_computation.2 | async-start | bytes 2097152 | tf_op jit(solution)/shard_map/all_to_all | solution.py:84

commit v21 on v20

--- a/solution.py
+++ b/solution.py
@@ -55,6 +55,7 @@
     y_pay = jnp.concatenate([y_high, y_low], axis=1)
     own = jnp.concatenate([x_own, lax.ppermute(y_pay, HI + ("tok",), swap)], axis=1)
     other = jnp.concatenate([x_other, lax.ppermute(y_pay, HI + ("tok",), mirror)], axis=1)
+    own, other, wins = lax.optimization_barrier((own, other, wins))
     even_first = hy_index == 0
     pair = jnp.stack([jnp.where(even_first, own, other), jnp.where(even_first, other, own)])
     spread = jnp.broadcast_to(pair[None], (half_count,) + pair.shape)

time: 127 us -> 136 us (1.071)
  starting transfers between devices: 59.6 us -> 43.2 us
  blocking collectives: 13.3 us -> 27.2 us
  waiting for transfers between devices: 42.3 us -> 52.4 us
    all_to_all x1, waiting for transfers between devices: 4.91 us -> 23.4 us  [local(): full = lax.all_to_all(spread, 'hx', 0, 0, tiled=True)]
    all_to_all x1, starting transfers between devices: 21.5 us -> 6.16 us  [local(): full = lax.all_to_all(spread, 'hx', 0, 0, tiled=True)]
    all_gather x1, blocking collectives: 13.3 us -> 27.2 us  [local(): lax.all_gather(win_lo.reshape(tokens, group * ROW_DEV), 'tok', axis=0, ti...]
    ppermute x1, waiting for transfers between devices: 4.21 us -> 0.01 us  [local(): lax.ppermute(y_pay, HI + ('tok',), mirror)]
    all_to_all x1, waiting for transfers between devices: 26.9 us -> 24.8 us  [local(): got = lax.all_to_all(send, ('mp', 'lo'), 0, 0, tiled=True)]
    ppermute x1, waiting for transfers between devices: 2.04 us -> 0.01 us  [local(): lax.ppermute(y_pay, HI + ('tok',), swap)]
  transfers between devices with their start and end apart: 7 -> 7, of which waited for: 5 -> 3; matrix products, arithmetic and copies ran while one was open for 1% -> 1% of each run, Pallas kernels for 0% -> 0%
where the time goes in v21:
time: 136 us; the launch traced here: 134 us
  waiting for transfers between devices  52.4 us (39%)
  starting transfers between devices  43.2 us (32%)
  blocking collectives  27.2 us (20%)
  local copies, waits for them, and re-layouts  4.82 us (4%)
  other arithmetic  3.36 us (2%)
  matrix products  2.37 us (2%)
    all_gather x1, blocking collectives, local(): lax.all_gather(win_lo.reshape(tokens, group * ROW_DEV), 'tok', axis=0, ti...  27.2 us
    all_to_all x1, waiting for transfers between devices, local(): got = lax.all_to_all(send, ('mp', 'lo'), 0, 0, tiled=True)  24.8 us
    all_to_all x1, waiting for transfers between devices, local(): full = lax.all_to_all(spread, 'hx', 0, 0, tiled=True)  23.4 us
    all_to_all x1, starting transfers between devices, local(): got_y = lax.all_to_all(send_y, HI + ('lo',), 1, 1, tiled=True)  10.5 us
    ppermute x1, starting transfers between devices, local(): lax.ppermute(y_pay, HI + ('tok',), swap)  8.97 us
    ppermute x1, starting transfers between devices, local(): x_own = lax.ppermute(x_local, HI + ('tok',), swap)  8.17 us
    all_to_all x1, starting transfers between devices, local(): full = lax.all_to_all(spread, 'hx', 0, 0, tiled=True)  6.16 us
    all_to_all x1, starting transfers between devices, local(): got = lax.all_to_all(send, ('mp', 'lo'), 0, 0, tiled=True)  5.59 us
  transfers between devices with their start and end apart: 7, of which 3 were waited for; matrix products, arithmetic and copies ran while one was open for 1% of the time, Pallas kernels for 0%

profile of v21, /device:TPU:1, one launch (start us, length us, event | category | flops | bytes accessed | tf_op | source)
XLA Modules:
  0.0 134.3 jit_solution(16673648405426526968)
XLA Ops:
  0.6 0.0 copy-start
  0.6 0.8 slice.44
  1.5 0.1 copy.60
  1.6 0.3 copy-done
  1.8 0.0 copy-start.1
  1.8 1.4 %reduce-precision_convert_fusion = (bf16[128,512]{1,0:T(8,128)(2,1)S(1)}, bf16[128,512]{1,0:T(8,128)(2,1)S(1)}) fusion(bf16[1,512,896]{2,1,0:T(8,128)(2,1)S(1)} %copy-done, bf16[1,128,896]{2,1,0:T(8,128)(2,1)} %param.2), kind=kOutput, calls=%fused_computation.16 | convolution fusion | flops 117702656 | bytes 1409024 | tf_op jit(solution)/shard_map/dot_general | solution.py:34
  3.3 0.1 copy.58
  3.4 0.1 copy.59
  3.6 0.9 pad_maximum_fusion
  4.4 10.5 %all-to-all-start = ((bf16[128,32,64]{0,2,1:T(8,128)(2,1)}), bf16[128,32,64]{0,2,1:T(8,128)(2,1)S(1)}, u32[]{:S(2)}, u32[]{:S(2)}) async-start(bf16[128,32,64]{0,2,1:T(8,128)(2,1)} %pad_maximum_fusion), calls=%async_computation | async-start | bytes 1048576 | tf_op jit(solution)/shard_map/all_to_all | solution.py:42
  14.9 0.0 copy-done.1
  15.0 8.2 %collective-permute-start = (bf16[128,896]{1,0:T(8,128)(2,1)S(1)}, bf16[128,896]{1,0:T(8,128)(2,1)S(1)}, u32[]{:S(2)}, u32[]{:S(2)}) collective-permute-start(bf16[128,896]{1,0:T(8,128)(2,1)S(1)} %bitcast.51), channel_id=1, source_target_pairs={{0,0},{1,32},{2,64},{3,96},{4,128},{5,160},{6,192},{7,224},{32,1},... | collective-permute-start | bytes 688136 | tf_op jit(solution)/shard_map/ppermute | solution.py:53
  23.1 1.9 %collective-permute-start.2 = (bf16[128,896]{1,0:T(8,128)(2,1)S(1)}, bf16[128,896]{1,0:T(8,128)(2,1)S(1)}, u32[]{:S(2)}, u32[]{:S(2)}) collective-permute-start(bf16[128,896]{1,0:T(8,128)(2,1)S(1)} %bitcast.52), channel_id=1, source_target_pairs={{0,32},{1,0},{2,96},{3,64},{4,160},{5,128},{6,224},{7,192},{32,33}... | collective-permute-start | bytes 688136 | tf_op jit(solution)/shard_map/ppermute | solution.py:54
  25.1 4.2 %all-to-all-done = bf16[128,32,64]{0,2,1:T(8,128)(2,1)S(1)} async-done(((bf16[128,32,64]{0,2,1:T(8,128)(2,1)}), bf16[128,32,64]{0,2,1:T(8,128)(2,1)S(1)}, u32[]{:S(2)}, u32[]{:S(2)}) %all-to-all-start) | async-done | bytes 524320 | tf_op jit(solution)/shard_map/all_to_all | solution.py:42
  29.3 9.0 %collective-permute-start.1 = (bf16[128,32]{0,1:T(8,128)(2,1)S(1)}, bf16[128,32]{0,1:T(8,128)(2,1)S(1)}, u32[]{:S(2)}, u32[]{:S(2)}) collective-permute-start(bf16[128,32]{0,1:T(8,128)(2,1)S(1)} %pad_maximum_fusion.5), channel_id=1, source_target_pairs={{0,0},{1,32},{2,64},{3,96},{4,128},{5,160},{6,192},{7,224},{32,1},... | collective-permute-start | bytes 24584 | tf_op jit(solution)/shard_map/ppermute | solution.py:56
  38.3 1.9 %collective-permute-start.3 = (bf16[128,32]{0,1:T(8,128)(2,1)S(1)}, bf16[128,32]{0,1:T(8,128)(2,1)S(1)}, u32[]{:S(2)}, u32[]{:S(2)}) collective-permute-start(bf16[128,32]{0,1:T(8,128)(2,1)S(1)} %pad_maximum_fusion.5), channel_id=1, source_target_pairs={{0,32},{1,0},{2,96},{3,64},{4,160},{5,128},{6,224},{7,192},{32,33}... | collective-permute-start | bytes 24584 | tf_op jit(solution)/shard_map/ppermute | solution.py:57
  40.3 27.2 %all_gather.3 = bf16[1024,128]{0,1:T(8,128)(2,1)S(1)} all-gather(bf16[128,128]{0,1:T(8,128)(2,1)S(1)} %bitcast.53), channel_id=1, replica_groups=mesh['mp'=2,'hx'=4,'hy'=2,'lo'=4,'tok'=8] {'tok'}, dimensions={0}, use_global_device_ids=true | all-gather | bytes 294912 | tf_op jit(solution)/shard_map/all_gather | solution.py:48
  67.5 0.0 collective-permute-done.1
  67.5 0.1 copy.61
  67.6 0.0 collective-permute-done.3
  67.6 0.1 copy.62
  67.7 0.0 collective-permute-done
  67.8 0.0 collective-permute-done.2
  67.9 0.1 pad_maximum_fusion.1
  67.9 0.3 copy.63
  68.2 1.5 %broadcast_in_dim.36 = bf16[4,2,128,928]{2,3,1,0:T(8,128)(2,1)} broadcast(bf16[2,128,928]{1,2,0:T(8,128)(2,1)S(1)} %copy.63), dimensions={1,2,3} | broadcast | bytes 2375680 | tf_op jit(solution)/shard_map/broadcast_in_dim | solution.py:61
  69.7 6.2 %all-to-all-start.1 = ((bf16[4,2,128,928]{2,3,1,0:T(8,128)(2,1)}), bf16[4,2,128,928]{2,3,1,0:T(8,128)(2,1)S(1)}, u32[]{:S(2)}, u32[]{:S(2)}) async-start(bf16[4,2,128,928]{2,3,1,0:T(8,128)(2,1)} %broadcast_in_dim.36), calls=%async_computation.1 | async-start | bytes 3801088 | tf_op jit(solution)/shard_map/all_to_all | solution.py:62
  75.9 0.2 copy.75
  76.1 0.1 multiply_reduce_fusion
  76.2 0.1 copy.68
  76.3 0.1 broadcast_select_fusion
  76.4 23.4 %all-to-all-done.1 = bf16[4,2,128,928]{2,3,1,0:T(8,128)(2,1)S(1)} async-done(((bf16[4,2,128,928]{2,3,1,0:T(8,128)(2,1)}), bf16[4,2,128,928]{2,3,1,0:T(8,128)(2,1)S(1)}, u32[]{:S(2)}, u32[]{:S(2)}) %all-to-all-start.1) | async-done | bytes 1900576 | tf_op jit(solution)/shard_map/all_to_all | solution.py:62
  99.8 0.2 fusion.5
  100.0 0.1 copy.67
  100.1 0.7 fusion.2
  100.9 1.1 maximum_maximum_fusion
  102.0 5.6 %all-to-all-start.2 = ((f32[8,32,976]{2,1,0:T(8,128)}), f32[8,32,976]{2,1,0:T(8,128)S(1)}, u32[]{:S(2)}, u32[]{:S(2)}) async-start(f32[8,32,976]{2,1,0:T(8,128)} %maximum_maximum_fusion), calls=%async_computation.2 | async-start | bytes 2097152 | tf_op jit(solution)/shard_map/all_to_all | solution.py:85
  107.6 24.8 %all-to-all-done.2 = f32[8,32,976]{2,1,0:T(8,128)S(1)} async-done(((f32[8,32,976]{2,1,0:T(8,128)}), f32[8,32,976]{2,1,0:T(8,128)S(1)}, u32[]{:S(2)}, u32[]{:S(2)}) %all-to-all-start.2) | async-done | bytes 999456 | tf_op jit(solution)/shard_map/all_to_all | solution.py:85
  132.4 0.1 reduce_sum.38
  132.5 0.1 slice_reduce_fusion
  132.6 0.1 copy.70
  132.7 0.1 copy.71
  132.8 0.1 fusion.8
  132.8 0.8 copy.76
  133.6 0.6 add.27
  (16 shorter events, 0.3 us)
Async XLA Ops:
  0.6 1.2 copy-start
  1.8 13.1 %copy-start.1 = (bf16[1,128,896]{2,1,0:T(8,128)(2,1)S(1)}, bf16[1,128,896]{2,1,0:T(8,128)(2,1)}, u32[]{:S(2)}) copy-start(bf16[1,128,896]{2,1,0:T(8,128)(2,1)} %param.2) | copy-start | bytes 688132
  4.4 24.8 %all-to-all-start = ((bf16[128,32,64]{0,2,1:T(8,128)(2,1)}), bf16[128,32,64]{0,2,1:T(8,128)(2,1)S(1)}, u32[]{:S(2)}, u32[]{:S(2)}) async-start(bf16[128,32,64]{0,2,1:T(8,128)(2,1)} %pad_maximum_fusion), calls=%async_computation | async-start | bytes 1048576 | tf_op jit(solution)/shard_map/all_to_all | solution.py:42
  15.0 52.8 %collective-permute-start = (bf16[128,896]{1,0:T(8,128)(2,1)S(1)}, bf16[128,896]{1,0:T(8,128)(2,1)S(1)}, u32[]{:S(2)}, u32[]{:S(2)}) collective-permute-start(bf16[128,896]{1,0:T(8,128)(2,1)S(1)} %bitcast.51), channel_id=1, source_target_pairs={{0,0},{1,32},{2,64},{3,96},{4,128},{5,160},{6,192},{7,224},{32,1},... | collective-permute-start | bytes 688136 | tf_op jit(solution)/shard_map/ppermute | solution.py:53
  23.1 44.7 %collective-permute-start.2 = (bf16[128,896]{1,0:T(8,128)(2,1)S(1)}, bf16[128,896]{1,0:T(8,128)(2,1)S(1)}, u32[]{:S(2)}, u32[]{:S(2)}) collective-permute-start(bf16[128,896]{1,0:T(8,128)(2,1)S(1)} %bitcast.52), channel_id=1, source_target_pairs={{0,32},{1,0},{2,96},{3,64},{4,160},{5,128},{6,224},{7,192},{32,33}... | collective-permute-start | bytes 688136 | tf_op jit(solution)/shard_map/ppermute | solution.py:54
  29.3 38.2 %collective-permute-start.1 = (bf16[128,32]{0,1:T(8,128)(2,1)S(1)}, bf16[128,32]{0,1:T(8,128)(2,1)S(1)}, u32[]{:S(2)}, u32[]{:S(2)}) collective-permute-start(bf16[128,32]{0,1:T(8,128)(2,1)S(1)} %pad_maximum_fusion.5), channel_id=1, source_target_pairs={{0,0},{1,32},{2,64},{3,96},{4,128},{5,160},{6,192},{7,224},{32,1},... | collective-permute-start | bytes 24584 | tf_op jit(solution)/shard_map/ppermute | solution.py:56
  38.3 29.3 %collective-permute-start.3 = (bf16[128,32]{0,1:T(8,128)(2,1)S(1)}, bf16[128,32]{0,1:T(8,128)(2,1)S(1)}, u32[]{:S(2)}, u32[]{:S(2)}) collective-permute-start(bf16[128,32]{0,1:T(8,128)(2,1)S(1)} %pad_maximum_fusion.5), channel_id=1, source_target_pairs={{0,32},{1,0},{2,96},{3,64},{4,160},{5,128},{6,224},{7,192},{32,33}... | collective-permute-start | bytes 24584 | tf_op jit(solution)/shard_map/ppermute | solution.py:57
  69.7 30.1 %all-to-all-start.1 = ((bf16[4,2,128,928]{2,3,1,0:T(8,128)(2,1)}), bf16[4,2,128,928]{2,3,1,0:T(8,128)(2,1)S(1)}, u32[]{:S(2)}, u32[]{:S(2)}) async-start(bf16[4,2,128,928]{2,3,1,0:T(8,128)(2,1)} %broadcast_in_dim.36), calls=%async_computation.1 | async-start | bytes 3801088 | tf_op jit(solution)/shard_map/all_to_all | solution.py:62
  102.0 30.4 %all-to-all-start.2 = ((f32[8,32,976]{2,1,0:T(8,128)}), f32[8,32,976]{2,1,0:T(8,128)S(1)}, u32[]{:S(2)}, u32[]{:S(2)}) async-start(f32[8,32,976]{2,1,0:T(8,128)} %maximum_maximum_fusion), calls=%async_computation.2 | async-start | bytes 2097152 | tf_op jit(solution)/shard_map/all_to_all | solution.py:85

commit v22 on v20

--- a/solution.py
+++ b/solution.py
@@ -31,27 +31,29 @@
 
     swap = [(h * tok_count + t, t * tok_count + h) for h in range(hi_count) for t in range(tok_count)]
 
+    mirror = [(h * tok_count + t, (t ^ 1) * tok_count + h) for h in range(hi_count) for t in range(tok_count)]
+    x_own = lax.ppermute(x_local, HI + ("tok",), swap)
+    x_other = lax.ppermute(x_local, HI + ("tok",), mirror)
+
+    win_lo = lax.all_gather(x_local[:, :ROW_DEV], "lo", axis=1, tiled=True)
+    wins = lax.all_gather(win_lo, "tok", axis=0, tiled=True)
+
     y_part = lax.dot_general(
         x_local, w_local, (((1,), (1,)), ((), ())), preferred_element_type=jnp.float32
     )
     y_part_round = lax.reduce_precision(y_part, exponent_bits=8, mantissa_bits=7)
     y_part_high = y_part_round.astype(jnp.bfloat16).reshape(tokens, blk_count, col_group)
     y_part_low = (y_part - y_part_round).astype(jnp.bfloat16).reshape(tokens, blk_count, col_group)
-    win_spread = jnp.broadcast_to(x_local[:, None, :ROW_DEV], (tokens, blk_count, ROW_DEV))
-    send_y = jnp.concatenate([y_part_high, y_part_low, win_spread], axis=2)
+    send_y = jnp.concatenate([y_part_high, y_part_low], axis=2)
     got_y = lax.all_to_all(send_y, HI + ("lo",), 1, 1, tiled=True)
+    got_y, wins = lax.optimization_barrier((got_y, wins))
     y_mine = jnp.sum(
-        got_y[:, :, :col_group].astype(jnp.float32) + got_y[:, :, col_group:2 * col_group].astype(jnp.float32),
+        got_y[:, :, :col_group].astype(jnp.float32) + got_y[:, :, col_group:].astype(jnp.float32),
         axis=1,
     )
-    win_lo = lax.dynamic_slice_in_dim(got_y[:, :, 2 * col_group:], hi_index * group, group, 1)
-    wins = lax.all_gather(win_lo.reshape(tokens, group * ROW_DEV), "tok", axis=0, tiled=True)
     y_round = lax.reduce_precision(y_mine, exponent_bits=8, mantissa_bits=7)
     y_high = y_round.astype(jnp.bfloat16)
     y_low = (y_mine - y_round).astype(jnp.bfloat16)
-    mirror = [(h * tok_count + t, (t ^ 1) * tok_count + h) for h in range(hi_count) for t in range(tok_count)]
-    x_own = lax.ppermute(x_local, HI + ("tok",), swap)
-    x_other = lax.ppermute(x_local, HI + ("tok",), mirror)
     y_pay = jnp.concatenate([y_high, y_low], axis=1)
     own = jnp.concatenate([x_own, lax.ppermute(y_pay, HI + ("tok",), swap)], axis=1)
     other = jnp.concatenate([x_other, lax.ppermute(y_pay, HI + ("tok",), mirror)], axis=1)

time: 127 us -> 153 us (1.20)
  blocking collectives: 13.3 us -> 42.6 us
  starting transfers between devices: 59.6 us -> 44.5 us
  waiting for transfers between devices: 42.3 us -> 54.7 us
    all_gather x1 -> x2, blocking collectives: 13.3 us -> 42.6 us  [the longest x1 30.1 us: local(): wins = lax.all_gather(win_lo, 'tok', axis=0, tiled=True)]
    all_to_all x1, waiting for transfers between devices: 4.91 us -> 23.4 us  [local(): full = lax.all_to_all(spread, 'hx', 0, 0, tiled=True)]
    ppermute x1, starting transfers between devices: 8.97 us -> 1.92 us  [local(): lax.ppermute(y_pay, HI + ('tok',), swap)]
    all_to_all x1, starting transfers between devices: 21.5 us -> 15.4 us  [local(): full = lax.all_to_all(spread, 'hx', 0, 0, tiled=True)]
    all_to_all x1, waiting for transfers between devices: 4.2 us -> 0.01 us  [local(): got_y = lax.all_to_all(send_y, HI + ('lo',), 1, 1, tiled=True)]
    ppermute x1, waiting for transfers between devices: 2.04 us -> 4.99 us  [local(): lax.ppermute(y_pay, HI + ('tok',), swap)]
    ppermute x1, waiting for transfers between devices: 4.21 us -> 1.35 us  [local(): lax.ppermute(y_pay, HI + ('tok',), mirror)]
    all_to_all x1, waiting for transfers between devices: 26.9 us -> 25 us  [local(): got = lax.all_to_all(send, ('mp', 'lo'), 0, 0, tiled=True)]
  transfers between devices with their start and end apart: 7 -> 7, of which waited for: 5 -> 4; matrix products, arithmetic and copies ran while one was open for 1% -> 0% of each run, Pallas kernels for 0% -> 0%
where the time goes in v22:
time: 153 us
  waiting for transfers between devices  54.7 us (36%)
  starting transfers between devices  44.5 us (29%)
  blocking collectives  42.6 us (28%)
  local copies, waits for them, and re-layouts  4.4 us (3%)
  other arithmetic  3.23 us (2%)
  matrix products  2.3 us (2%)
    all_gather x1, blocking collectives, local(): wins = lax.all_gather(win_lo, 'tok', axis=0, tiled=True)  30.1 us
    all_to_all x1, waiting for transfers between devices, local(): got = lax.all_to_all(send, ('mp', 'lo'), 0, 0, tiled=True)  25 us
    all_to_all x1, waiting for transfers between devices, local(): full = lax.all_to_all(spread, 'hx', 0, 0, tiled=True)  23.4 us
    all_to_all x1, starting transfers between devices, local(): full = lax.all_to_all(spread, 'hx', 0, 0, tiled=True)  15.4 us
    all_gather x1, blocking collectives, local(): win_lo = lax.all_gather(x_local[:, :ROW_DEV], 'lo', axis=1, tiled=True)  12.5 us
    all_to_all x1, starting transfers between devices, local(): got_y = lax.all_to_all(send_y, HI + ('lo',), 1, 1, tiled=True)  10.5 us
    ppermute x1, starting transfers between devices, local(): x_own = lax.ppermute(x_local, HI + ('tok',), swap)  8.17 us
    ppermute x1, waiting for transfers between devices, local(): lax.ppermute(y_pay, HI + ('tok',), swap)  4.99 us
  transfers between devices with their start and end apart: 7, of which 4 were waited for; matrix products, arithmetic and copies ran while one was open for 0% of the time, Pallas kernels for 0%

profile of v22, /device:TPU:1, one launch (start us, length us, event | category | flops | bytes accessed | tf_op | source)
XLA Modules:
  0.0 152.5 jit_solution(3683078693824957340)
XLA Ops:
  0.6 0.0 copy-start
  0.6 0.0 copy-start.1
  0.7 1.2 copy-done
  1.8 1.4 reduce-precision_convert_fusion
  3.2 0.1 copy.48
  3.3 0.1 copy.49
  3.4 0.7 pad_maximum_fusion.2
  4.2 10.5 %all-to-all-start = ((bf16[128,32,32]{0,2,1:T(8,128)(2,1)}), bf16[128,32,32]{0,2,1:T(8,128)(2,1)S(1)}, u32[]{:S(2)}, u32[]{:S(2)}) async-start(bf16[128,32,32]{0,2,1:T(8,128)(2,1)} %pad_maximum_fusion.2), calls=%async_computation | async-start | bytes 524288 | tf_op jit(solution)/shard_map/all_to_all | solution.py:48
  14.7 0.0 copy-done.1
  14.7 0.2 copy.47
  14.9 8.2 %collective-permute-start = (bf16[128,896]{0,1:T(8,128)(2,1)S(1)}, bf16[128,896]{0,1:T(8,128)(2,1)S(1)}, u32[]{:S(2)}, u32[]{:S(2)}) collective-permute-start(bf16[128,896]{0,1:T(8,128)(2,1)S(1)} %bitcast.50), channel_id=1, source_target_pairs={{0,0},{1,32},{2,64},{3,96},{4,128},{5,160},{6,192},{7,224},{32,1},... | collective-permute-start | bytes 688136 | tf_op jit(solution)/shard_map/ppermute | solution.py:35
  23.0 1.9 %collective-permute-start.2 = (bf16[128,896]{0,1:T(8,128)(2,1)S(1)}, bf16[128,896]{0,1:T(8,128)(2,1)S(1)}, u32[]{:S(2)}, u32[]{:S(2)}) collective-permute-start(bf16[128,896]{0,1:T(8,128)(2,1)S(1)} %bitcast.51), channel_id=1, source_target_pairs={{0,32},{1,0},{2,96},{3,64},{4,160},{5,128},{6,224},{7,192},{32,33}... | collective-permute-start | bytes 688136 | tf_op jit(solution)/shard_map/ppermute | solution.py:36
  25.0 12.5 %all_gather.6 = bf16[128,128]{0,1:T(8,128)(2,1)S(1)} all-gather(bf16[128,32]{0,1:T(8,128)(2,1)S(1)} %slice.40), channel_id=1, replica_groups=mesh['mp'=2,'hx'=4,'hy'=2,'lo'=4,'tok'=8] {'lo'}, dimensions={1}, use_global_device_ids=true | all-gather | bytes 40960 | tf_op jit(solution)/shard_map/all_gather | solution.py:38
  37.4 30.1 %all_gather.7 = bf16[1024,128]{0,1:T(8,128)(2,1)S(1)} all-gather(bf16[128,128]{0,1:T(8,128)(2,1)S(1)} %all_gather.6), channel_id=1, replica_groups=mesh['mp'=2,'hx'=4,'hy'=2,'lo'=4,'tok'=8] {'tok'}, dimensions={0}, use_global_device_ids=true | all-gather | bytes 294912 | tf_op jit(solution)/shard_map/all_gather | solution.py:39
  67.5 0.0 all-to-all-done
  67.6 1.9 %collective-permute-start.1 = (bf16[128,32]{0,1:T(8,128)(2,1)S(1)}, bf16[128,32]{0,1:T(8,128)(2,1)S(1)}, u32[]{:S(2)}, u32[]{:S(2)}) collective-permute-start(bf16[128,32]{0,1:T(8,128)(2,1)S(1)} %pad_maximum_fusion.5), channel_id=1, source_target_pairs={{0,0},{1,32},{2,64},{3,96},{4,128},{5,160},{6,192},{7,224},{32,1},... | collective-permute-start | bytes 24584 | tf_op jit(solution)/shard_map/ppermute | solution.py:58
  69.5 1.9 %collective-permute-start.3 = (bf16[128,32]{0,1:T(8,128)(2,1)S(1)}, bf16[128,32]{0,1:T(8,128)(2,1)S(1)}, u32[]{:S(2)}, u32[]{:S(2)}) collective-permute-start(bf16[128,32]{0,1:T(8,128)(2,1)S(1)} %pad_maximum_fusion.5), channel_id=1, source_target_pairs={{0,32},{1,0},{2,96},{3,64},{4,160},{5,128},{6,224},{7,192},{32,33}... | collective-permute-start | bytes 24584 | tf_op jit(solution)/shard_map/ppermute | solution.py:59
  71.5 0.0 collective-permute-done
  71.5 0.0 collective-permute-done.2
  71.5 5.0 %collective-permute-done.1 = bf16[128,32]{0,1:T(8,128)(2,1)S(1)} collective-permute-done((bf16[128,32]{0,1:T(8,128)(2,1)S(1)}, bf16[128,32]{0,1:T(8,128)(2,1)S(1)}, u32[]{:S(2)}, u32[]{:S(2)}) %collective-permute-start.1) | collective-permute-done | bytes 8224 | tf_op jit(solution)/shard_map/ppermute | solution.py:58
  76.5 1.4 collective-permute-done.3
  77.9 0.1 broadcast_select_fusion.1
  78.0 1.5 broadcast_in_dim.29
  79.5 15.4 %all-to-all-start.1 = ((bf16[4,2,128,928]{2,3,1,0:T(8,128)(2,1)}), bf16[4,2,128,928]{2,3,1,0:T(8,128)(2,1)S(1)}, u32[]{:S(2)}, u32[]{:S(2)}) async-start(bf16[4,2,128,928]{2,3,1,0:T(8,128)(2,1)} %broadcast_in_dim.29), calls=%async_computation.1 | async-start | bytes 3801088 | tf_op jit(solution)/shard_map/all_to_all | solution.py:63
  94.9 0.2 copy.61
  95.1 0.1 multiply_reduce_fusion
  95.2 0.1 copy.54
  95.3 0.1 broadcast_select_fusion.2
  95.4 23.4 %all-to-all-done.1 = bf16[4,2,128,928]{2,3,1,0:T(8,128)(2,1)S(1)} async-done(((bf16[4,2,128,928]{2,3,1,0:T(8,128)(2,1)}), bf16[4,2,128,928]{2,3,1,0:T(8,128)(2,1)S(1)}, u32[]{:S(2)}, u32[]{:S(2)}) %all-to-all-start.1) | async-done | bytes 1900576 | tf_op jit(solution)/shard_map/all_to_all | solution.py:63
  118.7 0.2 fusion.5
  118.9 0.1 copy.53
  119.1 0.7 fusion.2
  119.8 1.1 maximum_maximum_fusion
  121.0 4.7 %all-to-all-start.2 = ((f32[8,32,976]{2,1,0:T(8,128)}), f32[8,32,976]{2,1,0:T(8,128)S(1)}, u32[]{:S(2)}, u32[]{:S(2)}) async-start(f32[8,32,976]{2,1,0:T(8,128)} %maximum_maximum_fusion), calls=%async_computation.2 | async-start | bytes 2097152 | tf_op jit(solution)/shard_map/all_to_all | solution.py:86
  125.7 25.0 %all-to-all-done.2 = f32[8,32,976]{2,1,0:T(8,128)S(1)} async-done(((f32[8,32,976]{2,1,0:T(8,128)}), f32[8,32,976]{2,1,0:T(8,128)S(1)}, u32[]{:S(2)}, u32[]{:S(2)}) %all-to-all-start.2) | async-done | bytes 999456 | tf_op jit(solution)/shard_map/all_to_all | solution.py:86
  150.7 0.1 reduce_sum.38
  150.8 0.1 slice_reduce_fusion
  150.9 0.1 copy.56
  151.0 0.1 copy.57
  151.0 0.1 fusion.8
  151.1 0.8 copy.62
  151.9 0.6 add.23
  (12 shorter events, 0.2 us)
Async XLA Ops:
  0.6 1.2 copy-start
  0.6 14.0 %copy-start.1 = (bf16[1,128,896]{2,1,0:T(8,128)(2,1)S(1)}, bf16[1,128,896]{2,1,0:T(8,128)(2,1)}, u32[]{:S(2)}) copy-start(bf16[1,128,896]{2,1,0:T(8,128)(2,1)} %param.2) | copy-start | bytes 688132
  4.2 63.4 %all-to-all-start = ((bf16[128,32,32]{0,2,1:T(8,128)(2,1)}), bf16[128,32,32]{0,2,1:T(8,128)(2,1)S(1)}, u32[]{:S(2)}, u32[]{:S(2)}) async-start(bf16[128,32,32]{0,2,1:T(8,128)(2,1)} %pad_maximum_fusion.2), calls=%async_computation | async-start | bytes 524288 | tf_op jit(solution)/shard_map/all_to_all | solution.py:48
  14.9 56.6 %collective-permute-start = (bf16[128,896]{0,1:T(8,128)(2,1)S(1)}, bf16[128,896]{0,1:T(8,128)(2,1)S(1)}, u32[]{:S(2)}, u32[]{:S(2)}) collective-permute-start(bf16[128,896]{0,1:T(8,128)(2,1)S(1)} %bitcast.50), channel_id=1, source_target_pairs={{0,0},{1,32},{2,64},{3,96},{4,128},{5,160},{6,192},{7,224},{32,1},... | collective-permute-start | bytes 688136 | tf_op jit(solution)/shard_map/ppermute | solution.py:35
  23.0 48.5 %collective-permute-start.2 = (bf16[128,896]{0,1:T(8,128)(2,1)S(1)}, bf16[128,896]{0,1:T(8,128)(2,1)S(1)}, u32[]{:S(2)}, u32[]{:S(2)}) collective-permute-start(bf16[128,896]{0,1:T(8,128)(2,1)S(1)} %bitcast.51), channel_id=1, source_target_pairs={{0,32},{1,0},{2,96},{3,64},{4,160},{5,128},{6,224},{7,192},{32,33}... | collective-permute-start | bytes 688136 | tf_op jit(solution)/shard_map/ppermute | solution.py:36
  67.6 8.9 %collective-permute-start.1 = (bf16[128,32]{0,1:T(8,128)(2,1)S(1)}, bf16[128,32]{0,1:T(8,128)(2,1)S(1)}, u32[]{:S(2)}, u32[]{:S(2)}) collective-permute-start(bf16[128,32]{0,1:T(8,128)(2,1)S(1)} %pad_maximum_fusion.5), channel_id=1, source_target_pairs={{0,0},{1,32},{2,64},{3,96},{4,128},{5,160},{6,192},{7,224},{32,1},... | collective-permute-start | bytes 24584 | tf_op jit(solution)/shard_map/ppermute | solution.py:58
  69.5 8.3 %collective-permute-start.3 = (bf16[128,32]{0,1:T(8,128)(2,1)S(1)}, bf16[128,32]{0,1:T(8,128)(2,1)S(1)}, u32[]{:S(2)}, u32[]{:S(2)}) collective-permute-start(bf16[128,32]{0,1:T(8,128)(2,1)S(1)} %pad_maximum_fusion.5), channel_id=1, source_target_pairs={{0,32},{1,0},{2,96},{3,64},{4,160},{5,128},{6,224},{7,192},{32,33}... | collective-permute-start | bytes 24584 | tf_op jit(solution)/shard_map/ppermute | solution.py:59
  79.5 39.2 %all-to-all-start.1 = ((bf16[4,2,128,928]{2,3,1,0:T(8,128)(2,1)}), bf16[4,2,128,928]{2,3,1,0:T(8,128)(2,1)S(1)}, u32[]{:S(2)}, u32[]{:S(2)}) async-start(bf16[4,2,128,928]{2,3,1,0:T(8,128)(2,1)} %broadcast_in_dim.29), calls=%async_computation.1 | async-start | bytes 3801088 | tf_op jit(solution)/shard_map/all_to_all | solution.py:63
  121.0 29.7 %all-to-all-start.2 = ((f32[8,32,976]{2,1,0:T(8,128)}), f32[8,32,976]{2,1,0:T(8,128)S(1)}, u32[]{:S(2)}, u32[]{:S(2)}) async-start(f32[8,32,976]{2,1,0:T(8,128)} %maximum_maximum_fusion), calls=%async_computation.2 | async-start | bytes 2097152 | tf_op jit(solution)/shard_map/all_to_all | solution.py:86

commit v23 on v20

--- a/solution.py
+++ b/solution.py
@@ -34,27 +34,39 @@
     y_part = lax.dot_general(
         x_local, w_local, (((1,), (1,)), ((), ())), preferred_element_type=jnp.float32
     )
-    y_part_round = lax.reduce_precision(y_part, exponent_bits=8, mantissa_bits=7)
-    y_part_high = y_part_round.astype(jnp.bfloat16).reshape(tokens, blk_count, col_group)
-    y_part_low = (y_part - y_part_round).astype(jnp.bfloat16).reshape(tokens, blk_count, col_group)
-    win_spread = jnp.broadcast_to(x_local[:, None, :ROW_DEV], (tokens, blk_count, ROW_DEV))
-    send_y = jnp.concatenate([y_part_high, y_part_low, win_spread], axis=2)
-    got_y = lax.all_to_all(send_y, HI + ("lo",), 1, 1, tiled=True)
-    y_mine = jnp.sum(
-        got_y[:, :, :col_group].astype(jnp.float32) + got_y[:, :, col_group:2 * col_group].astype(jnp.float32),
-        axis=1,
-    )
-    win_lo = lax.dynamic_slice_in_dim(got_y[:, :, 2 * col_group:], hi_index * group, group, 1)
+    y_part = y_part.reshape(tokens, half_count, 2, group, col_group)
+    y_near = jnp.take(y_part, hy_index, axis=2).reshape(tokens, half_count * group, col_group)
+    y_far = jnp.take(y_part, 1 - hy_index, axis=2).reshape(tokens, half_count * group, col_group)
+
+    def halves(v):
+        r = lax.reduce_precision(v, exponent_bits=8, mantissa_bits=7)
+        return [r.astype(jnp.bfloat16), (v - r).astype(jnp.bfloat16)]
+
+    win_spread = jnp.broadcast_to(x_local[:, None, :ROW_DEV], (tokens, half_count * group, ROW_DEV))
+    send_y = jnp.concatenate(halves(y_near) + halves(y_far) + [win_spread], axis=2)
+    got_y = lax.all_to_all(send_y, ("hx", "lo"), 1, 1, tiled=True)
+    got_f = got_y[:, :, :4 * col_group].astype(jnp.float32)
+    y_near_sum = jnp.sum(got_f[:, :, :col_group] + got_f[:, :, col_group:2 * col_group], axis=1)
+    y_far_sum = jnp.sum(got_f[:, :, 2 * col_group:3 * col_group] + got_f[:, :, 3 * col_group:], axis=1)
+    win_lo = lax.dynamic_slice_in_dim(got_y[:, :, 4 * col_group:], lax.axis_index("hx") * group, group, 1)
     wins = lax.all_gather(win_lo.reshape(tokens, group * ROW_DEV), "tok", axis=0, tiled=True)
-    y_round = lax.reduce_precision(y_mine, exponent_bits=8, mantissa_bits=7)
-    y_high = y_round.astype(jnp.bfloat16)
-    y_low = (y_mine - y_round).astype(jnp.bfloat16)
+
     mirror = [(h * tok_count + t, (t ^ 1) * tok_count + h) for h in range(hi_count) for t in range(tok_count)]
     x_own = lax.ppermute(x_local, HI + ("tok",), swap)
     x_other = lax.ppermute(x_local, HI + ("tok",), mirror)
-    y_pay = jnp.concatenate([y_high, y_low], axis=1)
-    own = jnp.concatenate([x_own, lax.ppermute(y_pay, HI + ("tok",), swap)], axis=1)
-    other = jnp.concatenate([x_other, lax.ppermute(y_pay, HI + ("tok",), mirror)], axis=1)
+    swap_far = [(h * tok_count + t, t * tok_count + (h ^ 1)) for h in range(hi_count) for t in range(tok_count)]
+    mirror_far = [(h * tok_count + t, (t ^ 1) * tok_count + (h ^ 1)) for h in range(hi_count) for t in range(tok_count)]
+    near_pay = jnp.concatenate(halves(y_near_sum), axis=1)
+    far_pay = jnp.concatenate(halves(y_far_sum), axis=1)
+
+    def whole_y(near, far):
+        parts = [near[:, :col_group], near[:, col_group:], far[:, :col_group], far[:, col_group:]]
+        return jnp.concatenate(halves(sum(p.astype(jnp.float32) for p in parts)), axis=1)
+
+    y_own = whole_y(lax.ppermute(near_pay, HI + ("tok",), swap), lax.ppermute(far_pay, HI + ("tok",), swap_far))
+    y_other = whole_y(lax.ppermute(near_pay, HI + ("tok",), mirror), lax.ppermute(far_pay, HI + ("tok",), mirror_far))
+    own = jnp.concatenate([x_own, y_own], axis=1)
+    other = jnp.concatenate([x_other, y_other], axis=1)
     even_first = hy_index == 0
     pair = jnp.stack([jnp.where(even_first, own, other), jnp.where(even_first, other, own)])
     spread = jnp.broadcast_to(pair[None], (half_count,) + pair.shape)

time: 127 us -> 141 us (1.11)
  the two profiles are of different devices: /device:TPU:1 before, /device:TPU:256 now
where the time goes in v23:
time: 141 us; the launch traced here: 140 us
  waiting for transfers between devices  47.9 us (34%)
  starting transfers between devices  45.3 us (32%)
  blocking collectives  36.3 us (26%)
  local copies, waits for them, and re-layouts  4.89 us (3%)
  other arithmetic  2.66 us (2%)
  matrix products  2.27 us (2%)
    all_to_all x1, waiting for transfers between devices, local(): got = lax.all_to_all(send, ('mp', 'lo'), 0, 0, tiled=True)  27.5 us
    all_to_all x1, blocking collectives, local(): got_y = lax.all_to_all(send_y, ('hx', 'lo'), 1, 1, tiled=True)  20.9 us
    ppermute x1, starting transfers between devices, local(): x_other = lax.ppermute(x_local, HI + ('tok',), mirror)  19.6 us
    all_gather x1, blocking collectives, local(): lax.all_gather(win_lo.reshape(tokens, group * ROW_DEV), 'tok', axis=0, ti...  15.4 us
    ppermute x1, waiting for transfers between devices, local(): lax.ppermute(far_pay, HI + ('tok',), mirror_far)  11.4 us
    all_to_all x1, waiting for transfers between devices, local(): full = lax.all_to_all(spread, 'hx', 0, 0, tiled=True)  8.93 us
    ppermute x1, starting transfers between devices, local(): lax.ppermute(near_pay, HI + ('tok',), swap)  8.6 us
    all_to_all x1, starting transfers between devices, local(): full = lax.all_to_all(spread, 'hx', 0, 0, tiled=True)  3.59 us
  transfers between devices with their start and end apart: 8, of which 3 were waited for; matrix products, arithmetic and copies ran while one was open for 1% of the time, Pallas kernels for 0%

profile of v23, /device:TPU:256, one launch (start us, length us, event | category | flops | bytes accessed | tf_op | source)
XLA Modules:
  0.0 140.3 jit_solution(1139294769510984908)
XLA Ops:
  0.6 0.0 copy-start
  0.7 0.8 slice.101
  1.5 0.1 copy.60
  1.6 0.3 copy-done
  1.8 1.3 fusion.8
  3.2 0.0 copy-start.1
  3.4 20.9 %all_to_all.15 = bf16[128,16,96]{0,2,1:T(8,128)(2,1)S(1)} all-to-all(bf16[128,16,96]{0,2,1:T(8,128)(2,1)S(1)} %broadcast_dynamic-update-slice_fusion), channel_id=1, replica_groups=mesh['mp'=2,'hx'=4,'hy'=2,'lo'=4,'tok'=8] {'hx','lo'}, dimensions={1} | all-to-all | bytes 786432 | tf_op jit(solution)/shard_map/all_to_all | solution.py:47
  24.5 1.9 %collective-permute-start.2 = (bf16[128,32]{0,1:T(8,128)(2,1)S(1)}, bf16[128,32]{0,1:T(8,128)(2,1)S(1)}, u32[]{:S(2)}, u32[]{:S(2)}) collective-permute-start(bf16[128,32]{0,1:T(8,128)(2,1)S(1)} %pad_maximum_fusion.5), channel_id=1, source_target_pairs={{0,1},{1,33},{2,65},{3,97},{4,129},{5,161},{6,193},{7,225},{32,0},... | collective-permute-start | bytes 24584 | tf_op jit(solution)/shard_map/ppermute | solution.py:66
  26.4 8.6 %collective-permute-start.1 = (bf16[128,32]{0,1:T(8,128)(2,1)S(1)}, bf16[128,32]{0,1:T(8,128)(2,1)S(1)}, u32[]{:S(2)}, u32[]{:S(2)}) collective-permute-start(bf16[128,32]{0,1:T(8,128)(2,1)S(1)} %pad_maximum_fusion.4), channel_id=1, source_target_pairs={{0,0},{1,32},{2,64},{3,96},{4,128},{5,160},{6,192},{7,224},{32,1},... | collective-permute-start | bytes 24584 | tf_op jit(solution)/shard_map/ppermute | solution.py:66
  35.0 0.0 copy-done.1
  35.0 3.5 %collective-permute-start = (bf16[128,896]{1,0:T(8,128)(2,1)S(1)}, bf16[128,896]{1,0:T(8,128)(2,1)S(1)}, u32[]{:S(2)}, u32[]{:S(2)}) collective-permute-start(bf16[128,896]{1,0:T(8,128)(2,1)S(1)} %bitcast.63), channel_id=1, source_target_pairs={{0,0},{1,32},{2,64},{3,96},{4,128},{5,160},{6,192},{7,224},{32,1},... | collective-permute-start | bytes 688136 | tf_op jit(solution)/shard_map/ppermute | solution.py:55
  38.6 19.6 %collective-permute-start.3 = (bf16[128,896]{1,0:T(8,128)(2,1)S(1)}, bf16[128,896]{1,0:T(8,128)(2,1)S(1)}, u32[]{:S(2)}, u32[]{:S(2)}) collective-permute-start(bf16[128,896]{1,0:T(8,128)(2,1)S(1)} %bitcast.64), channel_id=1, source_target_pairs={{0,32},{1,0},{2,96},{3,64},{4,160},{5,128},{6,224},{7,192},{32,33}... | collective-permute-start | bytes 688136 | tf_op jit(solution)/shard_map/ppermute | solution.py:56
  58.2 1.9 %collective-permute-start.5 = (bf16[128,32]{0,1:T(8,128)(2,1)S(1)}, bf16[128,32]{0,1:T(8,128)(2,1)S(1)}, u32[]{:S(2)}, u32[]{:S(2)}) collective-permute-start(bf16[128,32]{0,1:T(8,128)(2,1)S(1)} %pad_maximum_fusion.5), channel_id=1, source_target_pairs={{0,33},{1,1},{2,97},{3,65},{4,161},{5,129},{6,225},{7,193},{32,32}... | collective-permute-start | bytes 24584 | tf_op jit(solution)/shard_map/ppermute | solution.py:67
  60.1 0.0 collective-permute-done.2
  60.1 2.6 %collective-permute-start.4 = (bf16[128,32]{0,1:T(8,128)(2,1)S(1)}, bf16[128,32]{0,1:T(8,128)(2,1)S(1)}, u32[]{:S(2)}, u32[]{:S(2)}) collective-permute-start(bf16[128,32]{0,1:T(8,128)(2,1)S(1)} %pad_maximum_fusion.4), channel_id=1, source_target_pairs={{0,32},{1,0},{2,96},{3,64},{4,160},{5,128},{6,224},{7,192},{32,33}... | collective-permute-start | bytes 24584 | tf_op jit(solution)/shard_map/ppermute | solution.py:67
  62.7 0.0 collective-permute-done.1
  62.8 0.1 copy.62
  62.9 11.4 %collective-permute-done.5 = bf16[128,32]{0,1:T(8,128)(2,1)S(1)} collective-permute-done((bf16[128,32]{0,1:T(8,128)(2,1)S(1)}, bf16[128,32]{0,1:T(8,128)(2,1)S(1)}, u32[]{:S(2)}, u32[]{:S(2)}) %collective-permute-start.5) | collective-permute-done | bytes 8224 | tf_op jit(solution)/shard_map/ppermute | solution.py:67
  74.2 0.0 collective-permute-done.4
  74.3 0.1 copy.64
  74.4 0.1 copy.63
  74.5 0.1 copy.65
  74.6 0.0 collective-permute-done
  74.6 0.0 collective-permute-done.3
  74.6 0.1 broadcast_select_fusion.1
  74.8 0.1 pad_maximum_fusion
  74.8 0.3 copy.66
  75.1 1.5 %broadcast_in_dim.45 = bf16[4,2,128,928]{2,3,1,0:T(8,128)(2,1)} broadcast(bf16[2,128,928]{1,2,0:T(8,128)(2,1)S(1)} %copy.66), dimensions={1,2,3} | broadcast | bytes 2375680 | tf_op jit(solution)/shard_map/broadcast_in_dim | solution.py:72
  76.6 3.6 %all-to-all-start.1 = ((bf16[4,2,128,928]{2,3,1,0:T(8,128)(2,1)}), bf16[4,2,128,928]{2,3,1,0:T(8,128)(2,1)S(1)}, u32[]{:S(2)}, u32[]{:S(2)}) async-start(bf16[4,2,128,928]{2,3,1,0:T(8,128)(2,1)} %broadcast_in_dim.45), calls=%async_computation.1 | async-start | bytes 3801088 | tf_op jit(solution)/shard_map/all_to_all | solution.py:73
  80.3 15.4 %all_gather.3 = bf16[1024,128]{0,1:T(8,128)(2,1)S(1)} all-gather(bf16[128,128]{0,1:T(8,128)(2,1)S(1)} %bitcast.67), channel_id=1, replica_groups=mesh['mp'=2,'hx'=4,'hy'=2,'lo'=4,'tok'=8] {'tok'}, dimensions={0}, use_global_device_ids=true | all-gather | bytes 294912 | tf_op jit(solution)/shard_map/all_gather | solution.py:52
  95.7 0.2 copy.61
  95.9 0.1 multiply_reduce_fusion
  96.0 0.1 copy.70
  96.1 0.1 broadcast_select_fusion.2
  96.1 8.9 %all-to-all-done.1 = bf16[4,2,128,928]{2,3,1,0:T(8,128)(2,1)S(1)} async-done(((bf16[4,2,128,928]{2,3,1,0:T(8,128)(2,1)}), bf16[4,2,128,928]{2,3,1,0:T(8,128)(2,1)S(1)}, u32[]{:S(2)}, u32[]{:S(2)}) %all-to-all-start.1) | async-done | bytes 1900576 | tf_op jit(solution)/shard_map/all_to_all | solution.py:73
  105.1 0.2 fusion.5
  105.3 0.1 copy.69
  105.4 0.7 fusion.2
  106.2 1.1 maximum_maximum_fusion
  107.3 3.6 %all-to-all-start.2 = ((f32[8,32,976]{2,1,0:T(8,128)}), f32[8,32,976]{2,1,0:T(8,128)S(1)}, u32[]{:S(2)}, u32[]{:S(2)}) async-start(f32[8,32,976]{2,1,0:T(8,128)} %maximum_maximum_fusion), calls=%async_computation.2 | async-start | bytes 2097152 | tf_op jit(solution)/shard_map/all_to_all | solution.py:96
  110.9 27.5 %all-to-all-done.2 = f32[8,32,976]{2,1,0:T(8,128)S(1)} async-done(((f32[8,32,976]{2,1,0:T(8,128)}), f32[8,32,976]{2,1,0:T(8,128)S(1)}, u32[]{:S(2)}, u32[]{:S(2)}) %all-to-all-start.2) | async-done | bytes 999456 | tf_op jit(solution)/shard_map/all_to_all | solution.py:96
  138.4 0.1 reduce_sum.48
  138.6 0.1 slice_reduce_fusion
  138.7 0.1 fusion.6
  138.8 0.1 copy.72
  138.8 0.1 copy.73
  138.9 0.8 copy.79
  139.7 0.6 add.58
  (24 shorter events, 0.4 us)
Async XLA Ops:
  0.6 1.2 copy-start
  3.2 31.8 %copy-start.1 = (bf16[1,128,896]{2,1,0:T(8,128)(2,1)S(1)}, bf16[1,128,896]{2,1,0:T(8,128)(2,1)}, u32[]{:S(2)}) copy-start(bf16[1,128,896]{2,1,0:T(8,128)(2,1)} %param.4) | copy-start | bytes 688132
  24.5 35.6 %collective-permute-start.2 = (bf16[128,32]{0,1:T(8,128)(2,1)S(1)}, bf16[128,32]{0,1:T(8,128)(2,1)S(1)}, u32[]{:S(2)}, u32[]{:S(2)}) collective-permute-start(bf16[128,32]{0,1:T(8,128)(2,1)S(1)} %pad_maximum_fusion.5), channel_id=1, source_target_pairs={{0,1},{1,33},{2,65},{3,97},{4,129},{5,161},{6,193},{7,225},{32,0},... | collective-permute-start | bytes 24584 | tf_op jit(solution)/shard_map/ppermute | solution.py:66
  26.4 36.3 %collective-permute-start.1 = (bf16[128,32]{0,1:T(8,128)(2,1)S(1)}, bf16[128,32]{0,1:T(8,128)(2,1)S(1)}, u32[]{:S(2)}, u32[]{:S(2)}) collective-permute-start(bf16[128,32]{0,1:T(8,128)(2,1)S(1)} %pad_maximum_fusion.4), channel_id=1, source_target_pairs={{0,0},{1,32},{2,64},{3,96},{4,128},{5,160},{6,192},{7,224},{32,1},... | collective-permute-start | bytes 24584 | tf_op jit(solution)/shard_map/ppermute | solution.py:66
  35.0 39.6 %collective-permute-start = (bf16[128,896]{1,0:T(8,128)(2,1)S(1)}, bf16[128,896]{1,0:T(8,128)(2,1)S(1)}, u32[]{:S(2)}, u32[]{:S(2)}) collective-permute-start(bf16[128,896]{1,0:T(8,128)(2,1)S(1)} %bitcast.63), channel_id=1, source_target_pairs={{0,0},{1,32},{2,64},{3,96},{4,128},{5,160},{6,192},{7,224},{32,1},... | collective-permute-start | bytes 688136 | tf_op jit(solution)/shard_map/ppermute | solution.py:55
  38.6 36.1 %collective-permute-start.3 = (bf16[128,896]{1,0:T(8,128)(2,1)S(1)}, bf16[128,896]{1,0:T(8,128)(2,1)S(1)}, u32[]{:S(2)}, u32[]{:S(2)}) collective-permute-start(bf16[128,896]{1,0:T(8,128)(2,1)S(1)} %bitcast.64), channel_id=1, source_target_pairs={{0,32},{1,0},{2,96},{3,64},{4,160},{5,128},{6,224},{7,192},{32,33}... | collective-permute-start | bytes 688136 | tf_op jit(solution)/shard_map/ppermute | solution.py:56
  58.2 16.1 %collective-permute-start.5 = (bf16[128,32]{0,1:T(8,128)(2,1)S(1)}, bf16[128,32]{0,1:T(8,128)(2,1)S(1)}, u32[]{:S(2)}, u32[]{:S(2)}) collective-permute-start(bf16[128,32]{0,1:T(8,128)(2,1)S(1)} %pad_maximum_fusion.5), channel_id=1, source_target_pairs={{0,33},{1,1},{2,97},{3,65},{4,161},{5,129},{6,225},{7,193},{32,32}... | collective-permute-start | bytes 24584 | tf_op jit(solution)/shard_map/ppermute | solution.py:67
  60.1 14.2 %collective-permute-start.4 = (bf16[128,32]{0,1:T(8,128)(2,1)S(1)}, bf16[128,32]{0,1:T(8,128)(2,1)S(1)}, u32[]{:S(2)}, u32[]{:S(2)}) collective-permute-start(bf16[128,32]{0,1:T(8,128)(2,1)S(1)} %pad_maximum_fusion.4), channel_id=1, source_target_pairs={{0,32},{1,0},{2,96},{3,64},{4,160},{5,128},{6,224},{7,192},{32,33}... | collective-permute-start | bytes 24584 | tf_op jit(solution)/shard_map/ppermute | solution.py:67
  76.6 28.4 %all-to-all-start.1 = ((bf16[4,2,128,928]{2,3,1,0:T(8,128)(2,1)}), bf16[4,2,128,928]{2,3,1,0:T(8,128)(2,1)S(1)}, u32[]{:S(2)}, u32[]{:S(2)}) async-start(bf16[4,2,128,928]{2,3,1,0:T(8,128)(2,1)} %broadcast_in_dim.45), calls=%async_computation.1 | async-start | bytes 3801088 | tf_op jit(solution)/shard_map/all_to_all | solution.py:73
  107.3 31.1 %all-to-all-start.2 = ((f32[8,32,976]{2,1,0:T(8,128)}), f32[8,32,976]{2,1,0:T(8,128)S(1)}, u32[]{:S(2)}, u32[]{:S(2)}) async-start(f32[8,32,976]{2,1,0:T(8,128)} %maximum_maximum_fusion), calls=%async_computation.2 | async-start | bytes 2097152 | tf_op jit(solution)/shard_map/all_to_all | solution.py:96

commit v24 on v20

--- a/solution.py
+++ b/solution.py
@@ -80,9 +80,8 @@
     diag_part = jnp.where(is_self, diag_term[None], 0.0)
 
     send = jnp.concatenate([pieces, diag_part], axis=2)
-    send = jnp.concatenate([send] * mp_count, axis=0)
-    got = lax.all_to_all(send, ("mp", "lo"), 0, 0, tiled=True)
-    got = jnp.sum(got.reshape(mp_count, group, ROW_DEV, -1), axis=0)
+    send = send + lax.ppermute(send, "mp", [(m, (m + 1) % mp_count) for m in range(mp_count)])
+    got = lax.all_to_all(send, "lo", 0, 0, tiled=True)
 
     gram = got[:, :, :span_width]
     slot = lax.broadcasted_iota(jnp.int32, gram.shape, 0)

time: 127 us -> 128 us (level)
  starting transfers between devices: 59.6 us -> 64.1 us
  waiting for transfers between devices: 42.3 us -> 38.8 us
    all_to_all x1, waiting for transfers between devices: 26.9 us -> 14.3 us  [local(): got = lax.all_to_all(send, 'lo', 0, 0, tiled=True)]
    ppermute x0 -> x1, waiting for transfers between devices: none -> 9.13 us  [local(): lax.ppermute(send, 'mp', [(m, (m + 1) % mp_count) for m in range(mp_count)])]
    ppermute x0 -> x1, starting transfers between devices: none -> 4 us  [local(): lax.ppermute(send, 'mp', [(m, (m + 1) % mp_count) for m in range(mp_count)])]
  transfers between devices with their start and end apart: 7 -> 8, of which waited for: 5 -> 6; matrix products, arithmetic and copies ran while one was open for 1% -> 1% of each run, Pallas kernels for 0% -> 0%
where the time goes in v24:
time: 128 us; the launch traced here: 127 us
  starting transfers between devices  64.1 us (50%)
  waiting for transfers between devices  38.8 us (30%)
  blocking collectives  13.3 us (10%)
  local copies, waits for them, and re-layouts  4.83 us (4%)
  other arithmetic  3.11 us (2%)
  matrix products  2.37 us (2%)
    all_to_all x1, starting transfers between devices, local(): full = lax.all_to_all(spread, 'hx', 0, 0, tiled=True)  21.5 us
    all_to_all x1, waiting for transfers between devices, local(): got = lax.all_to_all(send, 'lo', 0, 0, tiled=True)  14.3 us
    all_gather x1, blocking collectives, local(): lax.all_gather(win_lo.reshape(tokens, group * ROW_DEV), 'tok', axis=0, ti...  13.3 us
    all_to_all x1, starting transfers between devices, local(): got_y = lax.all_to_all(send_y, HI + ('lo',), 1, 1, tiled=True)  10.5 us
    ppermute x1, waiting for transfers between devices, local(): lax.ppermute(send, 'mp', [(m, (m + 1) % mp_count) for m in range(mp_count)])  9.13 us
    ppermute x1, starting transfers between devices, local(): lax.ppermute(y_pay, HI + ('tok',), swap)  8.97 us
    ppermute x1, starting transfers between devices, local(): x_own = lax.ppermute(x_local, HI + ('tok',), swap)  8.17 us
    all_to_all x1, starting transfers between devices, local(): got = lax.all_to_all(send, 'lo', 0, 0, tiled=True)  7.11 us
  transfers between devices with their start and end apart: 8, of which 6 were waited for; matrix products, arithmetic and copies ran while one was open for 1% of the time, Pallas kernels for 0%

profile of v24, /device:TPU:1, one launch (start us, length us, event | category | flops | bytes accessed | tf_op | source)
XLA Modules:
  0.0 127.3 jit_solution(3660870065377527696)
XLA Ops:
  0.6 0.0 copy-start
  0.6 0.8 slice.44
  1.5 0.1 copy.62
  1.6 0.3 copy-done
  1.8 0.0 copy-start.1
  1.8 1.4 %reduce-precision_convert_fusion = (bf16[128,512]{1,0:T(8,128)(2,1)S(1)}, bf16[128,512]{1,0:T(8,128)(2,1)S(1)}) fusion(bf16[1,512,896]{2,1,0:T(8,128)(2,1)S(1)} %copy-done, bf16[1,128,896]{2,1,0:T(8,128)(2,1)} %param.2), kind=kOutput, calls=%fused_computation.16 | convolution fusion | flops 117702656 | bytes 1409024 | tf_op jit(solution)/shard_map/dot_general | solution.py:34
  3.3 0.1 copy.60
  3.4 0.1 copy.61
  3.6 0.9 pad_maximum_fusion
  4.4 10.5 %all-to-all-start = ((bf16[128,32,64]{0,2,1:T(8,128)(2,1)}), bf16[128,32,64]{0,2,1:T(8,128)(2,1)S(1)}, u32[]{:S(2)}, u32[]{:S(2)}) async-start(bf16[128,32,64]{0,2,1:T(8,128)(2,1)} %pad_maximum_fusion), calls=%async_computation | async-start | bytes 1048576 | tf_op jit(solution)/shard_map/all_to_all | solution.py:42
  14.9 0.0 copy-done.1
  15.0 8.2 %collective-permute-start = (bf16[128,896]{1,0:T(8,128)(2,1)S(1)}, bf16[128,896]{1,0:T(8,128)(2,1)S(1)}, u32[]{:S(2)}, u32[]{:S(2)}) collective-permute-start(bf16[128,896]{1,0:T(8,128)(2,1)S(1)} %bitcast.50), channel_id=1, source_target_pairs={{0,0},{1,32},{2,64},{3,96},{4,128},{5,160},{6,192},{7,224},{32,1},... | collective-permute-start | bytes 688136 | tf_op jit(solution)/shard_map/ppermute | solution.py:53
  23.1 1.9 %collective-permute-start.2 = (bf16[128,896]{1,0:T(8,128)(2,1)S(1)}, bf16[128,896]{1,0:T(8,128)(2,1)S(1)}, u32[]{:S(2)}, u32[]{:S(2)}) collective-permute-start(bf16[128,896]{1,0:T(8,128)(2,1)S(1)} %bitcast.51), channel_id=1, source_target_pairs={{0,32},{1,0},{2,96},{3,64},{4,160},{5,128},{6,224},{7,192},{32,33}... | collective-permute-start | bytes 688136 | tf_op jit(solution)/shard_map/ppermute | solution.py:54
  25.1 4.2 %all-to-all-done = bf16[128,32,64]{0,2,1:T(8,128)(2,1)S(1)} async-done(((bf16[128,32,64]{0,2,1:T(8,128)(2,1)}), bf16[128,32,64]{0,2,1:T(8,128)(2,1)S(1)}, u32[]{:S(2)}, u32[]{:S(2)}) %all-to-all-start) | async-done | bytes 524320 | tf_op jit(solution)/shard_map/all_to_all | solution.py:42
  29.3 9.0 %collective-permute-start.1 = (bf16[128,32]{0,1:T(8,128)(2,1)S(1)}, bf16[128,32]{0,1:T(8,128)(2,1)S(1)}, u32[]{:S(2)}, u32[]{:S(2)}) collective-permute-start(bf16[128,32]{0,1:T(8,128)(2,1)S(1)} %pad_maximum_fusion.6), channel_id=1, source_target_pairs={{0,0},{1,32},{2,64},{3,96},{4,128},{5,160},{6,192},{7,224},{32,1},... | collective-permute-start | bytes 24584 | tf_op jit(solution)/shard_map/ppermute | solution.py:56
  38.3 1.9 %collective-permute-start.3 = (bf16[128,32]{0,1:T(8,128)(2,1)S(1)}, bf16[128,32]{0,1:T(8,128)(2,1)S(1)}, u32[]{:S(2)}, u32[]{:S(2)}) collective-permute-start(bf16[128,32]{0,1:T(8,128)(2,1)S(1)} %pad_maximum_fusion.6), channel_id=1, source_target_pairs={{0,32},{1,0},{2,96},{3,64},{4,160},{5,128},{6,224},{7,192},{32,33}... | collective-permute-start | bytes 24584 | tf_op jit(solution)/shard_map/ppermute | solution.py:57
  40.2 2.0 %collective-permute-done.1 = bf16[128,32]{0,1:T(8,128)(2,1)S(1)} collective-permute-done((bf16[128,32]{0,1:T(8,128)(2,1)S(1)}, bf16[128,32]{0,1:T(8,128)(2,1)S(1)}, u32[]{:S(2)}, u32[]{:S(2)}) %collective-permute-start.1) | collective-permute-done | bytes 8224 | tf_op jit(solution)/shard_map/ppermute | solution.py:56
  42.3 0.1 copy.64
  42.4 4.2 %collective-permute-done.3 = bf16[128,32]{0,1:T(8,128)(2,1)S(1)} collective-permute-done((bf16[128,32]{0,1:T(8,128)(2,1)S(1)}, bf16[128,32]{0,1:T(8,128)(2,1)S(1)}, u32[]{:S(2)}, u32[]{:S(2)}) %collective-permute-start.3) | collective-permute-done | bytes 8224 | tf_op jit(solution)/shard_map/ppermute | solution.py:57
  46.6 0.1 copy.65
  46.7 0.0 collective-permute-done
  46.7 0.0 collective-permute-done.2
  46.7 0.1 broadcast_select_fusion.1
  46.9 0.1 pad_maximum_fusion.1
  46.9 0.3 copy.66
  47.2 1.5 %broadcast_in_dim.36 = bf16[4,2,128,928]{2,3,1,0:T(8,128)(2,1)} broadcast(bf16[2,128,928]{1,2,0:T(8,128)(2,1)S(1)} %copy.66), dimensions={1,2,3} | broadcast | bytes 2375680 | tf_op jit(solution)/shard_map/broadcast_in_dim | solution.py:60
  48.7 21.5 %all-to-all-start.1 = ((bf16[4,2,128,928]{2,3,1,0:T(8,128)(2,1)}), bf16[4,2,128,928]{2,3,1,0:T(8,128)(2,1)S(1)}, u32[]{:S(2)}, u32[]{:S(2)}) async-start(bf16[4,2,128,928]{2,3,1,0:T(8,128)(2,1)} %broadcast_in_dim.36), calls=%async_computation.1 | async-start | bytes 3801088 | tf_op jit(solution)/shard_map/all_to_all | solution.py:61
  70.3 13.3 %all_gather.3 = bf16[1024,128]{0,1:T(8,128)(2,1)S(1)} all-gather(bf16[128,128]{0,1:T(8,128)(2,1)S(1)} %bitcast.54), channel_id=1, replica_groups=mesh['mp'=2,'hx'=4,'hy'=2,'lo'=4,'tok'=8] {'tok'}, dimensions={0}, use_global_device_ids=true | all-gather | bytes 294912 | tf_op jit(solution)/shard_map/all_gather | solution.py:48
  83.6 0.2 copy.63
  83.7 0.1 multiply_reduce_fusion
  83.9 0.1 copy.70
  84.0 0.1 broadcast_select_fusion.2
  84.0 4.9 %all-to-all-done.1 = bf16[4,2,128,928]{2,3,1,0:T(8,128)(2,1)S(1)} async-done(((bf16[4,2,128,928]{2,3,1,0:T(8,128)(2,1)}), bf16[4,2,128,928]{2,3,1,0:T(8,128)(2,1)S(1)}, u32[]{:S(2)}, u32[]{:S(2)}) %all-to-all-start.1) | async-done | bytes 1900576 | tf_op jit(solution)/shard_map/all_to_all | solution.py:61
  89.0 0.2 fusion.5
  89.2 0.1 copy.69
  89.3 0.7 fusion.2
  90.1 0.1 pad_maximum_fusion.3
  90.1 4.0 %collective-permute-start.4 = (f32[4,32,976]{2,1,0:T(8,128)S(1)}, f32[4,32,976]{2,1,0:T(8,128)S(1)}, u32[]{:S(2)}, u32[]{:S(2)}) collective-permute-start(f32[4,32,976]{2,1,0:T(8,128)S(1)} %pad_maximum_fusion.3), channel_id=1, source_target_pairs={{0,256},{256,0},{1,257},{257,1},{2,258},{258,2},{3,259},{259,3},{4... | collective-permute-start | bytes 1499144 | tf_op jit(solution)/shard_map/ppermute | solution.py:83
  94.2 9.1 %collective-permute-done.4 = f32[4,32,976]{2,1,0:T(8,128)S(1)} collective-permute-done((f32[4,32,976]{2,1,0:T(8,128)S(1)}, f32[4,32,976]{2,1,0:T(8,128)S(1)}, u32[]{:S(2)}, u32[]{:S(2)}) %collective-permute-start.4) | collective-permute-done | bytes 499744 | tf_op jit(solution)/shard_map/ppermute | solution.py:83
  103.3 0.9 fusion.20
  104.2 7.1 %all-to-all-start.2 = ((f32[4,32,976]{2,1,0:T(8,128)}), f32[4,32,976]{2,1,0:T(8,128)S(1)}, u32[]{:S(2)}, u32[]{:S(2)}) async-start(f32[4,32,976]{2,1,0:T(8,128)} %fusion.20), calls=%async_computation.2 | async-start | bytes 1048576 | tf_op jit(solution)/shard_map/all_to_all | solution.py:84
  111.3 14.3 %all-to-all-done.2 = f32[4,32,976]{2,1,0:T(8,128)S(1)} async-done(((f32[4,32,976]{2,1,0:T(8,128)}), f32[4,32,976]{2,1,0:T(8,128)S(1)}, u32[]{:S(2)}, u32[]{:S(2)}) %all-to-all-start.2) | async-done | bytes 499744 | tf_op jit(solution)/shard_map/all_to_all | solution.py:84
  125.6 0.1 copy.72
  125.7 0.1 copy.73
  125.7 0.1 fusion.8
  125.8 0.8 copy.78
  126.6 0.1 slice_reduce_fusion
  126.7 0.6 add.31
  (13 shorter events, 0.2 us)
Async XLA Ops:
  0.6 1.2 copy-start
  1.8 13.1 %copy-start.1 = (bf16[1,128,896]{2,1,0:T(8,128)(2,1)S(1)}, bf16[1,128,896]{2,1,0:T(8,128)(2,1)}, u32[]{:S(2)}) copy-start(bf16[1,128,896]{2,1,0:T(8,128)(2,1)} %param.2) | copy-start | bytes 688132
  4.4 24.8 %all-to-all-start = ((bf16[128,32,64]{0,2,1:T(8,128)(2,1)}), bf16[128,32,64]{0,2,1:T(8,128)(2,1)S(1)}, u32[]{:S(2)}, u32[]{:S(2)}) async-start(bf16[128,32,64]{0,2,1:T(8,128)(2,1)} %pad_maximum_fusion), calls=%async_computation | async-start | bytes 1048576 | tf_op jit(solution)/shard_map/all_to_all | solution.py:42
  15.0 31.8 %collective-permute-start = (bf16[128,896]{1,0:T(8,128)(2,1)S(1)}, bf16[128,896]{1,0:T(8,128)(2,1)S(1)}, u32[]{:S(2)}, u32[]{:S(2)}) collective-permute-start(bf16[128,896]{1,0:T(8,128)(2,1)S(1)} %bitcast.50), channel_id=1, source_target_pairs={{0,0},{1,32},{2,64},{3,96},{4,128},{5,160},{6,192},{7,224},{32,1},... | collective-permute-start | bytes 688136 | tf_op jit(solution)/shard_map/ppermute | solution.py:53
  23.1 23.6 %collective-permute-start.2 = (bf16[128,896]{1,0:T(8,128)(2,1)S(1)}, bf16[128,896]{1,0:T(8,128)(2,1)S(1)}, u32[]{:S(2)}, u32[]{:S(2)}) collective-permute-start(bf16[128,896]{1,0:T(8,128)(2,1)S(1)} %bitcast.51), channel_id=1, source_target_pairs={{0,32},{1,0},{2,96},{3,64},{4,160},{5,128},{6,224},{7,192},{32,33}... | collective-permute-start | bytes 688136 | tf_op jit(solution)/shard_map/ppermute | solution.py:54
  29.3 13.0 %collective-permute-start.1 = (bf16[128,32]{0,1:T(8,128)(2,1)S(1)}, bf16[128,32]{0,1:T(8,128)(2,1)S(1)}, u32[]{:S(2)}, u32[]{:S(2)}) collective-permute-start(bf16[128,32]{0,1:T(8,128)(2,1)S(1)} %pad_maximum_fusion.6), channel_id=1, source_target_pairs={{0,0},{1,32},{2,64},{3,96},{4,128},{5,160},{6,192},{7,224},{32,1},... | collective-permute-start | bytes 24584 | tf_op jit(solution)/shard_map/ppermute | solution.py:56
  38.3 8.3 %collective-permute-start.3 = (bf16[128,32]{0,1:T(8,128)(2,1)S(1)}, bf16[128,32]{0,1:T(8,128)(2,1)S(1)}, u32[]{:S(2)}, u32[]{:S(2)}) collective-permute-start(bf16[128,32]{0,1:T(8,128)(2,1)S(1)} %pad_maximum_fusion.6), channel_id=1, source_target_pairs={{0,32},{1,0},{2,96},{3,64},{4,160},{5,128},{6,224},{7,192},{32,33}... | collective-permute-start | bytes 24584 | tf_op jit(solution)/shard_map/ppermute | solution.py:57
  48.7 40.2 %all-to-all-start.1 = ((bf16[4,2,128,928]{2,3,1,0:T(8,128)(2,1)}), bf16[4,2,128,928]{2,3,1,0:T(8,128)(2,1)S(1)}, u32[]{:S(2)}, u32[]{:S(2)}) async-start(bf16[4,2,128,928]{2,3,1,0:T(8,128)(2,1)} %broadcast_in_dim.36), calls=%async_computation.1 | async-start | bytes 3801088 | tf_op jit(solution)/shard_map/all_to_all | solution.py:61
  90.1 13.1 %collective-permute-start.4 = (f32[4,32,976]{2,1,0:T(8,128)S(1)}, f32[4,32,976]{2,1,0:T(8,128)S(1)}, u32[]{:S(2)}, u32[]{:S(2)}) collective-permute-start(f32[4,32,976]{2,1,0:T(8,128)S(1)} %pad_maximum_fusion.3), channel_id=1, source_target_pairs={{0,256},{256,0},{1,257},{257,1},{2,258},{258,2},{3,259},{259,3},{4... | collective-permute-start | bytes 1499144 | tf_op jit(solution)/shard_map/ppermute | solution.py:83
  104.2 21.4 %all-to-all-start.2 = ((f32[4,32,976]{2,1,0:T(8,128)}), f32[4,32,976]{2,1,0:T(8,128)S(1)}, u32[]{:S(2)}, u32[]{:S(2)}) async-start(f32[4,32,976]{2,1,0:T(8,128)} %fusion.20), calls=%async_computation.2 | async-start | bytes 1048576 | tf_op jit(solution)/shard_map/all_to_all | solution.py:84

commit v25 on v20

--- a/solution.py
+++ b/solution.py
@@ -6,6 +6,7 @@
 
 ROW_DEV = 32
 HI = ("hx", "hy")
+TOK = ("tz", "tc")
 
 
 OFF_SCALE = 0.9
@@ -18,12 +19,12 @@
     cols = w_local.shape[0]
     hi_index = lax.axis_index(HI)
     lo_index = lax.axis_index("lo")
-    tok_index = lax.axis_index("tok")
+    tok_index = lax.axis_index(TOK)
     group = lax.axis_size("lo")
     hi_count = lax.axis_size(HI)
     half_count = lax.axis_size("hx")
     hy_index = lax.axis_index("hy")
-    tok_count = lax.axis_size("tok")
+    tok_count = lax.axis_size(TOK)
     mp_count = lax.axis_size("mp")
     blk_count = hi_count * group
     col_group = cols // blk_count
@@ -45,16 +46,17 @@
         axis=1,
     )
     win_lo = lax.dynamic_slice_in_dim(got_y[:, :, 2 * col_group:], hi_index * group, group, 1)
-    wins = lax.all_gather(win_lo.reshape(tokens, group * ROW_DEV), "tok", axis=0, tiled=True)
+    wins = lax.all_gather(win_lo.reshape(tokens, group * ROW_DEV), "tc", axis=0, tiled=True)
+    wins = lax.all_gather(wins, "tz", axis=0, tiled=True)
     y_round = lax.reduce_precision(y_mine, exponent_bits=8, mantissa_bits=7)
     y_high = y_round.astype(jnp.bfloat16)
     y_low = (y_mine - y_round).astype(jnp.bfloat16)
     mirror = [(h * tok_count + t, (t ^ 1) * tok_count + h) for h in range(hi_count) for t in range(tok_count)]
-    x_own = lax.ppermute(x_local, HI + ("tok",), swap)
-    x_other = lax.ppermute(x_local, HI + ("tok",), mirror)
+    x_own = lax.ppermute(x_local, HI + TOK, swap)
+    x_other = lax.ppermute(x_local, HI + TOK, mirror)
     y_pay = jnp.concatenate([y_high, y_low], axis=1)
-    own = jnp.concatenate([x_own, lax.ppermute(y_pay, HI + ("tok",), swap)], axis=1)
-    other = jnp.concatenate([x_other, lax.ppermute(y_pay, HI + ("tok",), mirror)], axis=1)
+    own = jnp.concatenate([x_own, lax.ppermute(y_pay, HI + TOK, swap)], axis=1)
+    other = jnp.concatenate([x_other, lax.ppermute(y_pay, HI + TOK, mirror)], axis=1)
     even_first = hy_index == 0
     pair = jnp.stack([jnp.where(even_first, own, other), jnp.where(even_first, other, own)])
     spread = jnp.broadcast_to(pair[None], (half_count,) + pair.shape)
@@ -99,13 +101,13 @@
 def solution(mesh):
     mp_count, blk_count, tok_count = (mesh.shape[a] for a in ("mp", "blk", "tok"))
     group = blk_count // tok_count
-    devices = np.asarray(mesh.devices).reshape(mp_count, tok_count // 2, 2, group, tok_count)
-    split = Mesh(devices, ("mp",) + HI + ("lo", "tok"))
-    placed = (P("mp", "tok", HI + ("lo",)), P("mp", None, HI + ("lo",)))
+    devices = np.asarray(mesh.devices).reshape(mp_count, tok_count // 2, 2, group, tok_count // 2, 2)
+    split = Mesh(devices, ("mp",) + HI + ("lo",) + TOK)
+    placed = (P("mp", TOK, HI + ("lo",)), P("mp", None, HI + ("lo",)))
     return jax.shard_map(
         local,
         mesh=split,
         in_specs=placed,
-        out_specs=(P(HI + ("lo",), "tok"), P(HI + ("lo",), "tok")),
+        out_specs=(P(HI + ("lo",), TOK), P(HI + ("lo",), TOK)),
         check_vma=False,
     )

time: 127 us -> 127 us (level)
    all_gather x1 -> x2, blocking collectives: 13.3 us -> 13.6 us  [the longest x1 11.7 us: local(): wins = lax.all_gather(wins, 'tz', axis=0, tiled=True)]
where the time goes in v25:
time: 127 us
  starting transfers between devices  59.6 us (47%)
  waiting for transfers between devices  42 us (33%)
  blocking collectives  13.6 us (11%)
  local copies, waits for them, and re-layouts  4.83 us (4%)
  other arithmetic  3.36 us (3%)
  matrix products  2.37 us (2%)
    all_to_all x1, waiting for transfers between devices, local(): got = lax.all_to_all(send, ('mp', 'lo'), 0, 0, tiled=True)  26.9 us
    all_to_all x1, starting transfers between devices, local(): full = lax.all_to_all(spread, 'hx', 0, 0, tiled=True)  21.5 us
    all_gather x1, blocking collectives, local(): wins = lax.all_gather(wins, 'tz', axis=0, tiled=True)  11.7 us
    all_to_all x1, starting transfers between devices, local(): got_y = lax.all_to_all(send_y, HI + ('lo',), 1, 1, tiled=True)  10.5 us
    ppermute x1, starting transfers between devices, local(): own = jnp.concatenate([x_own, lax.ppermute(y_pay, HI + TOK, swap)], axis=1)  8.97 us
    ppermute x1, starting transfers between devices, local(): x_own = lax.ppermute(x_local, HI + TOK, swap)  8.17 us
    all_to_all x1, starting transfers between devices, local(): got = lax.all_to_all(send, ('mp', 'lo'), 0, 0, tiled=True)  6.57 us
    all_to_all x1, waiting for transfers between devices, local(): full = lax.all_to_all(spread, 'hx', 0, 0, tiled=True)  4.64 us
  transfers between devices with their start and end apart: 7, of which 5 were waited for; matrix products, arithmetic and copies ran while one was open for 1% of the time, Pallas kernels for 0%

profile of v25, /device:TPU:1, one launch (start us, length us, event | category | flops | bytes accessed | tf_op | source)
XLA Modules:
  0.0 126.5 jit_solution(3996242547001588308)
XLA Ops:
  0.6 0.0 copy-start
  0.6 0.8 slice.44
  1.5 0.1 copy.60
  1.6 0.3 copy-done
  1.8 0.0 copy-start.1
  1.8 1.4 %reduce-precision_convert_fusion = (bf16[128,512]{1,0:T(8,128)(2,1)S(1)}, bf16[128,512]{1,0:T(8,128)(2,1)S(1)}) fusion(bf16[1,512,896]{2,1,0:T(8,128)(2,1)S(1)} %copy-done, bf16[1,128,896]{2,1,0:T(8,128)(2,1)} %param.2), kind=kOutput, calls=%fused_computation.16 | convolution fusion | flops 117702656 | bytes 1409024 | tf_op jit(solution)/shard_map/dot_general | solution.py:35
  3.3 0.1 copy.58
  3.4 0.1 copy.59
  3.6 0.9 pad_maximum_fusion
  4.4 10.5 %all-to-all-start = ((bf16[128,32,64]{0,2,1:T(8,128)(2,1)}), bf16[128,32,64]{0,2,1:T(8,128)(2,1)S(1)}, u32[]{:S(2)}, u32[]{:S(2)}) async-start(bf16[128,32,64]{0,2,1:T(8,128)(2,1)} %pad_maximum_fusion), calls=%async_computation | async-start | bytes 1048576 | tf_op jit(solution)/shard_map/all_to_all | solution.py:43
  14.9 0.0 copy-done.1
  15.0 8.2 %collective-permute-start = (bf16[128,896]{1,0:T(8,128)(2,1)S(1)}, bf16[128,896]{1,0:T(8,128)(2,1)S(1)}, u32[]{:S(2)}, u32[]{:S(2)}) collective-permute-start(bf16[128,896]{1,0:T(8,128)(2,1)S(1)} %bitcast.51), channel_id=1, source_target_pairs={{0,0},{1,32},{2,64},{3,96},{4,128},{5,160},{6,192},{7,224},{32,1},... | collective-permute-start | bytes 688136 | tf_op jit(solution)/shard_map/ppermute | solution.py:55
  23.1 1.9 %collective-permute-start.2 = (bf16[128,896]{1,0:T(8,128)(2,1)S(1)}, bf16[128,896]{1,0:T(8,128)(2,1)S(1)}, u32[]{:S(2)}, u32[]{:S(2)}) collective-permute-start(bf16[128,896]{1,0:T(8,128)(2,1)S(1)} %bitcast.52), channel_id=1, source_target_pairs={{0,32},{1,0},{2,96},{3,64},{4,160},{5,128},{6,224},{7,192},{32,33}... | collective-permute-start | bytes 688136 | tf_op jit(solution)/shard_map/ppermute | solution.py:56
  25.1 4.2 %all-to-all-done = bf16[128,32,64]{0,2,1:T(8,128)(2,1)S(1)} async-done(((bf16[128,32,64]{0,2,1:T(8,128)(2,1)}), bf16[128,32,64]{0,2,1:T(8,128)(2,1)S(1)}, u32[]{:S(2)}, u32[]{:S(2)}) %all-to-all-start) | async-done | bytes 524320 | tf_op jit(solution)/shard_map/all_to_all | solution.py:43
  29.3 9.0 %collective-permute-start.1 = (bf16[128,32]{0,1:T(8,128)(2,1)S(1)}, bf16[128,32]{0,1:T(8,128)(2,1)S(1)}, u32[]{:S(2)}, u32[]{:S(2)}) collective-permute-start(bf16[128,32]{0,1:T(8,128)(2,1)S(1)} %pad_maximum_fusion.5), channel_id=1, source_target_pairs={{0,0},{1,32},{2,64},{3,96},{4,128},{5,160},{6,192},{7,224},{32,1},... | collective-permute-start | bytes 24584 | tf_op jit(solution)/shard_map/ppermute | solution.py:58
  38.3 1.9 %collective-permute-start.3 = (bf16[128,32]{0,1:T(8,128)(2,1)S(1)}, bf16[128,32]{0,1:T(8,128)(2,1)S(1)}, u32[]{:S(2)}, u32[]{:S(2)}) collective-permute-start(bf16[128,32]{0,1:T(8,128)(2,1)S(1)} %pad_maximum_fusion.5), channel_id=1, source_target_pairs={{0,32},{1,0},{2,96},{3,64},{4,160},{5,128},{6,224},{7,192},{32,33}... | collective-permute-start | bytes 24584 | tf_op jit(solution)/shard_map/ppermute | solution.py:59
  40.2 2.0 %collective-permute-done.1 = bf16[128,32]{0,1:T(8,128)(2,1)S(1)} collective-permute-done((bf16[128,32]{0,1:T(8,128)(2,1)S(1)}, bf16[128,32]{0,1:T(8,128)(2,1)S(1)}, u32[]{:S(2)}, u32[]{:S(2)}) %collective-permute-start.1) | collective-permute-done | bytes 8224 | tf_op jit(solution)/shard_map/ppermute | solution.py:58
  42.3 0.1 copy.62
  42.4 4.2 %collective-permute-done.3 = bf16[128,32]{0,1:T(8,128)(2,1)S(1)} collective-permute-done((bf16[128,32]{0,1:T(8,128)(2,1)S(1)}, bf16[128,32]{0,1:T(8,128)(2,1)S(1)}, u32[]{:S(2)}, u32[]{:S(2)}) %collective-permute-start.3) | collective-permute-done | bytes 8224 | tf_op jit(solution)/shard_map/ppermute | solution.py:59
  46.6 0.1 copy.63
  46.7 0.0 collective-permute-done
  46.7 0.0 collective-permute-done.2
  46.7 0.1 broadcast_select_fusion.1
  46.9 0.1 pad_maximum_fusion.1
  46.9 0.3 copy.64
  47.2 1.5 %broadcast_in_dim.36 = bf16[4,2,128,928]{2,3,1,0:T(8,128)(2,1)} broadcast(bf16[2,128,928]{1,2,0:T(8,128)(2,1)S(1)} %copy.64), dimensions={1,2,3} | broadcast | bytes 2375680 | tf_op jit(solution)/shard_map/broadcast_in_dim | solution.py:62
  48.7 21.5 %all-to-all-start.1 = ((bf16[4,2,128,928]{2,3,1,0:T(8,128)(2,1)}), bf16[4,2,128,928]{2,3,1,0:T(8,128)(2,1)S(1)}, u32[]{:S(2)}, u32[]{:S(2)}) async-start(bf16[4,2,128,928]{2,3,1,0:T(8,128)(2,1)} %broadcast_in_dim.36), calls=%async_computation.1 | async-start | bytes 3801088 | tf_op jit(solution)/shard_map/all_to_all | solution.py:63
  70.3 1.9 %all_gather.6 = bf16[256,128]{0,1:T(8,128)(2,1)S(1)} all-gather(bf16[128,128]{0,1:T(8,128)(2,1)S(1)} %bitcast.55), channel_id=1, replica_groups=mesh['mp'=2,'hx'=4,'hy'=2,'lo'=4,'tz'=4,'tc'=2] {'tc'}, dimensions={0}, use_global_device_ids=true | all-gather | bytes 98304 | tf_op jit(solution)/shard_map/all_gather | solution.py:49
  72.1 11.7 %all_gather.7 = bf16[1024,128]{0,1:T(8,128)(2,1)S(1)} all-gather(bf16[256,128]{0,1:T(8,128)(2,1)S(1)} %all_gather.6), channel_id=1, replica_groups=mesh['mp'=2,'hx'=4,'hy'=2,'lo'=4,'tz'=4,'tc'=2] {'tz'}, dimensions={0}, use_global_device_ids=true | all-gather | bytes 327680 | tf_op jit(solution)/shard_map/all_gather | solution.py:50
  83.8 0.2 copy.61
  84.0 0.1 multiply_reduce_fusion
  84.2 0.1 copy.68
  84.2 0.1 broadcast_select_fusion.2
  84.3 4.6 %all-to-all-done.1 = bf16[4,2,128,928]{2,3,1,0:T(8,128)(2,1)S(1)} async-done(((bf16[4,2,128,928]{2,3,1,0:T(8,128)(2,1)}), bf16[4,2,128,928]{2,3,1,0:T(8,128)(2,1)S(1)}, u32[]{:S(2)}, u32[]{:S(2)}) %all-to-all-start.1) | async-done | bytes 1900576 | tf_op jit(solution)/shard_map/all_to_all | solution.py:63
  88.9 0.2 fusion.5
  89.2 0.1 copy.67
  89.3 0.7 fusion.2
  90.0 1.1 maximum_maximum_fusion
  91.2 6.6 %all-to-all-start.2 = ((f32[8,32,976]{2,1,0:T(8,128)}), f32[8,32,976]{2,1,0:T(8,128)S(1)}, u32[]{:S(2)}, u32[]{:S(2)}) async-start(f32[8,32,976]{2,1,0:T(8,128)} %maximum_maximum_fusion), calls=%async_computation.2 | async-start | bytes 2097152 | tf_op jit(solution)/shard_map/all_to_all | solution.py:86
  97.7 26.9 %all-to-all-done.2 = f32[8,32,976]{2,1,0:T(8,128)S(1)} async-done(((f32[8,32,976]{2,1,0:T(8,128)}), f32[8,32,976]{2,1,0:T(8,128)S(1)}, u32[]{:S(2)}, u32[]{:S(2)}) %all-to-all-start.2) | async-done | bytes 999456 | tf_op jit(solution)/shard_map/all_to_all | solution.py:86
  124.7 0.1 reduce_sum.38
  124.8 0.1 slice_reduce_fusion
  124.9 0.1 fusion.8
  125.0 0.1 copy.70
  125.0 0.1 copy.71
  125.1 0.8 copy.76
  125.9 0.6 add.31
  (13 shorter events, 0.2 us)
Async XLA Ops:
  0.6 1.2 copy-start
  1.8 13.1 %copy-start.1 = (bf16[1,128,896]{2,1,0:T(8,128)(2,1)S(1)}, bf16[1,128,896]{2,1,0:T(8,128)(2,1)}, u32[]{:S(2)}) copy-start(bf16[1,128,896]{2,1,0:T(8,128)(2,1)} %param.2) | copy-start | bytes 688132
  4.4 24.8 %all-to-all-start = ((bf16[128,32,64]{0,2,1:T(8,128)(2,1)}), bf16[128,32,64]{0,2,1:T(8,128)(2,1)S(1)}, u32[]{:S(2)}, u32[]{:S(2)}) async-start(bf16[128,32,64]{0,2,1:T(8,128)(2,1)} %pad_maximum_fusion), calls=%async_computation | async-start | bytes 1048576 | tf_op jit(solution)/shard_map/all_to_all | solution.py:43
  15.0 31.8 %collective-permute-start = (bf16[128,896]{1,0:T(8,128)(2,1)S(1)}, bf16[128,896]{1,0:T(8,128)(2,1)S(1)}, u32[]{:S(2)}, u32[]{:S(2)}) collective-permute-start(bf16[128,896]{1,0:T(8,128)(2,1)S(1)} %bitcast.51), channel_id=1, source_target_pairs={{0,0},{1,32},{2,64},{3,96},{4,128},{5,160},{6,192},{7,224},{32,1},... | collective-permute-start | bytes 688136 | tf_op jit(solution)/shard_map/ppermute | solution.py:55
  23.1 23.6 %collective-permute-start.2 = (bf16[128,896]{1,0:T(8,128)(2,1)S(1)}, bf16[128,896]{1,0:T(8,128)(2,1)S(1)}, u32[]{:S(2)}, u32[]{:S(2)}) collective-permute-start(bf16[128,896]{1,0:T(8,128)(2,1)S(1)} %bitcast.52), channel_id=1, source_target_pairs={{0,32},{1,0},{2,96},{3,64},{4,160},{5,128},{6,224},{7,192},{32,33}... | collective-permute-start | bytes 688136 | tf_op jit(solution)/shard_map/ppermute | solution.py:56
  29.3 13.0 %collective-permute-start.1 = (bf16[128,32]{0,1:T(8,128)(2,1)S(1)}, bf16[128,32]{0,1:T(8,128)(2,1)S(1)}, u32[]{:S(2)}, u32[]{:S(2)}) collective-permute-start(bf16[128,32]{0,1:T(8,128)(2,1)S(1)} %pad_maximum_fusion.5), channel_id=1, source_target_pairs={{0,0},{1,32},{2,64},{3,96},{4,128},{5,160},{6,192},{7,224},{32,1},... | collective-permute-start | bytes 24584 | tf_op jit(solution)/shard_map/ppermute | solution.py:58
  38.3 8.3 %collective-permute-start.3 = (bf16[128,32]{0,1:T(8,128)(2,1)S(1)}, bf16[128,32]{0,1:T(8,128)(2,1)S(1)}, u32[]{:S(2)}, u32[]{:S(2)}) collective-permute-start(bf16[128,32]{0,1:T(8,128)(2,1)S(1)} %pad_maximum_fusion.5), channel_id=1, source_target_pairs={{0,32},{1,0},{2,96},{3,64},{4,160},{5,128},{6,224},{7,192},{32,33}... | collective-permute-start | bytes 24584 | tf_op jit(solution)/shard_map/ppermute | solution.py:59
  48.7 40.2 %all-to-all-start.1 = ((bf16[4,2,128,928]{2,3,1,0:T(8,128)(2,1)}), bf16[4,2,128,928]{2,3,1,0:T(8,128)(2,1)S(1)}, u32[]{:S(2)}, u32[]{:S(2)}) async-start(bf16[4,2,128,928]{2,3,1,0:T(8,128)(2,1)} %broadcast_in_dim.36), calls=%async_computation.1 | async-start | bytes 3801088 | tf_op jit(solution)/shard_map/all_to_all | solution.py:63
  91.2 33.5 %all-to-all-start.2 = ((f32[8,32,976]{2,1,0:T(8,128)}), f32[8,32,976]{2,1,0:T(8,128)S(1)}, u32[]{:S(2)}, u32[]{:S(2)}) async-start(f32[8,32,976]{2,1,0:T(8,128)} %maximum_maximum_fusion), calls=%async_computation.2 | async-start | bytes 2097152 | tf_op jit(solution)/shard_map/all_to_all | solution.py:86

commit v26 on v25

--- a/solution.py
+++ b/solution.py
@@ -58,13 +58,14 @@
     own = jnp.concatenate([x_own, lax.ppermute(y_pay, HI + TOK, swap)], axis=1)
     other = jnp.concatenate([x_other, lax.ppermute(y_pay, HI + TOK, mirror)], axis=1)
     even_first = hy_index == 0
-    pair = jnp.stack([jnp.where(even_first, own, other), jnp.where(even_first, other, own)])
+    pair = jnp.stack([own, other])
     spread = jnp.broadcast_to(pair[None], (half_count,) + pair.shape)
     full = lax.all_to_all(spread, "hx", 0, 0, tiled=True)
     x_full = full[..., :span_width]
     y_tok = full[..., span_width:span_width + col_group].astype(jnp.float32) + full[..., span_width + col_group:].astype(jnp.float32)
 
     wins_split = wins.reshape(full.shape[:3] + (wins.shape[1],))
+    wins_split = jnp.where(even_first, wins_split, wins_split[:, ::-1])
     over_tokens = (((0, 1, 2), (0, 1, 2)), ((), ()))
     gram = lax.dot_general(wins_split, x_full, over_tokens, preferred_element_type=jnp.float32)
     cross = lax.dot_general(

time: 127 us -> 127 us (level)
  no operation moved by 1% of the time
where the time goes in v26:
time: 127 us; the launch traced here: 126 us
  starting transfers between devices  59.6 us (47%)
  waiting for transfers between devices  41.9 us (33%)
  blocking collectives  13.6 us (11%)
  local copies, waits for them, and re-layouts  4.84 us (4%)
  other arithmetic  3.38 us (3%)
  matrix products  2.37 us (2%)
    all_to_all x1, waiting for transfers between devices, local(): got = lax.all_to_all(send, ('mp', 'lo'), 0, 0, tiled=True)  26.9 us
    all_to_all x1, starting transfers between devices, local(): full = lax.all_to_all(spread, 'hx', 0, 0, tiled=True)  21.5 us
    all_gather x1, blocking collectives, local(): wins = lax.all_gather(wins, 'tz', axis=0, tiled=True)  11.7 us
    all_to_all x1, starting transfers between devices, local(): got_y = lax.all_to_all(send_y, HI + ('lo',), 1, 1, tiled=True)  10.5 us
    ppermute x1, starting transfers between devices, local(): own = jnp.concatenate([x_own, lax.ppermute(y_pay, HI + TOK, swap)], axis=1)  8.97 us
    ppermute x1, starting transfers between devices, local(): x_own = lax.ppermute(x_local, HI + TOK, swap)  8.17 us
    all_to_all x1, starting transfers between devices, local(): got = lax.all_to_all(send, ('mp', 'lo'), 0, 0, tiled=True)  6.57 us
    all_to_all x1, waiting for transfers between devices, local(): full = lax.all_to_all(spread, 'hx', 0, 0, tiled=True)  4.57 us
  transfers between devices with their start and end apart: 7, of which 5 were waited for; matrix products, arithmetic and copies ran while one was open for 1% of the time, Pallas kernels for 0%

profile of v26, /device:TPU:1, one launch (start us, length us, event | category | flops | bytes accessed | tf_op | source)
XLA Modules:
  0.0 126.5 jit_solution(3320195175853096435)
XLA Ops:
  0.6 0.0 copy-start
  0.6 0.8 slice.44
  1.5 0.1 copy.64
  1.6 0.3 copy-done
  1.8 0.0 copy-start.1
  1.8 1.4 %reduce-precision_convert_fusion = (bf16[128,512]{1,0:T(8,128)(2,1)S(1)}, bf16[128,512]{1,0:T(8,128)(2,1)S(1)}) fusion(bf16[1,512,896]{2,1,0:T(8,128)(2,1)S(1)} %copy-done, bf16[1,128,896]{2,1,0:T(8,128)(2,1)} %param.2), kind=kOutput, calls=%fused_computation.17 | convolution fusion | flops 117702656 | bytes 1409024 | tf_op jit(solution)/shard_map/dot_general | solution.py:35
  3.3 0.1 copy.62
  3.4 0.1 copy.63
  3.6 0.9 pad_maximum_fusion
  4.4 10.5 %all-to-all-start = ((bf16[128,32,64]{0,2,1:T(8,128)(2,1)}), bf16[128,32,64]{0,2,1:T(8,128)(2,1)S(1)}, u32[]{:S(2)}, u32[]{:S(2)}) async-start(bf16[128,32,64]{0,2,1:T(8,128)(2,1)} %pad_maximum_fusion), calls=%async_computation | async-start | bytes 1048576 | tf_op jit(solution)/shard_map/all_to_all | solution.py:43
  14.9 0.0 copy-done.1
  15.0 8.2 %collective-permute-start = (bf16[128,896]{1,0:T(8,128)(2,1)S(1)}, bf16[128,896]{1,0:T(8,128)(2,1)S(1)}, u32[]{:S(2)}, u32[]{:S(2)}) collective-permute-start(bf16[128,896]{1,0:T(8,128)(2,1)S(1)} %bitcast.50), channel_id=1, source_target_pairs={{0,0},{1,32},{2,64},{3,96},{4,128},{5,160},{6,192},{7,224},{32,1},... | collective-permute-start | bytes 688136 | tf_op jit(solution)/shard_map/ppermute | solution.py:55
  23.1 1.9 %collective-permute-start.2 = (bf16[128,896]{1,0:T(8,128)(2,1)S(1)}, bf16[128,896]{1,0:T(8,128)(2,1)S(1)}, u32[]{:S(2)}, u32[]{:S(2)}) collective-permute-start(bf16[128,896]{1,0:T(8,128)(2,1)S(1)} %bitcast.51), channel_id=1, source_target_pairs={{0,32},{1,0},{2,96},{3,64},{4,160},{5,128},{6,224},{7,192},{32,33}... | collective-permute-start | bytes 688136 | tf_op jit(solution)/shard_map/ppermute | solution.py:56
  25.1 4.2 %all-to-all-done = bf16[128,32,64]{0,2,1:T(8,128)(2,1)S(1)} async-done(((bf16[128,32,64]{0,2,1:T(8,128)(2,1)}), bf16[128,32,64]{0,2,1:T(8,128)(2,1)S(1)}, u32[]{:S(2)}, u32[]{:S(2)}) %all-to-all-start) | async-done | bytes 524320 | tf_op jit(solution)/shard_map/all_to_all | solution.py:43
  29.3 9.0 %collective-permute-start.1 = (bf16[128,32]{0,1:T(8,128)(2,1)S(1)}, bf16[128,32]{0,1:T(8,128)(2,1)S(1)}, u32[]{:S(2)}, u32[]{:S(2)}) collective-permute-start(bf16[128,32]{0,1:T(8,128)(2,1)S(1)} %pad_maximum_fusion.3), channel_id=1, source_target_pairs={{0,0},{1,32},{2,64},{3,96},{4,128},{5,160},{6,192},{7,224},{32,1},... | collective-permute-start | bytes 24584 | tf_op jit(solution)/shard_map/ppermute | solution.py:58
  38.3 1.9 %collective-permute-start.3 = (bf16[128,32]{0,1:T(8,128)(2,1)S(1)}, bf16[128,32]{0,1:T(8,128)(2,1)S(1)}, u32[]{:S(2)}, u32[]{:S(2)}) collective-permute-start(bf16[128,32]{0,1:T(8,128)(2,1)S(1)} %pad_maximum_fusion.3), channel_id=1, source_target_pairs={{0,32},{1,0},{2,96},{3,64},{4,160},{5,128},{6,224},{7,192},{32,33}... | collective-permute-start | bytes 24584 | tf_op jit(solution)/shard_map/ppermute | solution.py:59
  40.2 2.0 %collective-permute-done.1 = bf16[128,32]{0,1:T(8,128)(2,1)S(1)} collective-permute-done((bf16[128,32]{0,1:T(8,128)(2,1)S(1)}, bf16[128,32]{0,1:T(8,128)(2,1)S(1)}, u32[]{:S(2)}, u32[]{:S(2)}) %collective-permute-start.1) | collective-permute-done | bytes 8224 | tf_op jit(solution)/shard_map/ppermute | solution.py:58
  42.3 0.1 copy.67
  42.4 4.2 %collective-permute-done.3 = bf16[128,32]{0,1:T(8,128)(2,1)S(1)} collective-permute-done((bf16[128,32]{0,1:T(8,128)(2,1)S(1)}, bf16[128,32]{0,1:T(8,128)(2,1)S(1)}, u32[]{:S(2)}, u32[]{:S(2)}) %collective-permute-start.3) | collective-permute-done | bytes 8224 | tf_op jit(solution)/shard_map/ppermute | solution.py:59
  46.6 0.1 copy.68
  46.7 0.0 collective-permute-done
  46.8 0.0 collective-permute-done.2
  46.8 0.1 pad_maximum_fusion.1
  46.9 0.3 copy.69
  47.1 1.5 %broadcast_in_dim.36 = bf16[4,2,128,928]{2,3,1,0:T(8,128)(2,1)} broadcast(bf16[2,128,928]{1,2,0:T(8,128)(2,1)S(1)} %copy.69), dimensions={1,2,3} | broadcast | bytes 2375680 | tf_op jit(solution)/shard_map/broadcast_in_dim | solution.py:62
  48.7 21.5 %all-to-all-start.1 = ((bf16[4,2,128,928]{2,3,1,0:T(8,128)(2,1)}), bf16[4,2,128,928]{2,3,1,0:T(8,128)(2,1)S(1)}, u32[]{:S(2)}, u32[]{:S(2)}) async-start(bf16[4,2,128,928]{2,3,1,0:T(8,128)(2,1)} %broadcast_in_dim.36), calls=%async_computation.1 | async-start | bytes 3801088 | tf_op jit(solution)/shard_map/all_to_all | solution.py:63
  70.2 1.9 %all_gather.6 = bf16[256,128]{0,1:T(8,128)(2,1)S(1)} all-gather(bf16[128,128]{0,1:T(8,128)(2,1)S(1)} %bitcast.52), channel_id=1, replica_groups=mesh['mp'=2,'hx'=4,'hy'=2,'lo'=4,'tz'=4,'tc'=2] {'tc'}, dimensions={0}, use_global_device_ids=true | all-gather | bytes 98304 | tf_op jit(solution)/shard_map/all_gather | solution.py:49
  72.1 11.7 %all_gather.7 = bf16[1024,128]{0,1:T(8,128)(2,1)S(1)} all-gather(bf16[256,128]{0,1:T(8,128)(2,1)S(1)} %all_gather.6), channel_id=1, replica_groups=mesh['mp'=2,'hx'=4,'hy'=2,'lo'=4,'tz'=4,'tc'=2] {'tz'}, dimensions={0}, use_global_device_ids=true | all-gather | bytes 327680 | tf_op jit(solution)/shard_map/all_gather | solution.py:50
  83.8 0.2 copy.80
  84.0 0.1 multiply_reduce_fusion
  84.1 0.1 copy.73
  84.2 0.1 broadcast_select_fusion
  84.3 0.1 reverse_select_fusion
  84.3 4.6 %all-to-all-done.1 = bf16[4,2,128,928]{2,3,1,0:T(8,128)(2,1)S(1)} async-done(((bf16[4,2,128,928]{2,3,1,0:T(8,128)(2,1)}), bf16[4,2,128,928]{2,3,1,0:T(8,128)(2,1)S(1)}, u32[]{:S(2)}, u32[]{:S(2)}) %all-to-all-start.1) | async-done | bytes 1900576 | tf_op jit(solution)/shard_map/all_to_all | solution.py:63
  88.9 0.2 fusion.5
  89.1 0.1 copy.72
  89.2 0.7 fusion.2
  90.0 1.1 maximum_maximum_fusion
  91.1 6.6 %all-to-all-start.2 = ((f32[8,32,976]{2,1,0:T(8,128)}), f32[8,32,976]{2,1,0:T(8,128)S(1)}, u32[]{:S(2)}, u32[]{:S(2)}) async-start(f32[8,32,976]{2,1,0:T(8,128)} %maximum_maximum_fusion), calls=%async_computation.2 | async-start | bytes 2097152 | tf_op jit(solution)/shard_map/all_to_all | solution.py:87
  97.7 26.9 %all-to-all-done.2 = f32[8,32,976]{2,1,0:T(8,128)S(1)} async-done(((f32[8,32,976]{2,1,0:T(8,128)}), f32[8,32,976]{2,1,0:T(8,128)S(1)}, u32[]{:S(2)}, u32[]{:S(2)}) %all-to-all-start.2) | async-done | bytes 999456 | tf_op jit(solution)/shard_map/all_to_all | solution.py:87
  124.6 0.1 reduce_sum.38
  124.7 0.1 slice_reduce_fusion
  124.8 0.1 fusion.8
  124.9 0.1 copy.75
  125.0 0.1 copy.76
  125.1 0.8 copy.82
  125.9 0.6 add.31
  (15 shorter events, 0.3 us)
Async XLA Ops:
  0.6 1.2 copy-start
  1.8 13.1 %copy-start.1 = (bf16[1,128,896]{2,1,0:T(8,128)(2,1)S(1)}, bf16[1,128,896]{2,1,0:T(8,128)(2,1)}, u32[]{:S(2)}) copy-start(bf16[1,128,896]{2,1,0:T(8,128)(2,1)} %param.2) | copy-start | bytes 688132
  4.4 24.8 %all-to-all-start = ((bf16[128,32,64]{0,2,1:T(8,128)(2,1)}), bf16[128,32,64]{0,2,1:T(8,128)(2,1)S(1)}, u32[]{:S(2)}, u32[]{:S(2)}) async-start(bf16[128,32,64]{0,2,1:T(8,128)(2,1)} %pad_maximum_fusion), calls=%async_computation | async-start | bytes 1048576 | tf_op jit(solution)/shard_map/all_to_all | solution.py:43
  15.0 31.8 %collective-permute-start = (bf16[128,896]{1,0:T(8,128)(2,1)S(1)}, bf16[128,896]{1,0:T(8,128)(2,1)S(1)}, u32[]{:S(2)}, u32[]{:S(2)}) collective-permute-start(bf16[128,896]{1,0:T(8,128)(2,1)S(1)} %bitcast.50), channel_id=1, source_target_pairs={{0,0},{1,32},{2,64},{3,96},{4,128},{5,160},{6,192},{7,224},{32,1},... | collective-permute-start | bytes 688136 | tf_op jit(solution)/shard_map/ppermute | solution.py:55
  23.1 23.6 %collective-permute-start.2 = (bf16[128,896]{1,0:T(8,128)(2,1)S(1)}, bf16[128,896]{1,0:T(8,128)(2,1)S(1)}, u32[]{:S(2)}, u32[]{:S(2)}) collective-permute-start(bf16[128,896]{1,0:T(8,128)(2,1)S(1)} %bitcast.51), channel_id=1, source_target_pairs={{0,32},{1,0},{2,96},{3,64},{4,160},{5,128},{6,224},{7,192},{32,33}... | collective-permute-start | bytes 688136 | tf_op jit(solution)/shard_map/ppermute | solution.py:56
  29.3 13.0 %collective-permute-start.1 = (bf16[128,32]{0,1:T(8,128)(2,1)S(1)}, bf16[128,32]{0,1:T(8,128)(2,1)S(1)}, u32[]{:S(2)}, u32[]{:S(2)}) collective-permute-start(bf16[128,32]{0,1:T(8,128)(2,1)S(1)} %pad_maximum_fusion.3), channel_id=1, source_target_pairs={{0,0},{1,32},{2,64},{3,96},{4,128},{5,160},{6,192},{7,224},{32,1},... | collective-permute-start | bytes 24584 | tf_op jit(solution)/shard_map/ppermute | solution.py:58
  38.3 8.3 %collective-permute-start.3 = (bf16[128,32]{0,1:T(8,128)(2,1)S(1)}, bf16[128,32]{0,1:T(8,128)(2,1)S(1)}, u32[]{:S(2)}, u32[]{:S(2)}) collective-permute-start(bf16[128,32]{0,1:T(8,128)(2,1)S(1)} %pad_maximum_fusion.3), channel_id=1, source_target_pairs={{0,32},{1,0},{2,96},{3,64},{4,160},{5,128},{6,224},{7,192},{32,33}... | collective-permute-start | bytes 24584 | tf_op jit(solution)/shard_map/ppermute | solution.py:59
  48.7 40.2 %all-to-all-start.1 = ((bf16[4,2,128,928]{2,3,1,0:T(8,128)(2,1)}), bf16[4,2,128,928]{2,3,1,0:T(8,128)(2,1)S(1)}, u32[]{:S(2)}, u32[]{:S(2)}) async-start(bf16[4,2,128,928]{2,3,1,0:T(8,128)(2,1)} %broadcast_in_dim.36), calls=%async_computation.1 | async-start | bytes 3801088 | tf_op jit(solution)/shard_map/all_to_all | solution.py:63
  91.1 33.5 %all-to-all-start.2 = ((f32[8,32,976]{2,1,0:T(8,128)}), f32[8,32,976]{2,1,0:T(8,128)S(1)}, u32[]{:S(2)}, u32[]{:S(2)}) async-start(f32[8,32,976]{2,1,0:T(8,128)} %maximum_maximum_fusion), calls=%async_computation.2 | async-start | bytes 2097152 | tf_op jit(solution)/shard_map/all_to_all | solution.py:87

commit v27 on v26

--- a/solution.py
+++ b/solution.py
@@ -59,8 +59,7 @@
     other = jnp.concatenate([x_other, lax.ppermute(y_pay, HI + TOK, mirror)], axis=1)
     even_first = hy_index == 0
     pair = jnp.stack([own, other])
-    spread = jnp.broadcast_to(pair[None], (half_count,) + pair.shape)
-    full = lax.all_to_all(spread, "hx", 0, 0, tiled=True)
+    full = lax.all_gather(pair, "hx", axis=0, tiled=False)
     x_full = full[..., :span_width]
     y_tok = full[..., span_width:span_width + col_group].astype(jnp.float32) + full[..., span_width + col_group:].astype(jnp.float32)
 

time: 127 us -> 146 us (1.15)
  starting transfers between devices: 59.6 us -> 36.9 us
  blocking collectives: 13.6 us -> 31.5 us
  between operations: 0.86 us -> 14.3 us
  waiting for transfers between devices: 41.9 us -> 50.7 us
  matrix products: 2.37 us -> 4.57 us
  local copies, waits for them, and re-layouts: 4.84 us -> 2.9 us
    all_to_all x1 -> x0, starting transfers between devices: 21.5 us -> none  [local(): full = lax.all_to_all(spread, 'hx', 0, 0, tiled=True)]
    all_gather x1, blocking collectives: 11.7 us -> 29.7 us  [local(): wins = lax.all_gather(wins, 'tz', axis=0, tiled=True)]
    all_gather x0 -> x1, waiting for transfers between devices: none -> 17.7 us  [local(): full = lax.all_gather(pair, 'hx', axis=0, tiled=False)]
    all_to_all x1 -> x0, waiting for transfers between devices: 4.57 us -> none  [local(): full = lax.all_to_all(spread, 'hx', 0, 0, tiled=True)]
    ppermute x1, starting transfers between devices: 8.97 us -> 5.45 us  [local(): own = jnp.concatenate([x_own, lax.ppermute(y_pay, HI + TOK, swap)], axis=1)]
    ppermute x1, starting transfers between devices: 1.92 us -> 5.43 us  [local(): lax.ppermute(y_pay, HI + TOK, mirror)]
    ppermute x1, waiting for transfers between devices: 4.21 us -> 2.06 us  [local(): lax.ppermute(y_pay, HI + TOK, mirror)]
    broadcast_in_dim x1 -> x0, local copies, waits for them, and re-layouts: 1.51 us -> none  [local(): spread = jnp.broadcast_to(pair[None], (half_count,) + pair.shape)]
  transfers between devices with their start and end apart: 7 -> 7, of which waited for: 5 -> 5; matrix products, arithmetic and copies ran while one was open for 1% -> 0% of each run, Pallas kernels for 0% -> 0%
where the time goes in v27:
time: 146 us; the launch traced here: 145 us
  waiting for transfers between devices  50.7 us (35%)
  starting transfers between devices  36.9 us (25%)
  blocking collectives  31.5 us (22%)
  between operations  14.3 us (10%)
  matrix products  4.57 us (3%)
  other arithmetic  4.17 us (3%)
  local copies, waits for them, and re-layouts  2.9 us (2%)
    all_gather x1, blocking collectives, local(): wins = lax.all_gather(wins, 'tz', axis=0, tiled=True)  29.7 us
    all_to_all x1, waiting for transfers between devices, local(): got = lax.all_to_all(send, ('mp', 'lo'), 0, 0, tiled=True)  25.4 us
    all_gather x1, waiting for transfers between devices, local(): full = lax.all_gather(pair, 'hx', axis=0, tiled=False)  17.7 us
    all_to_all x1, starting transfers between devices, local(): got_y = lax.all_to_all(send_y, HI + ('lo',), 1, 1, tiled=True)  10.5 us
    ppermute x1, starting transfers between devices, local(): x_own = lax.ppermute(x_local, HI + TOK, swap)  8.17 us
    ppermute x1, starting transfers between devices, local(): own = jnp.concatenate([x_own, lax.ppermute(y_pay, HI + TOK, swap)], axis=1)  5.45 us
    ppermute x1, starting transfers between devices, local(): lax.ppermute(y_pay, HI + TOK, mirror)  5.43 us
    all_to_all x1, starting transfers between devices, local(): got = lax.all_to_all(send, ('mp', 'lo'), 0, 0, tiled=True)  5.41 us
  transfers between devices with their start and end apart: 7, of which 5 were waited for; matrix products, arithmetic and copies ran while one was open for 0% of the time, Pallas kernels for 0%

profile of v27, /device:TPU:1, one launch (start us, length us, event | category | flops | bytes accessed | tf_op | source)
XLA Modules:
  0.0 145.1 jit_solution(16147015643749850093)
XLA Ops:
  7.2 0.0 copy-start
  7.2 1.2 copy.56
  8.4 0.1 copy-done
  8.5 1.4 reduce-precision_convert_fusion
  9.8 0.1 copy.57
  10.0 0.1 copy.58
  10.1 0.9 pad_maximum_fusion
  11.0 10.5 %all-to-all-start = ((bf16[128,32,64]{0,2,1:T(8,128)(2,1)}), bf16[128,32,64]{0,2,1:T(8,128)(2,1)S(1)}, u32[]{:S(2)}, u32[]{:S(2)}) async-start(bf16[128,32,64]{0,2,1:T(8,128)(2,1)} %pad_maximum_fusion), calls=%async_computation | async-start | bytes 1048576 | tf_op jit(solution)/shard_map/all_to_all | solution.py:43
  21.5 0.0 all-gather.3.cloned.1.call-start
  21.5 8.2 %collective-permute-start = (bf16[128,896]{0,1:T(8,128)(2,1)S(1)}, bf16[128,896]{0,1:T(8,128)(2,1)S(1)}, u32[]{:S(2)}, u32[]{:S(2)}) collective-permute-start(bf16[128,896]{0,1:T(8,128)(2,1)S(1)} %bitcast.52), channel_id=1, source_target_pairs={{0,0},{1,32},{2,64},{3,96},{4,128},{5,160},{6,192},{7,224},{32,1},... | collective-permute-start | bytes 688136 | tf_op jit(solution)/shard_map/ppermute | solution.py:55
  29.7 1.9 %collective-permute-start.2 = (bf16[128,896]{0,1:T(8,128)(2,1)S(1)}, bf16[128,896]{0,1:T(8,128)(2,1)S(1)}, u32[]{:S(2)}, u32[]{:S(2)}) collective-permute-start(bf16[128,896]{0,1:T(8,128)(2,1)S(1)} %bitcast.53), channel_id=1, source_target_pairs={{0,32},{1,0},{2,96},{3,64},{4,160},{5,128},{6,224},{7,192},{32,33}... | collective-permute-start | bytes 688136 | tf_op jit(solution)/shard_map/ppermute | solution.py:56
  31.7 4.1 %all-to-all-done = bf16[128,32,64]{0,2,1:T(8,128)(2,1)S(1)} async-done(((bf16[128,32,64]{0,2,1:T(8,128)(2,1)}), bf16[128,32,64]{0,2,1:T(8,128)(2,1)S(1)}, u32[]{:S(2)}, u32[]{:S(2)}) %all-to-all-start) | async-done | bytes 524320 | tf_op jit(solution)/shard_map/all_to_all | solution.py:43
  35.9 5.4 %collective-permute-start.3 = (bf16[128,32]{0,1:T(8,128)(2,1)S(1)}, bf16[128,32]{0,1:T(8,128)(2,1)S(1)}, u32[]{:S(2)}, u32[]{:S(2)}) collective-permute-start(bf16[128,32]{0,1:T(8,128)(2,1)S(1)} %pad_maximum_fusion.3), channel_id=1, source_target_pairs={{0,32},{1,0},{2,96},{3,64},{4,160},{5,128},{6,224},{7,192},{32,33}... | collective-permute-start | bytes 24584 | tf_op jit(solution)/shard_map/ppermute | solution.py:59
  41.3 5.5 %collective-permute-start.1 = (bf16[128,32]{0,1:T(8,128)(2,1)S(1)}, bf16[128,32]{0,1:T(8,128)(2,1)S(1)}, u32[]{:S(2)}, u32[]{:S(2)}) collective-permute-start(bf16[128,32]{0,1:T(8,128)(2,1)S(1)} %pad_maximum_fusion.3), channel_id=1, source_target_pairs={{0,0},{1,32},{2,64},{3,96},{4,128},{5,160},{6,192},{7,224},{32,1},... | collective-permute-start | bytes 24584 | tf_op jit(solution)/shard_map/ppermute | solution.py:58
  46.8 0.0 collective-permute-done.2
  46.8 2.1 %collective-permute-done.3 = bf16[128,32]{0,1:T(8,128)(2,1)S(1)} collective-permute-done((bf16[128,32]{0,1:T(8,128)(2,1)S(1)}, bf16[128,32]{0,1:T(8,128)(2,1)S(1)}, u32[]{:S(2)}, u32[]{:S(2)}) %collective-permute-start.3) | collective-permute-done | bytes 8224 | tf_op jit(solution)/shard_map/ppermute | solution.py:59
  48.9 0.0 collective-permute-done
  48.9 1.3 collective-permute-done.1
  50.2 0.9 pad_maximum_fusion.2
  51.1 0.0 all-gather.3.cloned.1.call-update
  51.2 1.9 %all_gather.12 = bf16[256,128]{0,1:T(8,128)(2,1)S(1)} all-gather(bf16[128,128]{0,1:T(8,128)(2,1)S(1)} %bitcast.54), channel_id=1, replica_groups=mesh['mp'=2,'hx'=4,'hy'=2,'lo'=4,'tz'=4,'tc'=2] {'tc'}, dimensions={0}, use_global_device_ids=true | all-gather | bytes 98304 | tf_op jit(solution)/shard_map/all_gather | solution.py:49
  53.0 29.7 %all_gather.13 = bf16[1024,128]{0,1:T(8,128)(2,1)S(1)} all-gather(bf16[256,128]{0,1:T(8,128)(2,1)S(1)} %all_gather.12), channel_id=1, replica_groups=mesh['mp'=2,'hx'=4,'hy'=2,'lo'=4,'tz'=4,'tc'=2] {'tz'}, dimensions={0}, use_global_device_ids=true | all-gather | bytes 327680 | tf_op jit(solution)/shard_map/all_gather | solution.py:50
  82.7 0.2 copy.72
  82.9 0.1 multiply_reduce_fusion
  83.1 0.1 copy.64
  83.1 0.1 broadcast_select_fusion
  83.2 0.1 reverse_select_fusion
  83.3 17.7 %all-gather.3.cloned.1.call-done = bf16[8,128,928]{1,2,0:T(8,128)(2,1)} async-done(((bf16[2,128,928]{1,2,0:T(8,128)(2,1)}), bf16[8,128,928]{1,2,0:T(8,128)(2,1)}) %all-gather.3.cloned.1.call-update) | async-done | bytes 1900560 | tf_op jit(solution)/shard_map/all_gather | solution.py:62
  101.0 1.0 fusion.5
  102.0 2.2 %fusion.2 = f32[128,896]{1,0:T(8,128)S(1)} fusion(bf16[4,2,128,128]{3,2,1,0:T(8,128)(2,1)S(1)} %reverse_select_fusion, bf16[4,2,128,928]{2,3,1,0:T(8,128)(2,1)} %bitcast.57), kind=kOutput, calls=%fused_computation.2 | convolution fusion | flops 234881024 | bytes 2555904 | tf_op jit(solution)/shard_map/dot_general | solution.py:69
  104.2 0.1 copy.63
  104.3 0.1 pad_maximum_fusion.1
  104.4 1.1 maximum_maximum_fusion
  105.5 5.4 %all-to-all-start.1 = ((f32[8,32,976]{2,1,0:T(8,128)}), f32[8,32,976]{2,1,0:T(8,128)S(1)}, u32[]{:S(2)}, u32[]{:S(2)}) async-start(f32[8,32,976]{2,1,0:T(8,128)} %maximum_maximum_fusion), calls=%async_computation.1 | async-start | bytes 2097152 | tf_op jit(solution)/shard_map/all_to_all | solution.py:86
  110.9 25.4 %all-to-all-done.1 = f32[8,32,976]{2,1,0:T(8,128)S(1)} async-done(((f32[8,32,976]{2,1,0:T(8,128)}), f32[8,32,976]{2,1,0:T(8,128)S(1)}, u32[]{:S(2)}, u32[]{:S(2)}) %all-to-all-start.1) | async-done | bytes 999456 | tf_op jit(solution)/shard_map/all_to_all | solution.py:86
  136.4 0.1 reduce_sum.38
  136.5 0.1 slice_reduce_fusion
  136.6 0.1 fusion.8
  136.7 0.1 copy.66
  136.7 0.1 copy.67
  136.8 0.8 copy.73
  137.6 0.6 add.31
  (15 shorter events, 0.2 us)
Async XLA Ops:
  7.2 1.3 copy-start
  11.0 24.8 %all-to-all-start = ((bf16[128,32,64]{0,2,1:T(8,128)(2,1)}), bf16[128,32,64]{0,2,1:T(8,128)(2,1)S(1)}, u32[]{:S(2)}, u32[]{:S(2)}) async-start(bf16[128,32,64]{0,2,1:T(8,128)(2,1)} %pad_maximum_fusion), calls=%async_computation | async-start | bytes 1048576 | tf_op jit(solution)/shard_map/all_to_all | solution.py:43
  21.5 79.5 %all-gather.3.cloned.1.call-start = ((), (), s32[]{:S(2)}) async-start(), calls=%async_computation.2 | async-start | bytes 2375680 | tf_op jit(solution)/shard_map/all_gather | solution.py:62
  21.5 27.3 %collective-permute-start = (bf16[128,896]{0,1:T(8,128)(2,1)S(1)}, bf16[128,896]{0,1:T(8,128)(2,1)S(1)}, u32[]{:S(2)}, u32[]{:S(2)}) collective-permute-start(bf16[128,896]{0,1:T(8,128)(2,1)S(1)} %bitcast.52), channel_id=1, source_target_pairs={{0,0},{1,32},{2,64},{3,96},{4,128},{5,160},{6,192},{7,224},{32,1},... | collective-permute-start | bytes 688136 | tf_op jit(solution)/shard_map/ppermute | solution.py:55
  29.7 17.0 %collective-permute-start.2 = (bf16[128,896]{0,1:T(8,128)(2,1)S(1)}, bf16[128,896]{0,1:T(8,128)(2,1)S(1)}, u32[]{:S(2)}, u32[]{:S(2)}) collective-permute-start(bf16[128,896]{0,1:T(8,128)(2,1)S(1)} %bitcast.53), channel_id=1, source_target_pairs={{0,32},{1,0},{2,96},{3,64},{4,160},{5,128},{6,224},{7,192},{32,33}... | collective-permute-start | bytes 688136 | tf_op jit(solution)/shard_map/ppermute | solution.py:56
  35.9 13.0 %collective-permute-start.3 = (bf16[128,32]{0,1:T(8,128)(2,1)S(1)}, bf16[128,32]{0,1:T(8,128)(2,1)S(1)}, u32[]{:S(2)}, u32[]{:S(2)}) collective-permute-start(bf16[128,32]{0,1:T(8,128)(2,1)S(1)} %pad_maximum_fusion.3), channel_id=1, source_target_pairs={{0,32},{1,0},{2,96},{3,64},{4,160},{5,128},{6,224},{7,192},{32,33}... | collective-permute-start | bytes 24584 | tf_op jit(solution)/shard_map/ppermute | solution.py:59
  41.3 8.9 %collective-permute-start.1 = (bf16[128,32]{0,1:T(8,128)(2,1)S(1)}, bf16[128,32]{0,1:T(8,128)(2,1)S(1)}, u32[]{:S(2)}, u32[]{:S(2)}) collective-permute-start(bf16[128,32]{0,1:T(8,128)(2,1)S(1)} %pad_maximum_fusion.3), channel_id=1, source_target_pairs={{0,0},{1,32},{2,64},{3,96},{4,128},{5,160},{6,192},{7,224},{32,1},... | collective-permute-start | bytes 24584 | tf_op jit(solution)/shard_map/ppermute | solution.py:58
  105.5 30.8 %all-to-all-start.1 = ((f32[8,32,976]{2,1,0:T(8,128)}), f32[8,32,976]{2,1,0:T(8,128)S(1)}, u32[]{:S(2)}, u32[]{:S(2)}) async-start(f32[8,32,976]{2,1,0:T(8,128)} %maximum_maximum_fusion), calls=%async_computation.1 | async-start | bytes 2097152 | tf_op jit(solution)/shard_map/all_to_all | solution.py:86
Sparse Core Ops, SparseCore 0:
  51.2 49.7 all-gather.2

commit v28 on v26

--- a/solution.py
+++ b/solution.py
@@ -46,8 +46,9 @@
         axis=1,
     )
     win_lo = lax.dynamic_slice_in_dim(got_y[:, :, 2 * col_group:], hi_index * group, group, 1)
-    wins = lax.all_gather(win_lo.reshape(tokens, group * ROW_DEV), "tc", axis=0, tiled=True)
-    wins = lax.all_gather(wins, "tz", axis=0, tiled=True)
+    wins = lax.all_gather(win_lo.reshape(tokens, group * ROW_DEV), "tz", axis=0, tiled=False)
+    wins = lax.all_gather(wins, "tc", axis=1, tiled=False)
+    wins = wins.reshape(tok_count * tokens, group * ROW_DEV)
     y_round = lax.reduce_precision(y_mine, exponent_bits=8, mantissa_bits=7)
     y_high = y_round.astype(jnp.bfloat16)
     y_low = (y_mine - y_round).astype(jnp.bfloat16)

time: 127 us -> 127 us (level)
  no operation moved by 1% of the time
where the time goes in v28:
time: 127 us; the launch traced here: 126 us
  starting transfers between devices  59.6 us (47%)
  waiting for transfers between devices  42 us (33%)
  blocking collectives  13.5 us (11%)
  local copies, waits for them, and re-layouts  4.78 us (4%)
  other arithmetic  3.47 us (3%)
  matrix products  2.37 us (2%)
    all_to_all x1, waiting for transfers between devices, local(): got = lax.all_to_all(send, ('mp', 'lo'), 0, 0, tiled=True)  26.9 us
    all_to_all x1, starting transfers between devices, local(): full = lax.all_to_all(spread, 'hx', 0, 0, tiled=True)  21.5 us
    all_gather x1, blocking collectives, local(): lax.all_gather(win_lo.reshape(tokens, group * ROW_DEV), 'tz', axis=0, til...  11.5 us
    all_to_all x1, starting transfers between devices, local(): got_y = lax.all_to_all(send_y, HI + ('lo',), 1, 1, tiled=True)  10.5 us
    ppermute x1, starting transfers between devices, local(): own = jnp.concatenate([x_own, lax.ppermute(y_pay, HI + TOK, swap)], axis=1)  8.97 us
    ppermute x1, starting transfers between devices, local(): x_own = lax.ppermute(x_local, HI + TOK, swap)  8.17 us
    all_to_all x1, starting transfers between devices, local(): got = lax.all_to_all(send, ('mp', 'lo'), 0, 0, tiled=True)  6.57 us
    all_to_all x1, waiting for transfers between devices, local(): full = lax.all_to_all(spread, 'hx', 0, 0, tiled=True)  4.6 us
  transfers between devices with their start and end apart: 7, of which 5 were waited for; matrix products, arithmetic and copies ran while one was open for 1% of the time, Pallas kernels for 0%

profile of v28, /device:TPU:1, one launch (start us, length us, event | category | flops | bytes accessed | tf_op | source)
XLA Modules:
  0.0 126.5 jit_solution(9991669376370768524)
XLA Ops:
  0.6 0.0 copy-start
  0.6 0.8 slice.44
  1.5 0.1 copy.73
  1.6 0.3 copy-done
  1.8 0.0 copy-start.1
  1.8 1.4 %reduce-precision_convert_fusion = (bf16[128,512]{1,0:T(8,128)(2,1)S(1)}, bf16[128,512]{1,0:T(8,128)(2,1)S(1)}) fusion(bf16[1,512,896]{2,1,0:T(8,128)(2,1)S(1)} %copy-done, bf16[1,128,896]{2,1,0:T(8,128)(2,1)} %param.2), kind=kOutput, calls=%fused_computation.18 | convolution fusion | flops 117702656 | bytes 1409024 | tf_op jit(solution)/shard_map/dot_general | solution.py:35
  3.3 0.1 copy.71
  3.4 0.1 copy.72
  3.6 0.9 pad_maximum_fusion
  4.4 10.5 %all-to-all-start = ((bf16[128,32,64]{0,2,1:T(8,128)(2,1)}), bf16[128,32,64]{0,2,1:T(8,128)(2,1)S(1)}, u32[]{:S(2)}, u32[]{:S(2)}) async-start(bf16[128,32,64]{0,2,1:T(8,128)(2,1)} %pad_maximum_fusion), calls=%async_computation | async-start | bytes 1048576 | tf_op jit(solution)/shard_map/all_to_all | solution.py:43
  14.9 0.0 copy-done.1
  15.0 8.2 %collective-permute-start = (bf16[128,896]{1,0:T(8,128)(2,1)S(1)}, bf16[128,896]{1,0:T(8,128)(2,1)S(1)}, u32[]{:S(2)}, u32[]{:S(2)}) collective-permute-start(bf16[128,896]{1,0:T(8,128)(2,1)S(1)} %bitcast.52), channel_id=1, source_target_pairs={{0,0},{1,32},{2,64},{3,96},{4,128},{5,160},{6,192},{7,224},{32,1},... | collective-permute-start | bytes 688136 | tf_op jit(solution)/shard_map/ppermute | solution.py:56
  23.1 1.9 %collective-permute-start.2 = (bf16[128,896]{1,0:T(8,128)(2,1)S(1)}, bf16[128,896]{1,0:T(8,128)(2,1)S(1)}, u32[]{:S(2)}, u32[]{:S(2)}) collective-permute-start(bf16[128,896]{1,0:T(8,128)(2,1)S(1)} %bitcast.53), channel_id=1, source_target_pairs={{0,32},{1,0},{2,96},{3,64},{4,160},{5,128},{6,224},{7,192},{32,33}... | collective-permute-start | bytes 688136 | tf_op jit(solution)/shard_map/ppermute | solution.py:57
  25.1 4.2 %all-to-all-done = bf16[128,32,64]{0,2,1:T(8,128)(2,1)S(1)} async-done(((bf16[128,32,64]{0,2,1:T(8,128)(2,1)}), bf16[128,32,64]{0,2,1:T(8,128)(2,1)S(1)}, u32[]{:S(2)}, u32[]{:S(2)}) %all-to-all-start) | async-done | bytes 524320 | tf_op jit(solution)/shard_map/all_to_all | solution.py:43
  29.3 9.0 %collective-permute-start.1 = (bf16[128,32]{0,1:T(8,128)(2,1)S(1)}, bf16[128,32]{0,1:T(8,128)(2,1)S(1)}, u32[]{:S(2)}, u32[]{:S(2)}) collective-permute-start(bf16[128,32]{0,1:T(8,128)(2,1)S(1)} %pad_maximum_fusion.3), channel_id=1, source_target_pairs={{0,0},{1,32},{2,64},{3,96},{4,128},{5,160},{6,192},{7,224},{32,1},... | collective-permute-start | bytes 24584 | tf_op jit(solution)/shard_map/ppermute | solution.py:59
  38.3 1.9 %collective-permute-start.3 = (bf16[128,32]{0,1:T(8,128)(2,1)S(1)}, bf16[128,32]{0,1:T(8,128)(2,1)S(1)}, u32[]{:S(2)}, u32[]{:S(2)}) collective-permute-start(bf16[128,32]{0,1:T(8,128)(2,1)S(1)} %pad_maximum_fusion.3), channel_id=1, source_target_pairs={{0,32},{1,0},{2,96},{3,64},{4,160},{5,128},{6,224},{7,192},{32,33}... | collective-permute-start | bytes 24584 | tf_op jit(solution)/shard_map/ppermute | solution.py:60
  40.2 2.0 %collective-permute-done.1 = bf16[128,32]{0,1:T(8,128)(2,1)S(1)} collective-permute-done((bf16[128,32]{0,1:T(8,128)(2,1)S(1)}, bf16[128,32]{0,1:T(8,128)(2,1)S(1)}, u32[]{:S(2)}, u32[]{:S(2)}) %collective-permute-start.1) | collective-permute-done | bytes 8224 | tf_op jit(solution)/shard_map/ppermute | solution.py:59
  42.3 0.1 copy.75
  42.4 4.2 %collective-permute-done.3 = bf16[128,32]{0,1:T(8,128)(2,1)S(1)} collective-permute-done((bf16[128,32]{0,1:T(8,128)(2,1)S(1)}, bf16[128,32]{0,1:T(8,128)(2,1)S(1)}, u32[]{:S(2)}, u32[]{:S(2)}) %collective-permute-start.3) | collective-permute-done | bytes 8224 | tf_op jit(solution)/shard_map/ppermute | solution.py:60
  46.6 0.1 copy.76
  46.7 0.0 collective-permute-done
  46.8 0.0 collective-permute-done.2
  46.8 0.1 pad_maximum_fusion.1
  46.9 0.3 copy.77
  47.1 1.5 %broadcast_in_dim.36 = bf16[4,2,128,928]{2,3,1,0:T(8,128)(2,1)} broadcast(bf16[2,128,928]{1,2,0:T(8,128)(2,1)S(1)} %copy.77), dimensions={1,2,3} | broadcast | bytes 2375680 | tf_op jit(solution)/shard_map/broadcast_in_dim | solution.py:63
  48.7 21.5 %all-to-all-start.1 = ((bf16[4,2,128,928]{2,3,1,0:T(8,128)(2,1)}), bf16[4,2,128,928]{2,3,1,0:T(8,128)(2,1)S(1)}, u32[]{:S(2)}, u32[]{:S(2)}) async-start(bf16[4,2,128,928]{2,3,1,0:T(8,128)(2,1)} %broadcast_in_dim.36), calls=%async_computation.1 | async-start | bytes 3801088 | tf_op jit(solution)/shard_map/all_to_all | solution.py:64
  70.2 0.1 copy.74
  70.3 11.5 %all_gather.9 = bf16[4,128,128]{2,1,0:T(8,128)(2,1)S(1)} all-gather(bf16[1,128,128]{2,1,0:T(8,128)(2,1)S(1)} %copy.74), channel_id=1, replica_groups=mesh['mp'=2,'hx'=4,'hy'=2,'lo'=4,'tz'=4,'tc'=2] {'tz'}, dimensions={0}, use_global_device_ids=true | all-gather | bytes 163840 | tf_op jit(solution)/shard_map/all_gather | solution.py:49
  81.9 2.0 %all-gather = bf16[4,256,128]{2,1,0:T(8,128)(2,1)S(1)} all-gather(bf16[4,128,128]{2,1,0:T(8,128)(2,1)S(1)} %all_gather.9), channel_id=2, replica_groups=mesh['mp'=2,'hx'=4,'hy'=2,'lo'=4,'tz'=4,'tc'=2] {'tc'}, dimensions={1}, use_global_device_ids=true | all-gather | bytes 393216 | tf_op jit(solution)/shard_map/all_gather | solution.py:50
  83.8 0.2 multiply_reduce_fusion
  84.1 0.1 copy.81
  84.1 0.1 broadcast_select_fusion
  84.2 0.1 reverse_select_fusion
  84.3 4.6 %all-to-all-done.1 = bf16[4,2,128,928]{2,3,1,0:T(8,128)(2,1)S(1)} async-done(((bf16[4,2,128,928]{2,3,1,0:T(8,128)(2,1)}), bf16[4,2,128,928]{2,3,1,0:T(8,128)(2,1)S(1)}, u32[]{:S(2)}, u32[]{:S(2)}) %all-to-all-start.1) | async-done | bytes 1900576 | tf_op jit(solution)/shard_map/all_to_all | solution.py:64
  88.9 0.2 fusion.5
  89.1 0.1 copy.80
  89.2 0.7 fusion.2
  90.0 1.1 maximum_maximum_fusion
  91.1 6.6 %all-to-all-start.2 = ((f32[8,32,976]{2,1,0:T(8,128)}), f32[8,32,976]{2,1,0:T(8,128)S(1)}, u32[]{:S(2)}, u32[]{:S(2)}) async-start(f32[8,32,976]{2,1,0:T(8,128)} %maximum_maximum_fusion), calls=%async_computation.2 | async-start | bytes 2097152 | tf_op jit(solution)/shard_map/all_to_all | solution.py:88
  97.7 26.9 %all-to-all-done.2 = f32[8,32,976]{2,1,0:T(8,128)S(1)} async-done(((f32[8,32,976]{2,1,0:T(8,128)}), f32[8,32,976]{2,1,0:T(8,128)S(1)}, u32[]{:S(2)}, u32[]{:S(2)}) %all-to-all-start.2) | async-done | bytes 999456 | tf_op jit(solution)/shard_map/all_to_all | solution.py:88
  124.6 0.1 reduce_sum.38
  124.7 0.1 slice_reduce_fusion
  124.8 0.1 fusion.8
  124.9 0.1 copy.83
  125.0 0.1 copy.84
  125.1 0.8 copy.89
  125.9 0.6 add.31
  (15 shorter events, 0.3 us)
Async XLA Ops:
  0.6 1.2 copy-start
  1.8 13.1 %copy-start.1 = (bf16[1,128,896]{2,1,0:T(8,128)(2,1)S(1)}, bf16[1,128,896]{2,1,0:T(8,128)(2,1)}, u32[]{:S(2)}) copy-start(bf16[1,128,896]{2,1,0:T(8,128)(2,1)} %param.2) | copy-start | bytes 688132
  4.4 24.8 %all-to-all-start = ((bf16[128,32,64]{0,2,1:T(8,128)(2,1)}), bf16[128,32,64]{0,2,1:T(8,128)(2,1)S(1)}, u32[]{:S(2)}, u32[]{:S(2)}) async-start(bf16[128,32,64]{0,2,1:T(8,128)(2,1)} %pad_maximum_fusion), calls=%async_computation | async-start | bytes 1048576 | tf_op jit(solution)/shard_map/all_to_all | solution.py:43
  15.0 31.8 %collective-permute-start = (bf16[128,896]{1,0:T(8,128)(2,1)S(1)}, bf16[128,896]{1,0:T(8,128)(2,1)S(1)}, u32[]{:S(2)}, u32[]{:S(2)}) collective-permute-start(bf16[128,896]{1,0:T(8,128)(2,1)S(1)} %bitcast.52), channel_id=1, source_target_pairs={{0,0},{1,32},{2,64},{3,96},{4,128},{5,160},{6,192},{7,224},{32,1},... | collective-permute-start | bytes 688136 | tf_op jit(solution)/shard_map/ppermute | solution.py:56
  23.1 23.6 %collective-permute-start.2 = (bf16[128,896]{1,0:T(8,128)(2,1)S(1)}, bf16[128,896]{1,0:T(8,128)(2,1)S(1)}, u32[]{:S(2)}, u32[]{:S(2)}) collective-permute-start(bf16[128,896]{1,0:T(8,128)(2,1)S(1)} %bitcast.53), channel_id=1, source_target_pairs={{0,32},{1,0},{2,96},{3,64},{4,160},{5,128},{6,224},{7,192},{32,33}... | collective-permute-start | bytes 688136 | tf_op jit(solution)/shard_map/ppermute | solution.py:57
  29.3 13.0 %collective-permute-start.1 = (bf16[128,32]{0,1:T(8,128)(2,1)S(1)}, bf16[128,32]{0,1:T(8,128)(2,1)S(1)}, u32[]{:S(2)}, u32[]{:S(2)}) collective-permute-start(bf16[128,32]{0,1:T(8,128)(2,1)S(1)} %pad_maximum_fusion.3), channel_id=1, source_target_pairs={{0,0},{1,32},{2,64},{3,96},{4,128},{5,160},{6,192},{7,224},{32,1},... | collective-permute-start | bytes 24584 | tf_op jit(solution)/shard_map/ppermute | solution.py:59
  38.3 8.3 %collective-permute-start.3 = (bf16[128,32]{0,1:T(8,128)(2,1)S(1)}, bf16[128,32]{0,1:T(8,128)(2,1)S(1)}, u32[]{:S(2)}, u32[]{:S(2)}) collective-permute-start(bf16[128,32]{0,1:T(8,128)(2,1)S(1)} %pad_maximum_fusion.3), channel_id=1, source_target_pairs={{0,32},{1,0},{2,96},{3,64},{4,160},{5,128},{6,224},{7,192},{32,33}... | collective-permute-start | bytes 24584 | tf_op jit(solution)/shard_map/ppermute | solution.py:60
  48.7 40.2 %all-to-all-start.1 = ((bf16[4,2,128,928]{2,3,1,0:T(8,128)(2,1)}), bf16[4,2,128,928]{2,3,1,0:T(8,128)(2,1)S(1)}, u32[]{:S(2)}, u32[]{:S(2)}) async-start(bf16[4,2,128,928]{2,3,1,0:T(8,128)(2,1)} %broadcast_in_dim.36), calls=%async_computation.1 | async-start | bytes 3801088 | tf_op jit(solution)/shard_map/all_to_all | solution.py:64
  91.1 33.5 %all-to-all-start.2 = ((f32[8,32,976]{2,1,0:T(8,128)}), f32[8,32,976]{2,1,0:T(8,128)S(1)}, u32[]{:S(2)}, u32[]{:S(2)}) async-start(f32[8,32,976]{2,1,0:T(8,128)} %maximum_maximum_fusion), calls=%async_computation.2 | async-start | bytes 2097152 | tf_op jit(solution)/shard_map/all_to_all | solution.py:88
